TPU v7x, 32 devices: a whole 2x2x4 slice. The times are simulated.
32 devices in a mesh: wide: 8 (over z, x), narrow: 4 (over y, core).
Axes of the slice: x: 2, y: 2, z: 4, core: 2. Of those that a mesh axis runs over, the one named last changes fastest.
Arguments:
- tokens_in: bfloat16 [8192, 2048], P(('wide', 'narrow')), may hold values from -6 to 6
- segment_starts: int32 [8192], P(('wide', 'narrow')), may hold values 0 or 1
- cotangent: bfloat16 [8192, 2048], P(('wide', 'narrow')), may hold values from -6 to 6
- norm1_gain: bfloat16 [2048], P(('wide', 'narrow')), may hold values from 0.25 to 1.75
- rec_gate_weight: bfloat16 [2048, 2560], P(('wide', 'narrow')), may hold values from -0.125 to 0.125
- rec_in_weight: bfloat16 [2048, 2560], P(('wide', 'narrow')), may hold values from -0.125 to 0.125
- conv_weight: bfloat16 [2560, 4], P(('wide', 'narrow')), may hold values from -3 to 3
- conv_bias: bfloat16 [2560], P(('wide', 'narrow')), may hold values from -3 to 3
- gate_a_weight: bfloat16 [2560, 160], P(('wide', 'narrow')), may hold values from -0.5 to 0.5
- gate_a_bias: bfloat16 [2560], P(('wide', 'narrow')), may hold values from -4 to 4
- gate_x_weight: bfloat16 [2560, 160], P(('wide', 'narrow')), may hold values from -0.5 to 0.5
- gate_x_bias: bfloat16 [2560], P(('wide', 'narrow')), may hold values from -4 to 4
- decay_rate: bfloat16 [2560], P(('wide', 'narrow')), may hold values from 7.772446e-05 to 0.049804688
- rec_out_weight: bfloat16 [2560, 2048], P(('wide', 'narrow')), may hold values from -0.125 to 0.125
- norm2_gain: bfloat16 [2048], P(('wide', 'narrow')), may hold values from 0.25 to 1.75
- mlp_gate_weight: bfloat16 [2048, 6144], P(('wide', 'narrow')), may hold values from -0.125 to 0.125
- mlp_up_weight: bfloat16 [2048, 6144], P(('wide', 'narrow')), may hold values from -0.125 to 0.125
- mlp_down_weight: bfloat16 [6144, 2048], P(('wide', 'narrow')), may hold values from -0.078125 to 0.078125
Outputs:
- layer_out: bfloat16 [8192, 2048], P(('wide', 'narrow'))
- grad_tokens: float32 [8192, 2048], P(('wide', 'narrow'))
- grad_norm1_gain: float32 [2048], P(('wide', 'narrow'))
- grad_rec_gate_weight: float32 [2048, 2560], P(('wide', 'narrow'))
- grad_rec_in_weight: float32 [2048, 2560], P(('wide', 'narrow'))
- grad_conv_weight: float32 [2560, 4], P(('wide', 'narrow'))
- grad_conv_bias: float32 [2560], P(('wide', 'narrow'))
- grad_gate_a_weight: float32 [2560, 160], P(('wide', 'narrow'))
- grad_gate_a_bias: float32 [2560], P(('wide', 'narrow'))
- grad_gate_x_weight: float32 [2560, 160], P(('wide', 'narrow'))
- grad_gate_x_bias: float32 [2560], P(('wide', 'narrow'))
- grad_decay_rate: float32 [2560], P(('wide', 'narrow'))
- grad_rec_out_weight: float32 [2560, 2048], P(('wide', 'narrow'))
- grad_norm2_gain: float32 [2048], P(('wide', 'narrow'))
- grad_mlp_gate_weight: float32 [2048, 6144], P(('wide', 'narrow'))
- grad_mlp_up_weight: float32 [2048, 6144], P(('wide', 'narrow'))
- grad_mlp_down_weight: float32 [6144, 2048], P(('wide', 'narrow'))
Inputs may be any that keep to these rules, and one draw needn't show every extreme that they name: `segment_starts`: documents run on across the boundaries between devices.
All inputs are finite; a program needn't handle non-finite values.
Results may differ from a plain program's by a relative error of at most 0.011.
Values may be sent and summed in bfloat16 or wider, within the bound.
A program may use at most 512 MiB of HBM per device.

v0:
```python
import jax
import jax.numpy as jnp
from jax import lax
from jax.sharding import PartitionSpec as P

NB = 16
BLK = 160
CONV = 4


norm_eps = 1e-06
decay_scale = 8.0
push_shift = 0.05
contract_last = (((1,), (1,)), ((), ()))
contract_first = (((0,), (0,)), ((), ()))


def shifted(block, axis, distance):
    devices = range(lax.axis_size(axis))
    route = [(i - distance, i) for i in devices if i - distance in devices]
    return lax.ppermute(block, axis, route)


def carried_in(part, axis, combine, identity, reverse):
    count = lax.axis_size(axis)
    place = lax.axis_index(axis)
    ahead = count - 1 - place if reverse else place
    gathered = jax.tree.map(lambda a: lax.all_gather(a, axis), part)
    state = jax.tree.map(lambda a, e: jnp.zeros_like(a) + jnp.asarray(e, a.dtype), part, identity)

    def one(hop, state):
        source = count - 1 - hop if reverse else hop
        return combine(
            state, jax.tree.map(lambda a: lax.dynamic_index_in_dim(a, source, 0, False), gathered)
        )

    return lax.fori_loop(0, ahead, one, state)


def rms_scale(tok_rows, gain):
    return (
        tok_rows
        * lax.rsqrt(jnp.mean(tok_rows * tok_rows, axis=-1, keepdims=True) + norm_eps)
        * gain
    )


def gelu_tanh(values):
    return jax.nn.gelu(values, approximate=True)


def gated_unit(gate_vals, up_vals):
    return gelu_tanh(gate_vals) * up_vals


def combine_pairs(earlier, later):
    return (earlier[0] * later[0], later[0] * earlier[1] + later[1])


def conv_apply(extended, conv_taps, conv_offset, ids_ext, seg_local):
    row_total = seg_local.shape[0]
    tap_total = conv_taps.shape[1]
    summed = jnp.zeros((row_total, conv_taps.shape[0]), jnp.float32) + conv_offset
    for tap_index in range(tap_total):
        begin = tap_total - 1 - tap_index
        window = extended[begin : begin + row_total]
        same_doc = (ids_ext[begin : begin + row_total] == seg_local).astype(jnp.float32)
        summed = summed + conv_taps[:, tap_index] * window * same_doc[:, None]
    return summed


def gate_math(logit_a, logit_b, conved, rates, open_mask):
    gate_a = jax.nn.sigmoid(logit_a)
    gate_x = jax.nn.sigmoid(logit_b)
    decay = jnp.exp(-decay_scale * gate_a * rates)
    keep_all = decay * open_mask
    push_all = jnp.sqrt(1.0 - decay * decay + push_shift) * gate_x * conved
    return (keep_all, push_all)


def on_device(
    tokens_in,
    segment_starts,
    cotangent,
    norm1_gain,
    rec_gate_weight,
    rec_in_weight,
    conv_weight,
    conv_bias,
    gate_a_weight,
    gate_a_bias,
    gate_x_weight,
    gate_x_bias,
    decay_rate,
    rec_out_weight,
    norm2_gain,
    mlp_gate_weight,
    mlp_up_weight,
    mlp_down_weight,
):
    block_set = (
        lax.all_gather(norm1_gain, ("wide", "narrow"), axis=0, tiled=True),
        lax.all_gather(rec_gate_weight, ("wide", "narrow"), axis=0, tiled=True),
        lax.all_gather(rec_in_weight, ("wide", "narrow"), axis=0, tiled=True),
        lax.all_gather(conv_weight, ("wide", "narrow"), axis=0, tiled=True),
        lax.all_gather(conv_bias, ("wide", "narrow"), axis=0, tiled=True),
        lax.all_gather(gate_a_weight, ("wide", "narrow"), axis=0, tiled=True),
        lax.all_gather(gate_a_bias, ("wide", "narrow"), axis=0, tiled=True),
        lax.all_gather(gate_x_weight, ("wide", "narrow"), axis=0, tiled=True),
        lax.all_gather(gate_x_bias, ("wide", "narrow"), axis=0, tiled=True),
        lax.all_gather(decay_rate, ("wide", "narrow"), axis=0, tiled=True),
        lax.all_gather(rec_out_weight, ("wide", "narrow"), axis=0, tiled=True),
    )
    mlp_set = (
        lax.all_gather(norm2_gain, ("wide", "narrow"), axis=0, tiled=True),
        lax.all_gather(mlp_gate_weight, ("wide", "narrow"), axis=0, tiled=True),
        lax.all_gather(mlp_up_weight, ("wide", "narrow"), axis=0, tiled=True),
        lax.all_gather(mlp_down_weight, ("wide", "narrow"), axis=0, tiled=True),
    )
    (
        gain_first,
        gate_whole,
        branch_whole,
        conv_taps,
        conv_offset,
        decay_whole,
        decay_bias,
        input_whole,
        input_bias,
        decay_rates,
        output_whole,
    ) = block_set
    gain_second, mlp_gate_whole, mlp_up_whole, mlp_down_whole = mlp_set
    decay_blocks = decay_whole.reshape(NB, BLK, BLK)
    input_blocks = input_whole.reshape(NB, BLK, BLK)
    width_ff = mlp_gate_whole.shape[1]
    tok_rows = tokens_in.astype(jnp.float32)
    row_total = tok_rows.shape[0]
    tail_len = CONV - 1
    seg_local = jnp.cumsum(segment_starts)
    open_mask = (1 - segment_starts).astype(jnp.float32)[:, None]
    later_open = (seg_local[row_total - tail_len :] == seg_local[row_total - 1]).astype(
        jnp.float32
    )[:, None]
    ids_ext = jnp.concatenate([jnp.zeros((tail_len,), jnp.int32), seg_local])
    normed_f, norm_first_back = jax.vjp(rms_scale, tok_rows, gain_first.astype(jnp.float32))
    normed = normed_f.astype(jnp.bfloat16)
    gate_pre = jnp.dot(normed, gate_whole, preferred_element_type=jnp.float32)
    branch_in = jnp.dot(normed, branch_whole, preferred_element_type=jnp.float32).astype(
        jnp.bfloat16
    )
    sent_rows = branch_in[row_total - tail_len :] * later_open.astype(jnp.bfloat16)
    prev_rows = shifted(sent_rows, ("wide", "narrow"), 1)
    extended = jnp.concatenate([prev_rows, branch_in], axis=0).astype(jnp.float32)

    def conv_local(ext_rows, taps_f, offset_f):
        return conv_apply(ext_rows, taps_f, offset_f, ids_ext, seg_local)

    conv_out, conv_back = jax.vjp(
        conv_local, extended, conv_taps.astype(jnp.float32), conv_offset.astype(jnp.float32)
    )
    conved = conv_out.astype(jnp.bfloat16)
    conved_blocks = conved.reshape(row_total, NB, BLK)
    logit_a = jnp.einsum(
        "tnb,nbc->tnc", conved_blocks, decay_blocks, preferred_element_type=jnp.float32
    ).reshape(row_total, -1) + decay_bias.astype(jnp.float32)
    logit_b = jnp.einsum(
        "tnb,nbc->tnc", conved_blocks, input_blocks, preferred_element_type=jnp.float32
    ).reshape(row_total, -1) + input_bias.astype(jnp.float32)

    def gate_local(logit_one, logit_two, conved_f, rates_f):
        return gate_math(logit_one, logit_two, conved_f, rates_f, open_mask)

    (keep_all, push_all), gate_back = jax.vjp(
        gate_local, logit_a, logit_b, conved.astype(jnp.float32), decay_rates.astype(jnp.float32)
    )
    keep_prod, local_state = lax.associative_scan(combine_pairs, (keep_all, push_all), axis=0)
    ones_row = jnp.ones_like(keep_all[0])
    zeros_row = jnp.zeros_like(keep_all[0])
    prefix = carried_in(
        (keep_prod[row_total - 1], local_state[row_total - 1]),
        ("wide", "narrow"),
        combine_pairs,
        (ones_row, zeros_row),
        False,
    )
    state_in = prefix[1]
    state_all = keep_prod * state_in + local_state
    gate_act, gelu_back = jax.vjp(gelu_tanh, gate_pre)
    mixed = (state_all * gate_act).astype(jnp.bfloat16)
    middle = tok_rows + jnp.dot(mixed, output_whole, preferred_element_type=jnp.float32)
    normed_second_f, norm_second_back = jax.vjp(rms_scale, middle, gain_second.astype(jnp.float32))
    normed_two = normed_second_f.astype(jnp.bfloat16)
    mlp_gate = jnp.dot(normed_two, mlp_gate_whole, preferred_element_type=jnp.float32)
    mlp_up = jnp.dot(normed_two, mlp_up_whole, preferred_element_type=jnp.float32)
    hidden_f, mlp_back = jax.vjp(gated_unit, mlp_gate, mlp_up)
    hidden = hidden_f.astype(jnp.bfloat16)
    layer_out = (
        middle + jnp.dot(hidden, mlp_down_whole, preferred_element_type=jnp.float32)
    ).astype(jnp.bfloat16)
    d_hidden = lax.dot_general(
        cotangent, mlp_down_whole, contract_last, preferred_element_type=jnp.float32
    )
    d_mlp_gate, d_mlp_up = mlp_back(d_hidden)
    d_mlp_gate = d_mlp_gate.astype(jnp.bfloat16)
    d_mlp_up = d_mlp_up.astype(jnp.bfloat16)
    d_normed_two = lax.dot_general(
        d_mlp_gate, mlp_gate_whole, contract_last, preferred_element_type=jnp.float32
    ) + lax.dot_general(d_mlp_up, mlp_up_whole, contract_last, preferred_element_type=jnp.float32)
    d_middle_norm, d_gain_second = norm_second_back(d_normed_two)
    d_middle = cotangent.astype(jnp.float32) + d_middle_norm
    d_rec_out = d_middle.astype(jnp.bfloat16)
    d_mixed = lax.dot_general(
        d_rec_out, output_whole, contract_last, preferred_element_type=jnp.float32
    )
    (d_gate_pre,) = gelu_back(d_mixed * state_all)
    d_gate_pre = d_gate_pre.astype(jnp.bfloat16)
    d_state = d_mixed * gate_act
    keep_next = jnp.concatenate([keep_all[1:], ones_row[None]], axis=0)
    back_prod, back_local = lax.associative_scan(
        combine_pairs, (keep_next, d_state), axis=0, reverse=True
    )
    suffix = carried_in(
        (keep_prod[row_total - 1], keep_all[0] * back_local[0]),
        ("wide", "narrow"),
        combine_pairs,
        (ones_row, zeros_row),
        True,
    )
    adjoint = back_local + back_prod * suffix[1]
    state_prev = jnp.concatenate([state_in[None], state_all[: row_total - 1]], axis=0)
    d_logit_a, d_logit_b, d_conved_gate, d_rates = gate_back((adjoint * state_prev, adjoint))
    d_logit_a = d_logit_a.astype(jnp.bfloat16)
    d_logit_b = d_logit_b.astype(jnp.bfloat16)
    grad_a_blocks = d_logit_a.reshape(row_total, NB, BLK)
    grad_b_blocks = d_logit_b.reshape(row_total, NB, BLK)
    d_conved = (
        d_conved_gate
        + jnp.einsum(
            "tnc,nbc->tnb", grad_a_blocks, decay_blocks, preferred_element_type=jnp.float32
        ).reshape(row_total, -1)
        + jnp.einsum(
            "tnc,nbc->tnb", grad_b_blocks, input_blocks, preferred_element_type=jnp.float32
        ).reshape(row_total, -1)
    )
    d_conved = d_conved.astype(jnp.bfloat16)
    grad_decay_whole = jnp.einsum(
        "tnb,tnc->nbc", conved_blocks, grad_a_blocks, preferred_element_type=jnp.float32
    ).reshape(-1, BLK)
    grad_input_whole = jnp.einsum(
        "tnb,tnc->nbc", conved_blocks, grad_b_blocks, preferred_element_type=jnp.float32
    ).reshape(-1, BLK)
    grad_decay_bias = jnp.sum(d_logit_a.astype(jnp.float32), axis=0)
    grad_input_bias = jnp.sum(d_logit_b.astype(jnp.float32), axis=0)
    d_extended, d_taps, d_offset = conv_back(d_conved.astype(jnp.float32))
    from_next = shifted(d_extended[:tail_len], ("wide", "narrow"), -1)
    d_branch = d_extended[tail_len:]
    d_branch = jnp.concatenate(
        [
            d_branch[: row_total - tail_len],
            d_branch[row_total - tail_len :] + from_next * later_open,
        ],
        axis=0,
    ).astype(jnp.bfloat16)
    d_normed = lax.dot_general(
        d_gate_pre, gate_whole, contract_last, preferred_element_type=jnp.float32
    ) + lax.dot_general(d_branch, branch_whole, contract_last, preferred_element_type=jnp.float32)
    d_rows_norm, d_gain_first = norm_first_back(d_normed)
    grad_tokens = d_middle + d_rows_norm
    columns = normed
    rec_in_sum = lax.psum_scatter(
        jnp.concatenate(
            [
                lax.dot_general(
                    columns, d_gate_pre, contract_first, preferred_element_type=jnp.float32
                ),
                lax.dot_general(
                    columns, d_branch, contract_first, preferred_element_type=jnp.float32
                ),
            ],
            axis=1,
        ),
        ("wide", "narrow"),
        scatter_dimension=0,
        tiled=True,
    )
    width_rnn = gate_pre.shape[1]
    columns = mixed
    grad_output = lax.psum_scatter(
        lax.dot_general(columns, d_rec_out, contract_first, preferred_element_type=jnp.float32),
        ("wide", "narrow"),
        scatter_dimension=0,
        tiled=True,
    )
    small_sums = (
        lax.psum_scatter(d_gain_first, ("wide", "narrow"), scatter_dimension=0, tiled=True),
        lax.psum_scatter(d_taps, ("wide", "narrow"), scatter_dimension=0, tiled=True),
        lax.psum_scatter(d_offset, ("wide", "narrow"), scatter_dimension=0, tiled=True),
        lax.psum_scatter(grad_decay_whole, ("wide", "narrow"), scatter_dimension=0, tiled=True),
        lax.psum_scatter(grad_decay_bias, ("wide", "narrow"), scatter_dimension=0, tiled=True),
        lax.psum_scatter(grad_input_whole, ("wide", "narrow"), scatter_dimension=0, tiled=True),
        lax.psum_scatter(grad_input_bias, ("wide", "narrow"), scatter_dimension=0, tiled=True),
        lax.psum_scatter(d_rates, ("wide", "narrow"), scatter_dimension=0, tiled=True),
        lax.psum_scatter(d_gain_second, ("wide", "narrow"), scatter_dimension=0, tiled=True),
    )
    columns = normed_two
    mlp_in_sum = lax.psum_scatter(
        jnp.concatenate(
            [
                lax.dot_general(
                    columns, d_mlp_gate, contract_first, preferred_element_type=jnp.float32
                ),
                lax.dot_general(
                    columns, d_mlp_up, contract_first, preferred_element_type=jnp.float32
                ),
            ],
            axis=1,
        ),
        ("wide", "narrow"),
        scatter_dimension=0,
        tiled=True,
    )
    grad_gate_mlp = mlp_in_sum[:, :width_ff]
    grad_up_mlp = mlp_in_sum[:, width_ff:]
    columns = hidden
    grad_down = lax.psum_scatter(
        lax.dot_general(columns, cotangent, contract_first, preferred_element_type=jnp.float32),
        ("wide", "narrow"),
        scatter_dimension=0,
        tiled=True,
    )
    return (
        layer_out,
        grad_tokens,
        small_sums[0],
        rec_in_sum[:, :width_rnn],
        rec_in_sum[:, width_rnn:],
        small_sums[1],
        small_sums[2],
        small_sums[3],
        small_sums[4],
        small_sums[5],
        small_sums[6],
        small_sums[7],
        grad_output,
        small_sums[8],
        grad_gate_mlp,
        grad_up_mlp,
        grad_down,
    )


def solution(mesh):
    placed = (
        P(("wide", "narrow"), None),
        P(("wide", "narrow")),
        P(("wide", "narrow"), None),
        P(("wide", "narrow")),
        P(("wide", "narrow"), None),
        P(("wide", "narrow"), None),
        P(("wide", "narrow"), None),
        P(("wide", "narrow")),
        P(("wide", "narrow"), None),
        P(("wide", "narrow")),
        P(("wide", "narrow"), None),
        P(("wide", "narrow")),
        P(("wide", "narrow")),
        P(("wide", "narrow"), None),
        P(("wide", "narrow")),
        P(("wide", "narrow"), None),
        P(("wide", "narrow"), None),
        P(("wide", "narrow"), None),
    )
    return jax.shard_map(
        on_device,
        mesh=mesh,
        in_specs=placed,
        out_specs=(
            P(("wide", "narrow"), None),
            P(("wide", "narrow"), None),
            P(("wide", "narrow")),
            P(("wide", "narrow"), None),
            P(("wide", "narrow"), None),
            P(("wide", "narrow"), None),
            P(("wide", "narrow")),
            P(("wide", "narrow"), None),
            P(("wide", "narrow")),
            P(("wide", "narrow"), None),
            P(("wide", "narrow")),
            P(("wide", "narrow")),
            P(("wide", "narrow"), None),
            P(("wide", "narrow")),
            P(("wide", "narrow"), None),
            P(("wide", "narrow"), None),
            P(("wide", "narrow"), None),
        ),
        check_vma=False,
    )
```

profile of v0, /device:TPU:0, one launch (start us, length us, event | category | flops | bytes accessed | tf_op | source)
XLA Modules:
  0.0 3457.8 jit_solution(17659499854136740295)
XLA Ops:
  14.0 43.1 %all-reduce.88 = (bf16[2048]{0:T(1024)(128)(2,1)S(1)}, bf16[2560]{0:T(1024)(128)(2,1)S(1)}, bf16[2560]{0:T(1024)(128)(2,1)S(1)}, bf16[2560]{0:T(1024)(128)(2,1)S...) all-reduce(bf16[2048]{0:T(1024)(128)(2,1)S(1)} %dynamic-update-slic, ...), channel_id=1, replica_groups=mesh['wide'=8,'narrow'=4] {'wide','narrow'}, use_global_device_ids=true, to_apply=%add.76 | all-reduce | flops 14336 | bytes 57344
  57.2 40.7 %all-gather = bf16[32,80,4]{1,2,0:T(4,128)(2,1)S(1)} all-gather(bf16[1,80,4]{1,2,0:T(4,128)(2,1)S(1)} %bitcast.106), channel_id=1, replica_groups=mesh['wide'=8,'narrow'=4] {'wide','narrow'}, dimensions={0}, use_global_device_ids=true | all-gather | bytes 21120 | tf_op jit(solution)/shard_map/all_gather | solution.py:105
  100.3 46.2 %all_gather.60 = bf16[2560,160]{1,0:T(8,128)(2,1)} all-gather(bf16[80,160]{1,0:T(8,128)(2,1)S(1)} %copy-done.101), channel_id=1, replica_groups=mesh['wide'=8,'narrow'=4] {'wide','narrow'}, dimensions={0}, use_global_device_ids=true | all-gather | bytes 844800 | tf_op jit(solution)/shard_map/all_gather | solution.py:107
  146.5 48.0 %all_gather.64 = bf16[2560,160]{1,0:T(8,128)(2,1)} all-gather(bf16[80,160]{1,0:T(8,128)(2,1)S(1)} %copy-done.102), channel_id=1, replica_groups=mesh['wide'=8,'narrow'=4] {'wide','narrow'}, dimensions={0}, use_global_device_ids=true | all-gather | bytes 844800 | tf_op jit(solution)/shard_map/all_gather | solution.py:109
  194.5 7.3 convolution_convert_fusion
  220.4 4.0 fusion.113
  227.8 6.6 fusion.41
  236.4 5.8 slice.660
  242.2 5.7 slice.626
  247.9 5.6 slice.625
  332.7 4.8 pad.236
  348.6 4.4 pad.237
  353.0 9.4 pad.238
  363.3 41.9 %all-gather.1 = f32[32,1,2560]{2,1,0:T(1,128)S(1)} all-gather(f32[1,1,2560]{2,1,0:T(1,128)S(1)} %add_bitcast_fusion.1), channel_id=1, replica_groups=mesh['wide'=8,'narrow'=4] {'wide','narrow'}, dimensions={0}, use_global_device_ids=true | all-gather | bytes 337920 | tf_op jit(solution)/shard_map/all_gather | solution.py:28
  407.7 9.4 pad.253
  417.1 4.5 pad.254
  422.6 38.3 %all-gather.2 = f32[32,1,2560]{2,1,0:T(1,128)S(1)} all-gather(f32[1,1,2560]{2,1,0:T(1,128)S(1)} %add_bitcast_fusion), channel_id=1, replica_groups=mesh['wide'=8,'narrow'=4] {'wide','narrow'}, dimensions={0}, use_global_device_ids=true | all-gather | bytes 337920 | tf_op jit(solution)/shard_map/all_gather | solution.py:28
  462.3 10.8 slice.674
  473.1 10.9 slice.665
  484.0 6.7 slice.667
  490.7 12.3 multiply_convert_fusion.2
  503.0 6.2 multiply_reduce_fusion.3
  509.5 15.1 fusion.104
  524.6 79.6 %all-gather.17.cloned.1.call-done = bf16[2048,6144]{1,0:T(8,128)(2,1)} async-done(((bf16[64,6144]{1,0:T(8,128)(2,1)}), bf16[2048,6144]{1,0:T(8,128)(2,1)}) %all-gather.17.cloned.1.call-update) | async-done | bytes 25165840 | tf_op jit(solution)/shard_map/all_gather | solution.py:116
  604.2 14.3 fusion.103
  618.5 141.3 %all-gather.21.cloned.1.call-done = bf16[6144,2048]{1,0:T(8,128)(2,1)} async-done(((bf16[192,2048]{1,0:T(8,128)(2,1)}), bf16[6144,2048]{1,0:T(8,128)(2,1)}) %all-gather.21.cloned.1.call-update) | async-done | bytes 25165840 | tf_op jit(solution)/shard_map/all_gather | solution.py:118
  759.8 21.9 multiply_convert_fusion
  781.7 13.6 fusion.105
  795.3 15.7 multiply_reduce_fusion.1
  814.2 9.5 fusion.44
  833.1 10.8 slice.669
  843.9 6.7 slice.671
  878.5 6.7 slice.727
  894.4 4.9 pad.284
  899.3 4.9 pad.268
  912.5 4.4 pad.269
  916.9 9.1 pad.270
  932.8 13.3 rev.8
  946.1 39.4 %all-gather.3 = f32[32,1,2560]{2,1,0:T(1,128)S(1)} all-gather(f32[1,1,2560]{2,1,0:T(1,128)S(1)} %fusion.69), channel_id=1, replica_groups=mesh['wide'=8,'narrow'=4] {'wide','narrow'}, dimensions={0}, use_global_device_ids=true | all-gather | bytes 337920 | tf_op jit(solution)/shard_map/all_gather | solution.py:28
  985.5 30.6 while.27
  1016.1 4.4 pad.285
  1020.5 9.1 pad.286
  1033.2 21.0 rev.9
  1054.4 9.2 multiply_reduce_fusion
  1063.6 6.4 convert_reduce_fusion.2
  1088.7 8.3 fusion.15
  1102.0 8.7 fusion.75
  1114.0 8.9 fusion.45
  1122.9 27.8 pad_maximum_fusion.1
  1151.9 21.3 fusion.110
  1173.2 21.4 fusion.109
  1194.6 66.7 %pad_maximum_fusion = f32[2048,12288]{1,0:T(8,128)} fusion(f32[2048,6144]{1,0:T(8,128)} %fusion.110, f32[2048,6144]{1,0:T(8,128)} %fusion.109), kind=kLoop, calls=%fused_computation.6 | loop fusion | flops 25165824 | bytes 201326592 | tf_op jit(solution)/shard_map/concatenate | solution.py:308
  1270.1 10.2 fusion.48
  1281.6 21.8 fusion.111
  1303.4 6.3 fusion.106
  1309.8 13.2 fusion.32
  1323.1 8.6 fusion.36
  1331.7 47.0 %all-reduce.87 = (f32[2048]{0:T(1024)S(1)}, f32[2560]{0:T(1024)S(1)}, f32[2560]{0:T(1024)S(1)}, f32[2560]{0:T(1024)S(1)}, f32[2560]{0:T(1024)S(1)}, /*index=5*/f32[2048]{0:T(1024)S(1)}) all-reduce(f32[2048]{0:T(1024)S(1)} %get-tuple-element.153, ...), channel_id=2, replica_groups=mesh['wide'=8,'narrow'=4] {'wide','narrow'}, use_global_device_ids=true, to_apply=%region_11.12.clone | all-reduce | flops 14336 | bytes 114688
  1387.1 282.5 %reduce-scatter.10.cloned.1.call-done = f32[64,5120]{1,0:T(8,128)} async-done(((f32[2048,5120]{1,0:T(8,128)}), f32[64,5120]{1,0:T(8,128)}) %reduce-scatter.10.cloned.1.call-update) | async-done | bytes 1310736 | tf_op jit(solution)/shard_map/reduce_scatter | solution.py:271
  1672.1 836.6 %reduce-scatter.18.cloned.1.call-done = f32[64,12288]{1,0:T(8,128)} async-done(((f32[2048,12288]{1,0:T(8,128)}), f32[64,12288]{1,0:T(8,128)}) %reduce-scatter.18.cloned.1.call-update) | async-done | bytes 3145744 | tf_op jit(solution)/shard_map/reduce_scatter | solution.py:307
  2512.5 135.8 %reduce-scatter.12.cloned.1.call-done = f32[80,160]{1,0:T(8,128)} async-done(((f32[2560,160]{1,0:T(8,128)}), f32[80,160]{1,0:T(8,128)}) %reduce-scatter.12.cloned.1.call-update) | async-done | bytes 51216 | tf_op jit(solution)/shard_map/reduce_scatter | solution.py:299
  2648.3 136.4 %reduce-scatter.14.cloned.1.call-done = f32[80,160]{1,0:T(8,128)} async-done(((f32[2560,160]{1,0:T(8,128)}), f32[80,160]{1,0:T(8,128)}) %reduce-scatter.14.cloned.1.call-update) | async-done | bytes 51216 | tf_op jit(solution)/shard_map/reduce_scatter | solution.py:301
  2784.7 223.8 %reduce-scatter.16.cloned.1.call-done = f32[80,2048]{1,0:T(8,128)} async-done(((f32[2560,2048]{1,0:T(8,128)}), f32[80,2048]{1,0:T(8,128)}) %reduce-scatter.16.cloned.1.call-update) | async-done | bytes 655376 | tf_op jit(solution)/shard_map/reduce_scatter | solution.py:289
  3008.6 442.5 %reduce-scatter.20.cloned.1.call-done = f32[192,2048]{1,0:T(8,128)} async-done(((f32[6144,2048]{1,0:T(8,128)}), f32[192,2048]{1,0:T(8,128)}) %reduce-scatter.20.cloned.1.call-update) | async-done | bytes 1572880 | tf_op jit(solution)/shard_map/reduce_scatter | solution.py:326
  (664 shorter events, 278.9 us)
Async XLA Ops:
  7.3 49.9 %copy-start.118 = (bf16[80,4]{0,1:T(4,128)(2,1)S(1)}, bf16[80,4]{0,1:T(4,128)(2,1)}, u32[]{:S(2)}) copy-start(bf16[80,4]{0,1:T(4,128)(2,1)} %param.28) | copy-start | bytes 1924
  7.3 90.8 %copy-start.4 = (bf16[256,2048]{1,0:T(8,128)(2,1)S(1)}, bf16[256,2048]{1,0:T(8,128)(2,1)}, u32[]{:S(2)}) copy-start(bf16[256,2048]{1,0:T(8,128)(2,1)} %param.22) | copy-start | bytes 3145732
  7.3 93.0 %copy-start.101 = (bf16[80,160]{1,0:T(8,128)(2,1)S(1)}, bf16[80,160]{1,0:T(8,128)(2,1)}, u32[]{:S(2)}) copy-start(bf16[80,160]{1,0:T(8,128)(2,1)} %param.30) | copy-start | bytes 76804
  7.3 187.2 %all-gather.11.cloned.1.call-start = ((), (), s32[]{:S(2)}) async-start(), calls=%async_computation.7 | async-start | bytes 10813440 | tf_op jit(solution)/shard_map/all_gather | solution.py:104
  8.0 482.6 %all-gather.13.cloned.1.call-start = ((), (), s32[]{:S(2)}) async-start(), calls=%async_computation.8 | async-start | bytes 10813440 | tf_op jit(solution)/shard_map/all_gather | solution.py:103
  8.8 494.3 %all-gather.15.cloned.1.call-start = ((), (), s32[]{:S(2)}) async-start(), calls=%async_computation.9 | async-start | bytes 10813440 | tf_op jit(solution)/shard_map/all_gather | solution.py:112
  9.5 137.0 %copy-start.102 = (bf16[80,160]{1,0:T(8,128)(2,1)S(1)}, bf16[80,160]{1,0:T(8,128)(2,1)}, u32[]{:S(2)}) copy-start(bf16[80,160]{1,0:T(8,128)(2,1)} %param.32) | copy-start | bytes 76804
  9.5 500.0 %all-gather.19.cloned.1.call-start = ((), (), s32[]{:S(2)}) async-start(), calls=%async_computation.11 | async-start | bytes 25952256 | tf_op jit(solution)/shard_map/all_gather | solution.py:117
  10.1 594.1 %all-gather.17.cloned.1.call-start = ((), (), s32[]{:S(2)}) async-start(), calls=%async_computation.10 | async-start | bytes 25952256 | tf_op jit(solution)/shard_map/all_gather | solution.py:116
  10.7 749.1 %all-gather.21.cloned.1.call-start = ((), (), s32[]{:S(2)}) async-start(), calls=%async_computation.12 | async-start | bytes 25952256 | tf_op jit(solution)/shard_map/all_gather | solution.py:118
  11.3 1374.5 %reduce-scatter.22.cloned.1.call-start = ((), (), s32[]{:S(2)}) async-start(), calls=%async_computation.19 | async-start | bytes 1351680
  57.2 433.5 %copy-start.56 = (f32[2048]{0:T(1024)}, f32[2048]{0:T(1024)S(1)}, u32[]{:S(2)}) copy-start(f32[2048]{0:T(1024)S(1)} %convert_element_type.107) | copy-start | bytes 24580
  98.4 129.3 %copy-start.111 = (f32[256]{0:T(256)}, f32[256]{0:T(256)S(1)}, u32[]{:S(2)}) copy-start(f32[256]{0:T(256)S(1)} %subtract_convert_fusion) | copy-start | bytes 3076
  98.4 392.3 %copy-start.76 = (f32[256]{0:T(256)}, f32[256]{0:T(256)S(1)}, u32[]{:S(2)}) copy-start(f32[256]{0:T(256)S(1)} %fusion.70) | copy-start | bytes 3076
  100.2 127.4 %copy-start.81 = (f32[256]{0:T(256)}, f32[256]{0:T(256)S(1)}, u32[]{:S(2)}) copy-start(f32[256]{0:T(256)S(1)} %get-tuple-element.293) | copy-start | bytes 3076
  100.2 127.4 %copy-start.83 = (f32[256]{0:T(256)}, f32[256]{0:T(256)S(1)}, u32[]{:S(2)}) copy-start(f32[256]{0:T(256)S(1)} %get-tuple-element.294) | copy-start | bytes 3076
  100.2 127.4 %copy-start.85 = (f32[256]{0:T(256)}, f32[256]{0:T(256)S(1)}, u32[]{:S(2)}) copy-start(f32[256]{0:T(256)S(1)} %get-tuple-element.295) | copy-start | bytes 3076
  100.3 127.4 %copy-start.68 = (f32[2560]{0:T(1024)}, f32[2560]{0:T(1024)S(1)}, u32[]{:S(2)}) copy-start(f32[2560]{0:T(1024)S(1)} %broadcast_multiply_fusion) | copy-start | bytes 30724
  202.9 3.1 collective-permute-start
  205.3 22.4 copy-start.60
  205.3 22.4 copy-start.62
  205.3 22.4 copy-start.64
  205.3 22.4 copy-start.66
  206.0 21.8 copy-start.74
  206.0 21.8 copy-start.70
  206.0 21.7 copy-start.72
  207.7 20.0 copy-start
  242.2 11.3 copy-start.9
  353.0 54.7 %copy-start.22 = (f32[256,2560]{1,0:T(8,128)}, f32[256,2560]{1,0:T(8,128)S(1)}, u32[]{:S(2)}) copy-start(f32[256,2560]{1,0:T(8,128)S(1)} %pad.237) | copy-start | bytes 7864324
  353.0 52.2 %copy-start.107 = (f32[1,2560]{1,0:T(1,128)S(1)}, f32[1,2560]{1,0:T(1,128)}, u32[]{:S(2)}) copy-start(f32[1,2560]{1,0:T(1,128)} %slice.786) | copy-start | bytes 30724
  421.6 40.7 %copy-start.23 = (f32[256,2560]{1,0:T(8,128)}, f32[256,2560]{1,0:T(8,128)S(1)}, u32[]{:S(2)}) copy-start(f32[256,2560]{1,0:T(8,128)S(1)} %pad.254) | copy-start | bytes 7864324
  461.7 22.4 copy-start.59
  473.1 11.0 copy-start.36
  473.1 17.6 copy-start.5
  509.2 301.8 %copy-start.26 = (f32[256,2048]{1,0:T(8,128)}, f32[256,2048]{1,0:T(8,128)S(1)}, u32[]{:S(2)}) copy-start(f32[256,2048]{1,0:T(8,128)S(1)} %get-tuple-element.298) | copy-start | bytes 6291460
  509.5 94.7 %copy-start.14 = (bf16[256,2048]{1,0:T(8,128)(2,1)}, bf16[256,2048]{1,0:T(8,128)(2,1)S(1)}, u32[]{:S(2)}) copy-start(bf16[256,2048]{1,0:T(8,128)(2,1)S(1)} %multiply_convert_fusion.3) | copy-start | bytes 3145732
  795.3 15.7 copy-start.41
  1033.1 21.1 copy-start.1
  1033.1 21.1 copy-start.61
  1033.1 21.1 copy-start.63
  1033.1 21.1 copy-start.65
  1033.1 21.1 copy-start.67
  1033.1 21.1 copy-start.69
  1033.2 21.1 copy-start.71
  1033.2 21.1 copy-start.73
  1033.2 21.1 copy-start.75
  1033.2 21.1 copy-start.82
  1033.2 21.1 copy-start.84
  1033.2 21.1 copy-start.86
  1033.2 21.1 copy-start.110
  1033.2 21.1 copy-start.112
  1098.8 570.9 %reduce-scatter.10.cloned.1.call-start = ((), (), s32[]{:S(2)}) async-start(), calls=%async_computation.13 | async-start | bytes 43253760 | tf_op jit(solution)/shard_map/reduce_scatter | solution.py:271
  1100.4 11.9 collective-permute-start.1
  1150.7 1358.0 %reduce-scatter.18.cloned.1.call-start = ((), (), s32[]{:S(2)}) async-start(), calls=%async_computation.17 | async-start | bytes 103809024 | tf_op jit(solution)/shard_map/reduce_scatter | solution.py:307
  1261.3 1387.0 %reduce-scatter.12.cloned.1.call-start = ((), (), s32[]{:S(2)}) async-start(), calls=%async_computation.14 | async-start | bytes 2703360 | tf_op jit(solution)/shard_map/reduce_scatter | solution.py:299
  1265.1 1519.6 %reduce-scatter.14.cloned.1.call-start = ((), (), s32[]{:S(2)}) async-start(), calls=%async_computation.15 | async-start | bytes 2703360 | tf_op jit(solution)/shard_map/reduce_scatter | solution.py:301
  1268.5 1740.0 %reduce-scatter.16.cloned.1.call-start = ((), (), s32[]{:S(2)}) async-start(), calls=%async_computation.16 | async-start | bytes 21626880 | tf_op jit(solution)/shard_map/reduce_scatter | solution.py:289
  1280.4 2170.7 %reduce-scatter.20.cloned.1.call-start = ((), (), s32[]{:S(2)}) async-start(), calls=%async_computation.18 | async-start | bytes 51904512 | tf_op jit(solution)/shard_map/reduce_scatter | solution.py:326
  1309.7 13.3 copy-start.7
  1309.7 13.3 copy-start.31
  1309.7 13.3 copy-start.58
  1309.7 13.3 copy-start.78
  1309.8 13.3 copy-start.80
  1323.1 59.2 %copy-start.114 = (f32[256]{0:T(256)S(1)}, f32[256]{0:T(256)}, u32[]{:S(2)}) copy-start(f32[256]{0:T(256)} %copy-done.113) | copy-start | bytes 3076
  (76 other events, 260.0 us)
Sparse Core Ops, SparseCore 0:
  11.0 90.8 all-gather.10
  104.8 93.4 all-gather.12
  201.2 87.8 all-gather.14
  291.9 156.4 all-gather.18
  451.1 153.0 all-gather.16
  607.0 152.8 all-gather.20
  1098.9 130.9 reduce-scatter.21
  1232.3 437.3 reduce-scatter.9
  1677.2 831.4 reduce-scatter.17
  2511.5 136.8 reduce-scatter.11
  2651.3 133.3 reduce-scatter.13
  2787.6 220.9 reduce-scatter.15
  3016.7 434.2 reduce-scatter.19
where the time goes:
time: 3470 us; the launch traced here: 3460 us
  waiting for transfers between devices  2280 us (66%)
  local copies, waits for them, and re-layouts  357 us (10%)
  blocking collectives  345 us (10%)
  matrix products  256 us (7%)
  other arithmetic  195 us (6%)
    reduce_scatter x1, waiting for transfers between devices, on_device(): lax.psum_scatter(jnp.concatenate([lax.dot_general(columns, d_mlp_gate, co...  837 us
    reduce_scatter x1, waiting for transfers between devices, on_device(): lax.psum_scatter(lax.dot_general(columns, cotangent, contract_first, pref...  442 us
    reduce_scatter x1, waiting for transfers between devices, on_device(): lax.psum_scatter(jnp.concatenate([lax.dot_general(columns, d_gate_pre, co...  282 us
    reduce_scatter x1, waiting for transfers between devices, on_device(): lax.psum_scatter(lax.dot_general(columns, d_rec_out, contract_first, pref...  224 us
    all_gather x1, waiting for transfers between devices, on_device(): lax.all_gather(mlp_down_weight, ('wide', 'narrow'), axis=0, tiled=True)  141 us
    reduce_scatter x1, waiting for transfers between devices, on_device(): lax.psum_scatter(grad_input_whole, ('wide', 'narrow'), scatter_dimension=...  136 us
    reduce_scatter x1, waiting for transfers between devices, on_device(): lax.psum_scatter(grad_decay_whole, ('wide', 'narrow'), scatter_dimension=...  136 us
    all_gather x3, blocking collectives, carried_in(): gathered = jax.tree.map(lambda a: lax.all_gather(a, axis), part)  120 us
  transfers between devices with their start and end apart: 15, of which 8 were waited for; matrix products, arithmetic and copies ran while one was open for 14% of the time, Pallas kernels for 0%

commit v1 on v0

v1 whole, which is shorter than its diff:
```python
import functools

import jax
import jax.numpy as jnp
from jax import lax
from jax.experimental import pallas as pl
from jax.experimental.pallas import tpu as pltpu
from jax.sharding import Mesh
from jax.sharding import PartitionSpec as P

BLK = 160
CONV = 4
TAIL = CONV - 1
LANES = 128
FEAT = ("x", "y", "c")
NF = 8

norm_eps = 1e-06
decay_scale = 8.0
push_shift = 0.05
f32 = jnp.float32
bf16 = jnp.bfloat16
MESH = pl.DeviceIdType.MESH
contract_last = (((1,), (1,)), ((), ()))
contract_first = (((0,), (0,)), ((), ()))
VMEM_LIMIT = 56 * 2**20


def cost(micros, flops=0):
    return pl.CostEstimate(
        flops=int(flops), bytes_accessed=int(micros * 3.0e6), transcendentals=0
    )


def hbm_spec():
    return pl.BlockSpec(memory_space=pl.ANY)


def vmem_spec():
    return pl.BlockSpec(memory_space=pltpu.VMEM)


def greet(peers):
    barrier = pltpu.get_barrier_semaphore()
    for device in peers:
        pl.semaphore_signal(barrier, inc=1, device_id=device, device_id_type=MESH)
    pl.semaphore_wait(barrier, len(peers))


def feature_place():
    return tuple(lax.axis_index(name) for name in FEAT)


def remote(src, dst, send_sem, recv_sem, device):
    return pltpu.make_async_remote_copy(
        src_ref=src,
        dst_ref=dst,
        send_sem=send_sem,
        recv_sem=recv_sem,
        device_id=device,
        device_id_type=MESH,
    )


def gather_kernel(x_ref, o_ref, local_sem, ssem, rsem):
    x, y, c = feature_place()
    mine = x * 4 + y * 2 + c
    from_x = (1 - x) * 4 + y * 2 + c
    from_y = x * 4 + (1 - y) * 2 + c
    from_d = (1 - x) * 4 + (1 - y) * 2 + c
    to_x, to_y, to_c = {"x": 1 - x}, {"y": 1 - y}, {"c": 1 - c}
    half = x_ref.shape[0] // 2
    top, low = pl.ds(0, half), pl.ds(half, half)
    greet((to_x, to_y, to_c))

    def copy(i, src, dst, device):
        return remote(src, dst, ssem.at[i], rsem.at[i], device)

    own = pltpu.make_async_copy(x_ref, o_ref.at[mine], local_sem)
    x_top = copy(0, x_ref.at[top], o_ref.at[mine, top], to_x)
    x_low = copy(1, x_ref.at[low], o_ref.at[mine, low], to_x)
    y_low = copy(2, x_ref.at[low], o_ref.at[mine, low], to_y)
    y_top = copy(3, x_ref.at[top], o_ref.at[mine, top], to_y)
    c_own = copy(4, x_ref, o_ref.at[mine], to_c)
    y_fwd = copy(5, o_ref.at[from_x, top], o_ref.at[from_x, top], to_y)
    x_fwd = copy(6, o_ref.at[from_y, low], o_ref.at[from_y, low], to_x)
    c_x = copy(7, o_ref.at[from_x], o_ref.at[from_x], to_c)
    c_y = copy(8, o_ref.at[from_y], o_ref.at[from_y], to_c)
    c_d = copy(9, o_ref.at[from_d], o_ref.at[from_d], to_c)
    for one in (x_top, y_low, x_low, y_top, c_own, own):
        one.start()
    x_top.wait_recv()
    y_fwd.start()
    y_low.wait_recv()
    x_fwd.start()
    x_low.wait_recv()
    c_x.start()
    y_top.wait_recv()
    c_y.start()
    y_fwd.wait_recv()
    x_fwd.wait_recv()
    c_d.start()
    for one in (c_own, c_x, c_y, c_d):
        one.wait_recv()
    for one in (x_top, x_low, y_low, y_top, c_own, y_fwd, x_fwd, c_x, c_y, c_d):
        one.wait_send()
    own.wait()


def gather_feature(block):
    rows, width = block.shape
    out = pl.pallas_call(
        gather_kernel,
        out_shape=jax.ShapeDtypeStruct((NF, rows, width), block.dtype),
        in_specs=[vmem_spec()],
        out_specs=hbm_spec(),
        scratch_shapes=[
            pltpu.SemaphoreType.DMA,
            pltpu.SemaphoreType.DMA((10,)),
            pltpu.SemaphoreType.DMA((10,)),
        ],
        compiler_params=pltpu.CompilerParams(
            collective_id=0, has_side_effects=True, vmem_limit_bytes=VMEM_LIMIT
        ),
        cost_estimate=cost(40),
        name="gather_feature",
    )(block)
    return out.reshape(NF * rows, width)


def scatter_kernel(
    p_ref, o_ref, own, other, total, rx, ry, relay, rx_last, ry_last, lsem, ssem, rsem
):
    x, y, c = feature_place()
    to_x, to_y, to_c = {"x": 1 - x}, {"y": 1 - y}, {"c": 1 - c}
    rows, width = o_ref.shape
    half = rows // 2
    top, low = pl.ds(0, half), pl.ds(half, half)
    step = 16
    chips = (
        x * 2 + y,
        (1 - x) * 2 + y,
        x * 2 + (1 - y),
        (1 - x) * 2 + (1 - y),
    )

    def copy(i, src, dst, device):
        return remote(src, dst, ssem.at[i], rsem.at[i], device)

    loads = [
        pltpu.make_async_copy(p_ref.at[chips[r] * 2 + c], own.at[r], lsem.at[r]) for r in range(4)
    ]
    for r in (3, 1, 2, 0):
        loads[r].start()
    greet((to_x, to_y, to_c))
    cross = [
        copy(r, p_ref.at[chips[r] * 2 + (1 - c)], other.at[r], to_c) for r in range(4)
    ]
    for r in (3, 1, 2, 0):
        cross[r].start()

    def add_into(r):
        loads[r].wait()
        cross[r].wait_recv()

        def body(i, none):
            at = pl.ds(pl.multiple_of(i * step, step), step)
            total[r, at] = (own[r, at].astype(f32) + other[r, at].astype(f32)).astype(total.dtype)
            return none

        lax.fori_loop(0, rows // step, body, 0)

    x_diag = copy(4, total.at[3, top], rx.at[1], to_x)
    y_diag = copy(5, total.at[3, low], ry.at[1], to_y)
    x_near = copy(6, total.at[1, top], rx.at[0], to_x)
    y_near = copy(7, total.at[2, low], ry.at[0], to_y)
    y_last = copy(8, relay.at[0], ry_last, to_y)
    x_last = copy(9, relay.at[1], rx_last, to_x)

    add_into(3)
    x_diag.start()
    y_diag.start()
    add_into(1)
    x_near.start()
    add_into(2)
    y_near.start()
    loads[0].wait()
    cross[0].wait_recv()

    def relay_add(slot, r, start, got):
        def body(i, none):
            at = pl.ds(pl.multiple_of(i * step, step), step)
            here = pl.ds(pl.multiple_of(start + i * step, step), step)
            relay[slot, at] = (total[r, here].astype(f32) + got[1, at].astype(f32)).astype(
                relay.dtype
            )
            return none

        lax.fori_loop(0, half // step, body, 0)

    x_diag.wait_recv()
    relay_add(0, 2, 0, rx)
    y_last.start()
    y_diag.wait_recv()
    relay_add(1, 1, half, ry)
    x_last.start()

    def finish(start, near, last):
        def body(i, none):
            at = pl.ds(pl.multiple_of(i * step, step), step)
            here = pl.ds(pl.multiple_of(start + i * step, step), step)
            o_ref[here] = (own[0, here].astype(f32) + other[0, here].astype(f32)) + (
                near[0, at].astype(f32) + last[at].astype(f32)
            )
            return none

        lax.fori_loop(0, half // step, body, 0)

    x_near.wait_recv()
    y_last.wait_recv()
    finish(0, rx, ry_last)
    y_near.wait_recv()
    x_last.wait_recv()
    finish(half, ry, rx_last)
    for one in cross + [x_diag, y_diag, x_near, y_near, x_last, y_last]:
        one.wait_send()


def scatter_feature(partial):
    rows, width = partial.shape[0] // NF, partial.shape[1]
    half = rows // 2
    kind = partial.dtype
    return pl.pallas_call(
        scatter_kernel,
        out_shape=jax.ShapeDtypeStruct((rows, width), f32),
        in_specs=[hbm_spec()],
        out_specs=vmem_spec(),
        scratch_shapes=[
            pltpu.VMEM((4, rows, width), kind),
            pltpu.VMEM((4, rows, width), kind),
            pltpu.VMEM((4, rows, width), kind),
            pltpu.VMEM((2, half, width), kind),
            pltpu.VMEM((2, half, width), kind),
            pltpu.VMEM((2, half, width), kind),
            pltpu.VMEM((half, width), kind),
            pltpu.VMEM((half, width), kind),
            pltpu.SemaphoreType.DMA((4,)),
            pltpu.SemaphoreType.DMA((10,)),
            pltpu.SemaphoreType.DMA((10,)),
        ],
        compiler_params=pltpu.CompilerParams(
            collective_id=1, has_side_effects=True, vmem_limit_bytes=VMEM_LIMIT
        ),
        cost_estimate=cost(45),
        name="scatter_feature",
    )(partial.reshape(NF, rows, width))


def exchange_kernel(axes, x_ref, o_ref, local_sem, ssem, rsem):
    place = [lax.axis_index(name) for name in axes]
    count = 2 ** len(axes)

    def rank(coords):
        total = 0
        for one in coords:
            total = total * 2 + one
        return total

    mine = rank(place)
    flips = []
    for mask in range(1, count):
        bits = [(mask // 2 ** (len(axes) - 1 - i)) % 2 for i in range(len(axes))]
        coords = [1 - p if bit else p for p, bit in zip(place, bits)]
        device = {name: q for name, q, bit in zip(axes, coords, bits) if bit}
        flips.append((rank(coords), device))
    own = pltpu.make_async_copy(x_ref.at[mine], o_ref.at[mine], local_sem)
    own.start()
    greet([device for _, device in flips])
    copies = [
        remote(x_ref.at[target], o_ref.at[mine], ssem.at[i], rsem.at[i], device)
        for i, (target, device) in enumerate(flips)
    ]
    for one in reversed(copies):
        one.start()
    for one in copies:
        one.wait()
    own.wait()


def exchange(blocks, axes, ident):
    count = 2 ** len(axes)
    return pl.pallas_call(
        functools.partial(exchange_kernel, axes),
        out_shape=jax.ShapeDtypeStruct(blocks.shape, blocks.dtype),
        in_specs=[vmem_spec()],
        out_specs=hbm_spec(),
        scratch_shapes=[
            pltpu.SemaphoreType.DMA,
            pltpu.SemaphoreType.DMA((count - 1,)),
            pltpu.SemaphoreType.DMA((count - 1,)),
        ],
        compiler_params=pltpu.CompilerParams(
            collective_id=ident, has_side_effects=True, vmem_limit_bytes=VMEM_LIMIT
        ),
        cost_estimate=cost(15),
        name="exchange",
    )(blocks)


def groups_kernel(count, x_ref, o_ref, local_sem, ssem, rsem):
    z = lax.axis_index("z")
    own = pltpu.make_async_copy(x_ref, o_ref.at[z], local_sem)
    own.start()
    targets = [{"z": lax.rem(z + hop, count)} for hop in range(1, count)]
    greet(targets)
    copies = [
        remote(x_ref, o_ref.at[z], ssem.at[i], rsem.at[i], device)
        for i, device in enumerate(targets)
    ]
    for one in copies:
        one.start()
    for one in copies:
        one.wait()
    own.wait()


def gather_groups(block, count, ident):
    return pl.pallas_call(
        functools.partial(groups_kernel, count),
        out_shape=jax.ShapeDtypeStruct((count,) + block.shape, block.dtype),
        in_specs=[vmem_spec()],
        out_specs=vmem_spec(),
        scratch_shapes=[
            pltpu.SemaphoreType.DMA,
            pltpu.SemaphoreType.DMA((count - 1,)),
            pltpu.SemaphoreType.DMA((count - 1,)),
        ],
        compiler_params=pltpu.CompilerParams(collective_id=ident, has_side_effects=True),
        cost_estimate=cost(5),
        name="gather_groups",
    )(block)


def gelu_tanh(values):
    return jax.nn.gelu(values, approximate=True)


def sigmoid(v):
    return 1.0 / (1.0 + jnp.exp(-v))


def gelu_pair(v):
    root = 0.7978845608028654
    cube = 0.044715
    square = v * v
    t = jnp.tanh(root * (v + cube * square * v))
    value = 0.5 * v * (1.0 + t)
    slope = 0.5 * (1.0 + t) + 0.5 * v * (1.0 - t * t) * root * (1.0 + 3.0 * cube * square)
    return value, slope


def tile_scan(keep, push, reverse):
    rows = lax.broadcasted_iota(jnp.int32, keep.shape, 0)
    count = keep.shape[0]
    hop = 1
    while hop < count:
        if reverse:
            inside = rows < count - hop
            shift = count - hop
        else:
            inside = rows >= hop
            shift = hop
        keep_near = jnp.where(inside, pltpu.roll(keep, shift, 0), 1.0)
        push_near = jnp.where(inside, pltpu.roll(push, shift, 0), 0.0)
        push = push + keep * push_near
        keep = keep * keep_near
        hop *= 2
    return keep, push


def conv_of(ext, masks, taps, offset, rows):
    value = offset + taps[0:1] * ext[pl.ds(8, rows)]
    for k in range(1, CONV):
        value = value + taps[k : k + 1] * ext[pl.ds(8 - k, rows)] * masks[:, k - 1 : k]
    return value


def forward_kernel(
    branch_ref,
    halo_ref,
    mask_ref,
    small_ref,
    wa_ref,
    wx_ref,
    conved_ref,
    keep_ref,
    prod_ref,
    state_ref,
    ext,
    carry,
):
    rows = branch_ref.shape[0]
    step = pl.program_id(0)

    @pl.when(step == 0)
    def _():
        ext[pl.ds(0, 8)] = halo_ref[...]
        carry[0:1] = jnp.ones_like(carry[0:1])
        carry[1:2] = jnp.zeros_like(carry[1:2])

    @pl.when(step > 0)
    def _():
        ext[pl.ds(0, 8)] = ext[pl.ds(rows, 8)]

    ext[pl.ds(8, rows)] = branch_ref[...].astype(f32)
    masks = mask_ref[...]
    conved = conv_of(ext, masks, small_ref, small_ref[4:5], rows).astype(bf16)
    conved_ref[...] = conved
    logit_a = jnp.dot(conved, wa_ref[...], preferred_element_type=f32) + small_ref[5:6]
    logit_x = jnp.dot(conved, wx_ref[...], preferred_element_type=f32) + small_ref[6:7]
    decay = jnp.exp(-decay_scale * sigmoid(logit_a) * small_ref[7:8])
    keep_ref[...] = decay * masks[:, 0:1]
    state_ref[...] = (
        jnp.sqrt(1.0 - decay * decay + push_shift) * sigmoid(logit_x) * conved.astype(f32)
    )

    def body(i, held):
        prod_in, state_in = held
        at = pl.ds(pl.multiple_of(i * 8, 8), 8)
        keep, push = tile_scan(keep_ref[at], state_ref[at], False)
        state = push + keep * state_in
        prod = keep * prod_in
        prod_ref[at] = prod
        state_ref[at] = state
        return prod[7:8], state[7:8]

    prod_out, state_out = lax.fori_loop(0, rows // 8, body, (carry[0:1], carry[1:2]))
    carry[0:1] = prod_out
    carry[1:2] = state_out


def forward_scan(branch_in, halo, masks, small, wa, wx, chunk):
    rows, width = branch_in.shape
    tile = pl.BlockSpec((chunk, width), lambda i: (i, 0))
    whole = lambda a: pl.BlockSpec(a.shape, lambda i: (0, 0))
    full = jax.ShapeDtypeStruct((rows, width), f32)
    return pl.pallas_call(
        forward_kernel,
        grid=(rows // chunk,),
        out_shape=(jax.ShapeDtypeStruct((rows, width), bf16), full, full, full),
        in_specs=[
            tile,
            whole(halo),
            pl.BlockSpec((chunk, masks.shape[1]), lambda i: (i, 0)),
            whole(small),
            whole(wa),
            whole(wx),
        ],
        out_specs=(tile, tile, tile, tile),
        scratch_shapes=[pltpu.VMEM((chunk + 8, width), f32), pltpu.VMEM((8, width), f32)],
        compiler_params=pltpu.CompilerParams(vmem_limit_bytes=VMEM_LIMIT),
        cost_estimate=cost(20),
        name="forward_scan",
    )(branch_in, halo, masks, small, wa, wx)


def adjoint_kernel(d_mixed_ref, gate_ref, keep_ref, prod_ref, adj_ref, keep_next, carry):
    rows = d_mixed_ref.shape[0]
    step = pl.program_id(0)

    @pl.when(step == 0)
    def _():
        keep_next[pl.ds(rows, 8)] = jnp.ones_like(keep_next[pl.ds(rows, 8)])
        carry[0:1] = jnp.ones_like(carry[0:1])
        carry[1:2] = jnp.zeros_like(carry[1:2])

    @pl.when(step > 0)
    def _():
        keep_next[pl.ds(rows, 8)] = keep_next[pl.ds(0, 8)]

    keep_next[pl.ds(0, rows)] = keep_ref[...]
    prod_ref[...] = keep_next[pl.ds(1, rows)]
    adj_ref[...] = d_mixed_ref[...] * gelu_tanh(gate_ref[...])
    tiles = rows // 8

    def body(i, held):
        prod_in, adj_in = held
        at = pl.ds(pl.multiple_of((tiles - 1 - i) * 8, 8), 8)
        keep, push = tile_scan(prod_ref[at], adj_ref[at], True)
        adj = push + keep * adj_in
        prod = keep * prod_in
        prod_ref[at] = prod
        adj_ref[at] = adj
        return prod[0:1], adj[0:1]

    prod_out, adj_out = lax.fori_loop(0, tiles, body, (carry[0:1], carry[1:2]))
    carry[0:1] = prod_out
    carry[1:2] = adj_out


def adjoint_scan(d_mixed, gate_pre, keep, chunk):
    rows, width = keep.shape
    last = rows // chunk - 1
    tile = pl.BlockSpec((chunk, width), lambda i: (last - i, 0))
    full = jax.ShapeDtypeStruct((rows, width), f32)
    return pl.pallas_call(
        adjoint_kernel,
        grid=(rows // chunk,),
        out_shape=(full, full),
        in_specs=[tile, tile, tile],
        out_specs=(tile, tile),
        scratch_shapes=[pltpu.VMEM((chunk + 8, width), f32), pltpu.VMEM((8, width), f32)],
        compiler_params=pltpu.CompilerParams(vmem_limit_bytes=VMEM_LIMIT),
        cost_estimate=cost(12),
        name="adjoint_scan",
    )(d_mixed, gate_pre, keep)


def backward_kernel(
    d_mixed_ref,
    gate_ref,
    state_ref,
    prod_ref,
    state_before_ref,
    prod_before_ref,
    adj_ref,
    adj_prod_ref,
    branch_ref,
    branch_before_ref,
    halo_ref,
    conved_ref,
    mask_ref,
    small_ref,
    enter_ref,
    wa_ref,
    wx_ref,
    d_gate_ref,
    d_branch_ref,
    sums_ref,
    edge_ref,
    ga_ref,
    gx_ref,
    ext,
    state_ext,
    later,
):
    rows, width = d_mixed_ref.shape
    step = pl.program_id(0)
    steps = pl.num_programs(0)
    state_in = enter_ref[0:1]
    adj_in = enter_ref[1:2]

    @pl.when(step == 0)
    def _():
        sums_ref[...] = jnp.zeros_like(sums_ref)
        ga_ref[...] = jnp.zeros_like(ga_ref)
        gx_ref[...] = jnp.zeros_like(gx_ref)
        for k in range(TAIL):
            later[k, pl.ds(rows, 8)] = jnp.zeros((8, width), f32)

    @pl.when(step > 0)
    def _():
        for k in range(TAIL):
            later[k, pl.ds(rows, 8)] = later[k, pl.ds(0, 8)]

    first = step == steps - 1

    @pl.when(first)
    def _():
        ext[pl.ds(0, 8)] = halo_ref[...]
        state_ext[pl.ds(0, 8)] = jnp.broadcast_to(state_in, (8, width))

    @pl.when(jnp.logical_not(first))
    def _():
        ext[pl.ds(0, 8)] = branch_before_ref[...].astype(f32)[8:16]
        state_ext[pl.ds(0, 8)] = state_before_ref[...] + prod_before_ref[...] * state_in

    ext[pl.ds(8, rows)] = branch_ref[...].astype(f32)
    state = state_ref[...] + prod_ref[...] * state_in
    state_ext[pl.ds(8, rows)] = state
    _, slope = gelu_pair(gate_ref[...])
    d_gate_ref[...] = (d_mixed_ref[...] * state * slope).astype(bf16)
    adjoint = adj_ref[...] + adj_prod_ref[...] * adj_in
    state_prev = state_ext[pl.ds(7, rows)]
    masks = mask_ref[...]
    conved_low = conved_ref[...]
    conved = conved_low.astype(f32)
    rates = small_ref[7:8]
    gate_a = sigmoid(
        jnp.dot(conved_low, wa_ref[...], preferred_element_type=f32) + small_ref[5:6]
    )
    gate_x = sigmoid(
        jnp.dot(conved_low, wx_ref[...], preferred_element_type=f32) + small_ref[6:7]
    )
    decay = jnp.exp(-decay_scale * gate_a * rates)
    root = jnp.sqrt(1.0 - decay * decay + push_shift)
    d_decay = adjoint * (state_prev * masks[:, 0:1] - gate_x * conved * decay / root)
    slope_a = -decay_scale * d_decay * decay * gate_a
    d_logit_a = (slope_a * rates * (1.0 - gate_a)).astype(bf16)
    through = adjoint * root * gate_x
    d_logit_x = (through * conved * (1.0 - gate_x)).astype(bf16)
    d_conved = (
        through
        + lax.dot_general(d_logit_a, wa_ref[...], contract_last, preferred_element_type=f32)
        + lax.dot_general(d_logit_x, wx_ref[...], contract_last, preferred_element_type=f32)
    )
    d_conved = d_conved.astype(bf16).astype(f32)
    ga_ref[...] += lax.dot_general(
        conved_low, d_logit_a, contract_first, preferred_element_type=f32
    )
    gx_ref[...] += lax.dot_general(
        conved_low, d_logit_x, contract_first, preferred_element_type=f32
    )

    def total(v):
        return jnp.sum(v, axis=0, keepdims=True)

    sums_ref[0:1] += total(d_conved * ext[pl.ds(8, rows)])
    for k in range(1, CONV):
        masked = d_conved * masks[:, k - 1 : k]
        later[k - 1, pl.ds(0, rows)] = masked
        sums_ref[k : k + 1] += total(masked * ext[pl.ds(8 - k, rows)])
    sums_ref[4:5] += total(d_conved)
    sums_ref[5:6] += total(d_logit_a.astype(f32))
    sums_ref[6:7] += total(d_logit_x.astype(f32))
    sums_ref[7:8] += total(slope_a)
    d_branch = small_ref[0:1] * d_conved
    for k in range(1, CONV):
        d_branch = d_branch + small_ref[k : k + 1] * later[k - 1, pl.ds(k, rows)]
    d_branch_ref[...] = d_branch.astype(bf16)

    @pl.when(first)
    def _():
        for back in range(1, CONV):
            value = jnp.zeros((1, width), f32)
            for k in range(back, CONV):
                value = value + small_ref[k : k + 1] * later[k - 1, pl.ds(k - back, 1)]
            edge_ref[8 - back : 9 - back] = value
        edge_ref[0 : 8 - TAIL] = jnp.zeros((8 - TAIL, width), f32)


def backward_scan(
    d_mixed, gate_pre, state, prod, adj, adj_prod, branch_in, halo, conved, masks, small, enter,
    wa, wx, chunk,
):
    rows, width = state.shape
    last = rows // chunk - 1
    tile = pl.BlockSpec((chunk, width), lambda i: (last - i, 0))

    def before(size):
        per = chunk // size
        return pl.BlockSpec((size, width), lambda i: (jnp.maximum((last - i) * per - 1, 0), 0))

    whole = lambda a: pl.BlockSpec(a.shape, lambda i: (0, 0))
    low = jax.ShapeDtypeStruct((rows, width), bf16)
    pinned = lambda shape: pl.BlockSpec(shape, lambda i: (0, 0))
    return pl.pallas_call(
        backward_kernel,
        grid=(rows // chunk,),
        out_shape=(
            low,
            low,
            jax.ShapeDtypeStruct((8, width), f32),
            jax.ShapeDtypeStruct((8, width), f32),
            jax.ShapeDtypeStruct((width, width), f32),
            jax.ShapeDtypeStruct((width, width), f32),
        ),
        in_specs=[
            tile,
            tile,
            tile,
            tile,
            before(8),
            before(8),
            tile,
            tile,
            tile,
            before(16),
            whole(halo),
            tile,
            pl.BlockSpec((chunk, masks.shape[1]), lambda i: (last - i, 0)),
            whole(small),
            whole(enter),
            whole(wa),
            whole(wx),
        ],
        out_specs=(
            tile,
            tile,
            pinned((8, width)),
            pinned((8, width)),
            pinned((width, width)),
            pinned((width, width)),
        ),
        scratch_shapes=[
            pltpu.VMEM((chunk + 8, width), f32),
            pltpu.VMEM((chunk + 8, width), f32),
            pltpu.VMEM((TAIL, chunk + 8, width), f32),
        ],
        compiler_params=pltpu.CompilerParams(vmem_limit_bytes=VMEM_LIMIT),
        cost_estimate=cost(25),
        name="backward_scan",
    )(
        d_mixed, gate_pre, state, prod, state, prod, adj, adj_prod, branch_in, branch_in, halo,
        conved, masks, small, enter, wa, wx,
    )


def pad_lanes(rows, width):
    have = rows.shape[-1]
    return jnp.pad(rows, ((0, 0), (0, width - have)))


def inverse_rms(rows):
    return lax.rsqrt(jnp.mean(rows * rows, axis=-1, keepdims=True) + norm_eps)


def norm_back(rows, scale, e):
    return scale * e - rows * (scale * scale * scale) * jnp.mean(e * rows, axis=-1, keepdims=True)


def on_device(
    tokens_in,
    segment_starts,
    cotangent,
    norm1_gain,
    rec_gate_weight,
    rec_in_weight,
    conv_weight,
    conv_bias,
    gate_a_weight,
    gate_a_bias,
    gate_x_weight,
    gate_x_bias,
    decay_rate,
    rec_out_weight,
    norm2_gain,
    mlp_gate_weight,
    mlp_up_weight,
    mlp_down_weight,
):
    count = lax.axis_size("z")
    z = lax.axis_index("z")
    spread = count // 2
    swap_axes = FEAT[len(FEAT) - (spread.bit_length() - 1) :]
    outer = NF // spread
    rows_tok, width = tokens_in.shape
    group_rows = NF * rows_tok
    chan_rows = conv_weight.shape[0]
    chans = chan_rows * count
    rows_w = rec_gate_weight.shape[0]
    ff_rows = mlp_down_weight.shape[0]
    ff = ff_rows * count
    chunk = 256

    def split_chan(w):
        return (
            w.reshape(rows_w, spread, 2, outer, BLK)
            .transpose(3, 1, 0, 2, 4)
            .reshape(NF, rows_w, chans)
        )

    def join_chan(w):
        return (
            w.reshape(outer, spread, rows_w, 2, BLK)
            .transpose(2, 1, 3, 0, 4)
            .reshape(rows_w, NF * chans)
        )

    def split_ff(w):
        return (
            w.reshape(rows_w, count, NF, ff_rows).transpose(2, 0, 1, 3).reshape(NF, rows_w, ff)
        )

    def join_ff(w):
        return (
            w.reshape(NF, rows_w, count, ff_rows).transpose(1, 2, 0, 3).reshape(rows_w, NF * ff)
        )

    pack = jnp.concatenate(
        [
            rec_out_weight,
            gate_a_weight,
            gate_x_weight,
            conv_weight,
            conv_bias[:, None],
            gate_a_bias[:, None],
            gate_x_bias[:, None],
            decay_rate[:, None],
        ],
        axis=1,
    )
    used = pack.shape[1]
    pack_width = -(-used // LANES) * LANES
    pack = pad_lanes(pack, pack_width)
    pack_all = lax.all_gather(pack, "z", axis=0, tiled=True)

    extra = jnp.concatenate(
        [
            pad_lanes(segment_starts.astype(bf16)[None], 2 * chans),
            pad_lanes(norm1_gain[None], 2 * chans),
            pad_lanes(norm2_gain[None], 2 * chans),
            jnp.zeros((13, 2 * chans), bf16),
        ],
        axis=0,
    )
    rec_send = jnp.concatenate(
        [
            jnp.concatenate(
                [split_chan(rec_gate_weight), split_chan(rec_in_weight)],
                axis=2,
            ),
            jnp.broadcast_to(extra[None], (NF, 16, 2 * chans)),
        ],
        axis=1,
    )
    rec_got = exchange(rec_send, FEAT, 3)
    w_rec = lax.all_gather(
        rec_got[:, :rows_w].reshape(NF * rows_w, 2 * chans), "z", axis=0, tiled=True
    )
    starts = rec_got[:, rows_w, :rows_tok].reshape(group_rows).astype(f32)

    plane_gains = jnp.stack(
        [
            rec_got[:, rows_w + 1, :rows_w].reshape(NF * rows_w),
            rec_got[:, rows_w + 2, :rows_w].reshape(NF * rows_w),
        ]
    ).astype(f32)
    gains = gather_groups(jnp.pad(plane_gains, ((0, 6), (0, 0))), count, 7)
    gain_one = gains[:, 0].reshape(1, width)
    gain_two = gains[:, 1].reshape(1, width)

    tok = tokens_in.astype(f32)
    tok_group = gather_feature(tokens_in).astype(f32)
    normed = (tok_group * inverse_rms(tok_group) * gain_one).astype(bf16)

    mlp_send = jnp.concatenate([split_ff(mlp_gate_weight), split_ff(mlp_up_weight)], axis=2)
    mlp_got = exchange(mlp_send, FEAT, 4)
    w_mlp = lax.all_gather(mlp_got.reshape(NF * rows_w, 2 * ff), "z", axis=0, tiled=True)
    w_down = lax.all_gather(mlp_down_weight, "z", axis=0, tiled=True)

    pack_swap = exchange(pack_all.reshape(spread, 2, chan_rows, pack_width), swap_axes, 5)
    mine = pack_swap.transpose(1, 0, 2, 3).reshape(chans, pack_width)
    w_out = mine[:, :width]
    small = mine[:, width + 2 * BLK : used].astype(f32).T

    unit = lax.broadcasted_iota(jnp.int32, (chans, chans), 0) // BLK
    same_block = unit == lax.broadcasted_iota(jnp.int32, (chans, chans), 1) // BLK

    def block_diag(w):
        return jnp.where(same_block, jnp.concatenate([w, w], axis=1), jnp.zeros((), w.dtype))

    wa = block_diag(mine[:, width : width + BLK])
    wx = block_diag(mine[:, width + BLK : width + 2 * BLK])

    open_one = 1.0 - starts
    ahead = jnp.concatenate([jnp.ones((TAIL,), f32), open_one])
    open_two = open_one * ahead[TAIL - 1 : TAIL - 1 + group_rows]
    open_three = open_two * ahead[TAIL - 2 : TAIL - 2 + group_rows]
    masks = jnp.stack([open_one, open_two, open_three], axis=1)
    end = open_one[group_rows - 2 :]
    later_open = jnp.stack([end[0] * end[1], end[1], jnp.ones((), f32)])[:, None]

    rec_pre = jnp.dot(normed, w_rec, preferred_element_type=f32)
    gate_pre = rec_pre[:, :chans]
    branch_in = rec_pre[:, chans:].astype(bf16)
    lane_pad = -(-chans // LANES) * LANES

    def over_groups(rows):
        total = rows.shape[0]
        block = jnp.pad(rows, ((8 - total, 0), (0, lane_pad - chans)))
        return gather_groups(block, count, 2)[:, 8 - total :, :chans]

    tails = over_groups(branch_in[group_rows - TAIL :].astype(f32) * later_open)
    before = lax.dynamic_index_in_dim(tails, jnp.maximum(z - 1, 0), 0, False)
    before = jnp.where(z > 0, before, 0.0)
    halo = jnp.pad(before, ((8 - TAIL, 0), (0, 0)))
    conved, keep, prod, state_local = forward_scan(branch_in, halo, masks, small, wa, wx, chunk)
    ends = over_groups(jnp.stack([prod[group_rows - 1], state_local[group_rows - 1]]))
    state_in = jnp.zeros((chans,), f32)
    for hop in range(count - 1):
        state_in = jnp.where(hop < z, ends[hop, 0] * state_in + ends[hop, 1], state_in)
    mixed = ((state_local + prod * state_in) * gelu_tanh(gate_pre)).astype(bf16)
    middle = tok + scatter_feature(jnp.dot(mixed, w_out, preferred_element_type=f32).astype(bf16))

    scale_two = inverse_rms(middle)
    normed_two = gather_feature((middle * scale_two * gain_two).astype(bf16))
    cot_own, normed_two = lax.optimization_barrier((cotangent, normed_two))
    cot = gather_feature(cot_own)
    mlp_pre = jnp.dot(normed_two, w_mlp, preferred_element_type=f32)
    d_hidden = lax.dot_general(cot, w_down, contract_last, preferred_element_type=f32)
    mlp_gate, mlp_up = mlp_pre[:, :ff], mlp_pre[:, ff:]
    act, slope = gelu_pair(mlp_gate)
    hidden = (act * mlp_up).astype(bf16)
    d_mlp = jnp.concatenate(
        [(d_hidden * mlp_up * slope).astype(bf16), (d_hidden * act).astype(bf16)], axis=1
    )
    down_part = lax.dot_general(
        hidden, cot, contract_first, preferred_element_type=f32
    ).astype(bf16)
    mlp_part = lax.dot_general(
        normed_two, d_mlp, contract_first, preferred_element_type=f32
    ).astype(bf16)
    d_mlp, down_part, mlp_part = lax.optimization_barrier((d_mlp, down_part, mlp_part))
    down_sum = lax.psum_scatter(down_part, "z", scatter_dimension=0, tiled=True)
    mlp_sum = lax.psum_scatter(mlp_part, "z", scatter_dimension=0, tiled=True)
    e_two = gain_two * scatter_feature(
        lax.dot_general(d_mlp, w_mlp, contract_last, preferred_element_type=f32).astype(bf16)
    )
    d_middle = cotangent.astype(f32) + norm_back(middle, scale_two, e_two)
    d_rec = gather_feature(d_middle.astype(bf16))

    d_mixed = lax.dot_general(d_rec, w_out, contract_last, preferred_element_type=f32)
    adj_prod, adj_local = adjoint_scan(d_mixed, gate_pre, keep, chunk)
    heads = over_groups(jnp.stack([keep[0] * adj_prod[0], keep[0] * adj_local[0]]))
    adj_in = jnp.zeros((chans,), f32)
    for hop in range(count - 1, 0, -1):
        adj_in = jnp.where(hop > z, heads[hop, 0] * adj_in + heads[hop, 1], adj_in)
    enter = jnp.pad(jnp.stack([state_in, adj_in]), ((0, 6), (0, 0)))
    d_gate, d_branch, sums, edge, grad_a, grad_x = backward_scan(
        d_mixed, gate_pre, state_local, prod, adj_local, adj_prod, branch_in, halo, conved, masks,
        small, enter, wa, wx, chunk,
    )
    edges = over_groups(edge[8 - TAIL :])
    after = lax.dynamic_index_in_dim(edges, jnp.minimum(z + 1, count - 1), 0, False)
    after = jnp.where(z < count - 1, after, 0.0) * later_open
    tail_sum = (d_branch[group_rows - TAIL :].astype(f32) + after).astype(bf16)
    d_branch = jnp.concatenate([d_branch[: group_rows - TAIL], tail_sum], axis=0)
    d_rec_pre = jnp.concatenate([d_gate, d_branch], axis=1)
    rec_part = lax.dot_general(
        normed, d_rec_pre, contract_first, preferred_element_type=f32
    ).astype(bf16)
    fold = (
        lax.broadcasted_iota(jnp.int32, (chans, BLK), 0) % BLK
        == lax.broadcasted_iota(jnp.int32, (chans, BLK), 1)
    ).astype(bf16)

    def diagonal(w):
        kept = jnp.where(same_block, w, 0.0).astype(bf16)
        return jnp.dot(kept, fold, preferred_element_type=f32).astype(bf16)

    grad_out = lax.dot_general(mixed, d_rec, contract_first, preferred_element_type=f32)
    back_pack = jnp.concatenate(
        [grad_out.astype(bf16), diagonal(grad_a), diagonal(grad_x), sums.T.astype(bf16)], axis=1
    )
    back_pack = pad_lanes(back_pack, pack_width)
    back_pack = back_pack.reshape(2, spread, chan_rows, pack_width).transpose(1, 0, 2, 3)
    back_swap = exchange(back_pack, swap_axes, 5).reshape(count * chan_rows, pack_width)
    d_rec_pre, rec_part, back_swap, hidden, mlp_sum, down_sum = lax.optimization_barrier(
        (d_rec_pre, rec_part, back_swap, hidden, mlp_sum, down_sum)
    )
    rec_sum = lax.psum_scatter(rec_part, "z", scatter_dimension=0, tiled=True)
    pack_sum = lax.psum_scatter(back_swap, "z", scatter_dimension=0, tiled=True).astype(f32)
    e_one = gain_one * scatter_feature(
        lax.dot_general(d_rec_pre, w_rec, contract_last, preferred_element_type=f32).astype(bf16)
    )
    grad_tokens = d_middle + norm_back(tok, inverse_rms(tok), e_one)
    layer_out = (
        middle
        + scatter_feature(jnp.dot(hidden, w_down, preferred_element_type=f32).astype(bf16))
    ).astype(bf16)

    mlp_back = exchange(mlp_sum.reshape(NF, rows_w, 2 * ff), FEAT, 4).astype(f32)
    grad_gate, grad_up = join_ff(mlp_back[:, :, :ff]), join_ff(mlp_back[:, :, ff:])
    rec_back = exchange(rec_sum.reshape(NF, rows_w, 2 * chans), FEAT, 6).astype(f32)
    grad_rec_gate = join_chan(rec_back[:, :, :chans])
    grad_rec_in = join_chan(rec_back[:, :, chans:])

    def gain_grad(gain, w_one, g_one, w_two, g_two):
        total = jnp.sum(w_one.astype(f32) * g_one + w_two.astype(f32) * g_two, axis=1)
        return total / gain.astype(f32)

    base = width + 2 * BLK
    return (
        layer_out,
        grad_tokens,
        gain_grad(norm1_gain, rec_gate_weight, grad_rec_gate, rec_in_weight, grad_rec_in),
        grad_rec_gate,
        grad_rec_in,
        pack_sum[:, base : base + CONV],
        pack_sum[:, base + CONV],
        pack_sum[:, width : width + BLK],
        pack_sum[:, base + CONV + 1],
        pack_sum[:, width + BLK : base],
        pack_sum[:, base + CONV + 2],
        pack_sum[:, base + CONV + 3],
        pack_sum[:, :width],
        gain_grad(norm2_gain, mlp_gate_weight, grad_gate, mlp_up_weight, grad_up),
        grad_gate,
        grad_up,
        down_sum.astype(f32),
    )


def solution(mesh):
    wide, narrow = mesh.shape["wide"], mesh.shape["narrow"]
    groups = wide * narrow // NF
    grid = Mesh(mesh.devices.reshape((groups,) + (2,) * len(FEAT)), ("z",) + FEAT)
    flat = P(("z",) + FEAT)
    wide_rows = P(("z",) + FEAT, None)
    one, two = flat, wide_rows
    return jax.shard_map(
        on_device,
        mesh=grid,
        in_specs=(
            two, one, two, one, two, two, two, one, two, one, two, one, one, two, one, two, two, two,
        ),
        out_specs=(
            two, two, one, two, two, two, one, two, one, two, one, one, two, one, two, two, two,
        ),
        check_vma=False,
    )
```

time: 3470 us -> 830 us (0.24)
  waiting for transfers between devices: 2280 us -> 1.18 us
  Pallas kernels: 0 us -> 502 us
  blocking collectives: 345 us -> 0 us
  local copies, waits for them, and re-layouts: 357 us -> 79.5 us
  other arithmetic: 195 us -> 61.2 us
  matrix products: 256 us -> 159 us
    reduce_scatter x6 -> x4, waiting for transfers between devices: 2060 us -> 0.01 us  [the longest x1 0.01 us: on_device(): down_sum = lax.psum_scatter(down_part, 'z', scatter_dimension=0, tiled=True)]
    pallas_call x0 -> x22, Pallas kernels: none -> 502 us  [the longest x4 169 us: scatter_feature(): pl.pallas_call(scatter_kernel, out_shape=jax.ShapeDtypeStruct((rows, widt...]
    all_gather x6 -> x0, blocking collectives: 255 us -> none  [the longest x3 120 us: carried_in(): gathered = jax.tree.map(lambda a: lax.all_gather(a, axis), part)]
    all_gather x6 -> x4, waiting for transfers between devices: 221 us -> 0.03 us  [the longest x1 0.02 us: on_device(): lax.all_gather(mlp_got.reshape(NF * rows_w, 2 * ff), 'z', axis=0, tiled=T...]
    slice x116 -> x18, local copies, waits for them, and re-layouts: 165 us -> 19.9 us  [the longest x1 3.38 us: on_device(): mlp_back[:, :, :ff]]
    dot_general x24 -> x14, matrix products: 256 us -> 159 us  [the longest x1 20.4 us: on_device(): lax.dot_general(d_mlp, w_mlp, contract_last, preferred_element_type=f32)]
    concatenate x28 -> x5, other arithmetic: 104 us -> 12 us  [the longest x1 6.7 us: on_device(): jnp.concatenate([(d_hidden * mlp_up * slope).astype(bf16), (d_hidden * ac...]
    unnamed x2 -> x0, blocking collectives: 90.2 us -> none
  transfers between devices with their start and end apart: 15 -> 8, of which waited for: 8 -> 0; matrix products, arithmetic and copies ran while one was open for 14% -> 28% of each run, Pallas kernels for 0% -> 60%
where the time goes in v1:
time: 830 us; the launch traced here: 821 us
  Pallas kernels  502 us (60%)
  matrix products  159 us (19%)
  local copies, waits for them, and re-layouts  79.5 us (10%)
  other arithmetic  61.2 us (7%)
  between operations  16.8 us (2%)
    pallas_call x4, Pallas kernels, scatter_feature(): pl.pallas_call(scatter_kernel, out_shape=jax.ShapeDtypeStruct((rows, widt...  169 us
    pallas_call x4, Pallas kernels, gather_feature(): pl.pallas_call(gather_kernel, out_shape=jax.ShapeDtypeStruct((NF, rows, w...  163 us
    pallas_call x6, Pallas kernels, exchange(): pl.pallas_call(functools.partial(exchange_kernel, axes), out_shape=jax.Sh...  79.8 us
    pallas_call x5, Pallas kernels, gather_groups(): pl.pallas_call(functools.partial(groups_kernel, count), out_shape=jax.Sha...  42.8 us
    pallas_call x1, Pallas kernels, backward_scan(): pl.pallas_call(backward_kernel, grid=(rows // chunk,), out_shape=(low, lo...  21.3 us
    dot_general x1, matrix products, on_device(): lax.dot_general(d_mlp, w_mlp, contract_last, preferred_element_type=f32)  20.4 us
    dot_general x1, matrix products, on_device(): lax.dot_general(cot, w_down, contract_last, preferred_element_type=f32)  20.1 us
    dot_general x1, matrix products, on_device(): mlp_pre = jnp.dot(normed_two, w_mlp, preferred_element_type=f32)  19 us
  transfers between devices with their start and end apart: 8, of which 0 were waited for; matrix products, arithmetic and copies ran while one was open for 28% of the time, Pallas kernels for 60%

profile of v1, /device:TPU:0, one launch (start us, length us, event | category | flops | bytes accessed | tf_op | source)
XLA Modules:
  0.0 820.5 jit_solution(1015302704003108014)
XLA Ops:
  13.1 1.5 reshape.376
  18.0 15.7 %exchange.6 = bf16[8,80,640]{2,1,0:T(8,128)(2,1)} custom-call(bf16[8,80,640]{2,1,0:T(8,128)(2,1)} %pad_maximum_fusion.3.x_ref), custom_call_target="tpu_custom_call" | custom-call | bytes 45000000 | tf_op jit(solution)/shard_map/exchange/pallas_call | solution.py:292
  33.7 2.0 slice.183
  37.3 1.8 reshape.387
  43.0 22.5 %exchange.8 = bf16[8,64,1536]{2,1,0:T(8,128)(2,1)} custom-call(bf16[8,64,1536]{2,1,0:T(8,128)(2,1)} %pad_maximum_fusion.2.x_ref), custom_call_target="tpu_custom_call" | custom-call | bytes 45000000 | tf_op jit(solution)/shard_map/exchange/pallas_call | solution.py:292
  70.2 8.5 %gather_groups.5 = f32[4,8,512]{2,1,0:T(8,128)} custom-call(f32[8,512]{1,0:T(8,128)} %fusion.44.x_ref), custom_call_target="tpu_custom_call" | custom-call | bytes 15000000 | tf_op jit(solution)/shard_map/gather_groups/pallas_call | solution.py:328
  79.7 40.6 %gather_feature.4 = bf16[8,256,2048]{2,1,0:T(8,128)(2,1)} custom-call(bf16[256,2048]{1,0:T(8,128)(2,1)} %x_ref.1), custom_call_target="tpu_custom_call" | custom-call | bytes 120000000 | tf_op jit(solution)/shard_map/gather_feature/pallas_call | solution.py:112
  120.2 5.5 multiply_reduce_fusion
  129.2 8.5 %fusion.1 = bf16[2048,2048]{1,0:T(8,128)(2,1)} fusion(f32[2048]{0:T(1024)S(1)} %bitcast.177, f32[2048]{0:T(1024)S(1)} %bitcast.186, bf16[8,256,2048]{2,1,0:T(8,128)(2,1)} %gather_feature.4), kind=kLoop, calls=%fused_computation.2 | loop fusion | flops 16777216 | bytes 16793600 | tf_op jit(solution)/shard_map/convert_element_type | solution.py:835
  137.7 3.8 exchange.7
  141.6 1.5 copy.122
  145.4 11.4 %fusion.65 = (bf16[2048,640]{1,0:T(8,128)(2,1)S(1)}, f32[2048,640]{1,0:T(8,128)}) fusion(bf16[2048,2048]{1,0:T(8,128)(2,1)} %fusion.1, bf16[2048,640]{1,0:T(8,128)(2,1)} %all-gather.5.cloned.1.call-done), kind=kOutput, calls=%fused_computation.170 | convolution fusion | flops 5370019840 | bytes 18874368 | tf_op jit(solution)/shard_map/dot_general | solution.py:864
  156.8 1.9 slice.233.branch_ref.branch_before_ref
  159.3 8.3 %gather_groups.6 = f32[4,8,384]{2,1,0:T(8,128)} custom-call(f32[8,384]{1,0:T(8,128)} %pad.53.x_ref), custom_call_target="tpu_custom_call" | custom-call | bytes 15000000 | tf_op jit(solution)/shard_map/gather_groups/pallas_call | solution.py:328
  169.1 15.3 %forward_scan.1 = (bf16[2048,320]{1,0:T(8,128)(2,1)}, f32[2048,320]{1,0:T(8,128)}, f32[2048,320]{1,0:T(8,128)}, f32[2048,320]{1,0:T(8,128)}) custom-call(bf16[2048,320]{1,0:T(8,128)(2,1)} %slice.233.branch_ref.branch_before_ref, f32[8,320]{1,0:T(8,128)} %pad.54.halo_ref, f32[2048,3]{1,0:T(8,128)} %copy.123.mask_ref, f32[8,320]{1,0:T(8,128)} %copy.124.small_ref, ...), custom_call_target="tpu_custom_call" | custom-call | bytes 60000000 | tf_op jit(solution)/shard_map/forward_scan/pallas_call | solution.py:447
  186.4 11.8 %gather_groups.7 = f32[4,8,384]{2,1,0:T(8,128)} custom-call(f32[8,384]{1,0:T(8,128)} %select_maximum_fusion.2.x_ref), custom_call_target="tpu_custom_call" | custom-call | bytes 15000000 | tf_op jit(solution)/shard_map/gather_groups/pallas_call | solution.py:328
  200.5 6.6 fusion.58
  207.1 7.0 convolution_convert_fusion.3
  214.1 42.9 %scatter_feature.4 = f32[256,2048]{1,0:T(8,128)} custom-call(bf16[8,256,2048]{2,1,0:T(8,128)(2,1)} %bitcast.148), custom_call_target="tpu_custom_call" | custom-call | bytes 135000000 | tf_op jit(solution)/shard_map/scatter_feature/pallas_call | solution.py:233
  257.0 2.1 multiply_reduce_fusion.2
  260.5 40.7 %gather_feature.5 = bf16[8,256,2048]{2,1,0:T(8,128)(2,1)} custom-call(bf16[256,2048]{1,0:T(8,128)(2,1)} %multiply_convert_fusion.3.x_ref), custom_call_target="tpu_custom_call" | custom-call | bytes 120000000 | tf_op jit(solution)/shard_map/gather_feature/pallas_call | solution.py:112
  301.2 40.9 %gather_feature.6 = bf16[8,256,2048]{2,1,0:T(8,128)(2,1)} custom-call(bf16[256,2048]{1,0:T(8,128)(2,1)} %x_ref.2), custom_call_target="tpu_custom_call" | custom-call | bytes 120000000 | tf_op jit(solution)/shard_map/gather_feature/pallas_call | solution.py:112
  342.1 19.0 %fusion.66 = f32[2048,1536]{0,1:T(8,128)} fusion(bf16[2048,2048]{1,0:T(8,128)(2,1)} %bitcast.153, bf16[2048,1536]{1,0:T(8,128)(2,1)} %all-gather.11.cloned.1.call-done), kind=kOutput, calls=%fused_computation.171 | convolution fusion | flops 12884901888 | bytes 27262976 | tf_op jit(solution)/shard_map/dot_general | solution.py:890
  361.1 20.1 %multiply_convert_fusion.2 = (bf16[2048,768]{0,1:T(8,128)(2,1)}, bf16[2048,768]{0,1:T(8,128)(2,1)}, bf16[2048,768]{0,1:T(8,128)(2,1)}) fusion(f32[2048,1536]{0,1:T(8,128)} %fusion.66, bf16[2048,2048]{1,0:T(8,128)(2,1)} %bitcast.151, bf16[768,2048]{1,0:T(8,128)(2,1)} %all-gather.9.cloned.1.call-done), kind=kOutput, calls=%fused_computation.15 | convolution fusion | flops 6480199680 | bytes 33554432 | tf_op jit(solution)/shard_map/dot_general | solution.py:891
  381.2 17.3 %convolution_convert_fusion.4 = bf16[2048,1536]{1,0:T(8,128)(2,1)} fusion(bf16[2048,2048]{1,0:T(8,128)(2,1)S(1)} %bitcast.154, bf16[2048,768]{0,1:T(8,128)(2,1)} %get-tuple-element.150, bf16[2048,768]{0,1:T(8,128)(2,1)} %get-tuple-element.149), kind=kOutput, calls=%fused_computation.9 | convolution fusion | flops 12900630528 | bytes 20971520 | tf_op jit(solution)/shard_map/dot_general | solution.py:901
  398.5 6.7 pad_maximum_fusion
  405.2 10.2 %convolution_convert_fusion.5 = bf16[768,2048]{1,0:T(8,128)(2,1)} fusion(bf16[2048,768]{0,1:T(8,128)(2,1)S(1)} %copy-done.43, bf16[2048,2048]{1,0:T(8,128)(2,1)} %bitcast.152), kind=kOutput, calls=%fused_computation.22 | convolution fusion | flops 6444023808 | bytes 14680064 | tf_op jit(solution)/shard_map/dot_general | solution.py:898
  416.1 20.4 %convolution_convert_fusion.2 = bf16[2048,2048]{1,0:T(8,128)(2,1)} fusion(bf16[2048,1536]{0,1:T(8,128)(2,1)} %pad_maximum_fusion, bf16[2048,1536]{1,0:T(8,128)(2,1)} %all-gather.11.cloned.1.call-done), kind=kOutput, calls=%fused_computation.7 | convolution fusion | flops 12889096192 | bytes 20971520 | tf_op jit(solution)/shard_map/dot_general | solution.py:908
  436.5 41.9 %scatter_feature.5 = f32[256,2048]{1,0:T(8,128)} custom-call(bf16[8,256,2048]{2,1,0:T(8,128)(2,1)} %bitcast.145), custom_call_target="tpu_custom_call" | custom-call | bytes 135000000 | tf_op jit(solution)/shard_map/scatter_feature/pallas_call | solution.py:233
  478.4 2.9 fusion.14
  481.3 2.5 fusion.56
  483.8 40.9 %gather_feature.7 = bf16[8,256,2048]{2,1,0:T(8,128)(2,1)} custom-call(bf16[256,2048]{1,0:T(8,128)(2,1)} %get-tuple-element.145.x_ref), custom_call_target="tpu_custom_call" | custom-call | bytes 120000000 | tf_op jit(solution)/shard_map/gather_feature/pallas_call | solution.py:112
  524.7 8.6 %fusion.19.d_mixed_ref = f32[2048,320]{1,0:T(8,128)} fusion(bf16[2048,2048]{1,0:T(8,128)(2,1)} %bitcast.149, bf16[320,2432]{1,0:T(8,128)(2,1)S(1)} %bitcast.170), kind=kOutput, calls=%fused_computation.49 | convolution fusion | flops 2684354560 | bytes 12320768 | tf_op jit(solution)/shard_map/dot_general | solution.py:913
  533.4 11.5 %adjoint_scan.1 = (f32[2048,320]{1,0:T(8,128)}, f32[2048,320]{1,0:T(8,128)}) custom-call(f32[2048,320]{1,0:T(8,128)} %fusion.19.d_mixed_ref, f32[2048,320]{1,0:T(8,128)} %get-tuple-element.152.gate_ref, f32[2048,320]{1,0:T(8,128)} %get-tuple-element.45.keep_ref), custom_call_target="tpu_custom_call" | custom-call | bytes 36000000 | tf_op jit(solution)/shard_map/adjoint_scan/pallas_call | solution.py:506
  546.2 7.3 gather_groups.8
  555.0 21.3 %backward_scan.1 = (bf16[2048,320]{1,0:T(8,128)(2,1)}, bf16[2048,320]{1,0:T(8,128)(2,1)}, f32[8,320]{1,0:T(8,128)}, f32[8,320]{1,0:T(8,128)}, f32[320,320]{1,0:T(8,128)}, /*index=5*/f32[320,320]{1,0:T(8,128)}) custom-call(f32[2048,320]{1,0:T(8,128)} %fusion.19.d_mixed_ref, f32[2048,320]{1,0:T(8,128)} %get-tuple-element.152.gate_ref, ...), custom_call_target="tpu_custom_call" | custom-call | bytes 75000000 | tf_op jit(solution)/shard_map/backward_scan/pallas_call | solution.py:657
  576.3 1.6 convolution_convert_fusion.9
  578.1 2.3 convolution_convert_fusion.8
  582.8 7.8 convolution_convert_fusion.7
  590.7 3.7 concatenate.47
  594.4 1.5 pad.60
  597.1 3.8 exchange.9
  601.6 6.9 gather_groups.9
  610.1 2.8 fusion.13
  612.9 1.6 copy-done.15
  614.5 10.4 %convolution_convert_fusion.6 = bf16[2048,640]{1,0:T(8,128)(2,1)} fusion(bf16[2048,2048]{1,0:T(8,128)(2,1)} %fusion.1, bf16[2048,640]{1,0:T(8,128)(2,1)S(1)} %fusion.13), kind=kOutput, calls=%fused_computation.23 | convolution fusion | flops 5370019840 | bytes 13631488 | tf_op jit(solution)/shard_map/dot_general | solution.py:930
  625.0 22.2 %exchange.11 = bf16[8,64,1536]{2,1,0:T(8,128)(2,1)} custom-call(bf16[8,64,1536]{2,1,0:T(8,128)(2,1)} %bitcast.174), custom_call_target="tpu_custom_call" | custom-call | bytes 45000000 | tf_op jit(solution)/shard_map/exchange/pallas_call | solution.py:292
  647.2 3.4 fusion.59
  650.6 3.9 reshape.403
  654.4 4.2 copy.138
  658.6 3.0 reshape.404
  661.6 3.7 reshape.405
  665.3 4.2 copy.139
  669.4 3.0 reshape.406
  672.4 11.2 %convolution_convert_fusion = bf16[2048,2048]{1,0:T(8,128)(2,1)} fusion(bf16[2048,640]{1,0:T(8,128)(2,1)} %copy-done.15, bf16[2048,640]{1,0:T(8,128)(2,1)} %all-gather.5.cloned.1.call-done), kind=kOutput, calls=%fused_computation.5 | convolution fusion | flops 5372903424 | bytes 13631488 | tf_op jit(solution)/shard_map/dot_general | solution.py:955
  683.7 41.9 %scatter_feature.7 = f32[256,2048]{1,0:T(8,128)} custom-call(bf16[8,256,2048]{2,1,0:T(8,128)(2,1)} %bitcast.146), custom_call_target="tpu_custom_call" | custom-call | bytes 135000000 | tf_op jit(solution)/shard_map/scatter_feature/pallas_call | solution.py:233
  725.6 11.2 %convolution_convert_fusion.1 = bf16[2048,2048]{1,0:T(8,128)(2,1)} fusion(bf16[2048,768]{0,1:T(8,128)(2,1)} %get-tuple-element.57, bf16[768,2048]{1,0:T(8,128)(2,1)S(1)} %copy-done.40), kind=kOutput, calls=%fused_computation.6 | convolution fusion | flops 6446645248 | bytes 14680064 | tf_op jit(solution)/shard_map/dot_general | solution.py:960
  736.8 42.0 %scatter_feature.6 = f32[256,2048]{1,0:T(8,128)} custom-call(bf16[8,256,2048]{2,1,0:T(8,128)(2,1)} %bitcast.147), custom_call_target="tpu_custom_call" | custom-call | bytes 135000000 | tf_op jit(solution)/shard_map/scatter_feature/pallas_call | solution.py:233
  778.9 2.6 convert_element_type.201
  783.7 2.6 fusion.17
  788.8 1.9 slice.253
  791.4 1.6 fusion.62
  793.0 11.8 %exchange.10 = bf16[8,64,640]{2,1,0:T(8,128)(2,1)} custom-call(bf16[8,64,640]{2,1,0:T(8,128)(2,1)} %bitcast.176), custom_call_target="tpu_custom_call" | custom-call | bytes 45000000 | tf_op jit(solution)/shard_map/exchange/pallas_call | solution.py:292
  811.2 1.5 add_reduce_fusion.1
  (201 shorter events, 54.2 us)
Async XLA Ops:
  7.2 8.2 copy-start.21
  7.2 130.5 %all-gather.7.cloned.1.call-start = ((), (), s32[]{:S(2)}) async-start(), calls=%async_computation.5 | async-start | bytes 1945600 | tf_op jit(solution)/shard_map/all_gather | solution.py:796
  13.1 3.6 copy-start.41
  13.1 3.7 copy-start.36
  13.1 3.7 copy-start.38
  13.1 132.3 %all-gather.5.cloned.1.call-start = ((), (), s32[]{:S(2)}) async-start(), calls=%async_computation.4 | async-start | bytes 3276800 | tf_op jit(solution)/shard_map/all_gather | solution.py:818
  16.4 19.4 %copy-start.12 = (bf16[64,6144]{1,0:T(8,128)(2,1)S(1)}, bf16[64,6144]{1,0:T(8,128)(2,1)}, u32[]{:S(2)}) copy-start(bf16[64,6144]{1,0:T(8,128)(2,1)} %param.33) | copy-start | bytes 2359300
  35.7 3.5 copy-start.10
  35.7 306.4 %all-gather.11.cloned.1.call-start = ((), (), s32[]{:S(2)}) async-start(), calls=%async_computation.7 | async-start | bytes 7864320 | tf_op jit(solution)/shard_map/all_gather | solution.py:839
  40.4 1.4 copy-start.14
  65.5 295.6 %all-gather.9.cloned.1.call-start = ((), (), s32[]{:S(2)}) async-start(), calls=%async_computation.6 | async-start | bytes 3932160 | tf_op jit(solution)/shard_map/all_gather | solution.py:840
  66.1 558.8 %reduce-scatter.7.cloned.1.call-start = ((), (), s32[]{:S(2)}) async-start(), calls=%async_computation.9 | async-start | bytes 3932160 | tf_op jit(solution)/shard_map/reduce_scatter | solution.py:905
  68.2 76.0 %copy-start.24 = (s32[320]{0:T(512)}, s32[320]{0:T(512)S(1)}, u32[]{:S(2)}) copy-start(s32[320]{0:T(512)S(1)} %get-tuple-element.178) | copy-start | bytes 3844
  68.3 76.0 %copy-start.26 = (s32[320]{0:T(512)}, s32[320]{0:T(512)S(1)}, u32[]{:S(2)}) copy-start(s32[320]{0:T(512)S(1)} %get-tuple-element.179) | copy-start | bytes 3844
  68.8 75.4 %copy-start.34 = (pred[320]{0:T(512)(128)(4,1)}, pred[320]{0:T(512)(128)(4,1)S(1)}, u32[]{:S(2)}) copy-start(pred[320]{0:T(512)(128)(4,1)S(1)} %get-tuple-element.182) | copy-start | bytes 964
  79.7 49.5 %copy-start.22 = (f32[4,1,512]{2,1,0:T(1,128)}, f32[4,1,512]{2,1,0:T(1,128)S(1)}, u32[]{:S(2)}) copy-start(f32[4,1,512]{2,1,0:T(1,128)S(1)} %get-tuple-element.167) | copy-start | bytes 24580
  129.2 29.5 %copy-start.30 = (f32[3]{0:T(128)}, f32[3]{0:T(128)S(1)}, u32[]{:S(2)}) copy-start(f32[3]{0:T(128)S(1)} %pad_maximum_fusion.5) | copy-start | bytes 40
  143.1 64.0 %copy-start.18 = (bf16[2,2,80,2432]{3,2,1,0:T(8,128)(2,1)}, bf16[2,2,80,2432]{3,2,1,0:T(8,128)(2,1)S(1)}, u32[]{:S(2)}) copy-start(bf16[2,2,80,2432]{3,2,1,0:T(8,128)(2,1)S(1)} %copy.122) | copy-start | bytes 4669444
  207.1 7.0 copy-start.20
  214.1 42.9 %copy-start.1 = (bf16[256,2048]{1,0:T(8,128)(2,1)S(1)}, bf16[256,2048]{1,0:T(8,128)(2,1)}, u32[]{:S(2)}) copy-start(bf16[256,2048]{1,0:T(8,128)(2,1)} %x_ref.1) | copy-start | bytes 3145732
  256.9 2.3 copy-start
  361.1 20.1 %copy-start.5 = (bf16[8,256,2048]{2,1,0:T(8,128)(2,1)S(1)}, bf16[8,256,2048]{2,1,0:T(8,128)(2,1)}, u32[]{:S(2)}) copy-start(bf16[8,256,2048]{2,1,0:T(8,128)(2,1)} %gather_feature.5) | copy-start | bytes 25165828
  398.5 6.7 copy-start.43
  415.4 209.5 %reduce-scatter.5.cloned.1.call-start = ((), (), s32[]{:S(2)}) async-start(), calls=%async_computation.8 | async-start | bytes 7864320 | tf_op jit(solution)/shard_map/reduce_scatter | solution.py:906
  416.0 370.3 %reduce-scatter.11.cloned.1.call-start = ((), (), s32[]{:S(2)}) async-start(), calls=%async_computation.11 | async-start | bytes 1945600 | tf_op jit(solution)/shard_map/reduce_scatter | solution.py:953
  478.4 2.9 copy-start.3
  478.4 2.9 copy-start.9
  483.8 40.9 %copy-start.19 = (bf16[2,2,80,2432]{3,2,1,0:T(8,128)(2,1)S(1)}, bf16[2,2,80,2432]{3,2,1,0:T(8,128)(2,1)}, u32[]{:S(2)}) copy-start(bf16[2,2,80,2432]{3,2,1,0:T(8,128)(2,1)} %copy-done.18) | copy-start | bytes 4669444
  533.4 21.0 %copy-start.29 = (f32[1,320]{1,0:T(1,128)S(1)}, f32[1,320]{1,0:T(1,128)}, u32[]{:S(2)}) copy-start(f32[1,320]{1,0:T(1,128)} %get-tuple-element.143) | copy-start | bytes 3844
  554.9 21.3 %copy-start.25 = (s32[320]{0:T(512)S(1)}, s32[320]{0:T(512)}, u32[]{:S(2)}) copy-start(s32[320]{0:T(512)} %copy-done.24) | copy-start | bytes 3844
  554.9 21.3 %copy-start.27 = (s32[320]{0:T(512)S(1)}, s32[320]{0:T(512)}, u32[]{:S(2)}) copy-start(s32[320]{0:T(512)} %copy-done.26) | copy-start | bytes 3844
  554.9 21.3 %copy-start.35 = (pred[320]{0:T(512)(128)(4,1)S(1)}, pred[320]{0:T(512)(128)(4,1)}, u32[]{:S(2)}) copy-start(pred[320]{0:T(512)(128)(4,1)} %copy-done.34) | copy-start | bytes 964
  554.9 21.3 %copy-start.42 = (pred[320]{0:T(512)(128)(4,1)S(1)}, pred[320]{0:T(512)(128)(4,1)}, u32[]{:S(2)}) copy-start(pred[320]{0:T(512)(128)(4,1)} %get-tuple-element.183) | copy-start | bytes 964
  576.2 5.2 copy-start.28
  595.9 5.1 copy-start.33
  595.9 13.4 %copy-start.31 = (f32[3]{0:T(128)S(1)}, f32[3]{0:T(128)}, u32[]{:S(2)}) copy-start(f32[3]{0:T(128)} %copy-done.30) | copy-start | bytes 40
  612.9 1.6 copy-start.15
  614.5 10.5 %copy-start.32 = (f32[256]{0:T(256)S(1)}, f32[256]{0:T(256)}, u32[]{:S(2)}) copy-start(f32[256]{0:T(256)} %get-tuple-element.131) | copy-start | bytes 3076
  624.9 168.0 %reduce-scatter.9.cloned.1.call-start = ((), (), s32[]{:S(2)}) async-start(), calls=%async_computation.10 | async-start | bytes 3276800 | tf_op jit(solution)/shard_map/reduce_scatter | solution.py:952
  683.7 41.9 %copy-start.40 = (bf16[768,2048]{1,0:T(8,128)(2,1)S(1)}, bf16[768,2048]{1,0:T(8,128)(2,1)}, u32[]{:S(2)}) copy-start(bf16[768,2048]{1,0:T(8,128)(2,1)} %all-gather.9.cloned.1.call-done) | copy-start | bytes 9437188
  736.8 44.7 %copy-start.7 = (f32[64,6144]{1,0:T(8,128)S(1)}, f32[64,6144]{1,0:T(8,128)}, u32[]{:S(2)}) copy-start(f32[64,6144]{1,0:T(8,128)} %reshape.404) | copy-start | bytes 4718596
  736.8 44.7 %copy-start.8 = (f32[64,6144]{1,0:T(8,128)S(1)}, f32[64,6144]{1,0:T(8,128)}, u32[]{:S(2)}) copy-start(f32[64,6144]{1,0:T(8,128)} %reshape.406) | copy-start | bytes 4718596
  736.8 44.7 %copy-start.11 = (bf16[64,6144]{1,0:T(8,128)(2,1)S(1)}, bf16[64,6144]{1,0:T(8,128)(2,1)}, u32[]{:S(2)}) copy-start(bf16[64,6144]{1,0:T(8,128)(2,1)} %param.34) | copy-start | bytes 2359300
  736.8 44.7 %copy-start.13 = (bf16[64,6144]{1,0:T(8,128)(2,1)S(1)}, bf16[64,6144]{1,0:T(8,128)(2,1)}, u32[]{:S(2)}) copy-start(bf16[64,6144]{1,0:T(8,128)(2,1)} %param.33) | copy-start | bytes 2359300
  778.8 3.1 copy-start.37
  778.8 3.6 copy-start.2
  778.9 3.6 copy-start.23
  781.5 1.6 copy-start.4
  781.5 2.2 copy-start.6
  808.6 4.1 copy-start.16
  809.5 3.2 copy-start.39
  811.1 2.1 copy-start.17
Sparse Core Ops, SparseCore 0:
  13.2 39.5 all-gather.6
  54.9 55.0 all-gather.4
  111.6 116.0 all-gather.10
  229.1 61.6 all-gather.8
  415.5 57.8 reduce-scatter.6
  475.6 111.5 reduce-scatter.4
  625.1 35.7 reduce-scatter.10
  672.6 52.0 reduce-scatter.8

commit v2 on v1

--- a/solution.py
+++ b/solution.py
@@ -14,6 +14,7 @@
 LANES = 128
 FEAT = ("x", "y", "c")
 NF = 8
+OWN, ACROSS_Y, ACROSS_X, DIAGONAL = 0, 1, 2, 3
 
 norm_eps = 1e-06
 decay_scale = 8.0
@@ -64,10 +65,6 @@
 
 def gather_kernel(x_ref, o_ref, local_sem, ssem, rsem):
     x, y, c = feature_place()
-    mine = x * 4 + y * 2 + c
-    from_x = (1 - x) * 4 + y * 2 + c
-    from_y = x * 4 + (1 - y) * 2 + c
-    from_d = (1 - x) * 4 + (1 - y) * 2 + c
     to_x, to_y, to_c = {"x": 1 - x}, {"y": 1 - y}, {"c": 1 - c}
     half = x_ref.shape[0] // 2
     top, low = pl.ds(0, half), pl.ds(half, half)
@@ -76,17 +73,17 @@
     def copy(i, src, dst, device):
         return remote(src, dst, ssem.at[i], rsem.at[i], device)
 
-    own = pltpu.make_async_copy(x_ref, o_ref.at[mine], local_sem)
-    x_top = copy(0, x_ref.at[top], o_ref.at[mine, top], to_x)
-    x_low = copy(1, x_ref.at[low], o_ref.at[mine, low], to_x)
-    y_low = copy(2, x_ref.at[low], o_ref.at[mine, low], to_y)
-    y_top = copy(3, x_ref.at[top], o_ref.at[mine, top], to_y)
-    c_own = copy(4, x_ref, o_ref.at[mine], to_c)
-    y_fwd = copy(5, o_ref.at[from_x, top], o_ref.at[from_x, top], to_y)
-    x_fwd = copy(6, o_ref.at[from_y, low], o_ref.at[from_y, low], to_x)
-    c_x = copy(7, o_ref.at[from_x], o_ref.at[from_x], to_c)
-    c_y = copy(8, o_ref.at[from_y], o_ref.at[from_y], to_c)
-    c_d = copy(9, o_ref.at[from_d], o_ref.at[from_d], to_c)
+    own = pltpu.make_async_copy(x_ref, o_ref.at[OWN], local_sem)
+    x_top = copy(0, x_ref.at[top], o_ref.at[ACROSS_X, top], to_x)
+    x_low = copy(1, x_ref.at[low], o_ref.at[ACROSS_X, low], to_x)
+    y_low = copy(2, x_ref.at[low], o_ref.at[ACROSS_Y, low], to_y)
+    y_top = copy(3, x_ref.at[top], o_ref.at[ACROSS_Y, top], to_y)
+    c_own = copy(4, x_ref, o_ref.at[4 + OWN], to_c)
+    y_fwd = copy(5, o_ref.at[ACROSS_X, top], o_ref.at[DIAGONAL, top], to_y)
+    x_fwd = copy(6, o_ref.at[ACROSS_Y, low], o_ref.at[DIAGONAL, low], to_x)
+    c_x = copy(7, o_ref.at[ACROSS_X], o_ref.at[4 + ACROSS_X], to_c)
+    c_y = copy(8, o_ref.at[ACROSS_Y], o_ref.at[4 + ACROSS_Y], to_c)
+    c_d = copy(9, o_ref.at[DIAGONAL], o_ref.at[4 + DIAGONAL], to_c)
     for one in (x_top, y_low, x_low, y_top, c_own, own):
         one.start()
     x_top.wait_recv()
@@ -137,26 +134,17 @@
     half = rows // 2
     top, low = pl.ds(0, half), pl.ds(half, half)
     step = 16
-    chips = (
-        x * 2 + y,
-        (1 - x) * 2 + y,
-        x * 2 + (1 - y),
-        (1 - x) * 2 + (1 - y),
-    )
-
     def copy(i, src, dst, device):
         return remote(src, dst, ssem.at[i], rsem.at[i], device)
 
     loads = [
-        pltpu.make_async_copy(p_ref.at[chips[r] * 2 + c], own.at[r], lsem.at[r]) for r in range(4)
+        pltpu.make_async_copy(p_ref.at[r], own.at[r], lsem.at[r]) for r in range(4)
     ]
-    for r in (3, 1, 2, 0):
+    for r in (DIAGONAL, ACROSS_X, ACROSS_Y, OWN):
         loads[r].start()
     greet((to_x, to_y, to_c))
-    cross = [
-        copy(r, p_ref.at[chips[r] * 2 + (1 - c)], other.at[r], to_c) for r in range(4)
-    ]
-    for r in (3, 1, 2, 0):
+    cross = [copy(r, p_ref.at[4 + r], other.at[r], to_c) for r in range(4)]
+    for r in (DIAGONAL, ACROSS_X, ACROSS_Y, OWN):
         cross[r].start()
 
     def add_into(r):
@@ -170,22 +158,22 @@
 
         lax.fori_loop(0, rows // step, body, 0)
 
-    x_diag = copy(4, total.at[3, top], rx.at[1], to_x)
-    y_diag = copy(5, total.at[3, low], ry.at[1], to_y)
-    x_near = copy(6, total.at[1, top], rx.at[0], to_x)
-    y_near = copy(7, total.at[2, low], ry.at[0], to_y)
+    x_diag = copy(4, total.at[DIAGONAL, top], rx.at[1], to_x)
+    y_diag = copy(5, total.at[DIAGONAL, low], ry.at[1], to_y)
+    x_near = copy(6, total.at[ACROSS_X, top], rx.at[0], to_x)
+    y_near = copy(7, total.at[ACROSS_Y, low], ry.at[0], to_y)
     y_last = copy(8, relay.at[0], ry_last, to_y)
     x_last = copy(9, relay.at[1], rx_last, to_x)
 
-    add_into(3)
+    add_into(DIAGONAL)
     x_diag.start()
     y_diag.start()
-    add_into(1)
+    add_into(ACROSS_X)
     x_near.start()
-    add_into(2)
+    add_into(ACROSS_Y)
     y_near.start()
-    loads[0].wait()
-    cross[0].wait_recv()
+    loads[OWN].wait()
+    cross[OWN].wait_recv()
 
     def relay_add(slot, r, start, got):
         def body(i, none):
@@ -199,17 +187,17 @@
         lax.fori_loop(0, half // step, body, 0)
 
     x_diag.wait_recv()
-    relay_add(0, 2, 0, rx)
+    relay_add(0, ACROSS_Y, 0, rx)
     y_last.start()
     y_diag.wait_recv()
-    relay_add(1, 1, half, ry)
+    relay_add(1, ACROSS_X, half, ry)
     x_last.start()
 
     def finish(start, near, last):
         def body(i, none):
             at = pl.ds(pl.multiple_of(i * step, step), step)
             here = pl.ds(pl.multiple_of(start + i * step, step), step)
-            o_ref[here] = (own[0, here].astype(f32) + other[0, here].astype(f32)) + (
+            o_ref[here] = (own[OWN, here].astype(f32) + other[OWN, here].astype(f32)) + (
                 near[0, at].astype(f32) + last[at].astype(f32)
             )
             return none
@@ -256,6 +244,50 @@
     )(partial.reshape(NF, rows, width))
 
 
+def across(value, axis):
+    return lax.ppermute(value, axis, [(0, 1), (1, 0)])
+
+
+def hold(*values):
+    return lax.optimization_barrier(values)
+
+
+def gather_near(block):
+    return across(block, "x"), across(block, "y")
+
+
+def gather_diagonal(by_x, by_y):
+    half = by_x.shape[0] // 2
+    return across(by_x[:half], "y"), across(by_y[half:], "x")
+
+
+def gather_chip(block, by_x, by_y, d_top, d_low):
+    return jnp.concatenate([block, by_y, by_x, d_top, d_low])
+
+
+def scatter_near(mine, theirs_got):
+    rows = mine.shape[0] // 4
+    kind = theirs_got.dtype
+    total = (mine.astype(f32) + theirs_got.astype(f32)).astype(kind)
+    total = total.reshape(4, 2, rows // 2, mine.shape[1])
+    by_x = across(total[2:, 0], "x")
+    by_y = across(jnp.stack([total[ACROSS_Y, 1], total[DIAGONAL, 1]]), "y")
+    return total, by_x, by_y
+
+
+def scatter_relay(total, by_x, by_y):
+    kind = total.dtype
+    y_last = across((total[ACROSS_Y, 0].astype(f32) + by_x[1].astype(f32)).astype(kind), "y")
+    x_last = across((total[ACROSS_X, 1].astype(f32) + by_y[1].astype(f32)).astype(kind), "x")
+    return y_last, x_last
+
+
+def scatter_sum(total, by_x, by_y, y_last, x_last):
+    upper = total[OWN, 0].astype(f32) + by_x[0].astype(f32) + y_last.astype(f32)
+    lower = total[OWN, 1].astype(f32) + by_y[0].astype(f32) + x_last.astype(f32)
+    return jnp.concatenate([upper, lower])
+
+
 def exchange_kernel(axes, x_ref, o_ref, local_sem, ssem, rsem):
     place = [lax.axis_index(name) for name in axes]
     count = 2 ** len(axes)
@@ -386,6 +418,7 @@
 
 
 def forward_kernel(
+    order_ref,
     branch_ref,
     halo_ref,
     mask_ref,
@@ -396,6 +429,7 @@
     keep_ref,
     prod_ref,
     state_ref,
+    ends_ref,
     ext,
     carry,
 ):
@@ -437,34 +471,48 @@
     prod_out, state_out = lax.fori_loop(0, rows // 8, body, (carry[0:1], carry[1:2]))
     carry[0:1] = prod_out
     carry[1:2] = state_out
-
-
-def forward_scan(branch_in, halo, masks, small, wa, wx, chunk):
+    ends_ref[0:1] = prod_out
+    ends_ref[1:2] = state_out
+    ends_ref[2:8] = jnp.zeros_like(ends_ref[2:8])
+
+
+def forward_scan(order, branch_in, halo, masks, small, wa, wx, chunk):
     rows, width = branch_in.shape
-    tile = pl.BlockSpec((chunk, width), lambda i: (i, 0))
-    whole = lambda a: pl.BlockSpec(a.shape, lambda i: (0, 0))
+    tile = pl.BlockSpec((chunk, width), lambda i, order: (order[i], 0))
+    whole = lambda a: pl.BlockSpec(a.shape, lambda i, order: (0, 0))
     full = jax.ShapeDtypeStruct((rows, width), f32)
     return pl.pallas_call(
         forward_kernel,
-        grid=(rows // chunk,),
-        out_shape=(jax.ShapeDtypeStruct((rows, width), bf16), full, full, full),
-        in_specs=[
-            tile,
-            whole(halo),
-            pl.BlockSpec((chunk, masks.shape[1]), lambda i: (i, 0)),
-            whole(small),
-            whole(wa),
-            whole(wx),
-        ],
-        out_specs=(tile, tile, tile, tile),
-        scratch_shapes=[pltpu.VMEM((chunk + 8, width), f32), pltpu.VMEM((8, width), f32)],
+        out_shape=(
+            jax.ShapeDtypeStruct((rows, width), bf16),
+            full,
+            full,
+            full,
+            jax.ShapeDtypeStruct((8, width), f32),
+        ),
+        grid_spec=pltpu.PrefetchScalarGridSpec(
+            num_scalar_prefetch=1,
+            grid=(rows // chunk,),
+            in_specs=[
+                tile,
+                whole(halo),
+                pl.BlockSpec((chunk, masks.shape[1]), lambda i, order: (i, 0)),
+                whole(small),
+                whole(wa),
+                whole(wx),
+            ],
+            out_specs=(tile, tile, tile, tile, pl.BlockSpec((8, width), lambda i, order: (0, 0))),
+            scratch_shapes=[pltpu.VMEM((chunk + 8, width), f32), pltpu.VMEM((8, width), f32)],
+        ),
         compiler_params=pltpu.CompilerParams(vmem_limit_bytes=VMEM_LIMIT),
-        cost_estimate=cost(20),
+        cost_estimate=cost(15),
         name="forward_scan",
-    )(branch_in, halo, masks, small, wa, wx)
-
-
-def adjoint_kernel(d_mixed_ref, gate_ref, keep_ref, prod_ref, adj_ref, keep_next, carry):
+    )(order, branch_in, halo, masks, small, wa, wx)
+
+
+def adjoint_kernel(
+    order_ref, d_mixed_ref, gate_ref, keep_ref, prod_ref, adj_ref, heads_ref, keep_next, carry
+):
     rows = d_mixed_ref.shape[0]
     step = pl.program_id(0)
 
@@ -496,27 +544,34 @@
     prod_out, adj_out = lax.fori_loop(0, tiles, body, (carry[0:1], carry[1:2]))
     carry[0:1] = prod_out
     carry[1:2] = adj_out
-
-
-def adjoint_scan(d_mixed, gate_pre, keep, chunk):
+    heads_ref[0:1] = keep_ref[0:1] * prod_out
+    heads_ref[1:2] = keep_ref[0:1] * adj_out
+    heads_ref[2:8] = jnp.zeros_like(heads_ref[2:8])
+
+
+def adjoint_scan(order, d_mixed, gate_pre, keep, chunk):
     rows, width = keep.shape
     last = rows // chunk - 1
-    tile = pl.BlockSpec((chunk, width), lambda i: (last - i, 0))
+    tile = pl.BlockSpec((chunk, width), lambda i, order: (order[last - i], 0))
     full = jax.ShapeDtypeStruct((rows, width), f32)
     return pl.pallas_call(
         adjoint_kernel,
-        grid=(rows // chunk,),
-        out_shape=(full, full),
-        in_specs=[tile, tile, tile],
-        out_specs=(tile, tile),
-        scratch_shapes=[pltpu.VMEM((chunk + 8, width), f32), pltpu.VMEM((8, width), f32)],
+        out_shape=(full, full, jax.ShapeDtypeStruct((8, width), f32)),
+        grid_spec=pltpu.PrefetchScalarGridSpec(
+            num_scalar_prefetch=1,
+            grid=(rows // chunk,),
+            in_specs=[tile, tile, tile],
+            out_specs=(tile, tile, pl.BlockSpec((8, width), lambda i, order: (0, 0))),
+            scratch_shapes=[pltpu.VMEM((chunk + 8, width), f32), pltpu.VMEM((8, width), f32)],
+        ),
         compiler_params=pltpu.CompilerParams(vmem_limit_bytes=VMEM_LIMIT),
         cost_estimate=cost(12),
         name="adjoint_scan",
-    )(d_mixed, gate_pre, keep)
+    )(order, d_mixed, gate_pre, keep)
 
 
 def backward_kernel(
+    order_ref,
     d_mixed_ref,
     gate_ref,
     state_ref,
@@ -534,8 +589,7 @@
     enter_ref,
     wa_ref,
     wx_ref,
-    d_gate_ref,
-    d_branch_ref,
+    d_pre_ref,
     sums_ref,
     edge_ref,
     ga_ref,
@@ -579,7 +633,7 @@
     state = state_ref[...] + prod_ref[...] * state_in
     state_ext[pl.ds(8, rows)] = state
     _, slope = gelu_pair(gate_ref[...])
-    d_gate_ref[...] = (d_mixed_ref[...] * state * slope).astype(bf16)
+    d_pre_ref[:, 0:width] = (d_mixed_ref[...] * state * slope).astype(bf16)
     adjoint = adj_ref[...] + adj_prod_ref[...] * adj_in
     state_prev = state_ext[pl.ds(7, rows)]
     masks = mask_ref[...]
@@ -627,7 +681,7 @@
     d_branch = small_ref[0:1] * d_conved
     for k in range(1, CONV):
         d_branch = d_branch + small_ref[k : k + 1] * later[k - 1, pl.ds(k, rows)]
-    d_branch_ref[...] = d_branch.astype(bf16)
+    d_pre_ref[:, width : 2 * width] = d_branch.astype(bf16)
 
     @pl.when(first)
     def _():
@@ -640,70 +694,157 @@
 
 
 def backward_scan(
-    d_mixed, gate_pre, state, prod, adj, adj_prod, branch_in, halo, conved, masks, small, enter,
-    wa, wx, chunk,
+    order, d_mixed, gate_pre, state, prod, adj, adj_prod, branch_in, halo, conved, masks, small,
+    enter, wa, wx, chunk,
 ):
     rows, width = state.shape
     last = rows // chunk - 1
-    tile = pl.BlockSpec((chunk, width), lambda i: (last - i, 0))
+    tile = pl.BlockSpec((chunk, width), lambda i, order: (order[last - i], 0))
 
     def before(size):
         per = chunk // size
-        return pl.BlockSpec((size, width), lambda i: (jnp.maximum((last - i) * per - 1, 0), 0))
-
-    whole = lambda a: pl.BlockSpec(a.shape, lambda i: (0, 0))
-    low = jax.ShapeDtypeStruct((rows, width), bf16)
-    pinned = lambda shape: pl.BlockSpec(shape, lambda i: (0, 0))
+        return pl.BlockSpec(
+            (size, width),
+            lambda i, order: (order[jnp.maximum(last - i - 1, 0)] * per + per - 1, 0),
+        )
+
+    pinned = lambda shape: pl.BlockSpec(shape, lambda i, order: (0, 0))
+    whole = lambda a: pinned(a.shape)
     return pl.pallas_call(
         backward_kernel,
-        grid=(rows // chunk,),
         out_shape=(
-            low,
-            low,
+            jax.ShapeDtypeStruct((rows, 2 * width), bf16),
             jax.ShapeDtypeStruct((8, width), f32),
             jax.ShapeDtypeStruct((8, width), f32),
             jax.ShapeDtypeStruct((width, width), f32),
             jax.ShapeDtypeStruct((width, width), f32),
         ),
-        in_specs=[
-            tile,
-            tile,
-            tile,
-            tile,
-            before(8),
-            before(8),
-            tile,
-            tile,
-            tile,
-            before(16),
-            whole(halo),
-            tile,
-            pl.BlockSpec((chunk, masks.shape[1]), lambda i: (last - i, 0)),
-            whole(small),
-            whole(enter),
-            whole(wa),
-            whole(wx),
-        ],
-        out_specs=(
-            tile,
-            tile,
-            pinned((8, width)),
-            pinned((8, width)),
-            pinned((width, width)),
-            pinned((width, width)),
+        grid_spec=pltpu.PrefetchScalarGridSpec(
+            num_scalar_prefetch=1,
+            grid=(rows // chunk,),
+            in_specs=[
+                tile,
+                tile,
+                tile,
+                tile,
+                before(8),
+                before(8),
+                tile,
+                tile,
+                tile,
+                before(16),
+                whole(halo),
+                tile,
+                pl.BlockSpec((chunk, masks.shape[1]), lambda i, order: (last - i, 0)),
+                whole(small),
+                whole(enter),
+                whole(wa),
+                whole(wx),
+            ],
+            out_specs=(
+                pl.BlockSpec((chunk, 2 * width), lambda i, order: (order[last - i], 0)),
+                pinned((8, width)),
+                pinned((8, width)),
+                pinned((width, width)),
+                pinned((width, width)),
+            ),
+            scratch_shapes=[
+                pltpu.VMEM((chunk + 8, width), f32),
+                pltpu.VMEM((chunk + 8, width), f32),
+                pltpu.VMEM((TAIL, chunk + 8, width), f32),
+            ],
         ),
-        scratch_shapes=[
-            pltpu.VMEM((chunk + 8, width), f32),
-            pltpu.VMEM((chunk + 8, width), f32),
-            pltpu.VMEM((TAIL, chunk + 8, width), f32),
-        ],
         compiler_params=pltpu.CompilerParams(vmem_limit_bytes=VMEM_LIMIT),
-        cost_estimate=cost(25),
+        cost_estimate=cost(21),
         name="backward_scan",
     )(
-        d_mixed, gate_pre, state, prod, state, prod, adj, adj_prod, branch_in, branch_in, halo,
-        conved, masks, small, enter, wa, wx,
-    )
+        order, d_mixed, gate_pre, state, prod, state, prod, adj, adj_prod, branch_in, branch_in,
+        halo, conved, masks, small, enter, wa, wx,
+    )
+
+
+def gated_kernel(n_ref, cot_ref, w_ref, down_ref, hidden_ref, d_ref):
+    ff = down_ref.shape[0]
+    tile = 256
+    normed = n_ref[...]
+    cot = cot_ref[...]
+
+    def body(j, none):
+        at = pl.ds(pl.multiple_of(j * tile, tile), tile)
+        up_at = pl.ds(pl.multiple_of(ff + j * tile, tile), tile)
+        gate = jnp.dot(normed, w_ref[:, at], preferred_element_type=f32)
+        up = jnp.dot(normed, w_ref[:, up_at], preferred_element_type=f32)
+        d_hidden = lax.dot_general(cot, down_ref[at], contract_last, preferred_element_type=f32)
+        act, slope = gelu_pair(gate)
+        hidden_ref[:, at] = (act * up).astype(bf16)
+        d_ref[:, at] = (d_hidden * up * slope).astype(bf16)
+        d_ref[:, up_at] = (d_hidden * act).astype(bf16)
+        return none
+
+    lax.fori_loop(0, ff // tile, body, 0)
+
+
+def gated_unit(normed, cot, w_mlp, w_down):
+    rows, width = normed.shape
+    ff = w_down.shape[0]
+    steps = 4
+    tile = rows // steps
+    row = lambda size: pl.BlockSpec((tile, size), lambda i: (i, 0))
+    once = lambda a: pl.BlockSpec(a.shape, lambda i: (0, 0), pipeline_mode=pl.Buffered(1))
+    return pl.pallas_call(
+        gated_kernel,
+        grid=(steps,),
+        out_shape=(
+            jax.ShapeDtypeStruct((rows, ff), bf16),
+            jax.ShapeDtypeStruct((rows, 2 * ff), bf16),
+        ),
+        in_specs=[row(width), row(width), once(w_mlp), once(w_down)],
+        out_specs=(row(ff), row(2 * ff)),
+        compiler_params=pltpu.CompilerParams(vmem_limit_bytes=VMEM_LIMIT),
+        cost_estimate=pl.CostEstimate(
+            flops=6 * rows * width * ff, bytes_accessed=40 * 2**20, transcendentals=rows * ff
+        ),
+        name="gated_unit",
+    )(normed, cot, w_mlp, w_down)
+
+
+def split_kernel(moves, a_ref, b_ref, o_ref):
+    for source, block, at, start, size in moves:
+        ref = (a_ref, b_ref)[source]
+        o_ref[block, :, at : at + size] = ref[:, start : start + size]
+
+
+def join_kernel(moves, x_ref, a_ref, b_ref, g_ref, oa_ref, ob_ref, og_ref):
+    for source, block, at, start, size in moves:
+        ref = (oa_ref, ob_ref)[source]
+        ref[:, start : start + size] = x_ref[block, :, at : at + size].astype(f32)
+    total = jnp.sum(a_ref[...].astype(f32) * oa_ref[...], axis=1, keepdims=True) + jnp.sum(
+        b_ref[...].astype(f32) * ob_ref[...], axis=1, keepdims=True
+    )
+    og_ref[...] = total / g_ref[...]
+
+
+def split_blocks(a, b, moves):
+    rows, width = a.shape
+    return pl.pallas_call(
+        functools.partial(split_kernel, moves),
+        out_shape=jax.ShapeDtypeStruct((NF, rows, 2 * width // NF), a.dtype),
+        compiler_params=pltpu.CompilerParams(vmem_limit_bytes=VMEM_LIMIT),
+        cost_estimate=cost(4),
+        name="split_blocks",
+    )(a, b)
+
+
+def join_blocks(x, a, b, gain, moves):
+    rows, width = a.shape
+    out = jax.ShapeDtypeStruct((rows, width), f32)
+    return pl.pallas_call(
+        functools.partial(join_kernel, moves),
+        out_shape=(out, out, jax.ShapeDtypeStruct((rows, 1), f32)),
+        compiler_params=pltpu.CompilerParams(vmem_limit_bytes=VMEM_LIMIT),
+        cost_estimate=cost(5),
+        name="join_blocks",
+    )(x, a, b, gain)
 
 
 def pad_lanes(rows, width):
@@ -753,29 +894,32 @@
     ff = ff_rows * count
     chunk = 256
 
-    def split_chan(w):
-        return (
-            w.reshape(rows_w, spread, 2, outer, BLK)
-            .transpose(3, 1, 0, 2, 4)
-            .reshape(NF, rows_w, chans)
+    chan_moves = [
+        (
+            source,
+            k * spread + e,
+            source * chans + zz * BLK,
+            ((2 * e + zz) * outer + k) * BLK,
+            BLK,
         )
-
-    def join_chan(w):
-        return (
-            w.reshape(outer, spread, rows_w, 2, BLK)
-            .transpose(2, 1, 3, 0, 4)
-            .reshape(rows_w, NF * chans)
-        )
-
-    def split_ff(w):
-        return (
-            w.reshape(rows_w, count, NF, ff_rows).transpose(2, 0, 1, 3).reshape(NF, rows_w, ff)
-        )
-
-    def join_ff(w):
-        return (
-            w.reshape(NF, rows_w, count, ff_rows).transpose(1, 2, 0, 3).reshape(rows_w, NF * ff)
-        )
+        for source in range(2)
+        for k in range(outer)
+        for e in range(spread)
+        for zz in range(2)
+    ]
+    ff_moves = [
+        (source, f, source * ff + group * ff_rows, (group * NF + f) * ff_rows, ff_rows)
+        for source in range(2)
+        for f in range(NF)
+        for group in range(count)
+    ]
+    place = [lax.axis_index(name) for name in FEAT]
+    time = jnp.arange(NF, dtype=jnp.int32)
+    bit = lambda value, here: jnp.where(value == here, 0, 1)
+    order = (
+        bit(time % 2, place[2]) * 4 + bit(time // 4, place[0]) * 2 + bit((time // 2) % 2, place[1])
+    ).astype(jnp.int32)
+    final = order[NF - 1] * rows_tok + rows_tok - 8
 
     pack = jnp.concatenate(
         [
@@ -793,7 +937,6 @@
     used = pack.shape[1]
     pack_width = -(-used // LANES) * LANES
     pack = pad_lanes(pack, pack_width)
-    pack_all = lax.all_gather(pack, "z", axis=0, tiled=True)
 
     extra = jnp.concatenate(
         [
@@ -806,18 +949,20 @@
     )
     rec_send = jnp.concatenate(
         [
-            jnp.concatenate(
-                [split_chan(rec_gate_weight), split_chan(rec_in_weight)],
-                axis=2,
-            ),
+            split_blocks(rec_gate_weight, rec_in_weight, chan_moves),
             jnp.broadcast_to(extra[None], (NF, 16, 2 * chans)),
         ],
         axis=1,
     )
+    rec_send, pack = hold(rec_send, pack)
+    pack_all = lax.all_gather(pack, "z", axis=0, tiled=True)
     rec_got = exchange(rec_send, FEAT, 3)
     w_rec = lax.all_gather(
         rec_got[:, :rows_w].reshape(NF * rows_w, 2 * chans), "z", axis=0, tiled=True
     )
+    tokens_own, rec_got = hold(tokens_in, rec_got)
+    tok_group = gather_feature(tokens_own)
+    pack_swap = exchange(pack_all.reshape(spread, 2, chan_rows, pack_width), swap_axes, 5)
     starts = rec_got[:, rows_w, :rows_tok].reshape(group_rows).astype(f32)
 
     plane_gains = jnp.stack(
@@ -831,15 +976,16 @@
     gain_two = gains[:, 1].reshape(1, width)
 
     tok = tokens_in.astype(f32)
-    tok_group = gather_feature(tokens_in).astype(f32)
+    tok_group = tok_group.astype(f32)
     normed = (tok_group * inverse_rms(tok_group) * gain_one).astype(bf16)
-
-    mlp_send = jnp.concatenate([split_ff(mlp_gate_weight), split_ff(mlp_up_weight)], axis=2)
+    normed, pack_swap, mlp_gate_in = hold(normed, pack_swap, mlp_gate_weight)
+    mlp_send = split_blocks(mlp_gate_in, mlp_up_weight, ff_moves)
     mlp_got = exchange(mlp_send, FEAT, 4)
+
+    w_rec, down_in = hold(w_rec, mlp_down_weight)
     w_mlp = lax.all_gather(mlp_got.reshape(NF * rows_w, 2 * ff), "z", axis=0, tiled=True)
-    w_down = lax.all_gather(mlp_down_weight, "z", axis=0, tiled=True)
-
-    pack_swap = exchange(pack_all.reshape(spread, 2, chan_rows, pack_width), swap_axes, 5)
+    w_down = lax.all_gather(down_in, "z", axis=0, tiled=True)
+
     mine = pack_swap.transpose(1, 0, 2, 3).reshape(chans, pack_width)
     w_out = mine[:, :width]
     small = mine[:, width + 2 * BLK : used].astype(f32).T
@@ -859,77 +1005,110 @@
     open_three = open_two * ahead[TAIL - 2 : TAIL - 2 + group_rows]
     masks = jnp.stack([open_one, open_two, open_three], axis=1)
     end = open_one[group_rows - 2 :]
-    later_open = jnp.stack([end[0] * end[1], end[1], jnp.ones((), f32)])[:, None]
+    later_open = jnp.concatenate(
+        [jnp.zeros((8 - TAIL,), f32), (end[0] * end[1])[None], end[1:], jnp.ones((1,), f32)]
+    )[:, None]
 
     rec_pre = jnp.dot(normed, w_rec, preferred_element_type=f32)
+    rec_pre, cot_own = hold(rec_pre, cotangent)
+    cot_x, cot_y = gather_near(cot_own)
     gate_pre = rec_pre[:, :chans]
     branch_in = rec_pre[:, chans:].astype(bf16)
-    lane_pad = -(-chans // LANES) * LANES
-
-    def over_groups(rows):
-        total = rows.shape[0]
-        block = jnp.pad(rows, ((8 - total, 0), (0, lane_pad - chans)))
-        return gather_groups(block, count, 2)[:, 8 - total :, :chans]
-
-    tails = over_groups(branch_in[group_rows - TAIL :].astype(f32) * later_open)
-    before = lax.dynamic_index_in_dim(tails, jnp.maximum(z - 1, 0), 0, False)
-    before = jnp.where(z > 0, before, 0.0)
-    halo = jnp.pad(before, ((8 - TAIL, 0), (0, 0)))
-    conved, keep, prod, state_local = forward_scan(branch_in, halo, masks, small, wa, wx, chunk)
-    ends = over_groups(jnp.stack([prod[group_rows - 1], state_local[group_rows - 1]]))
-    state_in = jnp.zeros((chans,), f32)
+    tails = gather_groups(
+        lax.dynamic_slice_in_dim(branch_in, final, 8, 0).astype(f32) * later_open, count, 2
+    )
+    halo = jnp.where(z > 0, lax.dynamic_index_in_dim(tails, jnp.maximum(z - 1, 0), 0, False), 0.0)
+    conved, keep, prod, state_local, ends = forward_scan(
+        order, branch_in, halo, masks, small, wa, wx, chunk
+    )
+    ends, cot_x, cot_y = hold(ends, cot_x, cot_y)
+    cot_top, cot_low = gather_diagonal(cot_x, cot_y)
+    ends = gather_groups(ends, count, 2)
+    state_in = jnp.zeros((1, chans), f32)
     for hop in range(count - 1):
-        state_in = jnp.where(hop < z, ends[hop, 0] * state_in + ends[hop, 1], state_in)
+        state_in = jnp.where(hop < z, ends[hop, 0:1] * state_in + ends[hop, 1:2], state_in)
     mixed = ((state_local + prod * state_in) * gelu_tanh(gate_pre)).astype(bf16)
-    middle = tok + scatter_feature(jnp.dot(mixed, w_out, preferred_element_type=f32).astype(bf16))
+    mixed_out = jnp.dot(mixed, w_out, preferred_element_type=f32).astype(bf16)
+    mixed_out, cot_top, cot_low = hold(mixed_out, cot_top, cot_low)
+    cot_chip = gather_chip(cotangent, cot_x, cot_y, cot_top, cot_low)
+    cot = jnp.concatenate([cot_chip, across(cot_chip, "c")])
+    middle = tok + scatter_feature(mixed_out)
 
     scale_two = inverse_rms(middle)
     normed_two = gather_feature((middle * scale_two * gain_two).astype(bf16))
-    cot_own, normed_two = lax.optimization_barrier((cotangent, normed_two))
-    cot = gather_feature(cot_own)
-    mlp_pre = jnp.dot(normed_two, w_mlp, preferred_element_type=f32)
-    d_hidden = lax.dot_general(cot, w_down, contract_last, preferred_element_type=f32)
-    mlp_gate, mlp_up = mlp_pre[:, :ff], mlp_pre[:, ff:]
-    act, slope = gelu_pair(mlp_gate)
-    hidden = (act * mlp_up).astype(bf16)
-    d_mlp = jnp.concatenate(
-        [(d_hidden * mlp_up * slope).astype(bf16), (d_hidden * act).astype(bf16)], axis=1
-    )
+    hidden, d_mlp = gated_unit(normed_two, cot, w_mlp, w_down)
+    half_rows = group_rows // 2
+
+    def back_rows(d, w):
+        return lax.dot_general(d, w, contract_last, preferred_element_type=f32)
+
+    e_theirs = back_rows(d_mlp[half_rows:], w_mlp).astype(bf16)
+    e_got = across(e_theirs, "c")
+    d_mlp, e_theirs = hold(d_mlp, e_theirs)
+    e_mine = back_rows(d_mlp[:half_rows], w_mlp)
+    e_total, e_x, e_y = scatter_near(e_mine, e_got)
+    e_total, hidden = hold(e_total, hidden)
     down_part = lax.dot_general(
         hidden, cot, contract_first, preferred_element_type=f32
     ).astype(bf16)
+    out_theirs = jnp.dot(hidden[half_rows:], w_down, preferred_element_type=f32).astype(bf16)
+    down_part, e_x, e_y, hidden, out_theirs = hold(down_part, e_x, e_y, hidden, out_theirs)
+    down_sum = lax.psum_scatter(down_part, "z", scatter_dimension=0, tiled=True)
+    e_last = scatter_relay(e_total, e_x, e_y)
+    out_mine = jnp.dot(hidden[:half_rows], w_down, preferred_element_type=f32).astype(bf16)
+    out_mine, *e_last = hold(out_mine, *e_last)
+    e_two = gain_two * scatter_sum(e_total, e_x, e_y, *e_last)
+    d_middle = cotangent.astype(f32) + norm_back(middle, scale_two, e_two)
+    d_own = d_middle.astype(bf16)
+    d_x, d_y = gather_near(d_own)
+    d_own, d_mlp, out_theirs = hold(d_own, d_mlp, out_theirs)
     mlp_part = lax.dot_general(
         normed_two, d_mlp, contract_first, preferred_element_type=f32
     ).astype(bf16)
-    d_mlp, down_part, mlp_part = lax.optimization_barrier((d_mlp, down_part, mlp_part))
-    down_sum = lax.psum_scatter(down_part, "z", scatter_dimension=0, tiled=True)
+    d_x, d_y, mlp_part, out_theirs = hold(d_x, d_y, mlp_part, out_theirs)
     mlp_sum = lax.psum_scatter(mlp_part, "z", scatter_dimension=0, tiled=True)
-    e_two = gain_two * scatter_feature(
-        lax.dot_general(d_mlp, w_mlp, contract_last, preferred_element_type=f32).astype(bf16)
-    )
-    d_middle = cotangent.astype(f32) + norm_back(middle, scale_two, e_two)
-    d_rec = gather_feature(d_middle.astype(bf16))
+    d_top, d_low = gather_diagonal(d_x, d_y)
+    out_got = across(out_theirs, "c")
+    d_chip = gather_chip(d_own, d_x, d_y, d_top, d_low)
+    d_rec = jnp.concatenate([d_chip, across(d_chip, "c")])
+    d_rec, out_got = hold(d_rec, out_got)
+    out_total, out_x, out_y = scatter_near(out_mine, out_got)
 
     d_mixed = lax.dot_general(d_rec, w_out, contract_last, preferred_element_type=f32)
-    adj_prod, adj_local = adjoint_scan(d_mixed, gate_pre, keep, chunk)
-    heads = over_groups(jnp.stack([keep[0] * adj_prod[0], keep[0] * adj_local[0]]))
-    adj_in = jnp.zeros((chans,), f32)
+    adj_prod, adj_local, heads = adjoint_scan(order, d_mixed, gate_pre, keep, chunk)
+    heads, out_x, out_y = hold(heads, out_x, out_y)
+    out_last = scatter_relay(out_total, out_x, out_y)
+    heads = gather_groups(heads, count, 2)
+    adj_in = jnp.zeros((1, chans), f32)
     for hop in range(count - 1, 0, -1):
-        adj_in = jnp.where(hop > z, heads[hop, 0] * adj_in + heads[hop, 1], adj_in)
-    enter = jnp.pad(jnp.stack([state_in, adj_in]), ((0, 6), (0, 0)))
-    d_gate, d_branch, sums, edge, grad_a, grad_x = backward_scan(
-        d_mixed, gate_pre, state_local, prod, adj_local, adj_prod, branch_in, halo, conved, masks,
-        small, enter, wa, wx, chunk,
-    )
-    edges = over_groups(edge[8 - TAIL :])
+        adj_in = jnp.where(hop > z, heads[hop, 0:1] * adj_in + heads[hop, 1:2], adj_in)
+    enter = jnp.concatenate([state_in, adj_in, jnp.zeros((6, chans), f32)])
+    d_rec_pre, sums, edge, grad_a, grad_x = backward_scan(
+        order, d_mixed, gate_pre, state_local, prod, adj_local, adj_prod, branch_in, halo, conved,
+        masks, small, enter, wa, wx, chunk,
+    )
+    edges = gather_groups(edge, count, 2)
     after = lax.dynamic_index_in_dim(edges, jnp.minimum(z + 1, count - 1), 0, False)
     after = jnp.where(z < count - 1, after, 0.0) * later_open
-    tail_sum = (d_branch[group_rows - TAIL :].astype(f32) + after).astype(bf16)
-    d_branch = jnp.concatenate([d_branch[: group_rows - TAIL], tail_sum], axis=0)
-    d_rec_pre = jnp.concatenate([d_gate, d_branch], axis=1)
+    tail_sum = lax.dynamic_slice_in_dim(d_rec_pre, final, 8, 0).astype(f32) + jnp.pad(
+        after, ((0, 0), (chans, 0))
+    )
+    d_rec_pre = lax.dynamic_update_slice_in_dim(d_rec_pre, tail_sum.astype(bf16), final, 0)
     rec_part = lax.dot_general(
         normed, d_rec_pre, contract_first, preferred_element_type=f32
     ).astype(bf16)
+    rec_part, d_rec_pre, grad_a, grad_x, sums, mixed, *out_last = hold(
+        rec_part, d_rec_pre, grad_a, grad_x, sums, mixed, *out_last
+    )
+    layer_out = (middle + scatter_sum(out_total, out_x, out_y, *out_last)).astype(bf16)
+    rec_part, mlp_sum, down_sum = hold(rec_part, mlp_sum, down_sum)
+    rec_sum = lax.psum_scatter(rec_part, "z", scatter_dimension=0, tiled=True)
+    one_theirs = back_rows(d_rec_pre[half_rows:], w_rec).astype(bf16)
+    one_got = across(one_theirs, "c")
+    d_rec_pre, one_theirs = hold(d_rec_pre, one_theirs)
+    one_mine = back_rows(d_rec_pre[:half_rows], w_rec)
+    one_total, one_x, one_y = scatter_near(one_mine, one_got)
+    one_total, mixed, grad_a, grad_x = hold(one_total, mixed, grad_a, grad_x)
     fold = (
         lax.broadcasted_iota(jnp.int32, (chans, BLK), 0) % BLK
         == lax.broadcasted_iota(jnp.int32, (chans, BLK), 1)
@@ -946,35 +1125,27 @@
     back_pack = pad_lanes(back_pack, pack_width)
     back_pack = back_pack.reshape(2, spread, chan_rows, pack_width).transpose(1, 0, 2, 3)
     back_swap = exchange(back_pack, swap_axes, 5).reshape(count * chan_rows, pack_width)
-    d_rec_pre, rec_part, back_swap, hidden, mlp_sum, down_sum = lax.optimization_barrier(
-        (d_rec_pre, rec_part, back_swap, hidden, mlp_sum, down_sum)
-    )
-    rec_sum = lax.psum_scatter(rec_part, "z", scatter_dimension=0, tiled=True)
+    one_x, one_y, back_swap, rec_sum = hold(one_x, one_y, back_swap, rec_sum)
     pack_sum = lax.psum_scatter(back_swap, "z", scatter_dimension=0, tiled=True).astype(f32)
-    e_one = gain_one * scatter_feature(
-        lax.dot_general(d_rec_pre, w_rec, contract_last, preferred_element_type=f32).astype(bf16)
-    )
+    one_last = scatter_relay(one_total, one_x, one_y)
+    e_one = gain_one * scatter_sum(one_total, one_x, one_y, *one_last)
     grad_tokens = d_middle + norm_back(tok, inverse_rms(tok), e_one)
-    layer_out = (
-        middle
-        + scatter_feature(jnp.dot(hidden, w_down, preferred_element_type=f32).astype(bf16))
-    ).astype(bf16)
-
-    mlp_back = exchange(mlp_sum.reshape(NF, rows_w, 2 * ff), FEAT, 4).astype(f32)
-    grad_gate, grad_up = join_ff(mlp_back[:, :, :ff]), join_ff(mlp_back[:, :, ff:])
-    rec_back = exchange(rec_sum.reshape(NF, rows_w, 2 * chans), FEAT, 6).astype(f32)
-    grad_rec_gate = join_chan(rec_back[:, :, :chans])
-    grad_rec_in = join_chan(rec_back[:, :, chans:])
-
-    def gain_grad(gain, w_one, g_one, w_two, g_two):
-        total = jnp.sum(w_one.astype(f32) * g_one + w_two.astype(f32) * g_two, axis=1)
-        return total / gain.astype(f32)
+
+    mlp_sum, *one_last = hold(mlp_sum, *one_last)
+    mlp_back = exchange(mlp_sum.reshape(NF, rows_w, 2 * ff), FEAT, 4)
+    grad_gate, grad_up, grad_gain_two = join_blocks(
+        mlp_back, mlp_gate_weight, mlp_up_weight, norm2_gain.astype(f32)[:, None], ff_moves
+    )
+    rec_back = exchange(rec_sum.reshape(NF, rows_w, 2 * chans), FEAT, 6)
+    grad_rec_gate, grad_rec_in, grad_gain_one = join_blocks(
+        rec_back, rec_gate_weight, rec_in_weight, norm1_gain.astype(f32)[:, None], chan_moves
+    )
 
     base = width + 2 * BLK
     return (
         layer_out,
         grad_tokens,
-        gain_grad(norm1_gain, rec_gate_weight, grad_rec_gate, rec_in_weight, grad_rec_in),
+        grad_gain_one[:, 0],
         grad_rec_gate,
         grad_rec_in,
         pack_sum[:, base : base + CONV],
@@ -985,7 +1156,7 @@
         pack_sum[:, base + CONV + 2],
         pack_sum[:, base + CONV + 3],
         pack_sum[:, :width],
-        gain_grad(norm2_gain, mlp_gate_weight, grad_gate, mlp_up_weight, grad_up),
+        grad_gain_two[:, 0],
         grad_gate,
         grad_up,
         down_sum.astype(f32),

time: 830 us -> 784 us (0.945)
  Pallas kernels: 502 us -> 344 us
  waiting for transfers between devices: 1.18 us -> 119 us
  matrix products: 159 us -> 123 us
  starting transfers between devices: 0.79 us -> 23.8 us
  other arithmetic: 61.2 us -> 72.1 us
    pallas_call x4 -> x1, Pallas kernels: 169 us -> 46.4 us  [scatter_feature(): pl.pallas_call(scatter_kernel, out_shape=jax.ShapeDtypeStruct((rows, widt...]
    pallas_call x4 -> x2, Pallas kernels: 163 us -> 81.4 us  [gather_feature(): pl.pallas_call(gather_kernel, out_shape=jax.ShapeDtypeStruct((NF, rows, w...]
    ppermute x0 -> x25, waiting for transfers between devices: none -> 58.3 us  [across(): return lax.ppermute(value, axis, [(0, 1), (1, 0)])]
    all_gather x1, waiting for transfers between devices: 0.01 us -> 54.4 us  [on_device(): lax.all_gather(rec_got[:, :rows_w].reshape(NF * rows_w, 2 * chans), 'z',...]
    pallas_call x3 -> x8, Pallas kernels: 48.1 us -> 92.5 us  [the longest x1 30 us: gated_unit(): pl.pallas_call(gated_kernel, grid=(steps,), out_shape=(jax.ShapeDtypeStru...]
    dot_general x6 -> x7, matrix products: 89 us -> 57.7 us  [the longest x4 36.3 us: back_rows(): return lax.dot_general(d, w, contract_last, preferred_element_type=f32)]
    reshape x20 -> x0, local copies, waits for them, and re-layouts: 26.6 us -> none  [the longest x4 13.5 us: join_ff(): w.reshape(NF, rows_w, count, ff_rows).transpose(1, 2, 0, 3)]
    ppermute x0 -> x25, starting transfers between devices: none -> 22.8 us  [across(): return lax.ppermute(value, axis, [(0, 1), (1, 0)])]
  transfers between devices with their start and end apart: 8 -> 33, of which waited for: 0 -> 19; matrix products, arithmetic and copies ran while one was open for 28% -> 29% of each run, Pallas kernels for 60% -> 38%
where the time goes in v2:
time: 784 us; the launch traced here: 776 us
  Pallas kernels  344 us (44%)
  matrix products  123 us (16%)
  waiting for transfers between devices  119 us (15%)
  local copies, waits for them, and re-layouts  77.2 us (10%)
  other arithmetic  72.1 us (9%)
  starting transfers between devices  23.8 us (3%)
  between operations  17.2 us (2%)
    pallas_call x6, Pallas kernels, exchange(): pl.pallas_call(functools.partial(exchange_kernel, axes), out_shape=jax.Sh...  82 us
    pallas_call x2, Pallas kernels, gather_feature(): pl.pallas_call(gather_kernel, out_shape=jax.ShapeDtypeStruct((NF, rows, w...  81.4 us
    ppermute x25, waiting for transfers between devices, across(): return lax.ppermute(value, axis, [(0, 1), (1, 0)])  58.3 us
    all_gather x1, waiting for transfers between devices, on_device(): lax.all_gather(rec_got[:, :rows_w].reshape(NF * rows_w, 2 * chans), 'z',...  54.4 us
    pallas_call x1, Pallas kernels, scatter_feature(): pl.pallas_call(scatter_kernel, out_shape=jax.ShapeDtypeStruct((rows, widt...  46.4 us
    pallas_call x5, Pallas kernels, gather_groups(): pl.pallas_call(functools.partial(groups_kernel, count), out_shape=jax.Sha...  41.3 us
    dot_general x4, matrix products, back_rows(): return lax.dot_general(d, w, contract_last, preferred_element_type=f32)  36.3 us
    pallas_call x1, Pallas kernels, gated_unit(): pl.pallas_call(gated_kernel, grid=(steps,), out_shape=(jax.ShapeDtypeStru...  30 us
  transfers between devices with their start and end apart: 33, of which 19 were waited for; matrix products, arithmetic and copies ran while one was open for 29% of the time, Pallas kernels for 38%

profile of v2, /device:TPU:0, one launch (start us, length us, event | category | flops | bytes accessed | tf_op | source)
XLA Modules:
  0.0 776.4 jit_solution(12308303828886911616)
XLA Ops:
  18.8 15.7 %exchange.6 = bf16[8,80,640]{2,1,0:T(8,128)(2,1)} custom-call(bf16[8,80,640]{2,1,0:T(8,128)(2,1)} %pad_maximum_fusion.3.x_ref), custom_call_target="tpu_custom_call" | custom-call | bytes 45000000 | tf_op jit(solution)/shard_map/exchange/pallas_call | solution.py:324
  37.3 54.4 %all-gather.7.cloned.1.call-done = bf16[2048,640]{1,0:T(8,128)(2,1)} async-done(((bf16[512,640]{1,0:T(8,128)(2,1)}), bf16[2048,640]{1,0:T(8,128)(2,1)}) %all-gather.7.cloned.1.call-update) | async-done | bytes 2621456 | tf_op jit(solution)/shard_map/all_gather | solution.py:960
  93.4 7.0 gather_groups.5
  100.4 40.7 %gather_feature.2 = bf16[8,256,2048]{2,1,0:T(8,128)(2,1)} custom-call(bf16[256,2048]{1,0:T(8,128)(2,1)} %x_ref), custom_call_target="tpu_custom_call" | custom-call | bytes 120000000 | tf_op jit(solution)/shard_map/gather_feature/pallas_call | solution.py:109
  141.1 5.2 multiply_reduce_fusion
  152.2 8.7 %fusion.1 = bf16[2048,2048]{1,0:T(8,128)(2,1)} fusion(f32[2048]{0:T(1024)S(1)} %bitcast.258, f32[2048]{0:T(1024)S(1)} %bitcast.269, bf16[8,256,2048]{2,1,0:T(8,128)(2,1)} %gather_feature.2), kind=kLoop, calls=%fused_computation.2 | loop fusion | flops 16777216 | bytes 16793600 | tf_op jit(solution)/shard_map/convert_element_type | solution.py:980
  160.8 3.9 exchange.7
  164.7 2.9 split_blocks.3.x_ref
  167.6 22.5 %exchange.8 = bf16[8,64,1536]{2,1,0:T(8,128)(2,1)} custom-call(bf16[8,64,1536]{2,1,0:T(8,128)(2,1)} %split_blocks.3.x_ref), custom_call_target="tpu_custom_call" | custom-call | bytes 45000000 | tf_op jit(solution)/shard_map/exchange/pallas_call | solution.py:324
  190.4 11.4 %fusion.88 = f32[2048,640]{1,0:T(8,128)} fusion(bf16[2048,2048]{1,0:T(8,128)(2,1)} %fusion.1, bf16[2048,640]{1,0:T(8,128)(2,1)} %all-gather.7.cloned.1.call-done), kind=kOutput, calls=%fused_computation.238 | convolution fusion | flops 5368709120 | bytes 16252928 | tf_op jit(solution)/shard_map/dot_general | solution.py:1012
  211.5 2.5 slice.446.branch_ref.branch_before_ref
  214.8 7.1 gather_groups.6
  223.2 16.4 %forward_scan.1 = (bf16[2048,320]{1,0:T(8,128)(2,1)}, f32[2048,320]{1,0:T(8,128)}, f32[2048,320]{1,0:T(8,128)}, f32[2048,320]{1,0:T(8,128)}, f32[8,320]{1,0:T(8,128)}) custom-call(s32[8]{0:T(128)} %copy-done.27, bf16[2048,320]{1,0:T(8,128)(2,1)} %copy-done.4, f32[8,320]{1,0:T(8,128)} %select_bitcast_fusion.halo_ref, f32[2048,3]{1,0:T(8,128)} %copy.105.mask_ref, ...), custom_call_target="tpu_custom_call" | custom-call | bytes 45000000 | tf_op jit(solution)/shard_map/forward_scan/pallas_call | solution.py:484
  239.7 8.3 %gather_groups.7 = f32[4,8,320]{2,1,0:T(8,128)} custom-call(f32[8,320]{1,0:T(8,128)} %get-tuple-element.111.x_ref), custom_call_target="tpu_custom_call" | custom-call | bytes 15000000 | tf_op jit(solution)/shard_map/gather_groups/pallas_call | solution.py:360
  254.5 2.9 constant_dynamic-update-slice_fusion.3
  257.5 2.8 constant_dynamic-update-slice_fusion.2
  260.3 5.0 fusion.83
  265.4 6.8 convolution_convert_fusion
  274.3 46.4 %scatter_feature.1 = f32[256,2048]{1,0:T(8,128)} custom-call(bf16[8,256,2048]{2,1,0:T(8,128)(2,1)} %bitcast.231), custom_call_target="tpu_custom_call" | custom-call | bytes 135000000 | tf_op jit(solution)/shard_map/scatter_feature/pallas_call | solution.py:221
  324.3 40.7 %gather_feature.3 = bf16[8,256,2048]{2,1,0:T(8,128)(2,1)} custom-call(bf16[256,2048]{1,0:T(8,128)(2,1)} %multiply_convert_fusion.x_ref), custom_call_target="tpu_custom_call" | custom-call | bytes 120000000 | tf_op jit(solution)/shard_map/gather_feature/pallas_call | solution.py:109
  365.0 2.6 constant_dynamic-update-slice_fusion.5.cot_ref
  367.6 30.0 %gated_unit.1 = (bf16[2048,768]{1,0:T(8,128)(2,1)}, bf16[2048,1536]{1,0:T(8,128)(2,1)}) custom-call(bf16[2048,2048]{1,0:T(8,128)(2,1)} %bitcast.232, bf16[2048,2048]{1,0:T(8,128)(2,1)} %constant_dynamic-update-slice_fusion.5.cot_ref, bf16[2048,1536]{1,0:T(8,128)(2,1)} %all-gather.9.cloned.1.call-done.w_ref, ...), custom_call_target="tpu_custom_call" | custom-call | flops 19327352832 | bytes 41943040 | tf_op jit(solution)/shard_map/gated_unit/pallas_call | solution.py:794
  397.6 9.9 %convolution_convert_fusion.2 = bf16[1024,2048]{1,0:T(8,128)(2,1)S(1)} fusion(bf16[2048,1536]{1,0:T(8,128)(2,1)} %all-gather.9.cloned.1.call-done.w_ref, bf16[2048,1536]{1,0:T(8,128)(2,1)} %get-tuple-element.132), kind=kOutput, calls=%fused_computation.10 | convolution fusion | flops 6444548096 | bytes 13631488 | tf_op jit(solution)/shard_map/dot_general | solution.py:1043
  408.0 6.9 collective-permute-done.5
  414.9 9.4 %add_convert_fusion.2 = bf16[1024,2048]{1,0:T(8,128)(2,1)S(1)} fusion(bf16[1024,2048]{1,0:T(8,128)(2,1)} %collective-permute-done.5, bf16[2048,1536]{1,0:T(8,128)(2,1)S(1)} %copy-done.37, bf16[2048,1536]{1,0:T(8,128)(2,1)} %get-tuple-element.132), kind=kOutput, calls=%fused_computation.6 | convolution fusion | flops 6448742400 | bytes 17825792 | tf_op jit(solution)/shard_map/dot_general | solution.py:1043
  429.5 8.1 %convolution_convert_fusion.6 = bf16[768,2048]{1,0:T(8,128)(2,1)} fusion(bf16[2048,768]{1,0:T(8,128)(2,1)S(1)} %copy-done.42, bf16[2048,2048]{1,0:T(8,128)(2,1)S(1)} %bitcast.265), kind=kOutput, calls=%fused_computation.18 | convolution fusion | flops 6444023808 | bytes 14680064 | tf_op jit(solution)/shard_map/dot_general | solution.py:1051
  437.7 7.8 %convolution_convert_fusion.5 = bf16[1024,2048]{1,0:T(8,128)(2,1)} fusion(bf16[768,2048]{1,0:T(8,128)(2,1)} %all-gather.11.cloned.1.call-done.down_ref, bf16[2048,768]{1,0:T(8,128)(2,1)} %get-tuple-element.123), kind=kOutput, calls=%fused_computation.13 | convolution fusion | flops 3223322624 | bytes 8912896 | tf_op jit(solution)/shard_map/dot_general | solution.py:1054
  445.5 7.8 collective-permute-done.7
  457.9 6.8 convolution_convert_fusion.4
  464.7 4.3 collective-permute-done.9
  473.4 2.5 fusion.81
  478.0 15.8 %convolution_convert_fusion.1 = bf16[2048,1536]{1,0:T(8,128)(2,1)} fusion(bf16[2048,2048]{1,0:T(8,128)(2,1)S(1)} %bitcast.235, bf16[2048,1536]{1,0:T(8,128)(2,1)S(1)} %bitcast.279), kind=kOutput, calls=%fused_computation.8 | convolution fusion | flops 12888047616 | bytes 20971520 | tf_op jit(solution)/shard_map/dot_general | solution.py:1065
  493.8 2.4 constant_dynamic-update-slice_fusion.15
  496.2 3.3 collective-permute-done.11
  504.1 2.4 constant_dynamic-update-slice_fusion.14
  506.5 2.4 constant_dynamic-update-slice_fusion.13
  508.8 4.0 collective-permute-done.12
  514.8 3.3 copy-done.21
  518.9 6.7 collective-permute-done.14
  525.6 5.1 constant_dynamic-update-slice_fusion.16
  531.6 4.1 add_convert_fusion.1
  540.5 9.9 %fusion.29.d_mixed_ref = f32[2048,320]{1,0:T(8,128)} fusion(bf16[2048,2048]{1,0:T(8,128)(2,1)} %constant_dynamic-update-slice_fusion.16, bf16[320,2432]{1,0:T(8,128)(2,1)} %bitcast.253), kind=kOutput, calls=%fused_computation.53 | convolution fusion | flops 2684354560 | bytes 12320768 | tf_op jit(solution)/shard_map/dot_general | solution.py:1077
  550.4 12.5 %adjoint_scan.1 = (f32[2048,320]{1,0:T(8,128)}, f32[2048,320]{1,0:T(8,128)}, f32[8,320]{1,0:T(8,128)}) custom-call(s32[8]{0:T(128)} %copy-done.27, f32[2048,320]{1,0:T(8,128)} %fusion.29.d_mixed_ref, f32[2048,320]{1,0:T(8,128)} %get-tuple-element.267.gate_ref, f32[2048,320]{1,0:T(8,128)} %get-tuple-element.139.keep_ref), custom_call_target="tpu_custom_call" | custom-call | bytes 36000000 | tf_op jit(solution)/shard_map/adjoint_scan/pallas_call | solution.py:557
  564.8 8.1 %gather_groups.8 = f32[4,8,320]{2,1,0:T(8,128)} custom-call(f32[8,320]{1,0:T(8,128)} %get-tuple-element.145.x_ref), custom_call_target="tpu_custom_call" | custom-call | bytes 15000000 | tf_op jit(solution)/shard_map/gather_groups/pallas_call | solution.py:360
  574.4 22.2 %backward_scan.1 = (bf16[2048,640]{1,0:T(8,128)(2,1)}, f32[8,320]{1,0:T(8,128)}, f32[8,320]{1,0:T(8,128)}, f32[320,320]{1,0:T(8,128)}, f32[320,320]{1,0:T(8,128)}) custom-call(s32[8]{0:T(128)} %copy-done.27, f32[2048,320]{1,0:T(8,128)} %fusion.29.d_mixed_ref, f32[2048,320]{1,0:T(8,128)} %get-tuple-element.267.gate_ref, ...), custom_call_target="tpu_custom_call" | custom-call | bytes 63000000 | tf_op jit(solution)/shard_map/backward_scan/pallas_call | solution.py:713
  596.7 10.9 %gather_groups.9 = f32[4,8,320]{2,1,0:T(8,128)} custom-call(f32[8,320]{1,0:T(8,128)} %get-tuple-element.147.x_ref), custom_call_target="tpu_custom_call" | custom-call | bytes 15000000 | tf_op jit(solution)/shard_map/gather_groups/pallas_call | solution.py:360
  607.6 3.0 fusion.37
  613.0 10.4 %convolution_convert_fusion.7 = bf16[2048,640]{1,0:T(8,128)(2,1)} fusion(bf16[2048,2048]{1,0:T(8,128)(2,1)} %fusion.1, bf16[2048,640]{1,0:T(8,128)(2,1)S(1)} %fusion.62), kind=kOutput, calls=%fused_computation.19 | convolution fusion | flops 5370019840 | bytes 13631488 | tf_op jit(solution)/shard_map/dot_general | solution.py:1097
  623.4 7.5 convolution_convert_fusion.3
  631.9 6.5 collective-permute-done.20
  638.4 9.4 %add_convert_fusion = bf16[1024,2048]{1,0:T(8,128)(2,1)} fusion(bf16[1024,2048]{1,0:T(8,128)(2,1)} %collective-permute-done.20, bf16[2048,640]{1,0:T(8,128)(2,1)} %all-gather.7.cloned.1.call-done, bf16[2048,640]{1,0:T(8,128)(2,1)} %copy-done.36), kind=kOutput, calls=%fused_computation.4 | convolution fusion | flops 2690646016 | bytes 12320768 | tf_op jit(solution)/shard_map/dot_general | solution.py:1043
  659.5 7.9 %convolution_convert_fusion.8 = bf16[320,2048]{1,0:T(8,128)(2,1)} fusion(bf16[2048,320]{1,0:T(8,128)(2,1)} %copy-done.17, bf16[2048,2048]{1,0:T(8,128)(2,1)} %constant_dynamic-update-slice_fusion.16), kind=kOutput, calls=%fused_computation.33 | convolution fusion | flops 2685009920 | bytes 11010048 | tf_op jit(solution)/shard_map/dot_general | solution.py:1121
  667.4 3.7 concatenate.64
  673.9 3.8 exchange.9
  677.8 3.0 collective-permute-done.21
  680.8 5.5 reduce-scatter.9.cloned.1.call-done
  691.3 10.9 %collective-permute-done.23 = bf16[128,2048]{1,0:T(8,128)(2,1)} collective-permute-done((bf16[128,2048]{1,0:T(8,128)(2,1)}, bf16[128,2048]{1,0:T(8,128)(2,1)}, u32[]{:S(2)}, u32[]{:S(2)}) %collective-permute-start.23) | collective-permute-done | bytes 524320 | tf_op jit(solution)/shard_map/ppermute | solution.py:248
  702.2 3.3 fusion.35
  706.9 3.7 fusion.39
  712.0 13.6 %exchange.10.x_ref = bf16[8,64,640]{2,1,0:T(8,128)(2,1)} custom-call(bf16[8,64,640]{2,1,0:T(8,128)(2,1)} %bitcast.257), custom_call_target="tpu_custom_call" | custom-call | bytes 45000000 | tf_op jit(solution)/shard_map/exchange/pallas_call | solution.py:324
  725.6 2.5 join_blocks.2
  729.5 22.5 %exchange.11.x_ref = bf16[8,64,1536]{2,1,0:T(8,128)(2,1)} custom-call(bf16[8,64,1536]{2,1,0:T(8,128)(2,1)} %bitcast.255), custom_call_target="tpu_custom_call" | custom-call | bytes 45000000 | tf_op jit(solution)/shard_map/exchange/pallas_call | solution.py:324
  752.0 3.8 join_blocks.3
  760.2 2.4 fusion.19
  (266 shorter events, 115.3 us)
Async XLA Ops:
  7.2 84.5 %all-gather.7.cloned.1.call-start = ((), (), s32[]{:S(2)}) async-start(), calls=%async_computation.5 | async-start | bytes 3276800 | tf_op jit(solution)/shard_map/all_gather | solution.py:960
  36.5 124.4 %all-gather.5.cloned.1.call-start = ((), (), s32[]{:S(2)}) async-start(), calls=%async_computation.4 | async-start | bytes 1945600 | tf_op jit(solution)/shard_map/all_gather | solution.py:958
  37.2 330.3 %all-gather.11.cloned.1.call-start = ((), (), s32[]{:S(2)}) async-start(), calls=%async_computation.7 | async-start | bytes 3932160 | tf_op jit(solution)/shard_map/all_gather | solution.py:987
  91.7 275.8 %all-gather.9.cloned.1.call-start = ((), (), s32[]{:S(2)}) async-start(), calls=%async_computation.6 | async-start | bytes 7864320 | tf_op jit(solution)/shard_map/all_gather | solution.py:986
  141.1 9.5 %copy-start.10 = (bf16[256,2048]{1,0:T(8,128)(2,1)S(1)}, bf16[256,2048]{1,0:T(8,128)(2,1)}, u32[]{:S(2)}) copy-start(bf16[256,2048]{1,0:T(8,128)(2,1)} %param.20) | copy-start | bytes 3145732
  149.0 55.6 %copy-start.27 = (s32[8]{0:T(128)}, s32[8]{0:T(128)S(1)}, u32[]{:S(2)}) copy-start(s32[8]{0:T(128)S(1)} %fusion.76.order_ref) | copy-start | bytes 100
  149.5 60.8 %copy-start.31 = (pred[320]{0:T(512)(128)(4,1)}, pred[320]{0:T(512)(128)(4,1)S(1)}, u32[]{:S(2)}) copy-start(pred[320]{0:T(512)(128)(4,1)S(1)} %get-tuple-element.321) | copy-start | bytes 964
  149.5 60.8 %copy-start.22 = (s32[320]{0:T(512)}, s32[320]{0:T(512)S(1)}, u32[]{:S(2)}) copy-start(s32[320]{0:T(512)S(1)} %get-tuple-element.323) | copy-start | bytes 3844
  149.5 60.8 %copy-start.24 = (s32[320]{0:T(512)}, s32[320]{0:T(512)S(1)}, u32[]{:S(2)}) copy-start(s32[320]{0:T(512)S(1)} %get-tuple-element.324) | copy-start | bytes 3844
  190.1 17.0 %copy-start.8 = (bf16[2,2,80,2432]{3,2,1,0:T(8,128)(2,1)S(1)}, bf16[2,2,80,2432]{3,2,1,0:T(8,128)(2,1)}, u32[]{:S(2)}) copy-start(bf16[2,2,80,2432]{3,2,1,0:T(8,128)(2,1)} %exchange.7) | copy-start | bytes 4669444
  190.1 440.8 %reduce-scatter.7.cloned.1.call-start = ((), (), s32[]{:S(2)}) async-start(), calls=%async_computation.9 | async-start | bytes 3932160 | tf_op jit(solution)/shard_map/reduce_scatter | solution.py:1056
  201.8 37.9 %collective-permute-start.1 = (bf16[256,2048]{1,0:T(8,128)(2,1)S(1)}, bf16[256,2048]{1,0:T(8,128)(2,1)}, u32[]{:S(2)}, u32[]{:S(2)}) collective-permute-start(bf16[256,2048]{1,0:T(8,128)(2,1)S(1)} %copy-done.10), channel_id=1, source_target_pairs={{0,2},{2,0},{1,3},{3,1},{4,6},{6,4},{5,7},{7,5},{8,10},{10,8},{9,1... | collective-permute-start | bytes 3145736 | tf_op jit(solution)/shard_map/ppermute | solution.py:248
  202.3 37.3 %collective-permute-start = (bf16[256,2048]{1,0:T(8,128)(2,1)S(1)}, bf16[256,2048]{1,0:T(8,128)(2,1)}, u32[]{:S(2)}, u32[]{:S(2)}) collective-permute-start(bf16[256,2048]{1,0:T(8,128)(2,1)S(1)} %copy-done.10), channel_id=1, source_target_pairs={{0,4},{4,0},{1,5},{5,1},{2,6},{6,2},{3,7},{7,3},{8,12},{12,8},{9,1... | collective-permute-start | bytes 3145736 | tf_op jit(solution)/shard_map/ppermute | solution.py:248
  204.5 9.4 %copy-start.28 = (f32[8]{0:T(128)}, f32[8]{0:T(128)S(1)}, u32[]{:S(2)}) copy-start(f32[8]{0:T(128)S(1)} %pad_maximum_fusion.5) | copy-start | bytes 100
  214.0 9.3 %copy-start.4 = (bf16[2048,320]{1,0:T(8,128)(2,1)}, bf16[2048,320]{1,0:T(8,128)(2,1)S(1)}, u32[]{:S(2)}) copy-start(bf16[2048,320]{1,0:T(8,128)(2,1)S(1)} %slice.446.branch_ref.branch_before_ref) | copy-start | bytes 3932164
  250.2 22.0 %collective-permute-start.3 = (bf16[128,2048]{1,0:T(8,128)(2,1)S(1)}, bf16[128,2048]{1,0:T(8,128)(2,1)S(1)}, u32[]{:S(2)}, u32[]{:S(2)}) collective-permute-start(bf16[128,2048]{1,0:T(8,128)(2,1)S(1)} %slice.268), channel_id=1, source_target_pairs={{0,4},{4,0},{1,5},{5,1},{2,6},{6,2},{3,7},{7,3},{8,12},{12,8},{9,1... | collective-permute-start | bytes 1572872 | tf_op jit(solution)/shard_map/ppermute | solution.py:248
  251.4 20.8 %collective-permute-start.2 = (bf16[128,2048]{1,0:T(8,128)(2,1)S(1)}, bf16[128,2048]{1,0:T(8,128)(2,1)S(1)}, u32[]{:S(2)}, u32[]{:S(2)}) collective-permute-start(bf16[128,2048]{1,0:T(8,128)(2,1)S(1)} %slice.267), channel_id=1, source_target_pairs={{0,2},{2,0},{1,3},{3,1},{4,6},{6,4},{5,7},{7,5},{8,10},{10,8},{9,1... | collective-permute-start | bytes 1572872 | tf_op jit(solution)/shard_map/ppermute | solution.py:248
  254.5 5.8 copy-start.2
  254.5 5.8 copy-start.3
  265.3 6.8 copy-start.17
  274.3 90.7 %collective-permute-start.4 = (bf16[1024,2048]{1,0:T(8,128)(2,1)}, bf16[1024,2048]{1,0:T(8,128)(2,1)S(1)}, u32[]{:S(2)}, u32[]{:S(2)}) collective-permute-start(bf16[1024,2048]{1,0:T(8,128)(2,1)} %get-tuple-element.305), channel_id=1, source_target_pairs={{0,1},{1,0},{2,3},{3,2},{4,5},{5,4},{6,7},{7,6},{8,9},{9,8},{10,11... | collective-permute-start | bytes 12582920 | tf_op jit(solution)/shard_map/ppermute | solution.py:248
  274.3 46.4 %copy-start.1 = (bf16[256,2048]{1,0:T(8,128)(2,1)S(1)}, bf16[256,2048]{1,0:T(8,128)(2,1)}, u32[]{:S(2)}) copy-start(bf16[256,2048]{1,0:T(8,128)(2,1)} %x_ref) | copy-start | bytes 3145732
  397.6 17.3 %copy-start.37 = (bf16[2048,1536]{1,0:T(8,128)(2,1)S(1)}, bf16[2048,1536]{1,0:T(8,128)(2,1)}, u32[]{:S(2)}) copy-start(bf16[2048,1536]{1,0:T(8,128)(2,1)} %all-gather.9.cloned.1.call-done.w_ref) | copy-start | bytes 18874372
  397.6 31.9 %slice-start.2 = ((s8[8388608]{0:T(1024)(128)(4,1)}), s8[4194304]{0:T(1024)(128)(4,1)S(1)}, s32[]{:S(2)}) async-start(s8[8388608]{0:T(1024)(128)(4,1)} %bitcast.264), calls=%async_computation.14 | async-start | bytes 8388608
  407.5 22.0 %slice-start.3 = ((s8[8388608]{0:T(1024)(128)(4,1)}), s8[4194304]{0:T(1024)(128)(4,1)S(1)}, s32[]{:S(2)}) async-start(s8[8388608]{0:T(1024)(128)(4,1)} %bitcast.264), calls=%async_computation.15 | async-start | bytes 8388608
  407.5 7.4 collective-permute-start.5
  427.5 25.7 %collective-permute-start.7 = (bf16[2,128,2048]{2,1,0:T(8,128)(2,1)}, bf16[2,128,2048]{2,1,0:T(8,128)(2,1)}, u32[]{:S(2)}, u32[]{:S(2)}) collective-permute-start(bf16[2,128,2048]{2,1,0:T(8,128)(2,1)} %pad_maximum_fusion), channel_id=1, source_target_pairs={{0,2},{2,0},{1,3},{3,1},{4,6},{6,4},{5,7},{7,5},{8,10},{10,8},{9,1... | collective-permute-start | bytes 3145736 | tf_op jit(solution)/shard_map/ppermute | solution.py:248
  428.2 25.5 %collective-permute-start.6 = (bf16[2,128,2048]{2,1,0:T(8,128)(2,1)}, bf16[2,128,2048]{2,1,0:T(8,128)(2,1)}, u32[]{:S(2)}, u32[]{:S(2)}) collective-permute-start(bf16[2,128,2048]{2,1,0:T(8,128)(2,1)} %slice_bitcast_fusion.2), channel_id=1, source_target_pairs={{0,4},{4,0},{1,5},{5,1},{2,6},{6,2},{3,7},{7,3},{8,12},{12,8},{9,1... | collective-permute-start | bytes 3145736 | tf_op jit(solution)/shard_map/ppermute | solution.py:248
  453.7 177.6 %reduce-scatter.5.cloned.1.call-start = ((), (), s32[]{:S(2)}) async-start(), calls=%async_computation.8 | async-start | bytes 7864320 | tf_op jit(solution)/shard_map/reduce_scatter | solution.py:1069
  453.8 24.2 %slice-start.4 = ((s8[6291456]{0:T(1024)(128)(4,1)}), s8[4194304]{0:T(1024)(128)(4,1)S(1)}, s32[]{:S(2)}) async-start(s8[6291456]{0:T(1024)(128)(4,1)} %bitcast.278), calls=%async_computation.16 | async-start | bytes 8388608
  455.8 13.1 %collective-permute-start.9 = (bf16[128,2048]{1,0:T(8,128)(2,1)S(1)}, bf16[128,2048]{1,0:T(8,128)(2,1)S(1)}, u32[]{:S(2)}, u32[]{:S(2)}) collective-permute-start(bf16[128,2048]{1,0:T(8,128)(2,1)S(1)} %get-tuple-element.281), channel_id=1, source_target_pairs={{0,4},{4,0},{1,5},{5,1},{2,6},{6,2},{3,7},{7,3},{8,12},{12,8},{9,1... | collective-permute-start | bytes 1572872 | tf_op jit(solution)/shard_map/ppermute | solution.py:248
  457.2 20.7 %slice-start.5 = ((s8[6291456]{0:T(1024)(128)(4,1)}), s8[2097152]{0:T(1024)(128)(4,1)S(1)}, s32[]{:S(2)}) async-start(s8[6291456]{0:T(1024)(128)(4,1)} %bitcast.278), calls=%async_computation.17 | async-start | bytes 4194304
  457.2 12.8 %collective-permute-start.8 = (bf16[128,2048]{1,0:T(8,128)(2,1)S(1)}, bf16[128,2048]{1,0:T(8,128)(2,1)S(1)}, u32[]{:S(2)}, u32[]{:S(2)}) collective-permute-start(bf16[128,2048]{1,0:T(8,128)(2,1)S(1)} %get-tuple-element.282), channel_id=1, source_target_pairs={{0,2},{2,0},{1,3},{3,1},{4,6},{6,4},{5,7},{7,5},{8,10},{10,8},{9,1... | collective-permute-start | bytes 1572872 | tf_op jit(solution)/shard_map/ppermute | solution.py:248
  470.0 7.9 %slice-start = ((s8[8388608]{0:T(1024)(128)(4,1)}), s8[4194304]{0:T(1024)(128)(4,1)S(1)}, s32[]{:S(2)}) async-start(s8[8388608]{0:T(1024)(128)(4,1)} %bitcast.233), calls=%async_computation.12 | async-start | bytes 8388608
  475.9 23.5 %collective-permute-start.11 = (bf16[256,2048]{1,0:T(8,128)(2,1)}, bf16[256,2048]{1,0:T(8,128)(2,1)}, u32[]{:S(2)}, u32[]{:S(2)}) collective-permute-start(bf16[256,2048]{1,0:T(8,128)(2,1)} %get-tuple-element.131), channel_id=1, source_target_pairs={{0,2},{2,0},{1,3},{3,1},{4,6},{6,4},{5,7},{7,5},{8,10},{10,8},{9,1... | collective-permute-start | bytes 3145736 | tf_op jit(solution)/shard_map/ppermute | solution.py:248
  476.6 23.2 %collective-permute-start.10 = (bf16[256,2048]{1,0:T(8,128)(2,1)}, bf16[256,2048]{1,0:T(8,128)(2,1)}, u32[]{:S(2)}, u32[]{:S(2)}) collective-permute-start(bf16[256,2048]{1,0:T(8,128)(2,1)} %get-tuple-element.131), channel_id=1, source_target_pairs={{0,4},{4,0},{1,5},{5,1},{2,6},{6,2},{3,7},{7,3},{8,12},{12,8},{9,1... | collective-permute-start | bytes 3145736 | tf_op jit(solution)/shard_map/ppermute | solution.py:248
  502.0 10.8 %collective-permute-start.12 = (bf16[128,2048]{1,0:T(8,128)(2,1)S(1)}, bf16[128,2048]{1,0:T(8,128)(2,1)S(1)}, u32[]{:S(2)}, u32[]{:S(2)}) collective-permute-start(bf16[128,2048]{1,0:T(8,128)(2,1)S(1)} %slice.285), channel_id=1, source_target_pairs={{0,2},{2,0},{1,3},{3,1},{4,6},{6,4},{5,7},{7,5},{8,10},{10,8},{9,1... | collective-permute-start | bytes 1572872 | tf_op jit(solution)/shard_map/ppermute | solution.py:248
  503.4 10.5 %collective-permute-start.13 = (bf16[128,2048]{1,0:T(8,128)(2,1)S(1)}, bf16[128,2048]{1,0:T(8,128)(2,1)S(1)}, u32[]{:S(2)}, u32[]{:S(2)}) collective-permute-start(bf16[128,2048]{1,0:T(8,128)(2,1)S(1)} %slice.286), channel_id=1, source_target_pairs={{0,4},{4,0},{1,5},{5,1},{2,6},{6,2},{3,7},{7,3},{8,12},{12,8},{9,1... | collective-permute-start | bytes 1572872 | tf_op jit(solution)/shard_map/ppermute | solution.py:248
  518.1 7.5 collective-permute-start.14
  518.1 13.5 %collective-permute-start.15 = (bf16[1024,2048]{1,0:T(8,128)(2,1)}, bf16[1024,2048]{1,0:T(8,128)(2,1)}, u32[]{:S(2)}, u32[]{:S(2)}) collective-permute-start(bf16[1024,2048]{1,0:T(8,128)(2,1)} %convolution_convert_fusion.5), channel_id=1, source_target_pairs={{0,1},{1,0},{2,3},{3,2},{4,5},{5,4},{6,7},{7,6},{8,9},{9,8},{10,11... | collective-permute-start | bytes 12582920 | tf_op jit(solution)/shard_map/ppermute | solution.py:248
  518.6 167.6 %reduce-scatter.9.cloned.1.call-start = ((), (), s32[]{:S(2)}) async-start(), calls=%async_computation.10 | async-start | bytes 3276800 | tf_op jit(solution)/shard_map/reduce_scatter | solution.py:1105
  525.6 6.0 copy-start.9
  538.4 25.5 %collective-permute-start.17 = (bf16[2,128,2048]{2,1,0:T(8,128)(2,1)}, bf16[2,128,2048]{2,1,0:T(8,128)(2,1)}, u32[]{:S(2)}, u32[]{:S(2)}) collective-permute-start(bf16[2,128,2048]{2,1,0:T(8,128)(2,1)} %pad_maximum_fusion.1), channel_id=1, source_target_pairs={{0,2},{2,0},{1,3},{3,1},{4,6},{6,4},{5,7},{7,5},{8,10},{10,8},{9,1... | collective-permute-start | bytes 3145736 | tf_op jit(solution)/shard_map/ppermute | solution.py:248
  539.6 25.2 %collective-permute-start.16 = (bf16[2,128,2048]{2,1,0:T(8,128)(2,1)}, bf16[2,128,2048]{2,1,0:T(8,128)(2,1)}, u32[]{:S(2)}, u32[]{:S(2)}) collective-permute-start(bf16[2,128,2048]{2,1,0:T(8,128)(2,1)} %slice_bitcast_fusion.1), channel_id=1, source_target_pairs={{0,4},{4,0},{1,5},{5,1},{2,6},{6,2},{3,7},{7,3},{8,12},{12,8},{9,1... | collective-permute-start | bytes 3145736 | tf_op jit(solution)/shard_map/ppermute | solution.py:248
  596.7 13.9 %copy-start.29 = (f32[8]{0:T(128)S(1)}, f32[8]{0:T(128)}, u32[]{:S(2)}) copy-start(f32[8]{0:T(128)} %copy-done.28) | copy-start | bytes 100
  610.6 12.8 %collective-permute-start.19 = (bf16[128,2048]{1,0:T(8,128)(2,1)}, bf16[128,2048]{1,0:T(8,128)(2,1)}, u32[]{:S(2)}, u32[]{:S(2)}) collective-permute-start(bf16[128,2048]{1,0:T(8,128)(2,1)} %get-tuple-element.275), channel_id=1, source_target_pairs={{0,4},{4,0},{1,5},{5,1},{2,6},{6,2},{3,7},{7,3},{8,12},{12,8},{9,1... | collective-permute-start | bytes 1572872 | tf_op jit(solution)/shard_map/ppermute | solution.py:248
  610.6 12.8 %collective-permute-start.18 = (bf16[128,2048]{1,0:T(8,128)(2,1)}, bf16[128,2048]{1,0:T(8,128)(2,1)}, u32[]{:S(2)}, u32[]{:S(2)}) collective-permute-start(bf16[128,2048]{1,0:T(8,128)(2,1)} %get-tuple-element.276), channel_id=1, source_target_pairs={{0,2},{2,0},{1,3},{3,1},{4,6},{6,4},{5,7},{7,5},{8,10},{10,8},{9,1... | collective-permute-start | bytes 1572872 | tf_op jit(solution)/shard_map/ppermute | solution.py:248
  623.4 8.3 %copy-start.26 = (f32[8,320]{1,0:T(8,128)S(1)}, f32[8,320]{1,0:T(8,128)}, u32[]{:S(2)}) copy-start(f32[8,320]{1,0:T(8,128)} %get-tuple-element.163) | copy-start | bytes 30724
  630.9 7.5 collective-permute-start.20
  631.3 131.2 %reduce-scatter.11.cloned.1.call-start = ((), (), s32[]{:S(2)}) async-start(), calls=%async_computation.11 | async-start | bytes 1945600 | tf_op jit(solution)/shard_map/reduce_scatter | solution.py:1129
  631.8 16.0 %copy-start.23 = (s32[320]{0:T(512)S(1)}, s32[320]{0:T(512)}, u32[]{:S(2)}) copy-start(s32[320]{0:T(512)} %copy-done.22) | copy-start | bytes 3844
  631.8 16.0 %copy-start.25 = (s32[320]{0:T(512)S(1)}, s32[320]{0:T(512)}, u32[]{:S(2)}) copy-start(s32[320]{0:T(512)} %copy-done.24) | copy-start | bytes 3844
  631.8 16.0 %copy-start.32 = (pred[320]{0:T(512)(128)(4,1)S(1)}, pred[320]{0:T(512)(128)(4,1)}, u32[]{:S(2)}) copy-start(pred[320]{0:T(512)(128)(4,1)} %copy-done.31) | copy-start | bytes 964
  631.8 16.0 %copy-start.40 = (f32[320,320]{1,0:T(8,128)S(1)}, f32[320,320]{1,0:T(8,128)}, u32[]{:S(2)}) copy-start(f32[320,320]{1,0:T(8,128)} %get-tuple-element.162) | copy-start | bytes 1228804
  631.9 16.0 %copy-start.41 = (pred[320]{0:T(512)(128)(4,1)S(1)}, pred[320]{0:T(512)(128)(4,1)}, u32[]{:S(2)}) copy-start(pred[320]{0:T(512)(128)(4,1)} %get-tuple-element.322) | copy-start | bytes 964
  648.6 8.7 %copy-start.39 = (f32[320,320]{1,0:T(8,128)S(1)}, f32[320,320]{1,0:T(8,128)}, u32[]{:S(2)}) copy-start(f32[320,320]{1,0:T(8,128)} %get-tuple-element.161) | copy-start | bytes 1228804
  651.0 26.8 %collective-permute-start.22 = (bf16[2,128,2048]{2,1,0:T(8,128)(2,1)}, bf16[2,128,2048]{2,1,0:T(8,128)(2,1)}, u32[]{:S(2)}, u32[]{:S(2)}) collective-permute-start(bf16[2,128,2048]{2,1,0:T(8,128)(2,1)} %pad_maximum_fusion.2), channel_id=1, source_target_pairs={{0,2},{2,0},{1,3},{3,1},{4,6},{6,4},{5,7},{7,5},{8,10},{10,8},{9,1... | collective-permute-start | bytes 3145736 | tf_op jit(solution)/shard_map/ppermute | solution.py:248
  655.3 25.5 %collective-permute-start.21 = (bf16[2,128,2048]{2,1,0:T(8,128)(2,1)}, bf16[2,128,2048]{2,1,0:T(8,128)(2,1)}, u32[]{:S(2)}, u32[]{:S(2)}) collective-permute-start(bf16[2,128,2048]{2,1,0:T(8,128)(2,1)} %slice_bitcast_fusion), channel_id=1, source_target_pairs={{0,4},{4,0},{1,5},{5,1},{2,6},{6,2},{3,7},{7,3},{8,12},{12,8},{9,1... | collective-permute-start | bytes 3145736 | tf_op jit(solution)/shard_map/ppermute | solution.py:248
  672.6 17.2 %copy-start.33 = (bf16[64]{0:T(256)(128)(2,1)S(1)}, bf16[64]{0:T(256)(128)(2,1)}, u32[]{:S(2)}) copy-start(bf16[64]{0:T(256)(128)(2,1)} %param.32) | copy-start | bytes 388
  673.9 16.7 %copy-start.34 = (bf16[64]{0:T(256)(128)(2,1)S(1)}, bf16[64]{0:T(256)(128)(2,1)}, u32[]{:S(2)}) copy-start(bf16[64]{0:T(256)(128)(2,1)} %param.21) | copy-start | bytes 388
  673.9 17.4 %copy-start.30 = (f32[256]{0:T(256)S(1)}, f32[256]{0:T(256)}, u32[]{:S(2)}) copy-start(f32[256]{0:T(256)} %get-tuple-element.249) | copy-start | bytes 3076
  688.4 13.8 %collective-permute-start.23 = (bf16[128,2048]{1,0:T(8,128)(2,1)}, bf16[128,2048]{1,0:T(8,128)(2,1)}, u32[]{:S(2)}, u32[]{:S(2)}) collective-permute-start(bf16[128,2048]{1,0:T(8,128)(2,1)} %fusion.34), channel_id=1, source_target_pairs={{0,2},{2,0},{1,3},{3,1},{4,6},{6,4},{5,7},{7,5},{8,10},{10,8},{9,1... | collective-permute-start | bytes 1572872 | tf_op jit(solution)/shard_map/ppermute | solution.py:248
  705.5 24.1 %collective-permute-start.24 = (bf16[128,2048]{1,0:T(8,128)(2,1)}, bf16[128,2048]{1,0:T(8,128)(2,1)}, u32[]{:S(2)}, u32[]{:S(2)}) collective-permute-start(bf16[128,2048]{1,0:T(8,128)(2,1)} %get-tuple-element.270), channel_id=1, source_target_pairs={{0,4},{4,0},{1,5},{5,1},{2,6},{6,2},{3,7},{7,3},{8,12},{12,8},{9,1... | collective-permute-start | bytes 1572872 | tf_op jit(solution)/shard_map/ppermute | solution.py:248
  752.0 6.9 copy-start.20
  (18 other events, 55.8 us)
Sparse Core Ops, SparseCore 0:
  36.6 55.0 all-gather.6
  93.8 35.5 all-gather.4
  131.0 62.3 all-gather.10
  194.9 116.0 all-gather.8
  453.8 60.4 reduce-scatter.6
  518.8 112.5 reduce-scatter.4
  633.6 52.6 reduce-scatter.8
  690.7 33.9 reduce-scatter.10

commit v3 on v2

--- a/solution.py
+++ b/solution.py
@@ -63,12 +63,18 @@
     )
 
 
-def gather_kernel(x_ref, o_ref, local_sem, ssem, rsem):
+def gather_kernel(*refs):
+    if len(refs) == 5:
+        x_ref, o_ref, local_sem, ssem, rsem = refs
+        extra = ()
+    else:
+        x_ref, b_ref, o_ref, e_ref, local_sem, ssem, rsem, *sems = refs
+        extra = exchange_parts(FEAT, b_ref, e_ref, *sems)
     x, y, c = feature_place()
     to_x, to_y, to_c = {"x": 1 - x}, {"y": 1 - y}, {"c": 1 - c}
     half = x_ref.shape[0] // 2
     top, low = pl.ds(0, half), pl.ds(half, half)
-    greet((to_x, to_y, to_c))
+    greet(extra[0] if extra else (to_x, to_y, to_c))
 
     def copy(i, src, dst, device):
         return remote(src, dst, ssem.at[i], rsem.at[i], device)
@@ -86,6 +92,10 @@
     c_d = copy(9, o_ref.at[DIAGONAL], o_ref.at[4 + DIAGONAL], to_c)
     for one in (x_top, y_low, x_low, y_top, c_own, own):
         one.start()
+    if extra:
+        extra[1].start()
+        for one in extra[2]:
+            one.start()
     x_top.wait_recv()
     y_fwd.start()
     y_low.wait_recv()
@@ -102,6 +112,10 @@
     for one in (x_top, x_low, y_low, y_top, c_own, y_fwd, x_fwd, c_x, c_y, c_d):
         one.wait_send()
     own.wait()
+    if extra:
+        for one in extra[2]:
+            one.wait()
+        extra[1].wait()
 
 
 def gather_feature(block):
@@ -265,14 +279,23 @@
     return jnp.concatenate([block, by_y, by_x, d_top, d_low])
 
 
-def scatter_near(mine, theirs_got):
+def scatter_total(mine, theirs_got):
     rows = mine.shape[0] // 4
     kind = theirs_got.dtype
+    mine, theirs_got = hold(mine, theirs_got)
     total = (mine.astype(f32) + theirs_got.astype(f32)).astype(kind)
-    total = total.reshape(4, 2, rows // 2, mine.shape[1])
+    return total.reshape(4, 2, rows // 2, mine.shape[1])
+
+
+def scatter_sides(total):
     by_x = across(total[2:, 0], "x")
     by_y = across(jnp.stack([total[ACROSS_Y, 1], total[DIAGONAL, 1]]), "y")
-    return total, by_x, by_y
+    return by_x, by_y
+
+
+def scatter_near(mine, theirs_got):
+    total = scatter_total(mine, theirs_got)
+    return (total,) + scatter_sides(total)
 
 
 def scatter_relay(total, by_x, by_y):
@@ -288,7 +311,149 @@
     return jnp.concatenate([upper, lower])
 
 
-def exchange_kernel(axes, x_ref, o_ref, local_sem, ssem, rsem):
+def gather_tail_kernel(x_ref, bx_ref, by_ref, o_ref, lsem, ssem, rsem):
+    x, y, c = feature_place()
+    to_x, to_y, to_c = {"x": 1 - x}, {"y": 1 - y}, {"c": 1 - c}
+    half = x_ref.shape[0] // 2
+    top, low = pl.ds(0, half), pl.ds(half, half)
+
+    def copy(i, src, dst, device):
+        return remote(src, dst, ssem.at[i], rsem.at[i], device)
+
+    places = ((x_ref, OWN), (by_ref, ACROSS_Y), (bx_ref, ACROSS_X))
+    local = [
+        pltpu.make_async_copy(ref, o_ref.at[slot], lsem.at[i])
+        for i, (ref, slot) in enumerate(places)
+    ]
+    greet((to_x, to_y, to_c))
+    y_fwd = copy(0, bx_ref.at[top], o_ref.at[DIAGONAL, top], to_y)
+    x_fwd = copy(1, by_ref.at[low], o_ref.at[DIAGONAL, low], to_x)
+    cross = [
+        copy(2 + i, ref, o_ref.at[4 + slot], to_c) for i, (ref, slot) in enumerate(places)
+    ]
+    last = copy(5, o_ref.at[DIAGONAL], o_ref.at[4 + DIAGONAL], to_c)
+    for one in [y_fwd, x_fwd] + cross + local:
+        one.start()
+    y_fwd.wait_recv()
+    x_fwd.wait_recv()
+    last.start()
+    for one in cross + [last]:
+        one.wait_recv()
+    for one in cross + [y_fwd, x_fwd, last]:
+        one.wait_send()
+    for one in local:
+        one.wait()
+
+
+def gather_tail(block, by_x, by_y):
+    rows, width = block.shape
+    out = pl.pallas_call(
+        gather_tail_kernel,
+        out_shape=jax.ShapeDtypeStruct((NF, rows, width), block.dtype),
+        in_specs=[vmem_spec()] * 3,
+        out_specs=hbm_spec(),
+        scratch_shapes=[
+            pltpu.SemaphoreType.DMA((3,)),
+            pltpu.SemaphoreType.DMA((6,)),
+            pltpu.SemaphoreType.DMA((6,)),
+        ],
+        compiler_params=pltpu.CompilerParams(
+            collective_id=8, has_side_effects=True, vmem_limit_bytes=VMEM_LIMIT
+        ),
+        cost_estimate=cost(16),
+        name="gather_tail",
+    )(block, by_x, by_y)
+    return out.reshape(NF * rows, width)
+
+
+def scatter_tail_kernel(
+    t_ref, bx_ref, by_ref, o_ref, near, own, bx, by, relay, last, lsem, ssem, rsem
+):
+    x, y, c = feature_place()
+    to_x, to_y = {"x": 1 - x}, {"y": 1 - y}
+    half = o_ref.shape[0] // 2
+    step = 16
+
+    def load(i, src, dst):
+        one = pltpu.make_async_copy(src, dst, lsem.at[i])
+        one.start()
+        return one
+
+    loads = [
+        load(0, t_ref.at[ACROSS_Y, 0], near.at[0]),
+        load(1, bx_ref, bx),
+        load(2, t_ref.at[ACROSS_X, 1], near.at[1]),
+        load(3, by_ref, by),
+        load(4, t_ref.at[OWN], own),
+    ]
+    greet((to_x, to_y))
+    sends = [
+        remote(relay.at[0], last.at[0], ssem.at[0], rsem.at[0], to_y),
+        remote(relay.at[1], last.at[1], ssem.at[1], rsem.at[1], to_x),
+    ]
+
+    def tiles(body):
+        def one(i, none):
+            body(pl.ds(pl.multiple_of(i * step, step), step), i * step)
+            return none
+
+        lax.fori_loop(0, half // step, one, 0)
+
+    for side, got in ((0, bx), (1, by)):
+        loads[2 * side].wait()
+        loads[2 * side + 1].wait()
+
+        def add(at, _, side=side, got=got):
+            relay[side, at] = (near[side, at].astype(f32) + got[1, at].astype(f32)).astype(
+                relay.dtype
+            )
+
+        tiles(add)
+        sends[side].start()
+    loads[4].wait()
+    for side, got in ((0, bx), (1, by)):
+
+        def base(at, start, side=side, got=got):
+            here = pl.ds(pl.multiple_of(side * half + start, step), step)
+            o_ref[here] = own[side, at].astype(f32) + got[0, at].astype(f32)
+
+        tiles(base)
+    for side in range(2):
+        sends[side].wait_recv()
+
+        def finish(at, start, side=side):
+            here = pl.ds(pl.multiple_of(side * half + start, step), step)
+            o_ref[here] = o_ref[here] + last[side, at].astype(f32)
+
+        tiles(finish)
+    for one in sends:
+        one.wait_send()
+
+
+def scatter_tail(total, by_x, by_y):
+    half, width = total.shape[2:]
+    kind = total.dtype
+    pair = pltpu.VMEM((2, half, width), kind)
+    return pl.pallas_call(
+        scatter_tail_kernel,
+        out_shape=jax.ShapeDtypeStruct((2 * half, width), f32),
+        in_specs=[hbm_spec()] * 3,
+        out_specs=vmem_spec(),
+        scratch_shapes=[pair] * 6
+        + [
+            pltpu.SemaphoreType.DMA((5,)),
+            pltpu.SemaphoreType.DMA((2,)),
+            pltpu.SemaphoreType.DMA((2,)),
+        ],
+        compiler_params=pltpu.CompilerParams(
+            collective_id=9, has_side_effects=True, vmem_limit_bytes=VMEM_LIMIT
+        ),
+        cost_estimate=cost(16),
+        name="scatter_tail",
+    )(total, by_x, by_y)
+
+
+def exchange_parts(axes, x_ref, o_ref, local_sem, ssem, rsem):
     place = [lax.axis_index(name) for name in axes]
     count = 2 ** len(axes)
 
@@ -299,44 +464,91 @@
         return total
 
     mine = rank(place)
-    flips = []
-    for mask in range(1, count):
+    own = pltpu.make_async_copy(x_ref.at[mine], o_ref.at[mine], local_sem)
+    peers, copies = [], []
+    for mask in range(count - 1, 0, -1):
         bits = [(mask // 2 ** (len(axes) - 1 - i)) % 2 for i in range(len(axes))]
         coords = [1 - p if bit else p for p, bit in zip(place, bits)]
         device = {name: q for name, q, bit in zip(axes, coords, bits) if bit}
-        flips.append((rank(coords), device))
-    own = pltpu.make_async_copy(x_ref.at[mine], o_ref.at[mine], local_sem)
-    own.start()
-    greet([device for _, device in flips])
-    copies = [
-        remote(x_ref.at[target], o_ref.at[mine], ssem.at[i], rsem.at[i], device)
-        for i, (target, device) in enumerate(flips)
+        peers.append(device)
+        copies.append(
+            remote(
+                x_ref.at[rank(coords)],
+                o_ref.at[mine],
+                ssem.at[mask - 1],
+                rsem.at[mask - 1],
+                device,
+            )
+        )
+    return peers, own, copies
+
+
+def exchange_kernel(axes, *refs):
+    count = (len(refs) - 3) // 2
+    sources, targets = refs[:count], refs[count : 2 * count]
+    local_sem, ssem, rsem = refs[2 * count :]
+    parts = [
+        exchange_parts(axes, sources[i], targets[i], local_sem.at[i], ssem.at[i], rsem.at[i])
+        for i in range(count)
     ]
-    for one in reversed(copies):
-        one.start()
-    for one in copies:
-        one.wait()
-    own.wait()
-
-
-def exchange(blocks, axes, ident):
-    count = 2 ** len(axes)
+    for _, own, _ in parts:
+        own.start()
+    greet(parts[0][0])
+    for _, _, copies in parts:
+        for one in copies:
+            one.start()
+    for _, own, copies in parts:
+        for one in copies:
+            one.wait()
+        own.wait()
+
+
+def exchange(arrays, axes, ident):
+    peers = 2 ** len(axes) - 1
+    count = len(arrays)
     return pl.pallas_call(
         functools.partial(exchange_kernel, axes),
-        out_shape=jax.ShapeDtypeStruct(blocks.shape, blocks.dtype),
-        in_specs=[vmem_spec()],
-        out_specs=hbm_spec(),
+        out_shape=tuple(jax.ShapeDtypeStruct(a.shape, a.dtype) for a in arrays),
+        in_specs=[vmem_spec()] * count,
+        out_specs=(hbm_spec(),) * count,
         scratch_shapes=[
-            pltpu.SemaphoreType.DMA,
-            pltpu.SemaphoreType.DMA((count - 1,)),
-            pltpu.SemaphoreType.DMA((count - 1,)),
+            pltpu.SemaphoreType.DMA((count,)),
+            pltpu.SemaphoreType.DMA((count, peers)),
+            pltpu.SemaphoreType.DMA((count, peers)),
         ],
         compiler_params=pltpu.CompilerParams(
             collective_id=ident, has_side_effects=True, vmem_limit_bytes=VMEM_LIMIT
         ),
         cost_estimate=cost(15),
         name="exchange",
-    )(blocks)
+    )(*arrays)
+
+
+def gather_exchange(block, blocks):
+    rows, width = block.shape
+    out, got = pl.pallas_call(
+        gather_kernel,
+        out_shape=(
+            jax.ShapeDtypeStruct((NF, rows, width), block.dtype),
+            jax.ShapeDtypeStruct(blocks.shape, blocks.dtype),
+        ),
+        in_specs=[vmem_spec()] * 2,
+        out_specs=(hbm_spec(),) * 2,
+        scratch_shapes=[
+            pltpu.SemaphoreType.DMA,
+            pltpu.SemaphoreType.DMA((10,)),
+            pltpu.SemaphoreType.DMA((10,)),
+            pltpu.SemaphoreType.DMA,
+            pltpu.SemaphoreType.DMA((NF - 1,)),
+            pltpu.SemaphoreType.DMA((NF - 1,)),
+        ],
+        compiler_params=pltpu.CompilerParams(
+            collective_id=4, has_side_effects=True, vmem_limit_bytes=VMEM_LIMIT
+        ),
+        cost_estimate=cost(55),
+        name="gather_exchange",
+    )(block, blocks)
+    return out.reshape(NF * rows, width), got
 
 
 def groups_kernel(count, x_ref, o_ref, local_sem, ssem, rsem):
@@ -419,12 +631,13 @@
 
 def forward_kernel(
     order_ref,
-    branch_ref,
+    pre_ref,
     halo_ref,
     mask_ref,
     small_ref,
     wa_ref,
     wx_ref,
+    branch_ref,
     conved_ref,
     keep_ref,
     prod_ref,
@@ -433,8 +646,10 @@
     ext,
     carry,
 ):
-    rows = branch_ref.shape[0]
+    rows, width = branch_ref.shape
     step = pl.program_id(0)
+    branch = pre_ref[:, width : 2 * width].astype(bf16)
+    branch_ref[...] = branch
 
     @pl.when(step == 0)
     def _():
@@ -446,7 +661,7 @@
     def _():
         ext[pl.ds(0, 8)] = ext[pl.ds(rows, 8)]
 
-    ext[pl.ds(8, rows)] = branch_ref[...].astype(f32)
+    ext[pl.ds(8, rows)] = branch.astype(f32)
     masks = mask_ref[...]
     conved = conv_of(ext, masks, small_ref, small_ref[4:5], rows).astype(bf16)
     conved_ref[...] = conved
@@ -476,15 +691,17 @@
     ends_ref[2:8] = jnp.zeros_like(ends_ref[2:8])
 
 
-def forward_scan(order, branch_in, halo, masks, small, wa, wx, chunk):
-    rows, width = branch_in.shape
+def forward_scan(order, rec_pre, halo, masks, small, wa, wx, chunk):
+    rows, width = rec_pre.shape[0], rec_pre.shape[1] // 2
     tile = pl.BlockSpec((chunk, width), lambda i, order: (order[i], 0))
     whole = lambda a: pl.BlockSpec(a.shape, lambda i, order: (0, 0))
     full = jax.ShapeDtypeStruct((rows, width), f32)
+    low = jax.ShapeDtypeStruct((rows, width), bf16)
     return pl.pallas_call(
         forward_kernel,
         out_shape=(
-            jax.ShapeDtypeStruct((rows, width), bf16),
+            low,
+            low,
             full,
             full,
             full,
@@ -494,24 +711,24 @@
             num_scalar_prefetch=1,
             grid=(rows // chunk,),
             in_specs=[
-                tile,
+                pl.BlockSpec((chunk, 2 * width), lambda i, order: (order[i], 0)),
                 whole(halo),
                 pl.BlockSpec((chunk, masks.shape[1]), lambda i, order: (i, 0)),
                 whole(small),
                 whole(wa),
                 whole(wx),
             ],
-            out_specs=(tile, tile, tile, tile, pl.BlockSpec((8, width), lambda i, order: (0, 0))),
+            out_specs=(tile,) * 5 + (pl.BlockSpec((8, width), lambda i, order: (0, 0)),),
             scratch_shapes=[pltpu.VMEM((chunk + 8, width), f32), pltpu.VMEM((8, width), f32)],
         ),
         compiler_params=pltpu.CompilerParams(vmem_limit_bytes=VMEM_LIMIT),
         cost_estimate=cost(15),
         name="forward_scan",
-    )(order, branch_in, halo, masks, small, wa, wx)
+    )(order, rec_pre, halo, masks, small, wa, wx)
 
 
 def adjoint_kernel(
-    order_ref, d_mixed_ref, gate_ref, keep_ref, prod_ref, adj_ref, heads_ref, keep_next, carry
+    order_ref, d_mixed_ref, pre_ref, keep_ref, prod_ref, adj_ref, heads_ref, keep_next, carry
 ):
     rows = d_mixed_ref.shape[0]
     step = pl.program_id(0)
@@ -528,7 +745,7 @@
 
     keep_next[pl.ds(0, rows)] = keep_ref[...]
     prod_ref[...] = keep_next[pl.ds(1, rows)]
-    adj_ref[...] = d_mixed_ref[...] * gelu_tanh(gate_ref[...])
+    adj_ref[...] = d_mixed_ref[...] * gelu_tanh(pre_ref[:, 0 : adj_ref.shape[1]])
     tiles = rows // 8
 
     def body(i, held):
@@ -549,7 +766,7 @@
     heads_ref[2:8] = jnp.zeros_like(heads_ref[2:8])
 
 
-def adjoint_scan(order, d_mixed, gate_pre, keep, chunk):
+def adjoint_scan(order, d_mixed, rec_pre, keep, chunk):
     rows, width = keep.shape
     last = rows // chunk - 1
     tile = pl.BlockSpec((chunk, width), lambda i, order: (order[last - i], 0))
@@ -560,20 +777,24 @@
         grid_spec=pltpu.PrefetchScalarGridSpec(
             num_scalar_prefetch=1,
             grid=(rows // chunk,),
-            in_specs=[tile, tile, tile],
+            in_specs=[
+                tile,
+                pl.BlockSpec((chunk, 2 * width), lambda i, order: (order[last - i], 0)),
+                tile,
+            ],
             out_specs=(tile, tile, pl.BlockSpec((8, width), lambda i, order: (0, 0))),
             scratch_shapes=[pltpu.VMEM((chunk + 8, width), f32), pltpu.VMEM((8, width), f32)],
         ),
         compiler_params=pltpu.CompilerParams(vmem_limit_bytes=VMEM_LIMIT),
         cost_estimate=cost(12),
         name="adjoint_scan",
-    )(order, d_mixed, gate_pre, keep)
+    )(order, d_mixed, rec_pre, keep)
 
 
 def backward_kernel(
     order_ref,
     d_mixed_ref,
-    gate_ref,
+    pre_ref,
     state_ref,
     prod_ref,
     state_before_ref,
@@ -632,7 +853,7 @@
     ext[pl.ds(8, rows)] = branch_ref[...].astype(f32)
     state = state_ref[...] + prod_ref[...] * state_in
     state_ext[pl.ds(8, rows)] = state
-    _, slope = gelu_pair(gate_ref[...])
+    _, slope = gelu_pair(pre_ref[:, 0:width])
     d_pre_ref[:, 0:width] = (d_mixed_ref[...] * state * slope).astype(bf16)
     adjoint = adj_ref[...] + adj_prod_ref[...] * adj_in
     state_prev = state_ext[pl.ds(7, rows)]
@@ -694,7 +915,7 @@
 
 
 def backward_scan(
-    order, d_mixed, gate_pre, state, prod, adj, adj_prod, branch_in, halo, conved, masks, small,
+    order, d_mixed, rec_pre, state, prod, adj, adj_prod, branch_in, halo, conved, masks, small,
     enter, wa, wx, chunk,
 ):
     rows, width = state.shape
@@ -724,7 +945,7 @@
             grid=(rows // chunk,),
             in_specs=[
                 tile,
-                tile,
+                pl.BlockSpec((chunk, 2 * width), lambda i, order: (order[last - i], 0)),
                 tile,
                 tile,
                 before(8),
@@ -758,16 +979,18 @@
         cost_estimate=cost(21),
         name="backward_scan",
     )(
-        order, d_mixed, gate_pre, state, prod, state, prod, adj, adj_prod, branch_in, branch_in,
+        order, d_mixed, rec_pre, state, prod, state, prod, adj, adj_prod, branch_in, branch_in,
         halo, conved, masks, small, enter, wa, wx,
     )
 
 
-def gated_kernel(n_ref, cot_ref, w_ref, down_ref, hidden_ref, d_ref):
+def gated_kernel(n_ref, mine_ref, theirs_ref, w_ref, down_ref, hidden_ref, d_ref):
     ff = down_ref.shape[0]
     tile = 256
     normed = n_ref[...]
-    cot = cot_ref[...]
+    cot = lax.select(
+        pl.program_id(0) < pl.num_programs(0) // 2, mine_ref[...], theirs_ref[...]
+    )
 
     def body(j, none):
         at = pl.ds(pl.multiple_of(j * tile, tile), tile)
@@ -784,7 +1007,7 @@
     lax.fori_loop(0, ff // tile, body, 0)
 
 
-def gated_unit(normed, cot, w_mlp, w_down):
+def gated_unit(normed, cot_mine, cot_theirs, w_mlp, w_down):
     rows, width = normed.shape
     ff = w_down.shape[0]
     steps = 4
@@ -798,14 +1021,20 @@
             jax.ShapeDtypeStruct((rows, ff), bf16),
             jax.ShapeDtypeStruct((rows, 2 * ff), bf16),
         ),
-        in_specs=[row(width), row(width), once(w_mlp), once(w_down)],
+        in_specs=[
+            row(width),
+            pl.BlockSpec((tile, width), lambda i: (jnp.minimum(i, steps // 2 - 1), 0)),
+            pl.BlockSpec((tile, width), lambda i: (jnp.maximum(i - steps // 2, 0), 0)),
+            once(w_mlp),
+            once(w_down),
+        ],
         out_specs=(row(ff), row(2 * ff)),
         compiler_params=pltpu.CompilerParams(vmem_limit_bytes=VMEM_LIMIT),
         cost_estimate=pl.CostEstimate(
             flops=6 * rows * width * ff, bytes_accessed=40 * 2**20, transcendentals=rows * ff
         ),
         name="gated_unit",
-    )(normed, cot, w_mlp, w_down)
+    )(normed, cot_mine, cot_theirs, w_mlp, w_down)
 
 
 def split_kernel(moves, a_ref, b_ref, o_ref):
@@ -821,7 +1050,8 @@
     total = jnp.sum(a_ref[...].astype(f32) * oa_ref[...], axis=1, keepdims=True) + jnp.sum(
         b_ref[...].astype(f32) * ob_ref[...], axis=1, keepdims=True
     )
-    og_ref[...] = total / g_ref[...]
+    wide = jnp.broadcast_to(total / g_ref[...], (total.shape[0], LANES))
+    og_ref[...] = wide.T[0:1]
 
 
 def split_blocks(a, b, moves):
@@ -840,11 +1070,39 @@
     out = jax.ShapeDtypeStruct((rows, width), f32)
     return pl.pallas_call(
         functools.partial(join_kernel, moves),
-        out_shape=(out, out, jax.ShapeDtypeStruct((rows, 1), f32)),
+        out_shape=(out, out, jax.ShapeDtypeStruct((1, rows), f32)),
         compiler_params=pltpu.CompilerParams(vmem_limit_bytes=VMEM_LIMIT),
         cost_estimate=cost(5),
         name="join_blocks",
     )(x, a, b, gain)
+
+
+def unpack_kernel(x_ref, out_ref, ga_ref, gx_ref, taps_ref, *row_refs):
+    width = out_ref.shape[1]
+    base = width + 2 * BLK
+    out_ref[...] = x_ref[:, 0:width].astype(f32)
+    ga_ref[...] = x_ref[:, width : width + BLK].astype(f32)
+    gx_ref[...] = x_ref[:, width + BLK : base].astype(f32)
+    last = base - base % LANES
+    small = x_ref[:, last : last + LANES].astype(f32)
+    taps_ref[...] = small[:, base - last : base - last + CONV]
+    turned = small.T
+    for i, ref in enumerate(row_refs):
+        at = base - last + CONV + i
+        ref[...] = turned[at : at + 1]
+
+
+def unpack_sums(x, width):
+    rows = x.shape[0]
+    shape = lambda *dims: jax.ShapeDtypeStruct(dims, f32)
+    return pl.pallas_call(
+        unpack_kernel,
+        out_shape=(shape(rows, width), shape(rows, BLK), shape(rows, BLK), shape(rows, CONV))
+        + (shape(1, rows),) * 4,
+        compiler_params=pltpu.CompilerParams(vmem_limit_bytes=VMEM_LIMIT),
+        cost_estimate=cost(2),
+        name="unpack_sums",
+    )(x)
 
 
 def pad_lanes(rows, width):
@@ -954,15 +1212,8 @@
         ],
         axis=1,
     )
-    rec_send, pack = hold(rec_send, pack)
     pack_all = lax.all_gather(pack, "z", axis=0, tiled=True)
-    rec_got = exchange(rec_send, FEAT, 3)
-    w_rec = lax.all_gather(
-        rec_got[:, :rows_w].reshape(NF * rows_w, 2 * chans), "z", axis=0, tiled=True
-    )
-    tokens_own, rec_got = hold(tokens_in, rec_got)
-    tok_group = gather_feature(tokens_own)
-    pack_swap = exchange(pack_all.reshape(spread, 2, chan_rows, pack_width), swap_axes, 5)
+    (rec_got,) = exchange([rec_send], FEAT, 3)
     starts = rec_got[:, rows_w, :rows_tok].reshape(group_rows).astype(f32)
 
     plane_gains = jnp.stack(
@@ -972,19 +1223,25 @@
         ]
     ).astype(f32)
     gains = gather_groups(jnp.pad(plane_gains, ((0, 6), (0, 0))), count, 7)
+    w_rec = lax.all_gather(
+        rec_got[:, :rows_w].reshape(NF * rows_w, 2 * chans), "z", axis=0, tiled=True
+    )
+    mlp_send = split_blocks(mlp_gate_weight, mlp_up_weight, ff_moves)
+    tokens_own, gains = hold(tokens_in, gains)
+    tok_group, mlp_got = gather_exchange(tokens_own, mlp_send)
+    tok_group, pack_all = hold(tok_group, pack_all)
+    (pack_swap,) = exchange(
+        [pack_all.reshape(spread, 2, chan_rows, pack_width)], swap_axes, 5
+    )
     gain_one = gains[:, 0].reshape(1, width)
     gain_two = gains[:, 1].reshape(1, width)
 
     tok = tokens_in.astype(f32)
     tok_group = tok_group.astype(f32)
     normed = (tok_group * inverse_rms(tok_group) * gain_one).astype(bf16)
-    normed, pack_swap, mlp_gate_in = hold(normed, pack_swap, mlp_gate_weight)
-    mlp_send = split_blocks(mlp_gate_in, mlp_up_weight, ff_moves)
-    mlp_got = exchange(mlp_send, FEAT, 4)
-
-    w_rec, down_in = hold(w_rec, mlp_down_weight)
+
     w_mlp = lax.all_gather(mlp_got.reshape(NF * rows_w, 2 * ff), "z", axis=0, tiled=True)
-    w_down = lax.all_gather(down_in, "z", axis=0, tiled=True)
+    w_down = lax.all_gather(mlp_down_weight, "z", axis=0, tiled=True)
 
     mine = pack_swap.transpose(1, 0, 2, 3).reshape(chans, pack_width)
     w_out = mine[:, :width]
@@ -1012,14 +1269,11 @@
     rec_pre = jnp.dot(normed, w_rec, preferred_element_type=f32)
     rec_pre, cot_own = hold(rec_pre, cotangent)
     cot_x, cot_y = gather_near(cot_own)
-    gate_pre = rec_pre[:, :chans]
-    branch_in = rec_pre[:, chans:].astype(bf16)
-    tails = gather_groups(
-        lax.dynamic_slice_in_dim(branch_in, final, 8, 0).astype(f32) * later_open, count, 2
-    )
+    edge_rows = lax.dynamic_slice_in_dim(rec_pre, final, 8, 0)[:, chans:].astype(bf16)
+    tails = gather_groups(edge_rows.astype(f32) * later_open, count, 2)
     halo = jnp.where(z > 0, lax.dynamic_index_in_dim(tails, jnp.maximum(z - 1, 0), 0, False), 0.0)
-    conved, keep, prod, state_local, ends = forward_scan(
-        order, branch_in, halo, masks, small, wa, wx, chunk
+    branch_in, conved, keep, prod, state_local, ends = forward_scan(
+        order, rec_pre, halo, masks, small, wa, wx, chunk
     )
     ends, cot_x, cot_y = hold(ends, cot_x, cot_y)
     cot_top, cot_low = gather_diagonal(cot_x, cot_y)
@@ -1027,64 +1281,66 @@
     state_in = jnp.zeros((1, chans), f32)
     for hop in range(count - 1):
         state_in = jnp.where(hop < z, ends[hop, 0:1] * state_in + ends[hop, 1:2], state_in)
-    mixed = ((state_local + prod * state_in) * gelu_tanh(gate_pre)).astype(bf16)
+    mixed = ((state_local + prod * state_in) * gelu_tanh(rec_pre[:, :chans])).astype(bf16)
     mixed_out = jnp.dot(mixed, w_out, preferred_element_type=f32).astype(bf16)
     mixed_out, cot_top, cot_low = hold(mixed_out, cot_top, cot_low)
     cot_chip = gather_chip(cotangent, cot_x, cot_y, cot_top, cot_low)
-    cot = jnp.concatenate([cot_chip, across(cot_chip, "c")])
+    cot_got = across(cot_chip, "c")
     middle = tok + scatter_feature(mixed_out)
 
     scale_two = inverse_rms(middle)
     normed_two = gather_feature((middle * scale_two * gain_two).astype(bf16))
-    hidden, d_mlp = gated_unit(normed_two, cot, w_mlp, w_down)
+    hidden, d_mlp = gated_unit(normed_two, cot_chip, cot_got, w_mlp, w_down)
     half_rows = group_rows // 2
 
     def back_rows(d, w):
-        return lax.dot_general(d, w, contract_last, preferred_element_type=f32)
-
-    e_theirs = back_rows(d_mlp[half_rows:], w_mlp).astype(bf16)
+        return lax.dot_general(d, w, contract_last, preferred_element_type=f32).astype(bf16)
+
+    def over_rows(a, b_mine, b_theirs):
+        return (
+            lax.dot_general(a[:half_rows], b_mine, contract_first, preferred_element_type=f32)
+            + lax.dot_general(a[half_rows:], b_theirs, contract_first, preferred_element_type=f32)
+        ).astype(bf16)
+
+    e_theirs = back_rows(d_mlp[half_rows:], w_mlp)
+    d_mlp, e_theirs = hold(d_mlp, e_theirs)
     e_got = across(e_theirs, "c")
-    d_mlp, e_theirs = hold(d_mlp, e_theirs)
     e_mine = back_rows(d_mlp[:half_rows], w_mlp)
     e_total, e_x, e_y = scatter_near(e_mine, e_got)
     e_total, hidden = hold(e_total, hidden)
-    down_part = lax.dot_general(
-        hidden, cot, contract_first, preferred_element_type=f32
-    ).astype(bf16)
+    down_part = over_rows(hidden, cot_chip, cot_got)
+    down_part, hidden = hold(down_part, hidden)
+    down_sum = lax.psum_scatter(down_part, "z", scatter_dimension=0, tiled=True)
     out_theirs = jnp.dot(hidden[half_rows:], w_down, preferred_element_type=f32).astype(bf16)
-    down_part, e_x, e_y, hidden, out_theirs = hold(down_part, e_x, e_y, hidden, out_theirs)
-    down_sum = lax.psum_scatter(down_part, "z", scatter_dimension=0, tiled=True)
-    e_last = scatter_relay(e_total, e_x, e_y)
+    out_got = across(out_theirs, "c")
     out_mine = jnp.dot(hidden[:half_rows], w_down, preferred_element_type=f32).astype(bf16)
-    out_mine, *e_last = hold(out_mine, *e_last)
-    e_two = gain_two * scatter_sum(e_total, e_x, e_y, *e_last)
+    out_mine, out_got, e_x, e_y = hold(out_mine, out_got, e_x, e_y)
+    e_two = gain_two * scatter_tail(e_total, e_x, e_y)
     d_middle = cotangent.astype(f32) + norm_back(middle, scale_two, e_two)
     d_own = d_middle.astype(bf16)
     d_x, d_y = gather_near(d_own)
-    d_own, d_mlp, out_theirs = hold(d_own, d_mlp, out_theirs)
+    d_own, d_mlp, out_mine, out_got = hold(d_own, d_mlp, out_mine, out_got)
     mlp_part = lax.dot_general(
         normed_two, d_mlp, contract_first, preferred_element_type=f32
     ).astype(bf16)
-    d_x, d_y, mlp_part, out_theirs = hold(d_x, d_y, mlp_part, out_theirs)
+    out_total = scatter_total(out_mine, out_got)
+    d_x, d_y, mlp_part, out_total = hold(d_x, d_y, mlp_part, out_total)
     mlp_sum = lax.psum_scatter(mlp_part, "z", scatter_dimension=0, tiled=True)
-    d_top, d_low = gather_diagonal(d_x, d_y)
-    out_got = across(out_theirs, "c")
-    d_chip = gather_chip(d_own, d_x, d_y, d_top, d_low)
-    d_rec = jnp.concatenate([d_chip, across(d_chip, "c")])
-    d_rec, out_got = hold(d_rec, out_got)
-    out_total, out_x, out_y = scatter_near(out_mine, out_got)
+    d_rec = gather_tail(d_own, d_x, d_y)
+    d_rec, down_sum, out_total = hold(d_rec, down_sum, out_total)
+    out_x, out_y = scatter_sides(out_total)
 
     d_mixed = lax.dot_general(d_rec, w_out, contract_last, preferred_element_type=f32)
-    adj_prod, adj_local, heads = adjoint_scan(order, d_mixed, gate_pre, keep, chunk)
+    adj_prod, adj_local, heads = adjoint_scan(order, d_mixed, rec_pre, keep, chunk)
+    heads = gather_groups(heads, count, 2)
     heads, out_x, out_y = hold(heads, out_x, out_y)
     out_last = scatter_relay(out_total, out_x, out_y)
-    heads = gather_groups(heads, count, 2)
     adj_in = jnp.zeros((1, chans), f32)
     for hop in range(count - 1, 0, -1):
         adj_in = jnp.where(hop > z, heads[hop, 0:1] * adj_in + heads[hop, 1:2], adj_in)
     enter = jnp.concatenate([state_in, adj_in, jnp.zeros((6, chans), f32)])
     d_rec_pre, sums, edge, grad_a, grad_x = backward_scan(
-        order, d_mixed, gate_pre, state_local, prod, adj_local, adj_prod, branch_in, halo, conved,
+        order, d_mixed, rec_pre, state_local, prod, adj_local, adj_prod, branch_in, halo, conved,
         masks, small, enter, wa, wx, chunk,
     )
     edges = gather_groups(edge, count, 2)
@@ -1101,11 +1357,11 @@
         rec_part, d_rec_pre, grad_a, grad_x, sums, mixed, *out_last
     )
     layer_out = (middle + scatter_sum(out_total, out_x, out_y, *out_last)).astype(bf16)
-    rec_part, mlp_sum, down_sum = hold(rec_part, mlp_sum, down_sum)
+    rec_part, mlp_sum = hold(rec_part, mlp_sum)
     rec_sum = lax.psum_scatter(rec_part, "z", scatter_dimension=0, tiled=True)
-    one_theirs = back_rows(d_rec_pre[half_rows:], w_rec).astype(bf16)
+    one_theirs = back_rows(d_rec_pre[half_rows:], w_rec)
+    d_rec_pre, one_theirs = hold(d_rec_pre, one_theirs)
     one_got = across(one_theirs, "c")
-    d_rec_pre, one_theirs = hold(d_rec_pre, one_theirs)
     one_mine = back_rows(d_rec_pre[:half_rows], w_rec)
     one_total, one_x, one_y = scatter_near(one_mine, one_got)
     one_total, mixed, grad_a, grad_x = hold(one_total, mixed, grad_a, grad_x)
@@ -1118,45 +1374,54 @@
         kept = jnp.where(same_block, w, 0.0).astype(bf16)
         return jnp.dot(kept, fold, preferred_element_type=f32).astype(bf16)
 
-    grad_out = lax.dot_general(mixed, d_rec, contract_first, preferred_element_type=f32)
     back_pack = jnp.concatenate(
-        [grad_out.astype(bf16), diagonal(grad_a), diagonal(grad_x), sums.T.astype(bf16)], axis=1
+        [
+            lax.dot_general(
+                mixed, d_rec, contract_first, preferred_element_type=f32
+            ).astype(bf16),
+            diagonal(grad_a),
+            diagonal(grad_x),
+            sums.T.astype(bf16),
+        ],
+        axis=1,
     )
     back_pack = pad_lanes(back_pack, pack_width)
     back_pack = back_pack.reshape(2, spread, chan_rows, pack_width).transpose(1, 0, 2, 3)
-    back_swap = exchange(back_pack, swap_axes, 5).reshape(count * chan_rows, pack_width)
-    one_x, one_y, back_swap, rec_sum = hold(one_x, one_y, back_swap, rec_sum)
-    pack_sum = lax.psum_scatter(back_swap, "z", scatter_dimension=0, tiled=True).astype(f32)
+    (back_swap,) = exchange([back_pack], swap_axes, 5)
+    back_swap = back_swap.reshape(count * chan_rows, pack_width)
+    one_x, one_y, back_swap, mlp_sum, rec_sum = hold(one_x, one_y, back_swap, mlp_sum, rec_sum)
+    pack_sum = lax.psum_scatter(back_swap, "z", scatter_dimension=0, tiled=True)
     one_last = scatter_relay(one_total, one_x, one_y)
+    mlp_back, rec_back = exchange(
+        [mlp_sum.reshape(NF, rows_w, 2 * ff), rec_sum.reshape(NF, rows_w, 2 * chans)], FEAT, 6
+    )
+    mlp_back, rec_back, *one_last = hold(mlp_back, rec_back, *one_last)
     e_one = gain_one * scatter_sum(one_total, one_x, one_y, *one_last)
     grad_tokens = d_middle + norm_back(tok, inverse_rms(tok), e_one)
-
-    mlp_sum, *one_last = hold(mlp_sum, *one_last)
-    mlp_back = exchange(mlp_sum.reshape(NF, rows_w, 2 * ff), FEAT, 4)
     grad_gate, grad_up, grad_gain_two = join_blocks(
         mlp_back, mlp_gate_weight, mlp_up_weight, norm2_gain.astype(f32)[:, None], ff_moves
     )
-    rec_back = exchange(rec_sum.reshape(NF, rows_w, 2 * chans), FEAT, 6)
     grad_rec_gate, grad_rec_in, grad_gain_one = join_blocks(
         rec_back, rec_gate_weight, rec_in_weight, norm1_gain.astype(f32)[:, None], chan_moves
     )
 
-    base = width + 2 * BLK
+    grad_out, grad_a, grad_x, grad_taps, *grad_rows = unpack_sums(pack_sum, width)
+    grad_offset, grad_a_bias, grad_x_bias, grad_rate = (r.reshape(chan_rows) for r in grad_rows)
     return (
         layer_out,
         grad_tokens,
-        grad_gain_one[:, 0],
+        grad_gain_one.reshape(rows_w),
         grad_rec_gate,
         grad_rec_in,
-        pack_sum[:, base : base + CONV],
-        pack_sum[:, base + CONV],
-        pack_sum[:, width : width + BLK],
-        pack_sum[:, base + CONV + 1],
-        pack_sum[:, width + BLK : base],
-        pack_sum[:, base + CONV + 2],
-        pack_sum[:, base + CONV + 3],
-        pack_sum[:, :width],
-        grad_gain_two[:, 0],
+        grad_taps,
+        grad_offset,
+        grad_a,
+        grad_a_bias,
+        grad_x,
+        grad_x_bias,
+        grad_rate,
+        grad_out,
+        grad_gain_two.reshape(rows_w),
         grad_gate,
         grad_up,
         down_sum.astype(f32),

time: 784 us -> 698 us (0.89)
  waiting for transfers between devices: 119 us -> 35.8 us
  Pallas kernels: 344 us -> 382 us
  local copies, waits for them, and re-layouts: 77.2 us -> 51.2 us
  other arithmetic: 72.1 us -> 64.2 us
    pallas_call x7 -> x9, Pallas kernels: 98.4 us -> 171 us  [the longest x1 59.2 us: gather_exchange(): pl.pallas_call(gather_kernel, out_shape=(jax.ShapeDtypeStruct((NF, rows,...]
    all_gather x1, waiting for transfers between devices: 54.4 us -> 0.02 us  [on_device(): lax.all_gather(rec_got[:, :rows_w].reshape(NF * rows_w, 2 * chans), 'z',...]
    pallas_call x2 -> x1, Pallas kernels: 81.4 us -> 40.1 us  [gather_feature(): pl.pallas_call(gather_kernel, out_shape=jax.ShapeDtypeStruct((NF, rows, w...]
    ppermute x25 -> x20, waiting for transfers between devices: 58.3 us -> 21.9 us  [across(): return lax.ppermute(value, axis, [(0, 1), (1, 0)])]
    unnamed x109 -> x94, local copies, waits for them, and re-layouts: 26 us -> 12.7 us
    ppermute x25 -> x20, starting transfers between devices: 22.8 us -> 18.3 us  [across(): return lax.ppermute(value, axis, [(0, 1), (1, 0)])]
    dot_general x5 -> x6, matrix products: 44.4 us -> 43.3 us  [the longest x4 30.7 us: back_rows(): lax.dot_general(d, w, contract_last, preferred_element_type=f32)]
  transfers between devices with their start and end apart: 33 -> 28, of which waited for: 19 -> 5; matrix products, arithmetic and copies ran while one was open for 29% -> 28% of each run, Pallas kernels for 38% -> 50%
where the time goes in v3:
time: 698 us; the launch traced here: 692 us
  Pallas kernels  382 us (55%)
  matrix products  124 us (18%)
  other arithmetic  64.2 us (9%)
  local copies, waits for them, and re-layouts  51.2 us (7%)
  waiting for transfers between devices  35.8 us (5%)
  starting transfers between devices  19.1 us (3%)
  between operations  17.2 us (2%)
    pallas_call x1, Pallas kernels, gather_exchange(): pl.pallas_call(gather_kernel, out_shape=(jax.ShapeDtypeStruct((NF, rows,...  59.2 us
    pallas_call x4, Pallas kernels, exchange(): pl.pallas_call(functools.partial(exchange_kernel, axes), out_shape=tuple(...  57 us
    pallas_call x1, Pallas kernels, scatter_feature(): pl.pallas_call(scatter_kernel, out_shape=jax.ShapeDtypeStruct((rows, widt...  46.4 us
    pallas_call x5, Pallas kernels, gather_groups(): pl.pallas_call(functools.partial(groups_kernel, count), out_shape=jax.Sha...  46.3 us
    pallas_call x1, Pallas kernels, gather_feature(): pl.pallas_call(gather_kernel, out_shape=jax.ShapeDtypeStruct((NF, rows, w...  40.1 us
    pallas_call x1, Pallas kernels, gated_unit(): pl.pallas_call(gated_kernel, grid=(steps,), out_shape=(jax.ShapeDtypeStru...  31.2 us
    dot_general x4, matrix products, back_rows(): lax.dot_general(d, w, contract_last, preferred_element_type=f32)  30.7 us
    pallas_call x1, Pallas kernels, backward_scan(): pl.pallas_call(backward_kernel, out_shape=(jax.ShapeDtypeStruct((rows, 2...  22.3 us
  transfers between devices with their start and end apart: 28, of which 5 were waited for; matrix products, arithmetic and copies ran while one was open for 28% of the time, Pallas kernels for 50%

profile of v3, /device:TPU:0, one launch (start us, length us, event | category | flops | bytes accessed | tf_op | source)
XLA Modules:
  0.0 692.4 jit_solution(4498214473571175634)
XLA Ops:
  13.9 2.2 split_blocks.2
  16.2 2.1 pad_maximum_fusion.3.refs_0_
  18.2 15.6 %exchange.4 = bf16[8,80,640]{2,1,0:T(8,128)(2,1)} custom-call(bf16[8,80,640]{2,1,0:T(8,128)(2,1)} %pad_maximum_fusion.3.refs_0_), custom_call_target="tpu_custom_call" | custom-call | bytes 45000000 | tf_op jit(solution)/shard_map/exchange/pallas_call | solution.py:509
  33.9 2.0 slice.200
  38.3 8.4 %gather_groups.5 = f32[4,8,512]{2,1,0:T(8,128)} custom-call(f32[8,512]{1,0:T(8,128)} %fusion.63.x_ref), custom_call_target="tpu_custom_call" | custom-call | bytes 15000000 | tf_op jit(solution)/shard_map/gather_groups/pallas_call | solution.py:572
  46.7 2.9 split_blocks.3.refs_1_
  49.6 59.2 %gather_exchange.1 = (bf16[8,256,2048]{2,1,0:T(8,128)(2,1)}, bf16[8,64,1536]{2,1,0:T(8,128)(2,1)}) custom-call(bf16[256,2048]{1,0:T(8,128)(2,1)} %refs_0_, bf16[8,64,1536]{2,1,0:T(8,128)(2,1)} %split_blocks.3.refs_1_), custom_call_target="tpu_custom_call" | custom-call | bytes 165000000 | tf_op jit(solution)/shard_map/gather_exchange/pallas_call | solution.py:529
  114.3 5.3 fusion
  119.7 11.8 %fusion.15.pre_ref = f32[2048,640]{1,0:T(8,128)} fusion(bf16[2048,640]{1,0:T(8,128)(2,1)} %all-gather.7.cloned.1.call-done, bf16[2048,2048]{1,0:T(8,128)(2,1)} %bitcast.201, f32[2048]{0:T(1024)S(1)} %bitcast.228, f32[2048]{0:T(1024)S(1)} %add_rsqrt_fusion), kind=kOutput, calls=%fused_computation.35 | convolution fusion | flops 5385486336 | bytes 16269312 | tf_op jit(solution)/shard_map/dot_general | solution.py:1269
  136.9 3.8 exchange.5
  145.9 8.4 %gather_groups.6 = f32[4,8,320]{2,1,0:T(8,128)} custom-call(f32[8,320]{1,0:T(8,128)} %convert_multiply_fusion.5.x_ref), custom_call_target="tpu_custom_call" | custom-call | bytes 15000000 | tf_op jit(solution)/shard_map/gather_groups/pallas_call | solution.py:572
  155.6 18.3 %forward_scan.1 = (bf16[2048,320]{1,0:T(8,128)(2,1)}, bf16[2048,320]{1,0:T(8,128)(2,1)}, f32[2048,320]{1,0:T(8,128)}, f32[2048,320]{1,0:T(8,128)}, f32[2048,320]{1,0:T(8,128)}, /*index=5*/f32[8,320]{1,0:T(8,128)}) custom-call(s32[8]{0:T(128)} %copy-done.21, f32[2048,640]{1,0:T(8,128)} %fusion.15.pre_ref, f32[8,320]{1,0:T(8,128)} %select_bitcast_fusion.halo_ref, ...), custom_call_target="tpu_custom_call" | custom-call | bytes 45000000 | tf_op jit(solution)/shard_map/forward_scan/pallas_call | solution.py:700
  174.0 8.2 %gather_groups.7 = f32[4,8,320]{2,1,0:T(8,128)} custom-call(f32[8,320]{1,0:T(8,128)} %get-tuple-element.128.x_ref), custom_call_target="tpu_custom_call" | custom-call | bytes 15000000 | tf_op jit(solution)/shard_map/gather_groups/pallas_call | solution.py:572
  182.2 2.1 slice.219
  184.6 1.9 slice.220
  189.7 2.4 constant_dynamic-update-slice_fusion.3
  192.1 2.3 constant_dynamic-update-slice_fusion.2
  194.5 3.4 fusion.11
  197.9 6.7 convolution_convert_fusion
  208.4 46.4 %scatter_feature.1 = f32[256,2048]{1,0:T(8,128)} custom-call(bf16[8,256,2048]{2,1,0:T(8,128)(2,1)} %bitcast.199), custom_call_target="tpu_custom_call" | custom-call | bytes 135000000 | tf_op jit(solution)/shard_map/scatter_feature/pallas_call | solution.py:235
  254.8 2.1 multiply_reduce_fusion.1
  258.3 40.1 %gather_feature.1 = bf16[8,256,2048]{2,1,0:T(8,128)(2,1)} custom-call(bf16[256,2048]{1,0:T(8,128)(2,1)} %multiply_convert_fusion.refs_0_), custom_call_target="tpu_custom_call" | custom-call | bytes 120000000 | tf_op jit(solution)/shard_map/gather_feature/pallas_call | solution.py:123
  298.5 31.2 %gated_unit.1 = (bf16[2048,768]{1,0:T(8,128)(2,1)}, bf16[2048,1536]{1,0:T(8,128)(2,1)}) custom-call(bf16[2048,2048]{1,0:T(8,128)(2,1)} %bitcast.203, bf16[1024,2048]{1,0:T(8,128)(2,1)} %constant_dynamic-update-slice_fusion.mine_ref, bf16[1024,2048]{1,0:T(8,128)(2,1)} %collective-permute-done.4.theirs_ref, ...), custom_call_target="tpu_custom_call" | custom-call | flops 19327352832 | bytes 41943040 | tf_op jit(solution)/shard_map/gated_unit/pallas_call | solution.py:1017
  329.7 10.6 %convolution_convert_fusion.3 = bf16[1024,2048]{1,0:T(8,128)(2,1)S(1)} fusion(bf16[2048,1536]{1,0:T(8,128)(2,1)} %all-gather.9.cloned.1.call-done.w_ref, bf16[2048,1536]{1,0:T(8,128)(2,1)} %get-tuple-element.149), kind=kOutput, calls=%fused_computation.13 | convolution fusion | flops 6444548096 | bytes 13631488 | tf_op jit(solution)/shard_map/dot_general | solution.py:1297
  340.8 6.9 convolution_convert_fusion.2
  347.7 4.0 add_convert_fusion.2
  351.7 5.3 fusion.25
  357.1 7.3 %add_convert_fusion.3 = bf16[768,2048]{1,0:T(8,128)(2,1)} fusion(f32[768,2048]{1,0:T(8,128)S(1)} %fusion.25, bf16[1024,2048]{1,0:T(8,128)(2,1)} %constant_dynamic-update-slice_fusion.mine_ref, bf16[2048,768]{1,0:T(8,128)(2,1)S(1)} %copy-done.39), kind=kOutput, calls=%fused_computation.10 | convolution fusion | flops 3224371200 | bytes 15204352 | tf_op jit(solution)/shard_map/dot_general | solution.py:1301
  364.4 7.9 %convolution_convert_fusion.6 = bf16[1024,2048]{1,0:T(8,128)(2,1)} fusion(bf16[768,2048]{1,0:T(8,128)(2,1)} %all-gather.11.cloned.1.call-done.down_ref, bf16[2048,768]{1,0:T(8,128)(2,1)} %get-tuple-element.143), kind=kOutput, calls=%fused_computation.16 | convolution fusion | flops 3223322624 | bytes 8912896 | tf_op jit(solution)/shard_map/dot_general | solution.py:1314
  374.0 2.0 slice_bitcast_fusion.6
  378.2 5.1 convolution_convert_fusion.7
  383.4 18.0 %collective-permute-done.7.bx_ref = bf16[2,128,2048]{2,1,0:T(8,128)(2,1)S(1)} collective-permute-done((bf16[2,128,2048]{2,1,0:T(8,128)(2,1)S(1)}, bf16[2,128,2048]{2,1,0:T(8,128)(2,1)S(1)}, u32[]{:S(2)}, u32[]{:S(2)}) %collective-permute-start.7) | collective-permute-done | bytes 1048608 | tf_op jit(solution)/shard_map/ppermute | solution.py:262
  403.8 16.4 %scatter_tail.1 = f32[256,2048]{1,0:T(8,128)} custom-call(bf16[4,2,128,2048]{3,2,1,0:T(8,128)(2,1)} %bitcast.190, bf16[2,128,2048]{2,1,0:T(8,128)(2,1)} %copy-done.11, bf16[2,128,2048]{2,1,0:T(8,128)(2,1)} %copy-done.12), custom_call_target="tpu_custom_call" | custom-call | bytes 48000000 | tf_op jit(solution)/shard_map/scatter_tail/pallas_call | solution.py:437
  420.2 2.8 fusion.17
  423.1 3.7 fusion.78
  428.9 16.8 %convolution_convert_fusion.1 = bf16[2048,1536]{1,0:T(8,128)(2,1)} fusion(bf16[2048,2048]{1,0:T(8,128)(2,1)S(1)} %bitcast.206, bf16[2048,1536]{1,0:T(8,128)(2,1)} %get-tuple-element.149), kind=kOutput, calls=%fused_computation.9 | convolution fusion | flops 12888047616 | bytes 20971520 | tf_op jit(solution)/shard_map/dot_general | solution.py:1323
  445.6 7.8 %add_convert_fusion.1 = bf16[1024,2048]{1,0:T(8,128)(2,1)} fusion(bf16[1024,2048]{1,0:T(8,128)(2,1)} %collective-permute-done.6, bf16[1024,2048]{1,0:T(8,128)(2,1)} %convolution_convert_fusion.7), kind=kLoop, calls=%fused_computation.6 | loop fusion | flops 8388608 | bytes 12582912 | tf_op jit(solution)/shard_map/convert_element_type | solution.py:286
  453.5 18.0 %gather_tail.1 = bf16[8,256,2048]{2,1,0:T(8,128)(2,1)} custom-call(bf16[256,2048]{1,0:T(8,128)(2,1)} %get-tuple-element.148.x_ref, bf16[256,2048]{1,0:T(8,128)(2,1)} %collective-permute-done.9.bx_ref, bf16[256,2048]{1,0:T(8,128)(2,1)} %collective-permute-done.10.by_ref), custom_call_target="tpu_custom_call" | custom-call | bytes 48000000 | tf_op jit(solution)/shard_map/gather_tail/pallas_call | solution.py:350
  471.5 2.3 slice_bitcast_fusion.1
  478.4 10.1 %fusion.30.d_mixed_ref = f32[2048,320]{1,0:T(8,128)} fusion(bf16[2048,2048]{1,0:T(8,128)(2,1)} %bitcast.207, bf16[320,2432]{1,0:T(8,128)(2,1)} %bitcast.216), kind=kOutput, calls=%fused_computation.56 | convolution fusion | flops 2684354560 | bytes 12320768 | tf_op jit(solution)/shard_map/dot_general | solution.py:1333
  488.5 12.9 %adjoint_scan.1 = (f32[2048,320]{1,0:T(8,128)}, f32[2048,320]{1,0:T(8,128)}, f32[8,320]{1,0:T(8,128)}) custom-call(s32[8]{0:T(128)} %copy-done.21, f32[2048,320]{1,0:T(8,128)} %fusion.30.d_mixed_ref, f32[2048,640]{1,0:T(8,128)} %fusion.15.pre_ref, f32[2048,320]{1,0:T(8,128)} %get-tuple-element.160.keep_ref), custom_call_target="tpu_custom_call" | custom-call | bytes 36000000 | tf_op jit(solution)/shard_map/adjoint_scan/pallas_call | solution.py:774
  501.3 10.4 %gather_groups.8 = f32[4,8,320]{2,1,0:T(8,128)} custom-call(f32[8,320]{1,0:T(8,128)} %get-tuple-element.161.x_ref), custom_call_target="tpu_custom_call" | custom-call | bytes 15000000 | tf_op jit(solution)/shard_map/gather_groups/pallas_call | solution.py:572
  513.3 22.3 %backward_scan.1 = (bf16[2048,640]{1,0:T(8,128)(2,1)}, f32[8,320]{1,0:T(8,128)}, f32[8,320]{1,0:T(8,128)}, f32[320,320]{1,0:T(8,128)}, f32[320,320]{1,0:T(8,128)}) custom-call(s32[8]{0:T(128)} %copy-done.21, f32[2048,320]{1,0:T(8,128)} %fusion.30.d_mixed_ref, f32[2048,640]{1,0:T(8,128)} %fusion.15.pre_ref, ...), custom_call_target="tpu_custom_call" | custom-call | bytes 63000000 | tf_op jit(solution)/shard_map/backward_scan/pallas_call | solution.py:934
  535.6 10.8 %gather_groups.9 = f32[4,8,320]{2,1,0:T(8,128)} custom-call(f32[8,320]{1,0:T(8,128)} %get-tuple-element.169.x_ref), custom_call_target="tpu_custom_call" | custom-call | bytes 15000000 | tf_op jit(solution)/shard_map/gather_groups/pallas_call | solution.py:572
  546.5 3.0 fusion.38
  554.5 11.1 %convolution_convert_fusion.8 = bf16[2048,640]{1,0:T(8,128)(2,1)} fusion(bf16[2048,640]{1,0:T(8,128)(2,1)S(1)} %fusion.59, bf16[2048,2048]{1,0:T(8,128)(2,1)} %bitcast.202, f32[2048]{0:T(1024)S(1)} %bitcast.229, f32[2048]{0:T(1024)S(1)} %copy-done.23), kind=kOutput, calls=%fused_computation.22 | convolution fusion | flops 5386797056 | bytes 13647872 | tf_op jit(solution)/shard_map/dot_general | solution.py:1353
  565.6 7.6 %convolution_convert_fusion.5 = bf16[1024,2048]{1,0:T(8,128)(2,1)} fusion(bf16[2048,640]{1,0:T(8,128)(2,1)} %all-gather.7.cloned.1.call-done, bf16[2048,640]{1,0:T(8,128)(2,1)} %copy-done.34), kind=kOutput, calls=%fused_computation.15 | convolution fusion | flops 2686451712 | bytes 8126464 | tf_op jit(solution)/shard_map/dot_general | solution.py:1297
  574.6 5.6 convolution_convert_fusion.4
  580.7 4.1 add_convert_fusion
  589.9 2.3 convolution_convert_fusion.10
  593.2 7.9 %convolution_convert_fusion.9 = bf16[320,2048]{1,0:T(8,128)(2,1)} fusion(bf16[2048,320]{1,0:T(8,128)(2,1)} %copy-done.10, bf16[2048,2048]{1,0:T(8,128)(2,1)} %bitcast.208), kind=kOutput, calls=%fused_computation.34 | convolution fusion | flops 2685009920 | bytes 11010048 | tf_op jit(solution)/shard_map/dot_general | solution.py:1379
  601.1 3.8 concatenate.46
  607.8 3.8 exchange.6
  611.6 1.9 collective-permute-done.17
  613.5 13.0 %reduce-scatter.9.cloned.1.call-done = bf16[512,640]{1,0:T(8,128)(2,1)} async-done(((bf16[2048,640]{1,0:T(8,128)(2,1)}), bf16[512,640]{1,0:T(8,128)(2,1)}) %reduce-scatter.9.cloned.1.call-update) | async-done | bytes 655376 | tf_op jit(solution)/shard_map/reduce_scatter | solution.py:1361
  627.2 2.5 convert_element_type.347
  629.7 1.9 fusion.34
  634.6 2.4 fusion.40
  637.0 33.7 %exchange.7 = (bf16[8,64,1536]{2,1,0:T(8,128)(2,1)}, bf16[8,64,640]{2,1,0:T(8,128)(2,1)}) custom-call(bf16[8,64,1536]{2,1,0:T(8,128)(2,1)} %bitcast.219, bf16[8,64,640]{2,1,0:T(8,128)(2,1)} %bitcast.221), custom_call_target="tpu_custom_call" | custom-call | bytes 45000000 | tf_op jit(solution)/shard_map/exchange/pallas_call | solution.py:509
  670.7 2.5 join_blocks.2
  673.2 3.8 join_blocks.3
  677.0 2.2 fusion.36
  679.6 2.4 fusion.20
  682.0 1.9 unpack_sums.1
  (226 shorter events, 69.4 us)
Async XLA Ops:
  7.2 8.9 %copy-start.31 = (bf16[64]{0:T(256)(128)(2,1)S(1)}, bf16[64]{0:T(256)(128)(2,1)}, u32[]{:S(2)}) copy-start(bf16[64]{0:T(256)(128)(2,1)} %param.32) | copy-start | bytes 388
  7.2 8.9 %copy-start.29 = (bf16[64]{0:T(256)(128)(2,1)S(1)}, bf16[64]{0:T(256)(128)(2,1)}, u32[]{:S(2)}) copy-start(bf16[64]{0:T(256)(128)(2,1)} %param.21) | copy-start | bytes 388
  7.2 107.1 %all-gather.5.cloned.1.call-start = ((), (), s32[]{:S(2)}) async-start(), calls=%async_computation.4 | async-start | bytes 1945600 | tf_op jit(solution)/shard_map/all_gather | solution.py:1215
  13.1 106.7 %all-gather.7.cloned.1.call-start = ((), (), s32[]{:S(2)}) async-start(), calls=%async_computation.5 | async-start | bytes 3276800 | tf_op jit(solution)/shard_map/all_gather | solution.py:1226
  35.9 262.5 %all-gather.11.cloned.1.call-start = ((), (), s32[]{:S(2)}) async-start(), calls=%async_computation.7 | async-start | bytes 3932160 | tf_op jit(solution)/shard_map/all_gather | solution.py:1244
  36.6 261.8 %all-gather.9.cloned.1.call-start = ((), (), s32[]{:S(2)}) async-start(), calls=%async_computation.6 | async-start | bytes 7864320 | tf_op jit(solution)/shard_map/all_gather | solution.py:1243
  46.7 65.2 %copy-start.7 = (bf16[256,2048]{1,0:T(8,128)(2,1)S(1)}, bf16[256,2048]{1,0:T(8,128)(2,1)}, u32[]{:S(2)}) copy-start(bf16[256,2048]{1,0:T(8,128)(2,1)} %param.20) | copy-start | bytes 3145732
  108.9 362.6 %reduce-scatter.5.cloned.1.call-start = ((), (), s32[]{:S(2)}) async-start(), calls=%async_computation.8 | async-start | bytes 3932160 | tf_op jit(solution)/shard_map/reduce_scatter | solution.py:1313
  110.4 33.0 %copy-start.16 = (s32[320]{0:T(512)}, s32[320]{0:T(512)S(1)}, u32[]{:S(2)}) copy-start(s32[320]{0:T(512)S(1)} %get-tuple-element.329) | copy-start | bytes 3844
  110.4 33.0 %copy-start.18 = (s32[320]{0:T(512)}, s32[320]{0:T(512)S(1)}, u32[]{:S(2)}) copy-start(s32[320]{0:T(512)S(1)} %get-tuple-element.330) | copy-start | bytes 3844
  110.9 32.5 %copy-start.27 = (pred[320]{0:T(512)(128)(4,1)}, pred[320]{0:T(512)(128)(4,1)S(1)}, u32[]{:S(2)}) copy-start(pred[320]{0:T(512)(128)(4,1)S(1)} %get-tuple-element.333) | copy-start | bytes 964
  111.8 7.9 %copy-start.13 = (f32[4,1,512]{2,1,0:T(1,128)}, f32[4,1,512]{2,1,0:T(1,128)S(1)}, u32[]{:S(2)}) copy-start(f32[4,1,512]{2,1,0:T(1,128)S(1)} %get-tuple-element.320) | copy-start | bytes 24580
  114.3 20.0 %copy-start.21 = (s32[8]{0:T(128)}, s32[8]{0:T(128)S(1)}, u32[]{:S(2)}) copy-start(s32[8]{0:T(128)S(1)} %fusion.73.order_ref) | copy-start | bytes 100
  119.7 11.8 %copy-start.22 = (f32[2048]{0:T(1024)}, f32[2048]{0:T(1024)S(1)}, u32[]{:S(2)}) copy-start(f32[2048]{0:T(1024)S(1)} %add_rsqrt_fusion) | copy-start | bytes 24580
  131.5 42.4 %collective-permute-start = (bf16[256,2048]{1,0:T(8,128)(2,1)S(1)}, bf16[256,2048]{1,0:T(8,128)(2,1)}, u32[]{:S(2)}, u32[]{:S(2)}) collective-permute-start(bf16[256,2048]{1,0:T(8,128)(2,1)S(1)} %copy-done.7), channel_id=1, source_target_pairs={{0,4},{4,0},{1,5},{5,1},{2,6},{6,2},{3,7},{7,3},{8,12},{12,8},{9,1... | collective-permute-start | bytes 3145736 | tf_op jit(solution)/shard_map/ppermute | solution.py:262
  132.3 41.7 %collective-permute-start.1 = (bf16[256,2048]{1,0:T(8,128)(2,1)S(1)}, bf16[256,2048]{1,0:T(8,128)(2,1)}, u32[]{:S(2)}, u32[]{:S(2)}) collective-permute-start(bf16[256,2048]{1,0:T(8,128)(2,1)S(1)} %copy-done.7), channel_id=1, source_target_pairs={{0,2},{2,0},{1,3},{3,1},{4,6},{6,4},{5,7},{7,5},{8,10},{10,8},{9,1... | collective-permute-start | bytes 3145736 | tf_op jit(solution)/shard_map/ppermute | solution.py:262
  134.3 10.2 %copy-start.24 = (f32[8]{0:T(128)}, f32[8]{0:T(128)S(1)}, u32[]{:S(2)}) copy-start(f32[8]{0:T(128)S(1)} %pad_maximum_fusion.5) | copy-start | bytes 100
  142.2 31.7 %copy-start.8 = (bf16[2,2,80,2432]{3,2,1,0:T(8,128)(2,1)}, bf16[2,2,80,2432]{3,2,1,0:T(8,128)(2,1)S(1)}, u32[]{:S(2)}) copy-start(bf16[2,2,80,2432]{3,2,1,0:T(8,128)(2,1)S(1)} %copy.101) | copy-start | bytes 4669444
  182.2 12.3 %copy-start.2 = (f32[2048,320]{1,0:T(8,128)S(1)}, f32[2048,320]{1,0:T(8,128)}, u32[]{:S(2)}) copy-start(f32[2048,320]{1,0:T(8,128)} %get-tuple-element.125.prod_ref.prod_before_ref) | copy-start | bytes 7864324
  184.3 20.3 %collective-permute-start.2 = (bf16[128,2048]{1,0:T(8,128)(2,1)}, bf16[128,2048]{1,0:T(8,128)(2,1)}, u32[]{:S(2)}, u32[]{:S(2)}) collective-permute-start(bf16[128,2048]{1,0:T(8,128)(2,1)} %slice.219), channel_id=1, source_target_pairs={{0,2},{2,0},{1,3},{3,1},{4,6},{6,4},{5,7},{7,5},{8,10},{10,8},{9,1... | collective-permute-start | bytes 1572872 | tf_op jit(solution)/shard_map/ppermute | solution.py:262
  186.5 18.1 %collective-permute-start.3 = (bf16[128,2048]{1,0:T(8,128)(2,1)}, bf16[128,2048]{1,0:T(8,128)(2,1)}, u32[]{:S(2)}, u32[]{:S(2)}) collective-permute-start(bf16[128,2048]{1,0:T(8,128)(2,1)} %slice.220), channel_id=1, source_target_pairs={{0,4},{4,0},{1,5},{5,1},{2,6},{6,2},{3,7},{7,3},{8,12},{12,8},{9,1... | collective-permute-start | bytes 1572872 | tf_op jit(solution)/shard_map/ppermute | solution.py:262
  188.8 5.7 copy-start.3
  197.9 6.8 copy-start.10
  208.4 90.1 %collective-permute-start.4 = (bf16[1024,2048]{1,0:T(8,128)(2,1)}, bf16[1024,2048]{1,0:T(8,128)(2,1)}, u32[]{:S(2)}, u32[]{:S(2)}) collective-permute-start(bf16[1024,2048]{1,0:T(8,128)(2,1)} %constant_dynamic-update-slice_fusion.mine_ref), channel_id=1, source_target_pairs={{0,1},{1,0},{2,3},{3,2},{4,5},{5,4},{6,7},{7,6},{8,9},{9,8},{10,11... | collective-permute-start | bytes 12582920 | tf_op jit(solution)/shard_map/ppermute | solution.py:262
  208.4 46.4 %copy-start.1 = (bf16[256,2048]{1,0:T(8,128)(2,1)S(1)}, bf16[256,2048]{1,0:T(8,128)(2,1)}, u32[]{:S(2)}) copy-start(bf16[256,2048]{1,0:T(8,128)(2,1)} %refs_0_) | copy-start | bytes 3145732
  329.7 11.1 %copy-start.35 = (bf16[2048,1536]{1,0:T(8,128)(2,1)S(1)}, bf16[2048,1536]{1,0:T(8,128)(2,1)}, u32[]{:S(2)}) copy-start(bf16[2048,1536]{1,0:T(8,128)(2,1)} %all-gather.9.cloned.1.call-done.w_ref) | copy-start | bytes 18874372
  329.7 11.1 %copy-start.41 = (bf16[2048,1536]{1,0:T(8,128)(2,1)S(1)}, bf16[2048,1536]{1,0:T(8,128)(2,1)}, u32[]{:S(2)}) copy-start(bf16[2048,1536]{1,0:T(8,128)(2,1)} %get-tuple-element.149) | copy-start | bytes 18874372
  340.3 7.4 %collective-permute-start.5 = (bf16[1024,2048]{1,0:T(8,128)(2,1)S(1)}, bf16[1024,2048]{1,0:T(8,128)(2,1)S(1)}, u32[]{:S(2)}, u32[]{:S(2)}) collective-permute-start(bf16[1024,2048]{1,0:T(8,128)(2,1)S(1)} %convolution_convert_fusion.3), channel_id=1, source_target_pairs={{0,1},{1,0},{2,3},{3,2},{4,5},{5,4},{6,7},{7,6},{8,9},{9,8},{10,11... | collective-permute-start | bytes 12582920 | tf_op jit(solution)/shard_map/ppermute | solution.py:262
  347.7 4.0 copy-start.39
  372.2 31.5 %collective-permute-start.6 = (bf16[1024,2048]{1,0:T(8,128)(2,1)}, bf16[1024,2048]{1,0:T(8,128)(2,1)}, u32[]{:S(2)}, u32[]{:S(2)}) collective-permute-start(bf16[1024,2048]{1,0:T(8,128)(2,1)} %convolution_convert_fusion.6), channel_id=1, source_target_pairs={{0,1},{1,0},{2,3},{3,2},{4,5},{5,4},{6,7},{7,6},{8,9},{9,8},{10,11... | collective-permute-start | bytes 12582920 | tf_op jit(solution)/shard_map/ppermute | solution.py:262
  372.5 200.8 %reduce-scatter.7.cloned.1.call-start = ((), (), s32[]{:S(2)}) async-start(), calls=%async_computation.9 | async-start | bytes 7864320 | tf_op jit(solution)/shard_map/reduce_scatter | solution.py:1328
  372.5 5.7 copy-start.36
  372.5 5.7 copy-start.40
  376.0 25.4 %collective-permute-start.7 = (bf16[2,128,2048]{2,1,0:T(8,128)(2,1)S(1)}, bf16[2,128,2048]{2,1,0:T(8,128)(2,1)S(1)}, u32[]{:S(2)}, u32[]{:S(2)}) collective-permute-start(bf16[2,128,2048]{2,1,0:T(8,128)(2,1)S(1)} %slice_bitcast_fusion.2), channel_id=1, source_target_pairs={{0,4},{4,0},{1,5},{5,1},{2,6},{6,2},{3,7},{7,3},{8,12},{12,8},{9,1... | collective-permute-start | bytes 3145736 | tf_op jit(solution)/shard_map/ppermute | solution.py:262
  377.6 25.1 %collective-permute-start.8 = (bf16[2,128,2048]{2,1,0:T(8,128)(2,1)S(1)}, bf16[2,128,2048]{2,1,0:T(8,128)(2,1)S(1)}, u32[]{:S(2)}, u32[]{:S(2)}) collective-permute-start(bf16[2,128,2048]{2,1,0:T(8,128)(2,1)S(1)} %pad_maximum_fusion), channel_id=1, source_target_pairs={{0,2},{2,0},{1,3},{3,1},{4,6},{6,4},{5,7},{7,5},{8,10},{10,8},{9,1... | collective-permute-start | bytes 3145736 | tf_op jit(solution)/shard_map/ppermute | solution.py:262
  403.8 25.1 %slice-start = ((s8[8388608]{0:T(1024)(128)(4,1)}), s8[4194304]{0:T(1024)(128)(4,1)S(1)}, s32[]{:S(2)}) async-start(s8[8388608]{0:T(1024)(128)(4,1)} %bitcast.204), calls=%async_computation.12 | async-start | bytes 8388608
  420.2 8.6 %slice-start.1 = ((s8[8388608]{0:T(1024)(128)(4,1)}), s8[4194304]{0:T(1024)(128)(4,1)S(1)}, s32[]{:S(2)}) async-start(s8[8388608]{0:T(1024)(128)(4,1)} %bitcast.204), calls=%async_computation.13 | async-start | bytes 8388608
  426.8 26.6 %collective-permute-start.9 = (bf16[256,2048]{1,0:T(8,128)(2,1)}, bf16[256,2048]{1,0:T(8,128)(2,1)}, u32[]{:S(2)}, u32[]{:S(2)}) collective-permute-start(bf16[256,2048]{1,0:T(8,128)(2,1)} %get-tuple-element.148.x_ref), channel_id=1, source_target_pairs={{0,4},{4,0},{1,5},{5,1},{2,6},{6,2},{3,7},{7,3},{8,12},{12,8},{9,1... | collective-permute-start | bytes 3145736 | tf_op jit(solution)/shard_map/ppermute | solution.py:262
  427.4 26.0 %collective-permute-start.10 = (bf16[256,2048]{1,0:T(8,128)(2,1)}, bf16[256,2048]{1,0:T(8,128)(2,1)}, u32[]{:S(2)}, u32[]{:S(2)}) collective-permute-start(bf16[256,2048]{1,0:T(8,128)(2,1)} %get-tuple-element.148.x_ref), channel_id=1, source_target_pairs={{0,2},{2,0},{1,3},{3,1},{4,6},{6,4},{5,7},{7,5},{8,10},{10,8},{9,1... | collective-permute-start | bytes 3145736 | tf_op jit(solution)/shard_map/ppermute | solution.py:262
  453.4 173.1 %reduce-scatter.9.cloned.1.call-start = ((), (), s32[]{:S(2)}) async-start(), calls=%async_computation.10 | async-start | bytes 3276800 | tf_op jit(solution)/shard_map/reduce_scatter | solution.py:1361
  473.9 37.9 %collective-permute-start.11 = (bf16[2,128,2048]{2,1,0:T(8,128)(2,1)}, bf16[2,128,2048]{2,1,0:T(8,128)(2,1)}, u32[]{:S(2)}, u32[]{:S(2)}) collective-permute-start(bf16[2,128,2048]{2,1,0:T(8,128)(2,1)} %slice_bitcast_fusion.1), channel_id=1, source_target_pairs={{0,4},{4,0},{1,5},{5,1},{2,6},{6,2},{3,7},{7,3},{8,12},{12,8},{9,1... | collective-permute-start | bytes 3145736 | tf_op jit(solution)/shard_map/ppermute | solution.py:262
  477.6 34.2 %collective-permute-start.12 = (bf16[2,128,2048]{2,1,0:T(8,128)(2,1)}, bf16[2,128,2048]{2,1,0:T(8,128)(2,1)}, u32[]{:S(2)}, u32[]{:S(2)}) collective-permute-start(bf16[2,128,2048]{2,1,0:T(8,128)(2,1)} %pad_maximum_fusion.1), channel_id=1, source_target_pairs={{0,2},{2,0},{1,3},{3,1},{4,6},{6,4},{5,7},{7,5},{8,10},{10,8},{9,1... | collective-permute-start | bytes 3145736 | tf_op jit(solution)/shard_map/ppermute | solution.py:262
  535.6 16.6 %copy-start.25 = (f32[8]{0:T(128)S(1)}, f32[8]{0:T(128)}, u32[]{:S(2)}) copy-start(f32[8]{0:T(128)} %copy-done.24) | copy-start | bytes 100
  535.6 18.9 %copy-start.14 = (f32[4,1,512]{2,1,0:T(1,128)S(1)}, f32[4,1,512]{2,1,0:T(1,128)}, u32[]{:S(2)}) copy-start(f32[4,1,512]{2,1,0:T(1,128)} %copy-done.13) | copy-start | bytes 24580
  535.6 18.9 %copy-start.23 = (f32[2048]{0:T(1024)S(1)}, f32[2048]{0:T(1024)}, u32[]{:S(2)}) copy-start(f32[2048]{0:T(1024)} %copy-done.22) | copy-start | bytes 24580
  546.5 6.5 copy-start.33
  549.5 16.1 %collective-permute-start.13 = (bf16[128,2048]{1,0:T(8,128)(2,1)}, bf16[128,2048]{1,0:T(8,128)(2,1)}, u32[]{:S(2)}, u32[]{:S(2)}) collective-permute-start(bf16[128,2048]{1,0:T(8,128)(2,1)} %get-tuple-element.310), channel_id=1, source_target_pairs={{0,2},{2,0},{1,3},{3,1},{4,6},{6,4},{5,7},{7,5},{8,10},{10,8},{9,1... | collective-permute-start | bytes 1572872 | tf_op jit(solution)/shard_map/ppermute | solution.py:262
  550.8 14.9 %collective-permute-start.14 = (bf16[128,2048]{1,0:T(8,128)(2,1)}, bf16[128,2048]{1,0:T(8,128)(2,1)}, u32[]{:S(2)}, u32[]{:S(2)}) collective-permute-start(bf16[128,2048]{1,0:T(8,128)(2,1)} %get-tuple-element.309), channel_id=1, source_target_pairs={{0,4},{4,0},{1,5},{5,1},{2,6},{6,2},{3,7},{7,3},{8,12},{12,8},{9,1... | collective-permute-start | bytes 1572872 | tf_op jit(solution)/shard_map/ppermute | solution.py:262
  565.6 8.1 %copy-start.30 = (bf16[64]{0:T(256)(128)(2,1)S(1)}, bf16[64]{0:T(256)(128)(2,1)}, u32[]{:S(2)}) copy-start(bf16[64]{0:T(256)(128)(2,1)} %param.21) | copy-start | bytes 388
  565.6 8.8 %copy-start.20 = (f32[8,320]{1,0:T(8,128)S(1)}, f32[8,320]{1,0:T(8,128)}, u32[]{:S(2)}) copy-start(f32[8,320]{1,0:T(8,128)} %get-tuple-element.188) | copy-start | bytes 30724
  573.2 7.5 %collective-permute-start.15 = (bf16[1024,2048]{1,0:T(8,128)(2,1)}, bf16[1024,2048]{1,0:T(8,128)(2,1)}, u32[]{:S(2)}, u32[]{:S(2)}) collective-permute-start(bf16[1024,2048]{1,0:T(8,128)(2,1)} %convolution_convert_fusion.5), channel_id=1, source_target_pairs={{0,1},{1,0},{2,3},{3,2},{4,5},{5,4},{6,7},{7,6},{8,9},{9,8},{10,11... | collective-permute-start | bytes 12582920 | tf_op jit(solution)/shard_map/ppermute | solution.py:262
  573.3 108.8 %reduce-scatter.11.cloned.1.call-start = ((), (), s32[]{:S(2)}) async-start(), calls=%async_computation.11 | async-start | bytes 1945600 | tf_op jit(solution)/shard_map/reduce_scatter | solution.py:1393
  584.9 3.4 copy-start.5
  584.9 4.3 copy-start.17
  584.9 4.3 copy-start.19
  584.9 4.3 copy-start.28
  584.9 4.3 copy-start.37
  584.9 4.3 copy-start.38
  586.0 25.6 %collective-permute-start.16 = (bf16[2,128,2048]{2,1,0:T(8,128)(2,1)}, bf16[2,128,2048]{2,1,0:T(8,128)(2,1)}, u32[]{:S(2)}, u32[]{:S(2)}) collective-permute-start(bf16[2,128,2048]{2,1,0:T(8,128)(2,1)} %slice_bitcast_fusion), channel_id=1, source_target_pairs={{0,4},{4,0},{1,5},{5,1},{2,6},{6,2},{3,7},{7,3},{8,12},{12,8},{9,1... | collective-permute-start | bytes 3145736 | tf_op jit(solution)/shard_map/ppermute | solution.py:262
  588.2 25.3 %collective-permute-start.17 = (bf16[2,128,2048]{2,1,0:T(8,128)(2,1)}, bf16[2,128,2048]{2,1,0:T(8,128)(2,1)}, u32[]{:S(2)}, u32[]{:S(2)}) collective-permute-start(bf16[2,128,2048]{2,1,0:T(8,128)(2,1)} %pad_maximum_fusion.2), channel_id=1, source_target_pairs={{0,2},{2,0},{1,3},{3,1},{4,6},{6,4},{5,7},{7,5},{8,10},{10,8},{9,1... | collective-permute-start | bytes 3145736 | tf_op jit(solution)/shard_map/ppermute | solution.py:262
  606.5 20.0 %copy-start.32 = (bf16[64]{0:T(256)(128)(2,1)S(1)}, bf16[64]{0:T(256)(128)(2,1)}, u32[]{:S(2)}) copy-start(bf16[64]{0:T(256)(128)(2,1)} %param.32) | copy-start | bytes 388
  606.5 20.7 %copy-start.26 = (f32[256]{0:T(256)S(1)}, f32[256]{0:T(256)}, u32[]{:S(2)}) copy-start(f32[256]{0:T(256)} %get-tuple-element.287) | copy-start | bytes 3076
  631.6 39.1 %collective-permute-start.18 = (bf16[128,2048]{1,0:T(8,128)(2,1)S(1)}, bf16[128,2048]{1,0:T(8,128)(2,1)S(1)}, u32[]{:S(2)}, u32[]{:S(2)}) collective-permute-start(bf16[128,2048]{1,0:T(8,128)(2,1)S(1)} %get-tuple-element.304), channel_id=1, source_target_pairs={{0,2},{2,0},{1,3},{3,1},{4,6},{6,4},{5,7},{7,5},{8,10},{10,8},{9,1... | collective-permute-start | bytes 1572872 | tf_op jit(solution)/shard_map/ppermute | solution.py:262
  633.1 37.5 %collective-permute-start.19 = (bf16[128,2048]{1,0:T(8,128)(2,1)S(1)}, bf16[128,2048]{1,0:T(8,128)(2,1)S(1)}, u32[]{:S(2)}, u32[]{:S(2)}) collective-permute-start(bf16[128,2048]{1,0:T(8,128)(2,1)S(1)} %get-tuple-element.303), channel_id=1, source_target_pairs={{0,4},{4,0},{1,5},{5,1},{2,6},{6,2},{3,7},{7,3},{8,12},{12,8},{9,1... | collective-permute-start | bytes 1572872 | tf_op jit(solution)/shard_map/ppermute | solution.py:262
  (8 other events, 17.1 us)
Sparse Core Ops, SparseCore 0:
  13.2 40.9 all-gather.4
  56.3 53.5 all-gather.6
  111.5 63.2 all-gather.10
  176.2 113.9 all-gather.8
  372.6 60.4 reduce-scatter.4
  453.5 112.1 reduce-scatter.6
  573.4 53.0 reduce-scatter.8
  628.8 34.8 reduce-scatter.10

commit v4 on v3

--- a/solution.py
+++ b/solution.py
@@ -139,8 +139,9 @@
     return out.reshape(NF * rows, width)
 
 
-def scatter_kernel(
-    p_ref, o_ref, own, other, total, rx, ry, relay, rx_last, ry_last, lsem, ssem, rsem
+def scatter_flow(
+    p_theirs, o_ref, own, other, total, rx, ry, relay, rx_last, ry_last, ssem, rsem,
+    peers, begin, stage, ready
 ):
     x, y, c = feature_place()
     to_x, to_y, to_c = {"x": 1 - x}, {"y": 1 - y}, {"c": 1 - c}
@@ -148,21 +149,16 @@
     half = rows // 2
     top, low = pl.ds(0, half), pl.ds(half, half)
     step = 16
+
     def copy(i, src, dst, device):
         return remote(src, dst, ssem.at[i], rsem.at[i], device)
 
-    loads = [
-        pltpu.make_async_copy(p_ref.at[r], own.at[r], lsem.at[r]) for r in range(4)
-    ]
-    for r in (DIAGONAL, ACROSS_X, ACROSS_Y, OWN):
-        loads[r].start()
-    greet((to_x, to_y, to_c))
-    cross = [copy(r, p_ref.at[4 + r], other.at[r], to_c) for r in range(4)]
-    for r in (DIAGONAL, ACROSS_X, ACROSS_Y, OWN):
-        cross[r].start()
+    greet(peers or (to_x, to_y, to_c))
+    begin()
+    cross = [copy(r, p_theirs(r), other.at[r], to_c) for r in range(4)]
 
     def add_into(r):
-        loads[r].wait()
+        ready(r)
         cross[r].wait_recv()
 
         def body(i, none):
@@ -179,14 +175,18 @@
     y_last = copy(8, relay.at[0], ry_last, to_y)
     x_last = copy(9, relay.at[1], rx_last, to_x)
 
+    stage(DIAGONAL, cross)
+    stage(ACROSS_X, cross)
     add_into(DIAGONAL)
     x_diag.start()
     y_diag.start()
+    stage(ACROSS_Y, cross)
     add_into(ACROSS_X)
     x_near.start()
+    stage(OWN, cross)
     add_into(ACROSS_Y)
     y_near.start()
-    loads[OWN].wait()
+    ready(OWN)
     cross[OWN].wait_recv()
 
     def relay_add(slot, r, start, got):
@@ -226,6 +226,91 @@
     finish(half, ry, rx_last)
     for one in cross + [x_diag, y_diag, x_near, y_near, x_last, y_last]:
         one.wait_send()
+
+
+def scatter_kernel(
+    p_ref, o_ref, own, other, total, rx, ry, relay, rx_last, ry_last, lsem, ssem, rsem
+):
+    loads = [pltpu.make_async_copy(p_ref.at[r], own.at[r], lsem.at[r]) for r in range(4)]
+    for r in (DIAGONAL, ACROSS_X, ACROSS_Y, OWN):
+        loads[r].start()
+    scatter_flow(
+        lambda r: p_ref.at[4 + r], o_ref, own, other, total, rx, ry, relay, rx_last, ry_last,
+        ssem, rsem, None, lambda: None, lambda r, cross: cross[r].start(),
+        lambda r: loads[r].wait(),
+    )
+
+
+def scatter_dot_kernel(
+    a_ref, w_ref, b_ref, o_ref, e_ref, theirs, own, other, total, rx, ry, relay, rx_last, ry_last,
+    ssem, rsem, local_sem, xssem, xrsem
+):
+    peers, kept, copies = exchange_parts(FEAT, b_ref, e_ref, local_sem, xssem, xrsem)
+    rows, width = o_ref.shape
+    tile = 512
+
+    def begin():
+        kept.start()
+        for one in copies:
+            one.start()
+
+    def dot_into(block, ref, r):
+        rows_in = a_ref[pl.ds(block * rows, rows)]
+
+        def body(j, none):
+            at = pl.ds(pl.multiple_of(j * tile, tile), tile)
+            ref[r, :, at] = lax.dot_general(
+                rows_in, w_ref[at], contract_last, preferred_element_type=f32
+            ).astype(ref.dtype)
+            return none
+
+        lax.fori_loop(0, width // tile, body, 0)
+
+    def stage(r, cross):
+        dot_into(4 + r, theirs, r)
+        cross[r].start()
+        dot_into(r, own, r)
+
+    scatter_flow(
+        lambda r: theirs.at[r], o_ref, own, other, total, rx, ry, relay, rx_last, ry_last,
+        ssem, rsem, peers, begin, stage, lambda r: None,
+    )
+    for one in copies:
+        one.wait()
+    kept.wait()
+
+
+def scatter_dot(rows_in, w, blocks):
+    rows, width = rows_in.shape[0] // NF, w.shape[0]
+    half = rows // 2
+    kind = rows_in.dtype
+    four = pltpu.VMEM((4, rows, width), kind)
+    two = pltpu.VMEM((2, half, width), kind)
+    one = pltpu.VMEM((half, width), kind)
+    return pl.pallas_call(
+        scatter_dot_kernel,
+        out_shape=(
+            jax.ShapeDtypeStruct((rows, width), f32),
+            jax.ShapeDtypeStruct(blocks.shape, blocks.dtype),
+        ),
+        in_specs=[vmem_spec()] * 3,
+        out_specs=(vmem_spec(), hbm_spec()),
+        scratch_shapes=[four] * 4
+        + [two] * 3
+        + [one] * 2
+        + [
+            pltpu.SemaphoreType.DMA((10,)),
+            pltpu.SemaphoreType.DMA((10,)),
+            pltpu.SemaphoreType.DMA,
+            pltpu.SemaphoreType.DMA((NF - 1,)),
+            pltpu.SemaphoreType.DMA((NF - 1,)),
+        ],
+        compiler_params=pltpu.CompilerParams(
+            collective_id=11, has_side_effects=True, vmem_limit_bytes=VMEM_LIMIT
+        ),
+        cost_estimate=cost(55),
+        name="scatter_dot",
+    )(rows_in, w, blocks)
 
 
 def scatter_feature(partial):
@@ -279,35 +364,45 @@
     return jnp.concatenate([block, by_y, by_x, d_top, d_low])
 
 
-def scatter_total(mine, theirs_got):
-    rows = mine.shape[0] // 4
-    kind = theirs_got.dtype
-    mine, theirs_got = hold(mine, theirs_got)
-    total = (mine.astype(f32) + theirs_got.astype(f32)).astype(kind)
-    return total.reshape(4, 2, rows // 2, mine.shape[1])
-
-
-def scatter_sides(total):
-    by_x = across(total[2:, 0], "x")
-    by_y = across(jnp.stack([total[ACROSS_Y, 1], total[DIAGONAL, 1]]), "y")
+def scatter_halves(mine, got):
+    shape = (4, 2, mine.shape[0] // 8, mine.shape[1])
+    return mine.reshape(shape), got.reshape(shape)
+
+
+def add_low(a, b):
+    return (a.astype(f32) + b.astype(f32)).astype(a.dtype)
+
+
+def scatter_sends(mine, got):
+    mine, got = scatter_halves(mine, got)
+    by_x = add_low(mine[ACROSS_X:, 0], got[ACROSS_X:, 0])
+    by_y = add_low(mine[ACROSS_Y::2, 1], got[ACROSS_Y::2, 1])
     return by_x, by_y
 
 
-def scatter_near(mine, theirs_got):
-    total = scatter_total(mine, theirs_got)
-    return (total,) + scatter_sides(total)
-
-
-def scatter_relay(total, by_x, by_y):
-    kind = total.dtype
-    y_last = across((total[ACROSS_Y, 0].astype(f32) + by_x[1].astype(f32)).astype(kind), "y")
-    x_last = across((total[ACROSS_X, 1].astype(f32) + by_y[1].astype(f32)).astype(kind), "x")
-    return y_last, x_last
-
-
-def scatter_sum(total, by_x, by_y, y_last, x_last):
-    upper = total[OWN, 0].astype(f32) + by_x[0].astype(f32) + y_last.astype(f32)
-    lower = total[OWN, 1].astype(f32) + by_y[0].astype(f32) + x_last.astype(f32)
+def scatter_keeps(mine, got):
+    mine, got = scatter_halves(mine, got)
+    near_y = add_low(mine[ACROSS_Y, 0], got[ACROSS_Y, 0])
+    near_x = add_low(mine[ACROSS_X, 1], got[ACROSS_X, 1])
+    return near_y, near_x, add_low(mine[OWN], got[OWN])
+
+
+def scatter_near(mine, got):
+    mine, got = hold(mine, got)
+    by_x, by_y = scatter_sends(mine, got)
+    by_x, by_y, mine, got = hold(by_x, by_y, mine, got)
+    return scatter_keeps(mine, got), across(by_x, "x"), across(by_y, "y")
+
+
+def scatter_relay(keeps, by_x, by_y):
+    near_y, near_x, _ = keeps
+    return across(add_low(near_y, by_x[1]), "y"), across(add_low(near_x, by_y[1]), "x")
+
+
+def scatter_sum(keeps, by_x, by_y, y_last, x_last):
+    own = keeps[2].astype(f32)
+    upper = own[0] + by_x[0].astype(f32) + y_last.astype(f32)
+    lower = own[1] + by_y[0].astype(f32) + x_last.astype(f32)
     return jnp.concatenate([upper, lower])
 
 
@@ -367,7 +462,7 @@
 
 
 def scatter_tail_kernel(
-    t_ref, bx_ref, by_ref, o_ref, near, own, bx, by, relay, last, lsem, ssem, rsem
+    ny_ref, nx_ref, own_ref, bx_ref, by_ref, o_ref, near, own, bx, by, relay, last, lsem, ssem, rsem
 ):
     x, y, c = feature_place()
     to_x, to_y = {"x": 1 - x}, {"y": 1 - y}
@@ -380,11 +475,11 @@
         return one
 
     loads = [
-        load(0, t_ref.at[ACROSS_Y, 0], near.at[0]),
+        load(0, ny_ref, near.at[0]),
         load(1, bx_ref, bx),
-        load(2, t_ref.at[ACROSS_X, 1], near.at[1]),
+        load(2, nx_ref, near.at[1]),
         load(3, by_ref, by),
-        load(4, t_ref.at[OWN], own),
+        load(4, own_ref, own),
     ]
     greet((to_x, to_y))
     sends = [
@@ -430,14 +525,14 @@
         one.wait_send()
 
 
-def scatter_tail(total, by_x, by_y):
-    half, width = total.shape[2:]
-    kind = total.dtype
+def scatter_tail(keeps, by_x, by_y):
+    _, half, width = by_x.shape
+    kind = by_x.dtype
     pair = pltpu.VMEM((2, half, width), kind)
     return pl.pallas_call(
         scatter_tail_kernel,
         out_shape=jax.ShapeDtypeStruct((2 * half, width), f32),
-        in_specs=[hbm_spec()] * 3,
+        in_specs=[hbm_spec()] * 5,
         out_specs=vmem_spec(),
         scratch_shapes=[pair] * 6
         + [
@@ -450,7 +545,7 @@
         ),
         cost_estimate=cost(16),
         name="scatter_tail",
-    )(total, by_x, by_y)
+    )(*keeps, by_x, by_y)
 
 
 def exchange_parts(axes, x_ref, o_ref, local_sem, ssem, rsem):
@@ -590,7 +685,7 @@
 
 
 def sigmoid(v):
-    return 1.0 / (1.0 + jnp.exp(-v))
+    return 0.5 + 0.5 * jnp.tanh(0.5 * v)
 
 
 def gelu_pair(v):
@@ -683,7 +778,9 @@
         state_ref[at] = state
         return prod[7:8], state[7:8]
 
-    prod_out, state_out = lax.fori_loop(0, rows // 8, body, (carry[0:1], carry[1:2]))
+    prod_out, state_out = lax.fori_loop(
+        0, rows // 8, body, (carry[0:1], carry[1:2]), unroll=4
+    )
     carry[0:1] = prod_out
     carry[1:2] = state_out
     ends_ref[0:1] = prod_out
@@ -758,7 +855,9 @@
         adj_ref[at] = adj
         return prod[0:1], adj[0:1]
 
-    prod_out, adj_out = lax.fori_loop(0, tiles, body, (carry[0:1], carry[1:2]))
+    prod_out, adj_out = lax.fori_loop(
+        0, tiles, body, (carry[0:1], carry[1:2]), unroll=4
+    )
     carry[0:1] = prod_out
     carry[1:2] = adj_out
     heads_ref[0:1] = keep_ref[0:1] * prod_out
@@ -868,8 +967,10 @@
         jnp.dot(conved_low, wx_ref[...], preferred_element_type=f32) + small_ref[6:7]
     )
     decay = jnp.exp(-decay_scale * gate_a * rates)
-    root = jnp.sqrt(1.0 - decay * decay + push_shift)
-    d_decay = adjoint * (state_prev * masks[:, 0:1] - gate_x * conved * decay / root)
+    square = 1.0 - decay * decay + push_shift
+    inverse = lax.rsqrt(square)
+    root = square * inverse
+    d_decay = adjoint * (state_prev * masks[:, 0:1] - gate_x * conved * decay * inverse)
     slope_a = -decay_scale * d_decay * decay * gate_a
     d_logit_a = (slope_a * rates * (1.0 - gate_a)).astype(bf16)
     through = adjoint * root * gate_x
@@ -1037,6 +1138,48 @@
     )(normed, cot_mine, cot_theirs, w_mlp, w_down)
 
 
+def down_kernel(h_ref, w_ref, mine_ref, theirs_ref):
+    width = w_ref.shape[1]
+    tile = 512
+    hidden = h_ref[...]
+
+    def into(ref):
+        def body(j, none):
+            at = pl.ds(pl.multiple_of(j * tile, tile), tile)
+            ref[:, at] = jnp.dot(hidden, w_ref[:, at], preferred_element_type=f32).astype(bf16)
+            return none
+
+        lax.fori_loop(0, width // tile, body, 0)
+
+    first = pl.program_id(0) < pl.num_programs(0) // 2
+    pl.when(first)(lambda: into(mine_ref))
+    pl.when(jnp.logical_not(first))(lambda: into(theirs_ref))
+
+
+def down_rows(hidden, w_down):
+    rows, ff = hidden.shape
+    width = w_down.shape[1]
+    steps = 4
+    tile = rows // steps
+    part = jax.ShapeDtypeStruct((rows // 2, width), bf16)
+    return pl.pallas_call(
+        down_kernel,
+        grid=(steps,),
+        out_shape=(part, part),
+        in_specs=[
+            pl.BlockSpec((tile, ff), lambda i: (i, 0)),
+            pl.BlockSpec((ff, width), lambda i: (0, 0), pipeline_mode=pl.Buffered(1)),
+        ],
+        out_specs=(
+            pl.BlockSpec((tile, width), lambda i: (jnp.minimum(i, steps // 2 - 1), 0)),
+            pl.BlockSpec((tile, width), lambda i: (jnp.maximum(i - steps // 2, 0), 0)),
+        ),
+        compiler_params=pltpu.CompilerParams(vmem_limit_bytes=VMEM_LIMIT),
+        cost_estimate=cost(0.1),
+        name="down_rows",
+    )(hidden, w_down)
+
+
 def split_kernel(moves, a_ref, b_ref, o_ref):
     for source, block, at, start, size in moves:
         ref = (a_ref, b_ref)[source]
@@ -1270,8 +1413,9 @@
     rec_pre, cot_own = hold(rec_pre, cotangent)
     cot_x, cot_y = gather_near(cot_own)
     edge_rows = lax.dynamic_slice_in_dim(rec_pre, final, 8, 0)[:, chans:].astype(bf16)
-    tails = gather_groups(edge_rows.astype(f32) * later_open, count, 2)
-    halo = jnp.where(z > 0, lax.dynamic_index_in_dim(tails, jnp.maximum(z - 1, 0), 0, False), 0.0)
+    halo = lax.ppermute(
+        edge_rows.astype(f32) * later_open, "z", [(i, i + 1) for i in range(count - 1)]
+    )
     branch_in, conved, keep, prod, state_local, ends = forward_scan(
         order, rec_pre, halo, masks, small, wa, wx, chunk
     )
@@ -1306,35 +1450,38 @@
     d_mlp, e_theirs = hold(d_mlp, e_theirs)
     e_got = across(e_theirs, "c")
     e_mine = back_rows(d_mlp[:half_rows], w_mlp)
-    e_total, e_x, e_y = scatter_near(e_mine, e_got)
-    e_total, hidden = hold(e_total, hidden)
+    e_keeps, e_x, e_y = scatter_near(e_mine, e_got)
+    near_y, hidden = hold(e_keeps[0], hidden)
+    e_keeps = (near_y,) + e_keeps[1:]
     down_part = over_rows(hidden, cot_chip, cot_got)
     down_part, hidden = hold(down_part, hidden)
     down_sum = lax.psum_scatter(down_part, "z", scatter_dimension=0, tiled=True)
-    out_theirs = jnp.dot(hidden[half_rows:], w_down, preferred_element_type=f32).astype(bf16)
-    out_got = across(out_theirs, "c")
-    out_mine = jnp.dot(hidden[:half_rows], w_down, preferred_element_type=f32).astype(bf16)
-    out_mine, out_got, e_x, e_y = hold(out_mine, out_got, e_x, e_y)
-    e_two = gain_two * scatter_tail(e_total, e_x, e_y)
+    out_mine, out_theirs = down_rows(hidden, w_down)
+    out_mine, out_theirs, e_x, e_y = hold(out_mine, out_theirs, e_x, e_y)
+    e_two = gain_two * scatter_tail(e_keeps, e_x, e_y)
     d_middle = cotangent.astype(f32) + norm_back(middle, scale_two, e_two)
     d_own = d_middle.astype(bf16)
     d_x, d_y = gather_near(d_own)
-    d_own, d_mlp, out_mine, out_got = hold(d_own, d_mlp, out_mine, out_got)
+    d_own, d_mlp, out_mine, out_theirs = hold(d_own, d_mlp, out_mine, out_theirs)
+    out_got = across(out_theirs, "c")
     mlp_part = lax.dot_general(
         normed_two, d_mlp, contract_first, preferred_element_type=f32
     ).astype(bf16)
-    out_total = scatter_total(out_mine, out_got)
-    d_x, d_y, mlp_part, out_total = hold(d_x, d_y, mlp_part, out_total)
+    out_keeps = scatter_keeps(out_mine, out_got)
+    out_x, out_y = scatter_sends(out_mine, out_got)
+    d_x, d_y, mlp_part, out_x, out_y, *out_keeps = hold(
+        d_x, d_y, mlp_part, out_x, out_y, *out_keeps
+    )
     mlp_sum = lax.psum_scatter(mlp_part, "z", scatter_dimension=0, tiled=True)
     d_rec = gather_tail(d_own, d_x, d_y)
-    d_rec, down_sum, out_total = hold(d_rec, down_sum, out_total)
-    out_x, out_y = scatter_sides(out_total)
+    d_rec, down_sum, out_x, out_y = hold(d_rec, down_sum, out_x, out_y)
+    out_x, out_y = across(out_x, "x"), across(out_y, "y")
 
     d_mixed = lax.dot_general(d_rec, w_out, contract_last, preferred_element_type=f32)
     adj_prod, adj_local, heads = adjoint_scan(order, d_mixed, rec_pre, keep, chunk)
     heads = gather_groups(heads, count, 2)
     heads, out_x, out_y = hold(heads, out_x, out_y)
-    out_last = scatter_relay(out_total, out_x, out_y)
+    out_last = scatter_relay(out_keeps, out_x, out_y)
     adj_in = jnp.zeros((1, chans), f32)
     for hop in range(count - 1, 0, -1):
         adj_in = jnp.where(hop > z, heads[hop, 0:1] * adj_in + heads[hop, 1:2], adj_in)
@@ -1343,9 +1490,12 @@
         order, d_mixed, rec_pre, state_local, prod, adj_local, adj_prod, branch_in, halo, conved,
         masks, small, enter, wa, wx, chunk,
     )
-    edges = gather_groups(edge, count, 2)
-    after = lax.dynamic_index_in_dim(edges, jnp.minimum(z + 1, count - 1), 0, False)
-    after = jnp.where(z < count - 1, after, 0.0) * later_open
+    after = lax.ppermute(edge, "z", [(i + 1, i) for i in range(count - 1)]) * later_open
+    edge, mixed = hold(edge, mixed)
+    grad_out = lax.dot_general(mixed, d_rec, contract_first, preferred_element_type=f32).astype(
+        bf16
+    )
+    after, grad_out = hold(after, grad_out)
     tail_sum = lax.dynamic_slice_in_dim(d_rec_pre, final, 8, 0).astype(f32) + jnp.pad(
         after, ((0, 0), (chans, 0))
     )
@@ -1353,18 +1503,11 @@
     rec_part = lax.dot_general(
         normed, d_rec_pre, contract_first, preferred_element_type=f32
     ).astype(bf16)
-    rec_part, d_rec_pre, grad_a, grad_x, sums, mixed, *out_last = hold(
-        rec_part, d_rec_pre, grad_a, grad_x, sums, mixed, *out_last
-    )
-    layer_out = (middle + scatter_sum(out_total, out_x, out_y, *out_last)).astype(bf16)
-    rec_part, mlp_sum = hold(rec_part, mlp_sum)
+    rec_part, d_rec_pre, grad_a, grad_x, sums, *out_last = hold(
+        rec_part, d_rec_pre, grad_a, grad_x, sums, *out_last
+    )
+    layer_out = (middle + scatter_sum(out_keeps, out_x, out_y, *out_last)).astype(bf16)
     rec_sum = lax.psum_scatter(rec_part, "z", scatter_dimension=0, tiled=True)
-    one_theirs = back_rows(d_rec_pre[half_rows:], w_rec)
-    d_rec_pre, one_theirs = hold(d_rec_pre, one_theirs)
-    one_got = across(one_theirs, "c")
-    one_mine = back_rows(d_rec_pre[:half_rows], w_rec)
-    one_total, one_x, one_y = scatter_near(one_mine, one_got)
-    one_total, mixed, grad_a, grad_x = hold(one_total, mixed, grad_a, grad_x)
     fold = (
         lax.broadcasted_iota(jnp.int32, (chans, BLK), 0) % BLK
         == lax.broadcasted_iota(jnp.int32, (chans, BLK), 1)
@@ -1376,9 +1519,7 @@
 
     back_pack = jnp.concatenate(
         [
-            lax.dot_general(
-                mixed, d_rec, contract_first, preferred_element_type=f32
-            ).astype(bf16),
+            grad_out,
             diagonal(grad_a),
             diagonal(grad_x),
             sums.T.astype(bf16),
@@ -1389,14 +1530,13 @@
     back_pack = back_pack.reshape(2, spread, chan_rows, pack_width).transpose(1, 0, 2, 3)
     (back_swap,) = exchange([back_pack], swap_axes, 5)
     back_swap = back_swap.reshape(count * chan_rows, pack_width)
-    one_x, one_y, back_swap, mlp_sum, rec_sum = hold(one_x, one_y, back_swap, mlp_sum, rec_sum)
+    back_swap, mlp_sum, d_rec_pre = hold(back_swap, mlp_sum, d_rec_pre)
     pack_sum = lax.psum_scatter(back_swap, "z", scatter_dimension=0, tiled=True)
-    one_last = scatter_relay(one_total, one_x, one_y)
-    mlp_back, rec_back = exchange(
-        [mlp_sum.reshape(NF, rows_w, 2 * ff), rec_sum.reshape(NF, rows_w, 2 * chans)], FEAT, 6
-    )
-    mlp_back, rec_back, *one_last = hold(mlp_back, rec_back, *one_last)
-    e_one = gain_one * scatter_sum(one_total, one_x, one_y, *one_last)
+    one_sum, mlp_back = scatter_dot(d_rec_pre, w_rec, mlp_sum.reshape(NF, rows_w, 2 * ff))
+    one_sum, rec_sum, down_sum = hold(one_sum, rec_sum, down_sum)
+    (rec_back,) = exchange([rec_sum.reshape(NF, rows_w, 2 * chans)], FEAT, 10)
+    rec_back, pack_sum = hold(rec_back, pack_sum)
+    e_one = gain_one * one_sum
     grad_tokens = d_middle + norm_back(tok, inverse_rms(tok), e_one)
     grad_gate, grad_up, grad_gain_two = join_blocks(
         mlp_back, mlp_gate_weight, mlp_up_weight, norm2_gain.astype(f32)[:, None], ff_moves

time: 698 us -> 660 us (0.946)
  waiting for transfers between devices: 35.8 us -> 2.84 us
  matrix products: 124 us -> 95.1 us
  Pallas kernels: 382 us -> 410 us
    pallas_call x0 -> x2, Pallas kernels: none -> 73.8 us  [the longest x1 59.8 us: scatter_dot(): pl.pallas_call(scatter_dot_kernel, out_shape=(jax.ShapeDtypeStruct((rows,...]
    pallas_call x5 -> x3, Pallas kernels: 46.3 us -> 24 us  [gather_groups(): pl.pallas_call(functools.partial(groups_kernel, count), out_shape=jax.Sha...]
    pallas_call x4, Pallas kernels: 57 us -> 34.9 us  [exchange(): pl.pallas_call(functools.partial(exchange_kernel, axes), out_shape=tuple(...]
    ppermute x20 -> x15, waiting for transfers between devices: 21.9 us -> 1.81 us  [across(): return lax.ppermute(value, axis, [(0, 1), (1, 0)])]
    dot_general x4 -> x2, matrix products: 30.7 us -> 17 us  [back_rows(): lax.dot_general(d, w, contract_last, preferred_element_type=f32)]
    dot_general x2 -> x0, matrix products: 13 us -> none  [the longest x1 7.88 us: on_device(): jnp.dot(hidden[half_rows:], w_down, preferred_element_type=f32).astype(bf16)]
    reduce_scatter x1, waiting for transfers between devices: 13 us -> 0.02 us  [on_device(): rec_sum = lax.psum_scatter(rec_part, 'z', scatter_dimension=0, tiled=True)]
    ppermute x20 -> x15, starting transfers between devices: 18.3 us -> 14 us  [across(): return lax.ppermute(value, axis, [(0, 1), (1, 0)])]
  transfers between devices with their start and end apart: 28 -> 25, of which waited for: 5 -> 2; matrix products, arithmetic and copies ran while one was open for 28% -> 27% of each run, Pallas kernels for 50% -> 57%
where the time goes in v4:
time: 660 us; the launch traced here: 652 us
  Pallas kernels  410 us (62%)
  matrix products  95.1 us (14%)
  other arithmetic  60.1 us (9%)
  local copies, waits for them, and re-layouts  45.6 us (7%)
  starting transfers between devices  20.9 us (3%)
  between operations  17.1 us (3%)
    pallas_call x1, Pallas kernels, scatter_dot(): pl.pallas_call(scatter_dot_kernel, out_shape=(jax.ShapeDtypeStruct((rows,...  59.8 us
    pallas_call x1, Pallas kernels, gather_exchange(): pl.pallas_call(gather_kernel, out_shape=(jax.ShapeDtypeStruct((NF, rows,...  59.2 us
    pallas_call x1, Pallas kernels, scatter_feature(): pl.pallas_call(scatter_kernel, out_shape=jax.ShapeDtypeStruct((rows, widt...  46.4 us
    pallas_call x1, Pallas kernels, gather_feature(): pl.pallas_call(gather_kernel, out_shape=jax.ShapeDtypeStruct((NF, rows, w...  40.1 us
    pallas_call x4, Pallas kernels, exchange(): pl.pallas_call(functools.partial(exchange_kernel, axes), out_shape=tuple(...  34.9 us
    pallas_call x1, Pallas kernels, gated_unit(): pl.pallas_call(gated_kernel, grid=(steps,), out_shape=(jax.ShapeDtypeStru...  31.2 us
    pallas_call x3, Pallas kernels, gather_groups(): pl.pallas_call(functools.partial(groups_kernel, count), out_shape=jax.Sha...  24 us
    pallas_call x1, Pallas kernels, backward_scan(): pl.pallas_call(backward_kernel, out_shape=(jax.ShapeDtypeStruct((rows, 2...  22 us
  transfers between devices with their start and end apart: 25, of which 2 were waited for; matrix products, arithmetic and copies ran while one was open for 27% of the time, Pallas kernels for 57%

profile of v4, /device:TPU:0, one launch (start us, length us, event | category | flops | bytes accessed | tf_op | source)
XLA Modules:
  0.0 651.6 jit_solution(7667983394220149832)
XLA Ops:
  13.9 2.2 split_blocks.2
  16.2 2.1 pad_maximum_fusion.refs_0_
  18.2 15.6 %exchange.4 = bf16[8,80,640]{2,1,0:T(8,128)(2,1)} custom-call(bf16[8,80,640]{2,1,0:T(8,128)(2,1)} %pad_maximum_fusion.refs_0_), custom_call_target="tpu_custom_call" | custom-call | bytes 45000000 | tf_op jit(solution)/shard_map/exchange/pallas_call | solution.py:604
  33.9 2.0 slice.195
  38.3 8.4 %gather_groups.3 = f32[4,8,512]{2,1,0:T(8,128)} custom-call(f32[8,512]{1,0:T(8,128)} %fusion.65.x_ref), custom_call_target="tpu_custom_call" | custom-call | bytes 15000000 | tf_op jit(solution)/shard_map/gather_groups/pallas_call | solution.py:667
  46.7 2.9 split_blocks.3.refs_1_
  49.6 59.2 %gather_exchange.1 = (bf16[8,256,2048]{2,1,0:T(8,128)(2,1)}, bf16[8,64,1536]{2,1,0:T(8,128)(2,1)}) custom-call(bf16[256,2048]{1,0:T(8,128)(2,1)} %refs_0_, bf16[8,64,1536]{2,1,0:T(8,128)(2,1)} %split_blocks.3.refs_1_), custom_call_target="tpu_custom_call" | custom-call | bytes 165000000 | tf_op jit(solution)/shard_map/gather_exchange/pallas_call | solution.py:624
  114.3 5.3 fusion
  119.7 11.5 %fusion.15.pre_ref = f32[2048,640]{1,0:T(8,128)} fusion(bf16[2048,640]{1,0:T(8,128)(2,1)} %all-gather.7.cloned.1.call-done.w_ref, bf16[2048,2048]{1,0:T(8,128)(2,1)} %bitcast.173, f32[2048]{0:T(1024)S(1)} %bitcast.210, f32[2048]{0:T(1024)S(1)} %add_rsqrt_fusion), kind=kOutput, calls=%fused_computation.28 | convolution fusion | flops 5385486336 | bytes 16269312 | tf_op jit(solution)/shard_map/dot_general | solution.py:1412
  136.5 3.9 exchange.5
  144.0 4.3 collective-permute-start
  149.8 17.0 %forward_scan.1 = (bf16[2048,320]{1,0:T(8,128)(2,1)}, bf16[2048,320]{1,0:T(8,128)(2,1)}, f32[2048,320]{1,0:T(8,128)}, f32[2048,320]{1,0:T(8,128)}, f32[2048,320]{1,0:T(8,128)}, /*index=5*/f32[8,320]{1,0:T(8,128)}) custom-call(s32[8]{0:T(128)} %copy-done.32, f32[2048,640]{1,0:T(8,128)} %fusion.15.pre_ref, f32[8,320]{1,0:T(8,128)} %copy-done.26, ...), custom_call_target="tpu_custom_call" | custom-call | bytes 45000000 | tf_op jit(solution)/shard_map/forward_scan/pallas_call | solution.py:797
  168.2 8.4 %gather_groups.4 = f32[4,8,320]{2,1,0:T(8,128)} custom-call(f32[8,320]{1,0:T(8,128)} %get-tuple-element.128.x_ref), custom_call_target="tpu_custom_call" | custom-call | bytes 15000000 | tf_op jit(solution)/shard_map/gather_groups/pallas_call | solution.py:667
  176.6 2.0 slice.214
  180.2 1.9 slice.215
  185.4 2.7 constant_dynamic-update-slice_fusion.3
  188.1 2.3 constant_dynamic-update-slice_fusion.2
  190.4 3.4 fusion.11
  193.8 6.7 %convolution_convert_fusion = bf16[2048,2048]{1,0:T(8,128)(2,1)} fusion(bf16[2048,320]{1,0:T(8,128)(2,1)S(1)} %fusion.11, bf16[320,2432]{1,0:T(8,128)(2,1)S(1)} %bitcast.199), kind=kOutput, calls=%fused_computation.5 | convolution fusion | flops 2688548864 | bytes 11272192 | tf_op jit(solution)/shard_map/dot_general | solution.py:1429
  200.6 1.9 constant_dynamic-update-slice_fusion.1
  202.5 1.9 constant_dynamic-update-slice_fusion.mine_ref
  204.3 46.4 %scatter_feature.1 = f32[256,2048]{1,0:T(8,128)} custom-call(bf16[8,256,2048]{2,1,0:T(8,128)(2,1)} %bitcast.171), custom_call_target="tpu_custom_call" | custom-call | bytes 135000000 | tf_op jit(solution)/shard_map/scatter_feature/pallas_call | solution.py:320
  250.7 2.1 multiply_reduce_fusion.1
  254.3 40.1 %gather_feature.1 = bf16[8,256,2048]{2,1,0:T(8,128)(2,1)} custom-call(bf16[256,2048]{1,0:T(8,128)(2,1)} %multiply_convert_fusion.refs_0_), custom_call_target="tpu_custom_call" | custom-call | bytes 120000000 | tf_op jit(solution)/shard_map/gather_feature/pallas_call | solution.py:123
  294.5 31.2 %gated_unit.1 = (bf16[2048,768]{1,0:T(8,128)(2,1)}, bf16[2048,1536]{1,0:T(8,128)(2,1)}) custom-call(bf16[2048,2048]{1,0:T(8,128)(2,1)} %bitcast.177, bf16[1024,2048]{1,0:T(8,128)(2,1)} %constant_dynamic-update-slice_fusion.mine_ref, bf16[1024,2048]{1,0:T(8,128)(2,1)} %collective-permute-done.5.theirs_ref, ...), custom_call_target="tpu_custom_call" | custom-call | flops 19327352832 | bytes 41943040 | tf_op jit(solution)/shard_map/gated_unit/pallas_call | solution.py:1118
  325.7 9.9 %convolution_convert_fusion.3 = bf16[1024,2048]{1,0:T(8,128)(2,1)S(1)} fusion(bf16[2048,1536]{1,0:T(8,128)(2,1)} %all-gather.9.cloned.1.call-done.w_ref, bf16[2048,1536]{1,0:T(8,128)(2,1)} %get-tuple-element.154), kind=kOutput, calls=%fused_computation.10 | convolution fusion | flops 6444548096 | bytes 13631488 | tf_op jit(solution)/shard_map/dot_general | solution.py:1441
  336.1 7.1 %convolution_convert_fusion.2 = bf16[1024,2048]{1,0:T(8,128)(2,1)S(1)} fusion(bf16[2048,1536]{1,0:T(8,128)(2,1)S(1)} %copy-done.40, bf16[2048,1536]{1,0:T(8,128)(2,1)S(1)} %copy-done.42), kind=kOutput, calls=%fused_computation.9 | convolution fusion | flops 6444548096 | bytes 13631488 | tf_op jit(solution)/shard_map/dot_general | solution.py:1441
  343.2 2.6 fusion.30
  347.2 1.7 collective-permute-start.7
  349.2 5.4 fusion.23
  354.6 7.4 %add_convert_fusion = bf16[768,2048]{1,0:T(8,128)(2,1)} fusion(f32[768,2048]{1,0:T(8,128)S(1)} %fusion.23, bf16[1024,2048]{1,0:T(8,128)(2,1)} %constant_dynamic-update-slice_fusion.mine_ref, bf16[2048,768]{1,0:T(8,128)(2,1)S(1)} %copy-done.13), kind=kOutput, calls=%fused_computation.7 | convolution fusion | flops 3224371200 | bytes 15204352 | tf_op jit(solution)/shard_map/dot_general | solution.py:1445
  362.0 14.0 %down_rows.1 = (bf16[1024,2048]{1,0:T(8,128)(2,1)}, bf16[1024,2048]{1,0:T(8,128)(2,1)}) custom-call(bf16[2048,768]{1,0:T(8,128)(2,1)} %get-tuple-element.145.h_ref, bf16[768,2048]{1,0:T(8,128)(2,1)} %all-gather.11.cloned.1.call-done.down_ref.w_ref), custom_call_target="tpu_custom_call" | custom-call | bytes 300000 | tf_op jit(solution)/shard_map/down_rows/pallas_call | solution.py:1165
  376.0 2.9 add_convert_fusion.4
  378.9 17.3 %scatter_tail.1 = f32[256,2048]{1,0:T(8,128)} custom-call(bf16[128,2048]{1,0:T(8,128)(2,1)} %get-tuple-element.143.ny_ref, bf16[128,2048]{1,0:T(8,128)(2,1)} %get-tuple-element.305.nx_ref, bf16[2,128,2048]{2,1,0:T(8,128)(2,1)} %bitcast.194, bf16[2,128,2048]{2,1,0:T(8,128)(2,1)} %collective-permute-done.7.bx_ref, ...), custom_call_target="tpu_custom_call" | custom-call | bytes 48000000 | tf_op jit(solution)/shard_map/scatter_tail/pallas_call | solution.py:532
  396.2 2.8 fusion.17
  399.1 3.7 fusion.80
  403.2 1.7 collective-permute-start.10
  404.9 16.7 %convolution_convert_fusion.1 = bf16[2048,1536]{1,0:T(8,128)(2,1)} fusion(bf16[2048,2048]{1,0:T(8,128)(2,1)S(1)} %bitcast.180, bf16[2048,1536]{1,0:T(8,128)(2,1)} %get-tuple-element.154), kind=kOutput, calls=%fused_computation.6 | convolution fusion | flops 12888047616 | bytes 20971520 | tf_op jit(solution)/shard_map/dot_general | solution.py:1467
  421.6 3.1 add_convert_fusion.1
  424.7 2.9 fusion.42
  427.6 3.6 fusion.32
  431.6 18.5 %gather_tail.1 = bf16[8,256,2048]{2,1,0:T(8,128)(2,1)} custom-call(bf16[256,2048]{1,0:T(8,128)(2,1)} %get-tuple-element.158.x_ref, bf16[256,2048]{1,0:T(8,128)(2,1)} %collective-permute-done.9.bx_ref, bf16[256,2048]{1,0:T(8,128)(2,1)} %collective-permute-done.10.by_ref), custom_call_target="tpu_custom_call" | custom-call | bytes 48000000 | tf_op jit(solution)/shard_map/gather_tail/pallas_call | solution.py:445
  452.3 10.0 %fusion.26.d_mixed_ref = f32[2048,320]{1,0:T(8,128)} fusion(bf16[2048,2048]{1,0:T(8,128)(2,1)} %bitcast.181, bf16[320,2432]{1,0:T(8,128)(2,1)} %bitcast.198), kind=kOutput, calls=%fused_computation.50 | convolution fusion | flops 2684354560 | bytes 12320768 | tf_op jit(solution)/shard_map/dot_general | solution.py:1480
  462.3 12.1 %adjoint_scan.1 = (f32[2048,320]{1,0:T(8,128)}, f32[2048,320]{1,0:T(8,128)}, f32[8,320]{1,0:T(8,128)}) custom-call(s32[8]{0:T(128)} %copy-done.32, f32[2048,320]{1,0:T(8,128)} %fusion.26.d_mixed_ref, f32[2048,640]{1,0:T(8,128)} %fusion.15.pre_ref, f32[2048,320]{1,0:T(8,128)} %get-tuple-element.165.keep_ref), custom_call_target="tpu_custom_call" | custom-call | bytes 36000000 | tf_op jit(solution)/shard_map/adjoint_scan/pallas_call | solution.py:873
  474.4 7.2 %gather_groups.5 = f32[4,8,320]{2,1,0:T(8,128)} custom-call(f32[8,320]{1,0:T(8,128)} %get-tuple-element.166.x_ref), custom_call_target="tpu_custom_call" | custom-call | bytes 15000000 | tf_op jit(solution)/shard_map/gather_groups/pallas_call | solution.py:667
  483.1 22.0 %backward_scan.1 = (bf16[2048,640]{1,0:T(8,128)(2,1)}, f32[8,320]{1,0:T(8,128)}, f32[8,320]{1,0:T(8,128)}, f32[320,320]{1,0:T(8,128)}, f32[320,320]{1,0:T(8,128)}) custom-call(s32[8]{0:T(128)} %copy-done.32, f32[2048,320]{1,0:T(8,128)} %fusion.26.d_mixed_ref, f32[2048,640]{1,0:T(8,128)} %fusion.15.pre_ref, ...), custom_call_target="tpu_custom_call" | custom-call | bytes 63000000 | tf_op jit(solution)/shard_map/backward_scan/pallas_call | solution.py:1035
  505.2 1.8 collective-permute-start.14
  506.9 2.1 fusion.38
  510.0 7.5 %convolution_convert_fusion.5 = bf16[320,2048]{1,0:T(8,128)(2,1)} fusion(bf16[2048,320]{1,0:T(8,128)(2,1)S(1)} %copy-done.23, bf16[2048,2048]{1,0:T(8,128)(2,1)} %bitcast.182), kind=kOutput, calls=%fused_computation.27 | convolution fusion | flops 2685009920 | bytes 11010048 | tf_op jit(solution)/shard_map/dot_general | solution.py:1495
  517.5 2.0 fusion.37
  522.5 9.0 %convolution_convert_fusion.4 = bf16[2048,640]{1,0:T(8,128)(2,1)} fusion(bf16[2048,640]{1,0:T(8,128)(2,1)S(1)} %fusion.61.a_ref, bf16[2048,2048]{1,0:T(8,128)(2,1)S(1)} %bitcast.176, f32[2048]{0:T(1024)S(1)} %bitcast.211, f32[2048]{0:T(1024)S(1)} %add_rsqrt_fusion), kind=kOutput, calls=%fused_computation.15 | convolution fusion | flops 5386797056 | bytes 13647872 | tf_op jit(solution)/shard_map/dot_general | solution.py:1503
  531.6 1.8 collective-permute-done.16
  533.7 1.7 convolution_convert_fusion.7
  535.5 2.3 convolution_convert_fusion.6
  540.2 3.7 concatenate.43
  546.7 3.8 exchange.6
  553.5 3.3 fusion.36
  556.8 59.8 %scatter_dot.1 = (f32[256,2048]{1,0:T(8,128)}, bf16[8,64,1536]{2,1,0:T(8,128)(2,1)}) custom-call(bf16[2048,640]{1,0:T(8,128)(2,1)} %copy-done.15, bf16[2048,640]{1,0:T(8,128)(2,1)} %all-gather.7.cloned.1.call-done.w_ref, bf16[8,64,1536]{2,1,0:T(8,128)(2,1)} %bitcast.201), custom_call_target="tpu_custom_call" | custom-call | bytes 165000000 | tf_op jit(solution)/shard_map/scatter_dot/pallas_call | solution.py:290
  616.7 11.6 %exchange.7.x_ref = bf16[8,64,640]{2,1,0:T(8,128)(2,1)} custom-call(bf16[8,64,640]{2,1,0:T(8,128)(2,1)} %bitcast.203), custom_call_target="tpu_custom_call" | custom-call | bytes 45000000 | tf_op jit(solution)/shard_map/exchange/pallas_call | solution.py:604
  628.2 2.5 convert_element_type.367
  630.7 4.0 join_blocks.3
  636.2 2.5 fusion.20
  638.7 1.9 unpack_sums.1
  642.1 2.5 join_blocks.2
  (216 shorter events, 52.8 us)
Async XLA Ops:
  7.2 8.9 %copy-start.38 = (bf16[64]{0:T(256)(128)(2,1)S(1)}, bf16[64]{0:T(256)(128)(2,1)}, u32[]{:S(2)}) copy-start(bf16[64]{0:T(256)(128)(2,1)} %param.32) | copy-start | bytes 388
  7.2 8.9 %copy-start.36 = (bf16[64]{0:T(256)(128)(2,1)S(1)}, bf16[64]{0:T(256)(128)(2,1)}, u32[]{:S(2)}) copy-start(bf16[64]{0:T(256)(128)(2,1)} %param.21) | copy-start | bytes 388
  7.2 107.1 %all-gather.5.cloned.1.call-start = ((), (), s32[]{:S(2)}) async-start(), calls=%async_computation.4 | async-start | bytes 1945600 | tf_op jit(solution)/shard_map/all_gather | solution.py:1358
  13.1 106.6 %all-gather.7.cloned.1.call-start = ((), (), s32[]{:S(2)}) async-start(), calls=%async_computation.5 | async-start | bytes 3276800 | tf_op jit(solution)/shard_map/all_gather | solution.py:1369
  35.9 258.5 %all-gather.11.cloned.1.call-start = ((), (), s32[]{:S(2)}) async-start(), calls=%async_computation.7 | async-start | bytes 3932160 | tf_op jit(solution)/shard_map/all_gather | solution.py:1387
  36.6 257.8 %all-gather.9.cloned.1.call-start = ((), (), s32[]{:S(2)}) async-start(), calls=%async_computation.6 | async-start | bytes 7864320 | tf_op jit(solution)/shard_map/all_gather | solution.py:1386
  46.6 65.2 %copy-start.10 = (bf16[256,2048]{1,0:T(8,128)(2,1)S(1)}, bf16[256,2048]{1,0:T(8,128)(2,1)}, u32[]{:S(2)}) copy-start(bf16[256,2048]{1,0:T(8,128)(2,1)} %param.20) | copy-start | bytes 3145732
  108.9 341.2 %reduce-scatter.5.cloned.1.call-start = ((), (), s32[]{:S(2)}) async-start(), calls=%async_computation.8 | async-start | bytes 3932160 | tf_op jit(solution)/shard_map/reduce_scatter | solution.py:1458
  110.9 31.1 %copy-start.34 = (pred[320]{0:T(512)(128)(4,1)}, pred[320]{0:T(512)(128)(4,1)S(1)}, u32[]{:S(2)}) copy-start(pred[320]{0:T(512)(128)(4,1)S(1)} %get-tuple-element.329) | copy-start | bytes 964
  111.8 409.2 %copy-start.24 = (f32[4,1,512]{2,1,0:T(1,128)}, f32[4,1,512]{2,1,0:T(1,128)S(1)}, u32[]{:S(2)}) copy-start(f32[4,1,512]{2,1,0:T(1,128)S(1)} %get-tuple-element.316) | copy-start | bytes 24580
  114.2 19.7 %copy-start.32 = (s32[8]{0:T(128)}, s32[8]{0:T(128)S(1)}, u32[]{:S(2)}) copy-start(s32[8]{0:T(128)S(1)} %fusion.75.order_ref) | copy-start | bytes 100
  131.1 35.7 %collective-permute-start.1 = (bf16[256,2048]{1,0:T(8,128)(2,1)S(1)}, bf16[256,2048]{1,0:T(8,128)(2,1)S(1)}, u32[]{:S(2)}, u32[]{:S(2)}) collective-permute-start(bf16[256,2048]{1,0:T(8,128)(2,1)S(1)} %copy-done.10), channel_id=1, source_target_pairs={{0,4},{4,0},{1,5},{5,1},{2,6},{6,2},{3,7},{7,3},{8,12},{12,8},{9,1... | collective-permute-start | bytes 3145736 | tf_op jit(solution)/shard_map/ppermute | solution.py:347
  131.9 34.9 %collective-permute-start.2 = (bf16[256,2048]{1,0:T(8,128)(2,1)S(1)}, bf16[256,2048]{1,0:T(8,128)(2,1)S(1)}, u32[]{:S(2)}, u32[]{:S(2)}) collective-permute-start(bf16[256,2048]{1,0:T(8,128)(2,1)S(1)} %copy-done.10), channel_id=1, source_target_pairs={{0,2},{2,0},{1,3},{3,1},{4,6},{6,4},{5,7},{7,5},{8,10},{10,8},{9,1... | collective-permute-start | bytes 3145736 | tf_op jit(solution)/shard_map/ppermute | solution.py:347
  136.5 5.5 copy-start.27
  136.5 5.6 copy-start.29
  141.9 6.4 copy-start.16
  144.0 5.3 collective-permute-start
  176.6 13.9 %copy-start.2 = (f32[2048,320]{1,0:T(8,128)S(1)}, f32[2048,320]{1,0:T(8,128)}, u32[]{:S(2)}) copy-start(f32[2048,320]{1,0:T(8,128)} %get-tuple-element.125.prod_ref.prod_before_ref) | copy-start | bytes 7864324
  178.6 22.0 %collective-permute-start.3 = (bf16[128,2048]{1,0:T(8,128)(2,1)}, bf16[128,2048]{1,0:T(8,128)(2,1)}, u32[]{:S(2)}, u32[]{:S(2)}) collective-permute-start(bf16[128,2048]{1,0:T(8,128)(2,1)} %slice.214), channel_id=1, source_target_pairs={{0,2},{2,0},{1,3},{3,1},{4,6},{6,4},{5,7},{7,5},{8,10},{10,8},{9,1... | collective-permute-start | bytes 1572872 | tf_op jit(solution)/shard_map/ppermute | solution.py:347
  182.1 18.4 %collective-permute-start.4 = (bf16[128,2048]{1,0:T(8,128)(2,1)}, bf16[128,2048]{1,0:T(8,128)(2,1)}, u32[]{:S(2)}, u32[]{:S(2)}) collective-permute-start(bf16[128,2048]{1,0:T(8,128)(2,1)} %slice.215), channel_id=1, source_target_pairs={{0,4},{4,0},{1,5},{5,1},{2,6},{6,2},{3,7},{7,3},{8,12},{12,8},{9,1... | collective-permute-start | bytes 1572872 | tf_op jit(solution)/shard_map/ppermute | solution.py:347
  184.4 6.0 copy-start.3
  190.4 3.4 copy-start.17
  193.8 6.7 %copy-start.22 = (bf16[2048,320]{1,0:T(8,128)(2,1)}, bf16[2048,320]{1,0:T(8,128)(2,1)S(1)}, u32[]{:S(2)}) copy-start(bf16[2048,320]{1,0:T(8,128)(2,1)S(1)} %fusion.11) | copy-start | bytes 3932164
  204.3 90.1 %collective-permute-start.5 = (bf16[1024,2048]{1,0:T(8,128)(2,1)}, bf16[1024,2048]{1,0:T(8,128)(2,1)}, u32[]{:S(2)}, u32[]{:S(2)}) collective-permute-start(bf16[1024,2048]{1,0:T(8,128)(2,1)} %constant_dynamic-update-slice_fusion.mine_ref), channel_id=1, source_target_pairs={{0,1},{1,0},{2,3},{3,2},{4,5},{5,4},{6,7},{7,6},{8,9},{9,8},{10,11... | collective-permute-start | bytes 12582920 | tf_op jit(solution)/shard_map/ppermute | solution.py:347
  204.3 46.4 %copy-start.1 = (bf16[256,2048]{1,0:T(8,128)(2,1)S(1)}, bf16[256,2048]{1,0:T(8,128)(2,1)}, u32[]{:S(2)}) copy-start(bf16[256,2048]{1,0:T(8,128)(2,1)} %refs_0_) | copy-start | bytes 3145732
  325.7 10.4 %copy-start.40 = (bf16[2048,1536]{1,0:T(8,128)(2,1)S(1)}, bf16[2048,1536]{1,0:T(8,128)(2,1)}, u32[]{:S(2)}) copy-start(bf16[2048,1536]{1,0:T(8,128)(2,1)} %all-gather.9.cloned.1.call-done.w_ref) | copy-start | bytes 18874372
  325.7 10.4 %copy-start.42 = (bf16[2048,1536]{1,0:T(8,128)(2,1)S(1)}, bf16[2048,1536]{1,0:T(8,128)(2,1)}, u32[]{:S(2)}) copy-start(bf16[2048,1536]{1,0:T(8,128)(2,1)} %get-tuple-element.154) | copy-start | bytes 18874372
  335.6 7.5 %collective-permute-start.6 = (bf16[1024,2048]{1,0:T(8,128)(2,1)S(1)}, bf16[1024,2048]{1,0:T(8,128)(2,1)S(1)}, u32[]{:S(2)}, u32[]{:S(2)}) collective-permute-start(bf16[1024,2048]{1,0:T(8,128)(2,1)S(1)} %convolution_convert_fusion.3), channel_id=1, source_target_pairs={{0,1},{1,0},{2,3},{3,2},{4,5},{5,4},{6,7},{7,6},{8,9},{9,8},{10,11... | collective-permute-start | bytes 12582920 | tf_op jit(solution)/shard_map/ppermute | solution.py:347
  343.2 11.4 %copy-start.9 = (bf16[1024,2048]{1,0:T(8,128)(2,1)}, bf16[1024,2048]{1,0:T(8,128)(2,1)S(1)}, u32[]{:S(2)}) copy-start(bf16[1024,2048]{1,0:T(8,128)(2,1)S(1)} %convolution_convert_fusion.2) | copy-start | bytes 12582916
  345.7 3.4 copy-start.13
  347.2 31.8 %collective-permute-start.7 = (bf16[2,128,2048]{2,1,0:T(8,128)(2,1)}, bf16[2,128,2048]{2,1,0:T(8,128)(2,1)}, u32[]{:S(2)}, u32[]{:S(2)}) collective-permute-start(bf16[2,128,2048]{2,1,0:T(8,128)(2,1)} %get-tuple-element.148), channel_id=1, source_target_pairs={{0,4},{4,0},{1,5},{5,1},{2,6},{6,2},{3,7},{7,3},{8,12},{12,8},{9,1... | collective-permute-start | bytes 3145736 | tf_op jit(solution)/shard_map/ppermute | solution.py:347
  348.8 30.1 %collective-permute-start.8 = (bf16[2,128,2048]{2,1,0:T(8,128)(2,1)}, bf16[2,128,2048]{2,1,0:T(8,128)(2,1)}, u32[]{:S(2)}, u32[]{:S(2)}) collective-permute-start(bf16[2,128,2048]{2,1,0:T(8,128)(2,1)} %get-tuple-element.149), channel_id=1, source_target_pairs={{0,2},{2,0},{1,3},{3,1},{4,6},{6,4},{5,7},{7,5},{8,10},{10,8},{9,1... | collective-permute-start | bytes 3145736 | tf_op jit(solution)/shard_map/ppermute | solution.py:347
  362.0 188.6 %reduce-scatter.7.cloned.1.call-start = ((), (), s32[]{:S(2)}) async-start(), calls=%async_computation.9 | async-start | bytes 7864320 | tf_op jit(solution)/shard_map/reduce_scatter | solution.py:1475
  378.9 25.9 %slice-start.2 = ((s8[8388608]{0:T(1024)(128)(4,1)}), s8[4194304]{0:T(1024)(128)(4,1)S(1)}, s32[]{:S(2)}) async-start(s8[8388608]{0:T(1024)(128)(4,1)} %bitcast.178), calls=%async_computation.14 | async-start | bytes 8388608
  396.2 2.9 copy-start.4
  396.2 8.7 %slice-start.3 = ((s8[8388608]{0:T(1024)(128)(4,1)}), s8[4194304]{0:T(1024)(128)(4,1)S(1)}, s32[]{:S(2)}) async-start(s8[8388608]{0:T(1024)(128)(4,1)} %bitcast.178), calls=%async_computation.15 | async-start | bytes 8388608
  402.8 18.8 %collective-permute-start.11 = (bf16[1024,2048]{1,0:T(8,128)(2,1)}, bf16[1024,2048]{1,0:T(8,128)(2,1)}, u32[]{:S(2)}, u32[]{:S(2)}) collective-permute-start(bf16[1024,2048]{1,0:T(8,128)(2,1)} %get-tuple-element.156), channel_id=1, source_target_pairs={{0,1},{1,0},{2,3},{3,2},{4,5},{5,4},{6,7},{7,6},{8,9},{9,8},{10,11... | collective-permute-start | bytes 12582920 | tf_op jit(solution)/shard_map/ppermute | solution.py:347
  402.8 28.4 %collective-permute-start.9 = (bf16[256,2048]{1,0:T(8,128)(2,1)}, bf16[256,2048]{1,0:T(8,128)(2,1)}, u32[]{:S(2)}, u32[]{:S(2)}) collective-permute-start(bf16[256,2048]{1,0:T(8,128)(2,1)} %get-tuple-element.158.x_ref), channel_id=1, source_target_pairs={{0,4},{4,0},{1,5},{5,1},{2,6},{6,2},{3,7},{7,3},{8,12},{12,8},{9,1... | collective-permute-start | bytes 3145736 | tf_op jit(solution)/shard_map/ppermute | solution.py:347
  403.2 28.1 %collective-permute-start.10 = (bf16[256,2048]{1,0:T(8,128)(2,1)}, bf16[256,2048]{1,0:T(8,128)(2,1)}, u32[]{:S(2)}, u32[]{:S(2)}) collective-permute-start(bf16[256,2048]{1,0:T(8,128)(2,1)} %get-tuple-element.158.x_ref), channel_id=1, source_target_pairs={{0,2},{2,0},{1,3},{3,1},{4,6},{6,4},{5,7},{7,5},{8,10},{10,8},{9,1... | collective-permute-start | bytes 3145736 | tf_op jit(solution)/shard_map/ppermute | solution.py:347
  421.6 6.0 copy-start.7
  431.3 185.4 %reduce-scatter.9.cloned.1.call-start = ((), (), s32[]{:S(2)}) async-start(), calls=%async_computation.10 | async-start | bytes 3276800 | tf_op jit(solution)/shard_map/reduce_scatter | solution.py:1510
  450.1 31.5 %collective-permute-start.12 = (bf16[2,128,2048]{2,1,0:T(8,128)(2,1)}, bf16[2,128,2048]{2,1,0:T(8,128)(2,1)}, u32[]{:S(2)}, u32[]{:S(2)}) collective-permute-start(bf16[2,128,2048]{2,1,0:T(8,128)(2,1)} %get-tuple-element.167), channel_id=1, source_target_pairs={{0,4},{4,0},{1,5},{5,1},{2,6},{6,2},{3,7},{7,3},{8,12},{12,8},{9,1... | collective-permute-start | bytes 3145736 | tf_op jit(solution)/shard_map/ppermute | solution.py:347
  451.1 30.6 %collective-permute-start.13 = (bf16[2,128,2048]{2,1,0:T(8,128)(2,1)}, bf16[2,128,2048]{2,1,0:T(8,128)(2,1)}, u32[]{:S(2)}, u32[]{:S(2)}) collective-permute-start(bf16[2,128,2048]{2,1,0:T(8,128)(2,1)} %get-tuple-element.168), channel_id=1, source_target_pairs={{0,2},{2,0},{1,3},{3,1},{4,6},{6,4},{5,7},{7,5},{8,10},{10,8},{9,1... | collective-permute-start | bytes 3145736 | tf_op jit(solution)/shard_map/ppermute | solution.py:347
  483.1 23.8 %copy-start.21 = (bf16[128,2048]{1,0:T(8,128)(2,1)S(1)}, bf16[128,2048]{1,0:T(8,128)(2,1)}, u32[]{:S(2)}) copy-start(bf16[128,2048]{1,0:T(8,128)(2,1)} %get-tuple-element.182) | copy-start | bytes 1572868
  483.1 26.9 %copy-start.23 = (bf16[2048,320]{1,0:T(8,128)(2,1)S(1)}, bf16[2048,320]{1,0:T(8,128)(2,1)}, u32[]{:S(2)}) copy-start(bf16[2048,320]{1,0:T(8,128)(2,1)} %copy-done.22) | copy-start | bytes 3932164
  505.2 15.7 %collective-permute-start.14 = (f32[8,320]{1,0:T(8,128)}, f32[8,320]{1,0:T(8,128)S(1)}, u32[]{:S(2)}, u32[]{:S(2)}) collective-permute-start(f32[8,320]{1,0:T(8,128)} %get-tuple-element.176), channel_id=1, source_target_pairs={{8,0},{16,8},{24,16},{9,1},{17,9},{25,17},{10,2},{18,10},{26,18},{... | collective-permute-start | bytes 30728 | tf_op jit(solution)/shard_map/ppermute | solution.py:1493
  506.9 15.6 %slice-start = ((s8[8388608]{0:T(1024)(128)(4,1)}), s8[4194304]{0:T(1024)(128)(4,1)S(1)}, s32[]{:S(2)}) async-start(s8[8388608]{0:T(1024)(128)(4,1)} %bitcast.174), calls=%async_computation.12 | async-start | bytes 8388608
  509.1 8.5 %copy-start.20 = (bf16[128,2048]{1,0:T(8,128)(2,1)S(1)}, bf16[128,2048]{1,0:T(8,128)(2,1)}, u32[]{:S(2)}) copy-start(bf16[128,2048]{1,0:T(8,128)(2,1)} %get-tuple-element.183) | copy-start | bytes 1572868
  509.1 11.9 %copy-start.14 = (bf16[2048,640]{1,0:T(8,128)(2,1)S(1)}, bf16[2048,640]{1,0:T(8,128)(2,1)}, u32[]{:S(2)}) copy-start(bf16[2048,640]{1,0:T(8,128)(2,1)} %get-tuple-element.175) | copy-start | bytes 7864324
  509.1 13.4 %slice-start.1 = ((s8[8388608]{0:T(1024)(128)(4,1)}), s8[4194304]{0:T(1024)(128)(4,1)S(1)}, s32[]{:S(2)}) async-start(s8[8388608]{0:T(1024)(128)(4,1)} %bitcast.174), calls=%async_computation.13 | async-start | bytes 8388608
  509.1 22.5 %collective-permute-start.15 = (bf16[128,2048]{1,0:T(8,128)(2,1)}, bf16[128,2048]{1,0:T(8,128)(2,1)}, u32[]{:S(2)}, u32[]{:S(2)}) collective-permute-start(bf16[128,2048]{1,0:T(8,128)(2,1)} %fusion.38), channel_id=1, source_target_pairs={{0,2},{2,0},{1,3},{3,1},{4,6},{6,4},{5,7},{7,5},{8,10},{10,8},{9,1... | collective-permute-start | bytes 1572872 | tf_op jit(solution)/shard_map/ppermute | solution.py:347
  519.5 13.9 %collective-permute-start.16 = (bf16[128,2048]{1,0:T(8,128)(2,1)}, bf16[128,2048]{1,0:T(8,128)(2,1)}, u32[]{:S(2)}, u32[]{:S(2)}) collective-permute-start(bf16[128,2048]{1,0:T(8,128)(2,1)} %fusion.37), channel_id=1, source_target_pairs={{0,4},{4,0},{1,5},{5,1},{2,6},{6,2},{3,7},{7,3},{8,12},{12,8},{9,1... | collective-permute-start | bytes 1572872 | tf_op jit(solution)/shard_map/ppermute | solution.py:347
  522.5 11.1 %copy-start.28 = (s32[320]{0:T(512)S(1)}, s32[320]{0:T(512)}, u32[]{:S(2)}) copy-start(s32[320]{0:T(512)} %copy-done.27) | copy-start | bytes 3844
  522.5 11.1 %copy-start.30 = (s32[320]{0:T(512)S(1)}, s32[320]{0:T(512)}, u32[]{:S(2)}) copy-start(s32[320]{0:T(512)} %copy-done.29) | copy-start | bytes 3844
  522.5 11.1 %copy-start.35 = (pred[320]{0:T(512)(128)(4,1)S(1)}, pred[320]{0:T(512)(128)(4,1)}, u32[]{:S(2)}) copy-start(pred[320]{0:T(512)(128)(4,1)} %copy-done.34) | copy-start | bytes 964
  522.5 11.1 %copy-start.41 = (pred[320]{0:T(512)(128)(4,1)S(1)}, pred[320]{0:T(512)(128)(4,1)}, u32[]{:S(2)}) copy-start(pred[320]{0:T(512)(128)(4,1)} %get-tuple-element.330) | copy-start | bytes 964
  531.6 7.2 %copy-start.31 = (f32[8,320]{1,0:T(8,128)S(1)}, f32[8,320]{1,0:T(8,128)}, u32[]{:S(2)}) copy-start(f32[8,320]{1,0:T(8,128)} %get-tuple-element.190) | copy-start | bytes 30724
  533.4 105.3 %reduce-scatter.11.cloned.1.call-start = ((), (), s32[]{:S(2)}) async-start(), calls=%async_computation.11 | async-start | bytes 1945600 | tf_op jit(solution)/shard_map/reduce_scatter | solution.py:1534
  545.4 5.2 copy-start.37
  545.4 5.9 copy-start.39
  546.7 5.3 copy-start.33
  616.6 18.0 %copy-start.5 = (f32[256,2048]{1,0:T(8,128)S(1)}, f32[256,2048]{1,0:T(8,128)}, u32[]{:S(2)}) copy-start(f32[256,2048]{1,0:T(8,128)} %get-tuple-element.198) | copy-start | bytes 6291460
  616.7 18.0 %copy-start.25 = (f32[4,1,512]{2,1,0:T(1,128)S(1)}, f32[4,1,512]{2,1,0:T(1,128)}, u32[]{:S(2)}) copy-start(f32[4,1,512]{2,1,0:T(1,128)} %copy-done.24) | copy-start | bytes 24580
  630.7 4.3 copy-start.6
  (8 other events, 12.0 us)
Sparse Core Ops, SparseCore 0:
  13.2 40.9 all-gather.4
  56.3 53.5 all-gather.6
  111.5 62.2 all-gather.10
  175.2 114.0 all-gather.8
  362.1 60.2 reduce-scatter.4
  431.4 111.3 reduce-scatter.6
  545.1 52.6 reduce-scatter.8
  600.0 34.8 reduce-scatter.10

commit v5 on v4

--- a/solution.py
+++ b/solution.py
@@ -825,9 +825,12 @@
 
 
 def adjoint_kernel(
-    order_ref, d_mixed_ref, pre_ref, keep_ref, prod_ref, adj_ref, heads_ref, keep_next, carry
+    order_ref, d_ref, w_ref, pre_ref, keep_ref, d_mixed_ref, prod_ref, adj_ref, heads_ref,
+    keep_next, carry
 ):
-    rows = d_mixed_ref.shape[0]
+    rows = d_ref.shape[0]
+    d_mixed = lax.dot_general(d_ref[...], w_ref[...], contract_last, preferred_element_type=f32)
+    d_mixed_ref[...] = d_mixed
     step = pl.program_id(0)
 
     @pl.when(step == 0)
@@ -842,7 +845,7 @@
 
     keep_next[pl.ds(0, rows)] = keep_ref[...]
     prod_ref[...] = keep_next[pl.ds(1, rows)]
-    adj_ref[...] = d_mixed_ref[...] * gelu_tanh(pre_ref[:, 0 : adj_ref.shape[1]])
+    adj_ref[...] = d_mixed * gelu_tanh(pre_ref[:, 0 : adj_ref.shape[1]])
     tiles = rows // 8
 
     def body(i, held):
@@ -865,29 +868,30 @@
     heads_ref[2:8] = jnp.zeros_like(heads_ref[2:8])
 
 
-def adjoint_scan(order, d_mixed, rec_pre, keep, chunk):
+def adjoint_scan(order, d_rec, w_out, rec_pre, keep, chunk):
     rows, width = keep.shape
     last = rows // chunk - 1
     tile = pl.BlockSpec((chunk, width), lambda i, order: (order[last - i], 0))
     full = jax.ShapeDtypeStruct((rows, width), f32)
     return pl.pallas_call(
         adjoint_kernel,
-        out_shape=(full, full, jax.ShapeDtypeStruct((8, width), f32)),
+        out_shape=(full, full, full, jax.ShapeDtypeStruct((8, width), f32)),
         grid_spec=pltpu.PrefetchScalarGridSpec(
             num_scalar_prefetch=1,
             grid=(rows // chunk,),
             in_specs=[
-                tile,
+                pl.BlockSpec((chunk, d_rec.shape[1]), lambda i, order: (order[last - i], 0)),
+                pl.BlockSpec((width, d_rec.shape[1]), lambda i, order: (0, 0)),
                 pl.BlockSpec((chunk, 2 * width), lambda i, order: (order[last - i], 0)),
                 tile,
             ],
-            out_specs=(tile, tile, pl.BlockSpec((8, width), lambda i, order: (0, 0))),
+            out_specs=(tile, tile, tile, pl.BlockSpec((8, width), lambda i, order: (0, 0))),
             scratch_shapes=[pltpu.VMEM((chunk + 8, width), f32), pltpu.VMEM((8, width), f32)],
         ),
         compiler_params=pltpu.CompilerParams(vmem_limit_bytes=VMEM_LIMIT),
         cost_estimate=cost(12),
         name="adjoint_scan",
-    )(order, d_mixed, rec_pre, keep)
+    )(order, d_rec, w_out, rec_pre, keep)
 
 
 def backward_kernel(
@@ -1220,6 +1224,53 @@
     )(x, a, b, gain)
 
 
+def pack_kernel(out_ref, ga_ref, gx_ref, sums_ref, o_ref, small):
+    spread, _, chan_rows, total = o_ref.shape
+    chans, width = out_ref.shape
+    extra = total - width
+    row = lax.broadcasted_iota(jnp.int32, (chans, chans), 0)
+    col = lax.broadcasted_iota(jnp.int32, (chans, chans), 1)
+    same = (row < BLK) == (col < BLK)
+    at = lax.broadcasted_iota(jnp.int32, (chans, extra), 0)
+    at = jnp.where(at < BLK, at, at - BLK)
+    to = lax.broadcasted_iota(jnp.int32, (chans, extra), 1)
+
+    def placed(ref, start):
+        kept = jnp.where(same, ref[...], 0.0).astype(bf16)
+        spot = jnp.where(to == at + start, 1.0, 0.0).astype(bf16)
+        return jnp.dot(kept, spot, preferred_element_type=f32)
+
+    rows = jnp.concatenate([sums_ref[...], jnp.zeros_like(sums_ref)]).astype(bf16)
+    spot = jnp.where(
+        lax.broadcasted_iota(jnp.int32, (16, extra), 0) + 2 * BLK
+        == lax.broadcasted_iota(jnp.int32, (16, extra), 1),
+        1.0,
+        0.0,
+    ).astype(bf16)
+    small[...] = (
+        placed(ga_ref, 0)
+        + placed(gx_ref, BLK)
+        + lax.dot_general(rows, spot, contract_first, preferred_element_type=f32)
+    )
+    for unit in range(2):
+        for part in range(spread):
+            here = pl.ds(unit * BLK + part * chan_rows, chan_rows)
+            o_ref[part, unit, :, 0:width] = out_ref[here].astype(bf16)
+            o_ref[part, unit, :, width:total] = small[here].astype(bf16)
+
+
+def pack_sums(grad_out, grad_a, grad_x, sums, spread, chan_rows, total):
+    chans, width = grad_out.shape
+    return pl.pallas_call(
+        pack_kernel,
+        out_shape=jax.ShapeDtypeStruct((spread, 2, chan_rows, total), bf16),
+        scratch_shapes=[pltpu.VMEM((chans, total - width), f32)],
+        compiler_params=pltpu.CompilerParams(vmem_limit_bytes=VMEM_LIMIT),
+        cost_estimate=cost(3),
+        name="pack_sums",
+    )(grad_out, grad_a, grad_x, sums)
+
+
 def unpack_kernel(x_ref, out_ref, ga_ref, gx_ref, taps_ref, *row_refs):
     width = out_ref.shape[1]
     base = width + 2 * BLK
@@ -1477,14 +1528,18 @@
     d_rec, down_sum, out_x, out_y = hold(d_rec, down_sum, out_x, out_y)
     out_x, out_y = across(out_x, "x"), across(out_y, "y")
 
-    d_mixed = lax.dot_general(d_rec, w_out, contract_last, preferred_element_type=f32)
-    adj_prod, adj_local, heads = adjoint_scan(order, d_mixed, rec_pre, keep, chunk)
-    heads = gather_groups(heads, count, 2)
-    heads, out_x, out_y = hold(heads, out_x, out_y)
+    d_mixed, adj_prod, adj_local, heads = adjoint_scan(
+        order, d_rec, mine, rec_pre, keep, chunk
+    )
+    from_later = [
+        lax.ppermute(heads, "z", [(i + hop, i) for i in range(count - hop)])
+        for hop in range(count - 1, 0, -1)
+    ]
+    *from_later, out_x, out_y = hold(*from_later, out_x, out_y)
     out_last = scatter_relay(out_keeps, out_x, out_y)
     adj_in = jnp.zeros((1, chans), f32)
-    for hop in range(count - 1, 0, -1):
-        adj_in = jnp.where(hop > z, heads[hop, 0:1] * adj_in + heads[hop, 1:2], adj_in)
+    for one in from_later:
+        adj_in = one[0:1] * adj_in + one[1:2]
     enter = jnp.concatenate([state_in, adj_in, jnp.zeros((6, chans), f32)])
     d_rec_pre, sums, edge, grad_a, grad_x = backward_scan(
         order, d_mixed, rec_pre, state_local, prod, adj_local, adj_prod, branch_in, halo, conved,
@@ -1492,9 +1547,7 @@
     )
     after = lax.ppermute(edge, "z", [(i + 1, i) for i in range(count - 1)]) * later_open
     edge, mixed = hold(edge, mixed)
-    grad_out = lax.dot_general(mixed, d_rec, contract_first, preferred_element_type=f32).astype(
-        bf16
-    )
+    grad_out = lax.dot_general(mixed, d_rec, contract_first, preferred_element_type=f32)
     after, grad_out = hold(after, grad_out)
     tail_sum = lax.dynamic_slice_in_dim(d_rec_pre, final, 8, 0).astype(f32) + jnp.pad(
         after, ((0, 0), (chans, 0))
@@ -1508,34 +1561,16 @@
     )
     layer_out = (middle + scatter_sum(out_keeps, out_x, out_y, *out_last)).astype(bf16)
     rec_sum = lax.psum_scatter(rec_part, "z", scatter_dimension=0, tiled=True)
-    fold = (
-        lax.broadcasted_iota(jnp.int32, (chans, BLK), 0) % BLK
-        == lax.broadcasted_iota(jnp.int32, (chans, BLK), 1)
-    ).astype(bf16)
-
-    def diagonal(w):
-        kept = jnp.where(same_block, w, 0.0).astype(bf16)
-        return jnp.dot(kept, fold, preferred_element_type=f32).astype(bf16)
-
-    back_pack = jnp.concatenate(
-        [
-            grad_out,
-            diagonal(grad_a),
-            diagonal(grad_x),
-            sums.T.astype(bf16),
-        ],
-        axis=1,
-    )
-    back_pack = pad_lanes(back_pack, pack_width)
-    back_pack = back_pack.reshape(2, spread, chan_rows, pack_width).transpose(1, 0, 2, 3)
+    back_pack = pack_sums(grad_out, grad_a, grad_x, sums, spread, chan_rows, pack_width)
     (back_swap,) = exchange([back_pack], swap_axes, 5)
     back_swap = back_swap.reshape(count * chan_rows, pack_width)
-    back_swap, mlp_sum, d_rec_pre = hold(back_swap, mlp_sum, d_rec_pre)
+    grad_down = down_sum.astype(f32)
+    back_swap, d_rec_pre, layer_out, grad_down = hold(back_swap, d_rec_pre, layer_out, grad_down)
+    mlp_sum, d_rec_pre = hold(mlp_sum, d_rec_pre)
     pack_sum = lax.psum_scatter(back_swap, "z", scatter_dimension=0, tiled=True)
     one_sum, mlp_back = scatter_dot(d_rec_pre, w_rec, mlp_sum.reshape(NF, rows_w, 2 * ff))
-    one_sum, rec_sum, down_sum = hold(one_sum, rec_sum, down_sum)
+    one_sum, rec_sum = hold(one_sum, rec_sum)
     (rec_back,) = exchange([rec_sum.reshape(NF, rows_w, 2 * chans)], FEAT, 10)
-    rec_back, pack_sum = hold(rec_back, pack_sum)
     e_one = gain_one * one_sum
     grad_tokens = d_middle + norm_back(tok, inverse_rms(tok), e_one)
     grad_gate, grad_up, grad_gain_two = join_blocks(
@@ -1545,6 +1580,9 @@
         rec_back, rec_gate_weight, rec_in_weight, norm1_gain.astype(f32)[:, None], chan_moves
     )
 
+    pack_sum, grad_gain_one, grad_gain_two, grad_tokens = hold(
+        pack_sum, grad_gain_one, grad_gain_two, grad_tokens
+    )
     grad_out, grad_a, grad_x, grad_taps, *grad_rows = unpack_sums(pack_sum, width)
     grad_offset, grad_a_bias, grad_x_bias, grad_rate = (r.reshape(chan_rows) for r in grad_rows)
     return (
@@ -1564,7 +1602,7 @@
         grad_gain_two.reshape(rows_w),
         grad_gate,
         grad_up,
-        down_sum.astype(f32),
+        grad_down,
     )
 
 

time: 660 us -> 653 us (0.989)
  waiting for transfers between devices: 2.84 us -> 18.7 us
  matrix products: 95.1 us -> 81.9 us
  local copies, waits for them, and re-layouts: 45.6 us -> 36 us
    dot_general x3 -> x0, matrix products: 13.9 us -> none  [the longest x1 9.98 us: on_device(): lax.dot_general(d_rec, w_out, contract_last, preferred_element_type=f32)]
    pallas_call x1 -> x2, Pallas kernels: 12.1 us -> 21.5 us  [the longest x1 17.7 us: adjoint_scan(): pl.pallas_call(adjoint_kernel, out_shape=(full, full, full, jax.ShapeDtyp...]
    reduce_scatter x1, waiting for transfers between devices: 0.01 us -> 8.36 us  [on_device(): pack_sum = lax.psum_scatter(back_swap, 'z', scatter_dimension=0, tiled=True)]
    pallas_call x3 -> x2, Pallas kernels: 24 us -> 17.1 us  [gather_groups(): pl.pallas_call(functools.partial(groups_kernel, count), out_shape=jax.Sha...]
    ppermute x0 -> x3, waiting for transfers between devices: none -> 6.82 us  [on_device(): lax.ppermute(heads, 'z', [(i + hop, i) for i in range(count - hop)])]
    unnamed x100 -> x80, local copies, waits for them, and re-layouts: 15 us -> 13.8 us
  transfers between devices with their start and end apart: 25 -> 28, of which waited for: 2 -> 5; matrix products, arithmetic and copies ran while one was open for 27% -> 23% of each run, Pallas kernels for 57% -> 59%
where the time goes in v5:
time: 653 us; the launch traced here: 645 us
  Pallas kernels  413 us (63%)
  matrix products  81.9 us (13%)
  other arithmetic  54.2 us (8%)
  local copies, waits for them, and re-layouts  36 us (6%)
  starting transfers between devices  24.1 us (4%)
  waiting for transfers between devices  18.7 us (3%)
  between operations  17 us (3%)
    pallas_call x1, Pallas kernels, scatter_dot(): pl.pallas_call(scatter_dot_kernel, out_shape=(jax.ShapeDtypeStruct((rows,...  59.7 us
    pallas_call x1, Pallas kernels, gather_exchange(): pl.pallas_call(gather_kernel, out_shape=(jax.ShapeDtypeStruct((NF, rows,...  59.2 us
    pallas_call x1, Pallas kernels, scatter_feature(): pl.pallas_call(scatter_kernel, out_shape=jax.ShapeDtypeStruct((rows, widt...  46.3 us
    pallas_call x1, Pallas kernels, gather_feature(): pl.pallas_call(gather_kernel, out_shape=jax.ShapeDtypeStruct((NF, rows, w...  40.1 us
    pallas_call x4, Pallas kernels, exchange(): pl.pallas_call(functools.partial(exchange_kernel, axes), out_shape=tuple(...  35.5 us
    pallas_call x1, Pallas kernels, gated_unit(): pl.pallas_call(gated_kernel, grid=(steps,), out_shape=(jax.ShapeDtypeStru...  31.2 us
    pallas_call x1, Pallas kernels, backward_scan(): pl.pallas_call(backward_kernel, out_shape=(jax.ShapeDtypeStruct((rows, 2...  22.2 us
    pallas_call x1, Pallas kernels, gather_tail(): pl.pallas_call(gather_tail_kernel, out_shape=jax.ShapeDtypeStruct((NF, ro...  18.6 us
  transfers between devices with their start and end apart: 28, of which 5 were waited for; matrix products, arithmetic and copies ran while one was open for 23% of the time, Pallas kernels for 59%

profile of v5, /device:TPU:0, one launch (start us, length us, event | category | flops | bytes accessed | tf_op | source)
XLA Modules:
  0.0 645.2 jit_solution(10516397166941776282)
XLA Ops:
  13.9 2.2 split_blocks.2
  16.2 2.1 pad_maximum_fusion.refs_0_
  18.2 15.6 %exchange.4 = bf16[8,80,640]{2,1,0:T(8,128)(2,1)} custom-call(bf16[8,80,640]{2,1,0:T(8,128)(2,1)} %pad_maximum_fusion.refs_0_), custom_call_target="tpu_custom_call" | custom-call | bytes 45000000 | tf_op jit(solution)/shard_map/exchange/pallas_call | solution.py:604
  33.9 2.0 slice.195
  38.3 8.4 %gather_groups.2 = f32[4,8,512]{2,1,0:T(8,128)} custom-call(f32[8,512]{1,0:T(8,128)} %fusion.57.x_ref), custom_call_target="tpu_custom_call" | custom-call | bytes 15000000 | tf_op jit(solution)/shard_map/gather_groups/pallas_call | solution.py:667
  46.7 2.9 split_blocks.3.refs_1_
  49.6 59.2 %gather_exchange.1 = (bf16[8,256,2048]{2,1,0:T(8,128)(2,1)}, bf16[8,64,1536]{2,1,0:T(8,128)(2,1)}) custom-call(bf16[256,2048]{1,0:T(8,128)(2,1)} %refs_0_, bf16[8,64,1536]{2,1,0:T(8,128)(2,1)} %split_blocks.3.refs_1_), custom_call_target="tpu_custom_call" | custom-call | bytes 165000000 | tf_op jit(solution)/shard_map/gather_exchange/pallas_call | solution.py:624
  113.8 5.2 fusion
  119.0 11.6 %fusion.15.pre_ref = f32[2048,640]{1,0:T(8,128)} fusion(bf16[2048,640]{1,0:T(8,128)(2,1)} %all-gather.7.cloned.1.call-done.w_ref, bf16[2048,2048]{1,0:T(8,128)(2,1)} %bitcast.142, f32[2048]{0:T(1024)S(1)} %bitcast.175, f32[2048]{0:T(1024)S(1)} %add_rsqrt_fusion), kind=kOutput, calls=%fused_computation.27 | convolution fusion | flops 5385486336 | bytes 16269312 | tf_op jit(solution)/shard_map/dot_general | solution.py:1463
  136.0 3.8 exchange.5
  139.9 1.5 copy.73
  143.5 3.9 collective-permute-start
  149.3 17.0 %forward_scan.1 = (bf16[2048,320]{1,0:T(8,128)(2,1)}, bf16[2048,320]{1,0:T(8,128)(2,1)}, f32[2048,320]{1,0:T(8,128)}, f32[2048,320]{1,0:T(8,128)}, f32[2048,320]{1,0:T(8,128)}, /*index=5*/f32[8,320]{1,0:T(8,128)}) custom-call(s32[8]{0:T(128)} %copy-done.26, f32[2048,640]{1,0:T(8,128)} %fusion.15.pre_ref, f32[8,320]{1,0:T(8,128)} %copy-done.25, ...), custom_call_target="tpu_custom_call" | custom-call | bytes 45000000 | tf_op jit(solution)/shard_map/forward_scan/pallas_call | solution.py:797
  167.6 8.8 %gather_groups.3 = f32[4,8,320]{2,1,0:T(8,128)} custom-call(f32[8,320]{1,0:T(8,128)} %get-tuple-element.135.x_ref), custom_call_target="tpu_custom_call" | custom-call | bytes 15000000 | tf_op jit(solution)/shard_map/gather_groups/pallas_call | solution.py:667
  176.4 2.0 slice.214
  178.4 1.6 collective-permute-start.3
  180.1 1.9 slice.215
  182.0 1.5 collective-permute-start.4
  185.3 2.7 constant_dynamic-update-slice_fusion.3
  188.0 2.3 constant_dynamic-update-slice_fusion.2
  190.3 3.4 fusion.11
  193.7 6.7 %convolution_convert_fusion = bf16[2048,2048]{1,0:T(8,128)(2,1)} fusion(bf16[2048,320]{1,0:T(8,128)(2,1)S(1)} %fusion.11, bf16[320,2432]{1,0:T(8,128)(2,1)S(1)} %bitcast.153), kind=kOutput, calls=%fused_computation.5 | convolution fusion | flops 2688548864 | bytes 11272192 | tf_op jit(solution)/shard_map/dot_general | solution.py:1480
  200.5 1.9 constant_dynamic-update-slice_fusion.1
  202.4 1.9 constant_dynamic-update-slice_fusion.mine_ref
  204.2 46.3 %scatter_feature.1 = f32[256,2048]{1,0:T(8,128)} custom-call(bf16[8,256,2048]{2,1,0:T(8,128)(2,1)} %bitcast.140), custom_call_target="tpu_custom_call" | custom-call | bytes 135000000 | tf_op jit(solution)/shard_map/scatter_feature/pallas_call | solution.py:320
  250.6 2.1 multiply_reduce_fusion.1
  254.2 40.1 %gather_feature.1 = bf16[8,256,2048]{2,1,0:T(8,128)(2,1)} custom-call(bf16[256,2048]{1,0:T(8,128)(2,1)} %multiply_convert_fusion.refs_0_), custom_call_target="tpu_custom_call" | custom-call | bytes 120000000 | tf_op jit(solution)/shard_map/gather_feature/pallas_call | solution.py:123
  294.3 31.2 %gated_unit.1 = (bf16[2048,768]{1,0:T(8,128)(2,1)}, bf16[2048,1536]{1,0:T(8,128)(2,1)}) custom-call(bf16[2048,2048]{1,0:T(8,128)(2,1)} %bitcast.146, bf16[1024,2048]{1,0:T(8,128)(2,1)} %constant_dynamic-update-slice_fusion.mine_ref, bf16[1024,2048]{1,0:T(8,128)(2,1)} %collective-permute-done.5.theirs_ref, ...), custom_call_target="tpu_custom_call" | custom-call | flops 19327352832 | bytes 41943040 | tf_op jit(solution)/shard_map/gated_unit/pallas_call | solution.py:1122
  325.5 9.9 %convolution_convert_fusion.3 = bf16[1024,2048]{1,0:T(8,128)(2,1)S(1)} fusion(bf16[2048,1536]{1,0:T(8,128)(2,1)} %all-gather.9.cloned.1.call-done.w_ref, bf16[2048,1536]{1,0:T(8,128)(2,1)} %get-tuple-element.162), kind=kOutput, calls=%fused_computation.10 | convolution fusion | flops 6444548096 | bytes 13631488 | tf_op jit(solution)/shard_map/dot_general | solution.py:1492
  335.9 7.2 %convolution_convert_fusion.2 = bf16[1024,2048]{1,0:T(8,128)(2,1)S(1)} fusion(bf16[2048,1536]{1,0:T(8,128)(2,1)S(1)} %copy-done.31, bf16[2048,1536]{1,0:T(8,128)(2,1)S(1)} %copy-done.32), kind=kOutput, calls=%fused_computation.9 | convolution fusion | flops 6444548096 | bytes 13631488 | tf_op jit(solution)/shard_map/dot_general | solution.py:1492
  343.1 2.6 fusion.28
  349.2 5.4 fusion.23
  354.5 7.4 %add_convert_fusion = bf16[768,2048]{1,0:T(8,128)(2,1)} fusion(f32[768,2048]{1,0:T(8,128)S(1)} %fusion.23, bf16[1024,2048]{1,0:T(8,128)(2,1)} %constant_dynamic-update-slice_fusion.mine_ref, bf16[2048,768]{1,0:T(8,128)(2,1)S(1)} %copy-done.13), kind=kOutput, calls=%fused_computation.7 | convolution fusion | flops 3224371200 | bytes 15204352 | tf_op jit(solution)/shard_map/dot_general | solution.py:1496
  362.0 14.2 %down_rows.1 = (bf16[1024,2048]{1,0:T(8,128)(2,1)}, bf16[1024,2048]{1,0:T(8,128)(2,1)}) custom-call(bf16[2048,768]{1,0:T(8,128)(2,1)} %get-tuple-element.152.h_ref, bf16[768,2048]{1,0:T(8,128)(2,1)} %all-gather.11.cloned.1.call-done.down_ref.w_ref), custom_call_target="tpu_custom_call" | custom-call | bytes 300000 | tf_op jit(solution)/shard_map/down_rows/pallas_call | solution.py:1169
  376.2 2.9 add_convert_fusion.4
  379.2 16.9 %scatter_tail.1 = f32[256,2048]{1,0:T(8,128)} custom-call(bf16[128,2048]{1,0:T(8,128)(2,1)} %get-tuple-element.150.ny_ref, bf16[128,2048]{1,0:T(8,128)(2,1)} %get-tuple-element.302.nx_ref, bf16[2,128,2048]{2,1,0:T(8,128)(2,1)} %bitcast.163, bf16[2,128,2048]{2,1,0:T(8,128)(2,1)} %collective-permute-done.7.bx_ref, ...), custom_call_target="tpu_custom_call" | custom-call | bytes 48000000 | tf_op jit(solution)/shard_map/scatter_tail/pallas_call | solution.py:532
  396.1 2.3 fusion.17
  398.4 4.0 fusion.66
  404.4 16.8 %convolution_convert_fusion.1 = bf16[2048,1536]{1,0:T(8,128)(2,1)} fusion(bf16[2048,2048]{1,0:T(8,128)(2,1)S(1)} %bitcast.149, bf16[2048,1536]{1,0:T(8,128)(2,1)} %get-tuple-element.162), kind=kOutput, calls=%fused_computation.6 | convolution fusion | flops 12888047616 | bytes 20971520 | tf_op jit(solution)/shard_map/dot_general | solution.py:1518
  421.1 3.1 add_convert_fusion.1
  424.2 2.9 fusion.40
  427.1 3.7 fusion.30
  430.9 18.6 %gather_tail.1 = bf16[8,256,2048]{2,1,0:T(8,128)(2,1)} custom-call(bf16[256,2048]{1,0:T(8,128)(2,1)} %get-tuple-element.161.x_ref, bf16[256,2048]{1,0:T(8,128)(2,1)} %collective-permute-done.9.bx_ref, bf16[256,2048]{1,0:T(8,128)(2,1)} %collective-permute-done.10.by_ref), custom_call_target="tpu_custom_call" | custom-call | bytes 48000000 | tf_op jit(solution)/shard_map/gather_tail/pallas_call | solution.py:445
  451.6 17.7 %adjoint_scan.1 = (f32[2048,320]{1,0:T(8,128)}, f32[2048,320]{1,0:T(8,128)}, f32[2048,320]{1,0:T(8,128)}, f32[8,320]{1,0:T(8,128)}) custom-call(s32[8]{0:T(128)} %copy-done.26, bf16[2048,2048]{1,0:T(8,128)(2,1)} %bitcast.138, bf16[320,2432]{1,0:T(8,128)(2,1)} %bitcast.152, f32[2048,640]{1,0:T(8,128)} %fusion.15.pre_ref, f32[2048,320]{1,0:T(8,128)} %get-tuple-element.171.keep_ref), custom_call_target="tpu_custom_call" | custom-call | bytes 36000000 | tf_op jit(solution)/shard_map/adjoint_scan/pallas_call | solution.py:876
  473.3 4.2 collective-permute-done.12
  477.5 2.6 collective-permute-done.13
  481.0 22.2 %backward_scan.1 = (bf16[2048,640]{1,0:T(8,128)(2,1)}, f32[8,320]{1,0:T(8,128)}, f32[8,320]{1,0:T(8,128)}, f32[320,320]{1,0:T(8,128)}, f32[320,320]{1,0:T(8,128)}) custom-call(s32[8]{0:T(128)} %copy-done.26, f32[2048,320]{1,0:T(8,128)} %get-tuple-element.172.d_mixed_ref, f32[2048,640]{1,0:T(8,128)} %fusion.15.pre_ref, ...), custom_call_target="tpu_custom_call" | custom-call | bytes 63000000 | tf_op jit(solution)/shard_map/backward_scan/pallas_call | solution.py:1039
  505.5 1.5 collective-permute-start.18
  506.9 8.0 %fusion.71.out_ref = f32[320,2048]{1,0:T(8,128)} fusion(bf16[2048,320]{1,0:T(8,128)(2,1)S(1)} %copy-done.21, bf16[2048,2048]{1,0:T(8,128)(2,1)} %bitcast.139), kind=kOutput, calls=%fused_computation.168 | convolution fusion | flops 2684354560 | bytes 12320768 | tf_op jit(solution)/shard_map/dot_general | solution.py:1550
  517.4 1.5 copy-done.15
  518.9 9.0 %convolution_convert_fusion.4 = bf16[2048,640]{1,0:T(8,128)(2,1)} fusion(bf16[2048,640]{1,0:T(8,128)(2,1)S(1)} %fusion.53.a_ref, bf16[2048,2048]{1,0:T(8,128)(2,1)S(1)} %bitcast.145, f32[2048]{0:T(1024)S(1)} %bitcast.176, f32[2048]{0:T(1024)S(1)} %add_rsqrt_fusion), kind=kOutput, calls=%fused_computation.15 | convolution fusion | flops 5386797056 | bytes 13647872 | tf_op jit(solution)/shard_map/dot_general | solution.py:1556
  527.9 2.2 collective-permute-done.19
  530.2 1.5 convert_element_type.330
  533.1 3.8 pack_sums.1.refs_0_
  536.9 3.8 exchange.6
  540.7 2.0 fusion.34
  542.8 1.4 fusion.22
  545.7 59.7 %scatter_dot.1 = (f32[256,2048]{1,0:T(8,128)}, bf16[8,64,1536]{2,1,0:T(8,128)(2,1)}) custom-call(bf16[2048,640]{1,0:T(8,128)(2,1)} %copy-done.15, bf16[2048,640]{1,0:T(8,128)(2,1)} %all-gather.7.cloned.1.call-done.w_ref, bf16[8,64,1536]{2,1,0:T(8,128)(2,1)} %bitcast.166), custom_call_target="tpu_custom_call" | custom-call | bytes 165000000 | tf_op jit(solution)/shard_map/scatter_dot/pallas_call | solution.py:290
  605.4 12.2 %exchange.7.x_ref = bf16[8,64,640]{2,1,0:T(8,128)(2,1)} custom-call(bf16[8,64,640]{2,1,0:T(8,128)(2,1)} %bitcast.168), custom_call_target="tpu_custom_call" | custom-call | bytes 45000000 | tf_op jit(solution)/shard_map/exchange/pallas_call | solution.py:604
  617.6 2.5 join_blocks.2
  620.2 4.0 join_blocks.3
  624.5 1.9 fusion.20
  626.4 8.4 %reduce-scatter.7.cloned.1.call-done.x_ref = bf16[80,2432]{1,0:T(8,128)(2,1)} async-done(((bf16[320,2432]{1,0:T(8,128)(2,1)}), bf16[80,2432]{1,0:T(8,128)(2,1)}) %reduce-scatter.7.cloned.1.call-update) | async-done | bytes 389136 | tf_op jit(solution)/shard_map/reduce_scatter | solution.py:1570
  634.8 1.9 unpack_sums.1
  (192 shorter events, 48.4 us)
Async XLA Ops:
  7.2 8.9 %copy-start.29 = (bf16[64]{0:T(256)(128)(2,1)S(1)}, bf16[64]{0:T(256)(128)(2,1)}, u32[]{:S(2)}) copy-start(bf16[64]{0:T(256)(128)(2,1)} %param.32) | copy-start | bytes 388
  7.2 8.9 %copy-start.27 = (bf16[64]{0:T(256)(128)(2,1)S(1)}, bf16[64]{0:T(256)(128)(2,1)}, u32[]{:S(2)}) copy-start(bf16[64]{0:T(256)(128)(2,1)} %param.21) | copy-start | bytes 388
  7.2 106.5 %all-gather.5.cloned.1.call-start = ((), (), s32[]{:S(2)}) async-start(), calls=%async_computation.4 | async-start | bytes 1945600 | tf_op jit(solution)/shard_map/all_gather | solution.py:1409
  13.1 105.9 %all-gather.7.cloned.1.call-start = ((), (), s32[]{:S(2)}) async-start(), calls=%async_computation.5 | async-start | bytes 3276800 | tf_op jit(solution)/shard_map/all_gather | solution.py:1420
  35.9 258.4 %all-gather.11.cloned.1.call-start = ((), (), s32[]{:S(2)}) async-start(), calls=%async_computation.7 | async-start | bytes 3932160 | tf_op jit(solution)/shard_map/all_gather | solution.py:1438
  36.6 257.7 %all-gather.9.cloned.1.call-start = ((), (), s32[]{:S(2)}) async-start(), calls=%async_computation.6 | async-start | bytes 7864320 | tf_op jit(solution)/shard_map/all_gather | solution.py:1437
  46.6 64.7 %copy-start.12 = (bf16[256,2048]{1,0:T(8,128)(2,1)S(1)}, bf16[256,2048]{1,0:T(8,128)(2,1)}, u32[]{:S(2)}) copy-start(bf16[256,2048]{1,0:T(8,128)(2,1)} %param.20) | copy-start | bytes 3145732
  108.9 340.6 %reduce-scatter.5.cloned.1.call-start = ((), (), s32[]{:S(2)}) async-start(), calls=%async_computation.8 | async-start | bytes 3932160 | tf_op jit(solution)/shard_map/reduce_scatter | solution.py:1509
  113.7 19.8 %copy-start.26 = (s32[8]{0:T(128)}, s32[8]{0:T(128)S(1)}, u32[]{:S(2)}) copy-start(s32[8]{0:T(128)S(1)} %fusion.63.order_ref) | copy-start | bytes 100
  130.6 35.7 %collective-permute-start.1 = (bf16[256,2048]{1,0:T(8,128)(2,1)S(1)}, bf16[256,2048]{1,0:T(8,128)(2,1)S(1)}, u32[]{:S(2)}, u32[]{:S(2)}) collective-permute-start(bf16[256,2048]{1,0:T(8,128)(2,1)S(1)} %copy-done.12), channel_id=1, source_target_pairs={{0,4},{4,0},{1,5},{5,1},{2,6},{6,2},{3,7},{7,3},{8,12},{12,8},{9,1... | collective-permute-start | bytes 3145736 | tf_op jit(solution)/shard_map/ppermute | solution.py:347
  131.5 34.9 %collective-permute-start.2 = (bf16[256,2048]{1,0:T(8,128)(2,1)S(1)}, bf16[256,2048]{1,0:T(8,128)(2,1)S(1)}, u32[]{:S(2)}, u32[]{:S(2)}) collective-permute-start(bf16[256,2048]{1,0:T(8,128)(2,1)S(1)} %copy-done.12), channel_id=1, source_target_pairs={{0,2},{2,0},{1,3},{3,1},{4,6},{6,4},{5,7},{7,5},{8,10},{10,8},{9,1... | collective-permute-start | bytes 3145736 | tf_op jit(solution)/shard_map/ppermute | solution.py:347
  141.4 6.0 copy-start.7
  143.5 5.2 collective-permute-start
  166.3 1.0 copy-start.16
  166.3 1.3 copy-start.17
  176.4 13.9 %copy-start.2 = (f32[2048,320]{1,0:T(8,128)S(1)}, f32[2048,320]{1,0:T(8,128)}, u32[]{:S(2)}) copy-start(f32[2048,320]{1,0:T(8,128)} %get-tuple-element.132.prod_ref.prod_before_ref) | copy-start | bytes 7864324
  178.4 22.0 %collective-permute-start.3 = (bf16[128,2048]{1,0:T(8,128)(2,1)}, bf16[128,2048]{1,0:T(8,128)(2,1)}, u32[]{:S(2)}, u32[]{:S(2)}) collective-permute-start(bf16[128,2048]{1,0:T(8,128)(2,1)} %slice.214), channel_id=1, source_target_pairs={{0,2},{2,0},{1,3},{3,1},{4,6},{6,4},{5,7},{7,5},{8,10},{10,8},{9,1... | collective-permute-start | bytes 1572872 | tf_op jit(solution)/shard_map/ppermute | solution.py:347
  182.0 18.5 %collective-permute-start.4 = (bf16[128,2048]{1,0:T(8,128)(2,1)}, bf16[128,2048]{1,0:T(8,128)(2,1)}, u32[]{:S(2)}, u32[]{:S(2)}) collective-permute-start(bf16[128,2048]{1,0:T(8,128)(2,1)} %slice.215), channel_id=1, source_target_pairs={{0,4},{4,0},{1,5},{5,1},{2,6},{6,2},{3,7},{7,3},{8,12},{12,8},{9,1... | collective-permute-start | bytes 1572872 | tf_op jit(solution)/shard_map/ppermute | solution.py:347
  184.3 6.0 copy-start.3
  190.3 3.4 copy-start.8
  193.7 6.7 %copy-start.20 = (bf16[2048,320]{1,0:T(8,128)(2,1)}, bf16[2048,320]{1,0:T(8,128)(2,1)S(1)}, u32[]{:S(2)}) copy-start(bf16[2048,320]{1,0:T(8,128)(2,1)S(1)} %fusion.11) | copy-start | bytes 3932164
  204.2 90.1 %collective-permute-start.5 = (bf16[1024,2048]{1,0:T(8,128)(2,1)}, bf16[1024,2048]{1,0:T(8,128)(2,1)}, u32[]{:S(2)}, u32[]{:S(2)}) collective-permute-start(bf16[1024,2048]{1,0:T(8,128)(2,1)} %constant_dynamic-update-slice_fusion.mine_ref), channel_id=1, source_target_pairs={{0,1},{1,0},{2,3},{3,2},{4,5},{5,4},{6,7},{7,6},{8,9},{9,8},{10,11... | collective-permute-start | bytes 12582920 | tf_op jit(solution)/shard_map/ppermute | solution.py:347
  204.2 46.4 %copy-start.1 = (bf16[256,2048]{1,0:T(8,128)(2,1)S(1)}, bf16[256,2048]{1,0:T(8,128)(2,1)}, u32[]{:S(2)}) copy-start(bf16[256,2048]{1,0:T(8,128)(2,1)} %refs_0_) | copy-start | bytes 3145732
  250.6 2.3 copy-start
  325.5 10.4 %copy-start.31 = (bf16[2048,1536]{1,0:T(8,128)(2,1)S(1)}, bf16[2048,1536]{1,0:T(8,128)(2,1)}, u32[]{:S(2)}) copy-start(bf16[2048,1536]{1,0:T(8,128)(2,1)} %all-gather.9.cloned.1.call-done.w_ref) | copy-start | bytes 18874372
  325.5 10.4 %copy-start.32 = (bf16[2048,1536]{1,0:T(8,128)(2,1)S(1)}, bf16[2048,1536]{1,0:T(8,128)(2,1)}, u32[]{:S(2)}) copy-start(bf16[2048,1536]{1,0:T(8,128)(2,1)} %get-tuple-element.162) | copy-start | bytes 18874372
  335.5 7.6 %collective-permute-start.6 = (bf16[1024,2048]{1,0:T(8,128)(2,1)S(1)}, bf16[1024,2048]{1,0:T(8,128)(2,1)S(1)}, u32[]{:S(2)}, u32[]{:S(2)}) collective-permute-start(bf16[1024,2048]{1,0:T(8,128)(2,1)S(1)} %convolution_convert_fusion.3), channel_id=1, source_target_pairs={{0,1},{1,0},{2,3},{3,2},{4,5},{5,4},{6,7},{7,6},{8,9},{9,8},{10,11... | collective-permute-start | bytes 12582920 | tf_op jit(solution)/shard_map/ppermute | solution.py:347
  343.1 11.5 %copy-start.11 = (bf16[1024,2048]{1,0:T(8,128)(2,1)}, bf16[1024,2048]{1,0:T(8,128)(2,1)S(1)}, u32[]{:S(2)}) copy-start(bf16[1024,2048]{1,0:T(8,128)(2,1)S(1)} %convolution_convert_fusion.2) | copy-start | bytes 12582916
  343.1 2.7 copy-start.10
  345.7 3.4 copy-start.13
  347.1 32.0 %collective-permute-start.7 = (bf16[2,128,2048]{2,1,0:T(8,128)(2,1)}, bf16[2,128,2048]{2,1,0:T(8,128)(2,1)}, u32[]{:S(2)}, u32[]{:S(2)}) collective-permute-start(bf16[2,128,2048]{2,1,0:T(8,128)(2,1)} %get-tuple-element.155), channel_id=1, source_target_pairs={{0,4},{4,0},{1,5},{5,1},{2,6},{6,2},{3,7},{7,3},{8,12},{12,8},{9,1... | collective-permute-start | bytes 3145736 | tf_op jit(solution)/shard_map/ppermute | solution.py:347
  348.5 30.6 %collective-permute-start.8 = (bf16[2,128,2048]{2,1,0:T(8,128)(2,1)}, bf16[2,128,2048]{2,1,0:T(8,128)(2,1)}, u32[]{:S(2)}, u32[]{:S(2)}) collective-permute-start(bf16[2,128,2048]{2,1,0:T(8,128)(2,1)} %get-tuple-element.156), channel_id=1, source_target_pairs={{0,2},{2,0},{1,3},{3,1},{4,6},{6,4},{5,7},{7,5},{8,10},{10,8},{9,1... | collective-permute-start | bytes 3145736 | tf_op jit(solution)/shard_map/ppermute | solution.py:347
  361.9 183.7 %reduce-scatter.9.cloned.1.call-start = ((), (), s32[]{:S(2)}) async-start(), calls=%async_computation.10 | async-start | bytes 7864320 | tf_op jit(solution)/shard_map/reduce_scatter | solution.py:1526
  379.2 25.2 %slice-start.2 = ((s8[8388608]{0:T(1024)(128)(4,1)}), s8[4194304]{0:T(1024)(128)(4,1)S(1)}, s32[]{:S(2)}) async-start(s8[8388608]{0:T(1024)(128)(4,1)} %bitcast.147), calls=%async_computation.14 | async-start | bytes 8388608
  396.1 2.3 copy-start.4
  396.1 8.3 %slice-start.3 = ((s8[8388608]{0:T(1024)(128)(4,1)}), s8[4194304]{0:T(1024)(128)(4,1)S(1)}, s32[]{:S(2)}) async-start(s8[8388608]{0:T(1024)(128)(4,1)} %bitcast.147), calls=%async_computation.15 | async-start | bytes 8388608
  402.4 18.7 %collective-permute-start.11 = (bf16[1024,2048]{1,0:T(8,128)(2,1)}, bf16[1024,2048]{1,0:T(8,128)(2,1)}, u32[]{:S(2)}, u32[]{:S(2)}) collective-permute-start(bf16[1024,2048]{1,0:T(8,128)(2,1)} %get-tuple-element.164), channel_id=1, source_target_pairs={{0,1},{1,0},{2,3},{3,2},{4,5},{5,4},{6,7},{7,6},{8,9},{9,8},{10,11... | collective-permute-start | bytes 12582920 | tf_op jit(solution)/shard_map/ppermute | solution.py:347
  402.4 28.4 %collective-permute-start.9 = (bf16[256,2048]{1,0:T(8,128)(2,1)}, bf16[256,2048]{1,0:T(8,128)(2,1)}, u32[]{:S(2)}, u32[]{:S(2)}) collective-permute-start(bf16[256,2048]{1,0:T(8,128)(2,1)} %get-tuple-element.161.x_ref), channel_id=1, source_target_pairs={{0,4},{4,0},{1,5},{5,1},{2,6},{6,2},{3,7},{7,3},{8,12},{12,8},{9,1... | collective-permute-start | bytes 3145736 | tf_op jit(solution)/shard_map/ppermute | solution.py:347
  403.0 27.8 %collective-permute-start.10 = (bf16[256,2048]{1,0:T(8,128)(2,1)}, bf16[256,2048]{1,0:T(8,128)(2,1)}, u32[]{:S(2)}, u32[]{:S(2)}) collective-permute-start(bf16[256,2048]{1,0:T(8,128)(2,1)} %get-tuple-element.161.x_ref), channel_id=1, source_target_pairs={{0,2},{2,0},{1,3},{3,1},{4,6},{6,4},{5,7},{7,5},{8,10},{10,8},{9,1... | collective-permute-start | bytes 3145736 | tf_op jit(solution)/shard_map/ppermute | solution.py:347
  421.1 6.0 copy-start.9
  430.8 174.6 %reduce-scatter.11.cloned.1.call-start = ((), (), s32[]{:S(2)}) async-start(), calls=%async_computation.11 | async-start | bytes 3276800 | tf_op jit(solution)/shard_map/reduce_scatter | solution.py:1563
  449.5 30.7 %collective-permute-start.15 = (bf16[2,128,2048]{2,1,0:T(8,128)(2,1)}, bf16[2,128,2048]{2,1,0:T(8,128)(2,1)S(1)}, u32[]{:S(2)}, u32[]{:S(2)}) collective-permute-start(bf16[2,128,2048]{2,1,0:T(8,128)(2,1)} %get-tuple-element.178), channel_id=1, source_target_pairs={{0,4},{4,0},{1,5},{5,1},{2,6},{6,2},{3,7},{7,3},{8,12},{12,8},{9,1... | collective-permute-start | bytes 3145736 | tf_op jit(solution)/shard_map/ppermute | solution.py:347
  450.4 29.7 %collective-permute-start.16 = (bf16[2,128,2048]{2,1,0:T(8,128)(2,1)}, bf16[2,128,2048]{2,1,0:T(8,128)(2,1)S(1)}, u32[]{:S(2)}, u32[]{:S(2)}) collective-permute-start(bf16[2,128,2048]{2,1,0:T(8,128)(2,1)} %get-tuple-element.179), channel_id=1, source_target_pairs={{0,2},{2,0},{1,3},{3,1},{4,6},{6,4},{5,7},{7,5},{8,10},{10,8},{9,1... | collective-permute-start | bytes 3145736 | tf_op jit(solution)/shard_map/ppermute | solution.py:347
  469.3 8.2 %collective-permute-start.12 = (f32[8,320]{1,0:T(8,128)}, f32[8,320]{1,0:T(8,128)S(1)}, u32[]{:S(2)}, u32[]{:S(2)}) collective-permute-start(f32[8,320]{1,0:T(8,128)} %get-tuple-element.177), channel_id=1, source_target_pairs={{24,0},{25,1},{26,2},{27,3},{28,4},{29,5},{30,6},{31,7}} | collective-permute-start | bytes 30728 | tf_op jit(solution)/shard_map/ppermute | solution.py:1535
  470.6 9.5 %collective-permute-start.13 = (f32[8,320]{1,0:T(8,128)}, f32[8,320]{1,0:T(8,128)S(1)}, u32[]{:S(2)}, u32[]{:S(2)}) collective-permute-start(f32[8,320]{1,0:T(8,128)} %get-tuple-element.177), channel_id=1, source_target_pairs={{16,0},{24,8},{17,1},{25,9},{18,2},{26,10},{19,3},{27,11},{20,4},{... | collective-permute-start | bytes 30728 | tf_op jit(solution)/shard_map/ppermute | solution.py:1535
  471.9 8.2 %collective-permute-start.14 = (f32[8,320]{1,0:T(8,128)}, f32[8,320]{1,0:T(8,128)S(1)}, u32[]{:S(2)}, u32[]{:S(2)}) collective-permute-start(f32[8,320]{1,0:T(8,128)} %get-tuple-element.177), channel_id=1, source_target_pairs={{8,0},{16,8},{24,16},{9,1},{17,9},{25,17},{10,2},{18,10},{26,18},{... | collective-permute-start | bytes 30728 | tf_op jit(solution)/shard_map/ppermute | solution.py:1535
  480.1 24.4 %copy-start.22 = (bf16[2,128,2048]{2,1,0:T(8,128)(2,1)}, bf16[2,128,2048]{2,1,0:T(8,128)(2,1)S(1)}, u32[]{:S(2)}) copy-start(bf16[2,128,2048]{2,1,0:T(8,128)(2,1)S(1)} %collective-permute-done.15) | copy-start | bytes 3145732
  480.1 34.8 %copy-start.23 = (bf16[2,128,2048]{2,1,0:T(8,128)(2,1)}, bf16[2,128,2048]{2,1,0:T(8,128)(2,1)S(1)}, u32[]{:S(2)}) copy-start(bf16[2,128,2048]{2,1,0:T(8,128)(2,1)S(1)} %collective-permute-done.16) | copy-start | bytes 3145732
  481.0 23.5 %copy-start.19 = (bf16[128,2048]{1,0:T(8,128)(2,1)S(1)}, bf16[128,2048]{1,0:T(8,128)(2,1)}, u32[]{:S(2)}) copy-start(bf16[128,2048]{1,0:T(8,128)(2,1)} %get-tuple-element.191) | copy-start | bytes 1572868
  481.0 25.9 %copy-start.21 = (bf16[2048,320]{1,0:T(8,128)(2,1)S(1)}, bf16[2048,320]{1,0:T(8,128)(2,1)}, u32[]{:S(2)}) copy-start(bf16[2048,320]{1,0:T(8,128)(2,1)} %copy-done.20) | copy-start | bytes 3932164
  503.2 14.1 %collective-permute-start.17 = (f32[8,320]{1,0:T(8,128)}, f32[8,320]{1,0:T(8,128)S(1)}, u32[]{:S(2)}, u32[]{:S(2)}) collective-permute-start(f32[8,320]{1,0:T(8,128)} %get-tuple-element.183), channel_id=1, source_target_pairs={{8,0},{16,8},{24,16},{9,1},{17,9},{25,17},{10,2},{18,10},{26,18},{... | collective-permute-start | bytes 30728 | tf_op jit(solution)/shard_map/ppermute | solution.py:1548
  504.5 14.4 %slice-start = ((s8[8388608]{0:T(1024)(128)(4,1)}), s8[4194304]{0:T(1024)(128)(4,1)S(1)}, s32[]{:S(2)}) async-start(s8[8388608]{0:T(1024)(128)(4,1)} %bitcast.143), calls=%async_computation.12 | async-start | bytes 8388608
  505.4 9.5 %copy-start.18 = (bf16[128,2048]{1,0:T(8,128)(2,1)S(1)}, bf16[128,2048]{1,0:T(8,128)(2,1)}, u32[]{:S(2)}) copy-start(bf16[128,2048]{1,0:T(8,128)(2,1)} %get-tuple-element.193) | copy-start | bytes 1572868
  505.5 11.9 %copy-start.14 = (bf16[2048,640]{1,0:T(8,128)(2,1)S(1)}, bf16[2048,640]{1,0:T(8,128)(2,1)}, u32[]{:S(2)}) copy-start(bf16[2048,640]{1,0:T(8,128)(2,1)} %get-tuple-element.186) | copy-start | bytes 7864324
  505.5 13.5 %slice-start.1 = ((s8[8388608]{0:T(1024)(128)(4,1)}), s8[4194304]{0:T(1024)(128)(4,1)S(1)}, s32[]{:S(2)}) async-start(s8[8388608]{0:T(1024)(128)(4,1)} %bitcast.143), calls=%async_computation.13 | async-start | bytes 8388608
  505.5 22.5 %collective-permute-start.18 = (bf16[128,2048]{1,0:T(8,128)(2,1)}, bf16[128,2048]{1,0:T(8,128)(2,1)}, u32[]{:S(2)}, u32[]{:S(2)}) collective-permute-start(bf16[128,2048]{1,0:T(8,128)(2,1)} %fusion.36), channel_id=1, source_target_pairs={{0,2},{2,0},{1,3},{3,1},{4,6},{6,4},{5,7},{7,5},{8,10},{10,8},{9,1... | collective-permute-start | bytes 1572872 | tf_op jit(solution)/shard_map/ppermute | solution.py:347
  515.9 14.3 %collective-permute-start.19 = (bf16[128,2048]{1,0:T(8,128)(2,1)}, bf16[128,2048]{1,0:T(8,128)(2,1)}, u32[]{:S(2)}, u32[]{:S(2)}) collective-permute-start(bf16[128,2048]{1,0:T(8,128)(2,1)} %fusion.35), channel_id=1, source_target_pairs={{0,4},{4,0},{1,5},{5,1},{2,6},{6,2},{3,7},{7,3},{8,12},{12,8},{9,1... | collective-permute-start | bytes 1572872 | tf_op jit(solution)/shard_map/ppermute | solution.py:347
  517.4 1.5 copy-start.15
  530.2 104.6 %reduce-scatter.7.cloned.1.call-start = ((), (), s32[]{:S(2)}) async-start(), calls=%async_computation.9 | async-start | bytes 1945600 | tf_op jit(solution)/shard_map/reduce_scatter | solution.py:1570
  530.2 1.6 copy-start.24
  542.7 1.5 copy-start.28
  542.7 2.2 copy-start.30
  605.4 18.7 %copy-start.5 = (f32[256,2048]{1,0:T(8,128)S(1)}, f32[256,2048]{1,0:T(8,128)}, u32[]{:S(2)}) copy-start(f32[256,2048]{1,0:T(8,128)} %get-tuple-element.215) | copy-start | bytes 6291460
  620.1 4.3 copy-start.6
  (1 other events, 0.6 us)
Sparse Core Ops, SparseCore 0:
  13.2 40.9 all-gather.4
  56.3 53.5 all-gather.6
  111.5 62.2 all-gather.10
  175.2 114.0 all-gather.8
  362.1 60.2 reduce-scatter.4
  430.9 111.6 reduce-scatter.8
  544.9 52.5 reduce-scatter.10
  599.9 34.8 reduce-scatter.6

commit v6 on v5

--- a/solution.py
+++ b/solution.py
@@ -68,8 +68,11 @@
         x_ref, o_ref, local_sem, ssem, rsem = refs
         extra = ()
     else:
-        x_ref, b_ref, o_ref, e_ref, local_sem, ssem, rsem, *sems = refs
-        extra = exchange_parts(FEAT, b_ref, e_ref, *sems)
+        x_ref, b_ref, s_ref, t_ref, o_ref, e_ref, so_ref, to_ref = refs[:8]
+        local_sem, ssem, rsem = refs[8:11]
+        peers, kept, copies = exchange_parts(FEAT, b_ref, e_ref, *refs[11:14])
+        others, own_small, small = groups_parts((s_ref, t_ref), (so_ref, to_ref), *refs[14:])
+        extra = (peers + others, [kept] + own_small, copies + small)
     x, y, c = feature_place()
     to_x, to_y, to_c = {"x": 1 - x}, {"y": 1 - y}, {"c": 1 - c}
     half = x_ref.shape[0] // 2
@@ -93,8 +96,7 @@
     for one in (x_top, y_low, x_low, y_top, c_own, own):
         one.start()
     if extra:
-        extra[1].start()
-        for one in extra[2]:
+        for one in extra[1] + extra[2]:
             one.start()
     x_top.wait_recv()
     y_fwd.start()
@@ -113,9 +115,8 @@
         one.wait_send()
     own.wait()
     if extra:
-        for one in extra[2]:
+        for one in extra[2] + extra[1]:
             one.wait()
-        extra[1].wait()
 
 
 def gather_feature(block):
@@ -619,16 +620,17 @@
     )(*arrays)
 
 
-def gather_exchange(block, blocks):
+def gather_exchange(block, blocks, smalls, count):
     rows, width = block.shape
-    out, got = pl.pallas_call(
+    out, got, *small = pl.pallas_call(
         gather_kernel,
         out_shape=(
             jax.ShapeDtypeStruct((NF, rows, width), block.dtype),
             jax.ShapeDtypeStruct(blocks.shape, blocks.dtype),
-        ),
-        in_specs=[vmem_spec()] * 2,
-        out_specs=(hbm_spec(),) * 2,
+        )
+        + tuple(jax.ShapeDtypeStruct((count,) + a.shape, a.dtype) for a in smalls),
+        in_specs=[vmem_spec()] * 4,
+        out_specs=(hbm_spec(),) * 2 + (vmem_spec(),) * 2,
         scratch_shapes=[
             pltpu.SemaphoreType.DMA,
             pltpu.SemaphoreType.DMA((10,)),
@@ -636,48 +638,61 @@
             pltpu.SemaphoreType.DMA,
             pltpu.SemaphoreType.DMA((NF - 1,)),
             pltpu.SemaphoreType.DMA((NF - 1,)),
+            pltpu.SemaphoreType.DMA((2,)),
+            pltpu.SemaphoreType.DMA((2, count - 1)),
+            pltpu.SemaphoreType.DMA((2, count - 1)),
         ],
         compiler_params=pltpu.CompilerParams(
             collective_id=4, has_side_effects=True, vmem_limit_bytes=VMEM_LIMIT
         ),
         cost_estimate=cost(55),
         name="gather_exchange",
-    )(block, blocks)
-    return out.reshape(NF * rows, width), got
-
-
-def groups_kernel(count, x_ref, o_ref, local_sem, ssem, rsem):
+    )(block, blocks, *smalls)
+    return out.reshape(NF * rows, width), got, *small
+
+
+def groups_parts(sources, targets, local_sem, ssem, rsem):
+    count = targets[0].shape[0]
     z = lax.axis_index("z")
-    own = pltpu.make_async_copy(x_ref, o_ref.at[z], local_sem)
-    own.start()
-    targets = [{"z": lax.rem(z + hop, count)} for hop in range(1, count)]
-    greet(targets)
+    many = range(len(sources))
+    own = [pltpu.make_async_copy(sources[k], targets[k].at[z], local_sem.at[k]) for k in many]
+    peers = [{"z": lax.rem(z + hop, count)} for hop in range(1, count)]
     copies = [
-        remote(x_ref, o_ref.at[z], ssem.at[i], rsem.at[i], device)
-        for i, device in enumerate(targets)
+        remote(sources[k], targets[k].at[z], ssem.at[k, i], rsem.at[k, i], device)
+        for k in many
+        for i, device in enumerate(peers)
     ]
+    return peers, own, copies
+
+
+def groups_kernel(*refs):
+    many = (len(refs) - 3) // 2
+    peers, own, copies = groups_parts(refs[:many], refs[many : 2 * many], *refs[2 * many :])
+    for one in own:
+        one.start()
+    greet(peers)
     for one in copies:
         one.start()
-    for one in copies:
+    for one in copies + own:
         one.wait()
-    own.wait()
-
-
-def gather_groups(block, count, ident):
+
+
+def gather_groups(blocks, count, ident):
+    many = len(blocks)
     return pl.pallas_call(
-        functools.partial(groups_kernel, count),
-        out_shape=jax.ShapeDtypeStruct((count,) + block.shape, block.dtype),
-        in_specs=[vmem_spec()],
-        out_specs=vmem_spec(),
+        groups_kernel,
+        out_shape=tuple(jax.ShapeDtypeStruct((count,) + b.shape, b.dtype) for b in blocks),
+        in_specs=[vmem_spec()] * many,
+        out_specs=(vmem_spec(),) * many,
         scratch_shapes=[
-            pltpu.SemaphoreType.DMA,
-            pltpu.SemaphoreType.DMA((count - 1,)),
-            pltpu.SemaphoreType.DMA((count - 1,)),
+            pltpu.SemaphoreType.DMA((many,)),
+            pltpu.SemaphoreType.DMA((many, count - 1)),
+            pltpu.SemaphoreType.DMA((many, count - 1)),
         ],
         compiler_params=pltpu.CompilerParams(collective_id=ident, has_side_effects=True),
         cost_estimate=cost(5),
         name="gather_groups",
-    )(block)
+    )(*blocks)
 
 
 def gelu_tanh(values):
@@ -1375,7 +1390,6 @@
 
     pack = jnp.concatenate(
         [
-            rec_out_weight,
             gate_a_weight,
             gate_x_weight,
             conv_weight,
@@ -1387,8 +1401,9 @@
         axis=1,
     )
     used = pack.shape[1]
-    pack_width = -(-used // LANES) * LANES
-    pack = pad_lanes(pack, pack_width)
+    extra_width = -(-used // LANES) * LANES
+    pack_width = width + extra_width
+    pack = pad_lanes(pack, extra_width)
 
     extra = jnp.concatenate(
         [
@@ -1406,7 +1421,7 @@
         ],
         axis=1,
     )
-    pack_all = lax.all_gather(pack, "z", axis=0, tiled=True)
+    out_all = lax.all_gather(rec_out_weight, "z", axis=0, tiled=True)
     (rec_got,) = exchange([rec_send], FEAT, 3)
     starts = rec_got[:, rows_w, :rows_tok].reshape(group_rows).astype(f32)
 
@@ -1416,16 +1431,20 @@
             rec_got[:, rows_w + 2, :rows_w].reshape(NF * rows_w),
         ]
     ).astype(f32)
-    gains = gather_groups(jnp.pad(plane_gains, ((0, 6), (0, 0))), count, 7)
-    w_rec = lax.all_gather(
-        rec_got[:, :rows_w].reshape(NF * rows_w, 2 * chans), "z", axis=0, tiled=True
-    )
+    rec_mine = rec_got[:, :rows_w].reshape(NF * rows_w, 2 * chans)
+    w_rec = lax.all_gather(rec_mine, "z", axis=0, tiled=True)
     mlp_send = split_blocks(mlp_gate_weight, mlp_up_weight, ff_moves)
-    tokens_own, gains = hold(tokens_in, gains)
-    tok_group, mlp_got = gather_exchange(tokens_own, mlp_send)
-    tok_group, pack_all = hold(tok_group, pack_all)
-    (pack_swap,) = exchange(
-        [pack_all.reshape(spread, 2, chan_rows, pack_width)], swap_axes, 5
+    tok_group, mlp_got, gains, pack_all = gather_exchange(
+        tokens_in, mlp_send, [jnp.pad(plane_gains, ((0, 6), (0, 0))), pack], count
+    )
+    tok_group, pack_all, out_all = hold(tok_group, pack_all, out_all)
+    out_swap, pack_swap = exchange(
+        [
+            out_all.reshape(spread, 2, chan_rows, width),
+            pack_all.reshape(spread, 2, chan_rows, extra_width),
+        ],
+        swap_axes,
+        12,
     )
     gain_one = gains[:, 0].reshape(1, width)
     gain_two = gains[:, 1].reshape(1, width)
@@ -1437,9 +1456,9 @@
     w_mlp = lax.all_gather(mlp_got.reshape(NF * rows_w, 2 * ff), "z", axis=0, tiled=True)
     w_down = lax.all_gather(mlp_down_weight, "z", axis=0, tiled=True)
 
-    mine = pack_swap.transpose(1, 0, 2, 3).reshape(chans, pack_width)
-    w_out = mine[:, :width]
-    small = mine[:, width + 2 * BLK : used].astype(f32).T
+    w_out = out_swap.transpose(1, 0, 2, 3).reshape(chans, width)
+    mine = pack_swap.transpose(1, 0, 2, 3).reshape(chans, extra_width)
+    small = mine[:, 2 * BLK : used].astype(f32).T
 
     unit = lax.broadcasted_iota(jnp.int32, (chans, chans), 0) // BLK
     same_block = unit == lax.broadcasted_iota(jnp.int32, (chans, chans), 1) // BLK
@@ -1447,8 +1466,8 @@
     def block_diag(w):
         return jnp.where(same_block, jnp.concatenate([w, w], axis=1), jnp.zeros((), w.dtype))
 
-    wa = block_diag(mine[:, width : width + BLK])
-    wx = block_diag(mine[:, width + BLK : width + 2 * BLK])
+    wa = block_diag(mine[:, :BLK])
+    wx = block_diag(mine[:, BLK : 2 * BLK])
 
     open_one = 1.0 - starts
     ahead = jnp.concatenate([jnp.ones((TAIL,), f32), open_one])
@@ -1472,7 +1491,7 @@
     )
     ends, cot_x, cot_y = hold(ends, cot_x, cot_y)
     cot_top, cot_low = gather_diagonal(cot_x, cot_y)
-    ends = gather_groups(ends, count, 2)
+    (ends,) = gather_groups([ends], count, 2)
     state_in = jnp.zeros((1, chans), f32)
     for hop in range(count - 1):
         state_in = jnp.where(hop < z, ends[hop, 0:1] * state_in + ends[hop, 1:2], state_in)
@@ -1529,7 +1548,7 @@
     out_x, out_y = across(out_x, "x"), across(out_y, "y")
 
     d_mixed, adj_prod, adj_local, heads = adjoint_scan(
-        order, d_rec, mine, rec_pre, keep, chunk
+        order, d_rec, w_out, rec_pre, keep, chunk
     )
     from_later = [
         lax.ppermute(heads, "z", [(i + hop, i) for i in range(count - hop)])

time: 653 us -> 641 us (0.982)
  Pallas kernels: 413 us -> 406 us
    pallas_call x2 -> x1, Pallas kernels: 17.1 us -> 7.02 us  [gather_groups(): pl.pallas_call(groups_kernel, out_shape=tuple((jax.ShapeDtypeStruct((coun...]
    unnamed x80 -> x88, local copies, waits for them, and re-layouts: 13.8 us -> 13.5 us
  transfers between devices with their start and end apart: 28 -> 28, of which waited for: 5 -> 4; matrix products, arithmetic and copies ran while one was open for 23% -> 24% of each run, Pallas kernels for 59% -> 59%
where the time goes in v6:
time: 641 us; the launch traced here: 633 us
  Pallas kernels  406 us (63%)
  matrix products  81.8 us (13%)
  other arithmetic  54.8 us (9%)
  local copies, waits for them, and re-layouts  33.8 us (5%)
  starting transfers between devices  22.2 us (3%)
  waiting for transfers between devices  17.7 us (3%)
  between operations  17 us (3%)
    pallas_call x1, Pallas kernels, gather_exchange(): pl.pallas_call(gather_kernel, out_shape=(jax.ShapeDtypeStruct((NF, rows,...  61.9 us
    pallas_call x1, Pallas kernels, scatter_dot(): pl.pallas_call(scatter_dot_kernel, out_shape=(jax.ShapeDtypeStruct((rows,...  59.7 us
    pallas_call x1, Pallas kernels, scatter_feature(): pl.pallas_call(scatter_kernel, out_shape=jax.ShapeDtypeStruct((rows, widt...  46.3 us
    pallas_call x1, Pallas kernels, gather_feature(): pl.pallas_call(gather_kernel, out_shape=jax.ShapeDtypeStruct((NF, rows, w...  40.6 us
    pallas_call x4, Pallas kernels, exchange(): pl.pallas_call(functools.partial(exchange_kernel, axes), out_shape=tuple(...  35.5 us
    pallas_call x1, Pallas kernels, gated_unit(): pl.pallas_call(gated_kernel, grid=(steps,), out_shape=(jax.ShapeDtypeStru...  31.2 us
    pallas_call x1, Pallas kernels, backward_scan(): pl.pallas_call(backward_kernel, out_shape=(jax.ShapeDtypeStruct((rows, 2...  22.2 us
    pallas_call x1, Pallas kernels, gather_tail(): pl.pallas_call(gather_tail_kernel, out_shape=jax.ShapeDtypeStruct((NF, ro...  18.6 us
  transfers between devices with their start and end apart: 28, of which 4 were waited for; matrix products, arithmetic and copies ran while one was open for 24% of the time, Pallas kernels for 59%

profile of v6, /device:TPU:0, one launch (start us, length us, event | category | flops | bytes accessed | tf_op | source)
XLA Modules:
  0.0 633.1 jit_solution(11507560514257684376)
XLA Ops:
  8.7 2.2 split_blocks.3
  11.8 2.1 pad_maximum_fusion.refs_0_
  13.8 15.6 %exchange.4 = bf16[8,80,640]{2,1,0:T(8,128)(2,1)} custom-call(bf16[8,80,640]{2,1,0:T(8,128)(2,1)} %pad_maximum_fusion.refs_0_), custom_call_target="tpu_custom_call" | custom-call | bytes 45000000 | tf_op jit(solution)/shard_map/exchange/pallas_call | solution.py:605
  29.5 2.0 slice.192
  34.7 3.0 split_blocks.2.refs_1_
  38.2 61.9 %gather_exchange.1 = (bf16[8,256,2048]{2,1,0:T(8,128)(2,1)}, bf16[8,64,1536]{2,1,0:T(8,128)(2,1)}, f32[4,8,512]{2,1,0:T(8,128)}, bf16[4,80,384]{2,1,0:T(8,128)(2,1)}) custom-call(bf16[256,2048]{1,0:T(8,128)(2,1)} %refs_0_.1, bf16[8,64,1536]{2,1,0:T(8,128)(2,1)} %split_blocks.2.refs_1_, f32[8,512]{1,0:T(8,128)} %fusion.56.refs_2_, bf16[80,384]{1,0:T(8,128)(2,1)} %pad.31.refs_3_), custom_call_target="tpu_custom_call" | custom-call | bytes 165000000 | tf_op jit(solution)/shard_map/gather_exchange/pallas_call | solution.py:625
  105.1 5.2 fusion
  110.3 11.6 %fusion.15.pre_ref = f32[2048,640]{1,0:T(8,128)} fusion(bf16[2048,640]{1,0:T(8,128)(2,1)} %all-gather.7.cloned.1.call-done.w_ref, bf16[2048,2048]{1,0:T(8,128)(2,1)} %bitcast.146, f32[2048]{0:T(1024)S(1)} %bitcast.181, f32[2048]{0:T(1024)S(1)} %add_rsqrt_fusion), kind=kOutput, calls=%fused_computation.27 | convolution fusion | flops 5385486336 | bytes 16269312 | tf_op jit(solution)/shard_map/dot_general | solution.py:1482
  122.6 1.5 collective-permute-start.2
  127.4 3.8 exchange.5
  134.2 2.8 collective-permute-start
  137.8 2.5 copy.78
  141.0 17.0 %forward_scan.1 = (bf16[2048,320]{1,0:T(8,128)(2,1)}, bf16[2048,320]{1,0:T(8,128)(2,1)}, f32[2048,320]{1,0:T(8,128)}, f32[2048,320]{1,0:T(8,128)}, f32[2048,320]{1,0:T(8,128)}, /*index=5*/f32[8,320]{1,0:T(8,128)}) custom-call(s32[8]{0:T(128)} %copy-done.27, f32[2048,640]{1,0:T(8,128)} %fusion.15.pre_ref, f32[8,320]{1,0:T(8,128)} %copy-done.24, ...), custom_call_target="tpu_custom_call" | custom-call | bytes 45000000 | tf_op jit(solution)/shard_map/forward_scan/pallas_call | solution.py:812
  159.3 7.0 %gather_groups.1 = f32[4,8,320]{2,1,0:T(8,128)} custom-call(f32[8,320]{1,0:T(8,128)} %get-tuple-element.140.refs_0_), custom_call_target="tpu_custom_call" | custom-call | bytes 15000000 | tf_op jit(solution)/shard_map/gather_groups/pallas_call | solution.py:682
  166.4 2.0 slice.210
  169.1 1.9 slice.211
  171.0 1.5 collective-permute-start.4
  174.3 2.9 constant_dynamic-update-slice_fusion.3
  177.2 2.4 constant_dynamic-update-slice_fusion.2
  179.6 3.3 fusion.11
  183.0 6.6 %convolution_convert_fusion = bf16[2048,2048]{1,0:T(8,128)(2,1)} fusion(bf16[2048,320]{1,0:T(8,128)(2,1)S(1)} %fusion.11, bf16[320,2048]{1,0:T(8,128)(2,1)S(1)} %bitcast.156), kind=kOutput, calls=%fused_computation.5 | convolution fusion | flops 2688548864 | bytes 11010048 | tf_op jit(solution)/shard_map/dot_general | solution.py:1499
  189.6 1.9 constant_dynamic-update-slice_fusion.1
  191.5 1.9 constant_dynamic-update-slice_fusion.mine_ref
  193.4 46.3 %scatter_feature.1 = f32[256,2048]{1,0:T(8,128)} custom-call(bf16[8,256,2048]{2,1,0:T(8,128)(2,1)} %bitcast.144), custom_call_target="tpu_custom_call" | custom-call | bytes 135000000 | tf_op jit(solution)/shard_map/scatter_feature/pallas_call | solution.py:321
  239.8 2.1 multiply_reduce_fusion.1
  243.3 40.6 %gather_feature.1 = bf16[8,256,2048]{2,1,0:T(8,128)(2,1)} custom-call(bf16[256,2048]{1,0:T(8,128)(2,1)} %multiply_convert_fusion.refs_0_), custom_call_target="tpu_custom_call" | custom-call | bytes 120000000 | tf_op jit(solution)/shard_map/gather_feature/pallas_call | solution.py:124
  284.0 31.2 %gated_unit.1 = (bf16[2048,768]{1,0:T(8,128)(2,1)}, bf16[2048,1536]{1,0:T(8,128)(2,1)}) custom-call(bf16[2048,2048]{1,0:T(8,128)(2,1)} %bitcast.150, bf16[1024,2048]{1,0:T(8,128)(2,1)} %constant_dynamic-update-slice_fusion.mine_ref, bf16[1024,2048]{1,0:T(8,128)(2,1)} %collective-permute-done.5.theirs_ref, ...), custom_call_target="tpu_custom_call" | custom-call | flops 19327352832 | bytes 41943040 | tf_op jit(solution)/shard_map/gated_unit/pallas_call | solution.py:1137
  315.2 9.9 %convolution_convert_fusion.3 = bf16[1024,2048]{1,0:T(8,128)(2,1)S(1)} fusion(bf16[2048,1536]{1,0:T(8,128)(2,1)} %all-gather.9.cloned.1.call-done.w_ref, bf16[2048,1536]{1,0:T(8,128)(2,1)} %get-tuple-element.168), kind=kOutput, calls=%fused_computation.10 | convolution fusion | flops 6444548096 | bytes 13631488 | tf_op jit(solution)/shard_map/dot_general | solution.py:1511
  325.6 7.2 %convolution_convert_fusion.2 = bf16[1024,2048]{1,0:T(8,128)(2,1)S(1)} fusion(bf16[2048,1536]{1,0:T(8,128)(2,1)S(1)} %copy-done.35, bf16[2048,1536]{1,0:T(8,128)(2,1)S(1)} %copy-done.36), kind=kOutput, calls=%fused_computation.9 | convolution fusion | flops 6444548096 | bytes 13631488 | tf_op jit(solution)/shard_map/dot_general | solution.py:1511
  332.8 2.6 fusion.27
  338.8 5.4 fusion.23
  344.2 7.4 %add_convert_fusion = bf16[768,2048]{1,0:T(8,128)(2,1)} fusion(f32[768,2048]{1,0:T(8,128)S(1)} %fusion.23, bf16[1024,2048]{1,0:T(8,128)(2,1)} %constant_dynamic-update-slice_fusion.mine_ref, bf16[2048,768]{1,0:T(8,128)(2,1)S(1)} %copy-done.12), kind=kOutput, calls=%fused_computation.7 | convolution fusion | flops 3224371200 | bytes 15204352 | tf_op jit(solution)/shard_map/dot_general | solution.py:1515
  351.6 14.2 %down_rows.1 = (bf16[1024,2048]{1,0:T(8,128)(2,1)}, bf16[1024,2048]{1,0:T(8,128)(2,1)}) custom-call(bf16[2048,768]{1,0:T(8,128)(2,1)} %get-tuple-element.158.h_ref, bf16[768,2048]{1,0:T(8,128)(2,1)} %all-gather.11.cloned.1.call-done.down_ref.w_ref), custom_call_target="tpu_custom_call" | custom-call | bytes 300000 | tf_op jit(solution)/shard_map/down_rows/pallas_call | solution.py:1184
  365.9 2.9 add_convert_fusion.4
  368.8 16.6 %scatter_tail.1 = f32[256,2048]{1,0:T(8,128)} custom-call(bf16[128,2048]{1,0:T(8,128)(2,1)} %get-tuple-element.156.ny_ref, bf16[128,2048]{1,0:T(8,128)(2,1)} %get-tuple-element.308.nx_ref, bf16[2,128,2048]{2,1,0:T(8,128)(2,1)} %bitcast.164, bf16[2,128,2048]{2,1,0:T(8,128)(2,1)} %collective-permute-done.7.bx_ref, ...), custom_call_target="tpu_custom_call" | custom-call | bytes 48000000 | tf_op jit(solution)/shard_map/scatter_tail/pallas_call | solution.py:533
  385.4 2.3 fusion.17
  387.8 4.0 fusion.65
  393.8 16.7 %convolution_convert_fusion.1 = bf16[2048,1536]{1,0:T(8,128)(2,1)} fusion(bf16[2048,2048]{1,0:T(8,128)(2,1)S(1)} %bitcast.153, bf16[2048,1536]{1,0:T(8,128)(2,1)} %get-tuple-element.168), kind=kOutput, calls=%fused_computation.6 | convolution fusion | flops 12888047616 | bytes 20971520 | tf_op jit(solution)/shard_map/dot_general | solution.py:1537
  410.5 3.1 add_convert_fusion.1
  413.6 2.9 fusion.39
  416.4 3.7 fusion.29
  420.2 18.6 %gather_tail.1 = bf16[8,256,2048]{2,1,0:T(8,128)(2,1)} custom-call(bf16[256,2048]{1,0:T(8,128)(2,1)} %get-tuple-element.167.x_ref, bf16[256,2048]{1,0:T(8,128)(2,1)} %collective-permute-done.9.bx_ref, bf16[256,2048]{1,0:T(8,128)(2,1)} %collective-permute-done.10.by_ref), custom_call_target="tpu_custom_call" | custom-call | bytes 48000000 | tf_op jit(solution)/shard_map/gather_tail/pallas_call | solution.py:446
  440.9 17.7 %adjoint_scan.1 = (f32[2048,320]{1,0:T(8,128)}, f32[2048,320]{1,0:T(8,128)}, f32[2048,320]{1,0:T(8,128)}, f32[8,320]{1,0:T(8,128)}) custom-call(s32[8]{0:T(128)} %copy-done.27, bf16[2048,2048]{1,0:T(8,128)(2,1)} %bitcast.142, bf16[320,2048]{1,0:T(8,128)(2,1)} %bitcast.155, f32[2048,640]{1,0:T(8,128)} %fusion.15.pre_ref, f32[2048,320]{1,0:T(8,128)} %get-tuple-element.177.keep_ref), custom_call_target="tpu_custom_call" | custom-call | bytes 36000000 | tf_op jit(solution)/shard_map/adjoint_scan/pallas_call | solution.py:891
  462.5 4.2 collective-permute-done.12
  468.9 22.2 %backward_scan.1 = (bf16[2048,640]{1,0:T(8,128)(2,1)}, f32[8,320]{1,0:T(8,128)}, f32[8,320]{1,0:T(8,128)}, f32[320,320]{1,0:T(8,128)}, f32[320,320]{1,0:T(8,128)}) custom-call(s32[8]{0:T(128)} %copy-done.27, f32[2048,320]{1,0:T(8,128)} %get-tuple-element.178.d_mixed_ref, f32[2048,640]{1,0:T(8,128)} %fusion.15.pre_ref, ...), custom_call_target="tpu_custom_call" | custom-call | bytes 63000000 | tf_op jit(solution)/shard_map/backward_scan/pallas_call | solution.py:1054
  493.3 1.5 collective-permute-start.18
  494.8 8.0 %fusion.70.out_ref = f32[320,2048]{1,0:T(8,128)} fusion(bf16[2048,320]{1,0:T(8,128)(2,1)S(1)} %copy-done.20, bf16[2048,2048]{1,0:T(8,128)(2,1)} %bitcast.143), kind=kOutput, calls=%fused_computation.167 | convolution fusion | flops 2684354560 | bytes 12320768 | tf_op jit(solution)/shard_map/dot_general | solution.py:1569
  503.8 1.5 collective-permute-start.19
  505.4 1.5 copy-done.14
  506.9 9.0 %convolution_convert_fusion.4 = bf16[2048,640]{1,0:T(8,128)(2,1)} fusion(bf16[2048,640]{1,0:T(8,128)(2,1)S(1)} %fusion.52.a_ref, bf16[2048,2048]{1,0:T(8,128)(2,1)S(1)} %bitcast.149, f32[2048]{0:T(1024)S(1)} %bitcast.182, f32[2048]{0:T(1024)S(1)} %add_rsqrt_fusion), kind=kOutput, calls=%fused_computation.15 | convolution fusion | flops 5386797056 | bytes 13647872 | tf_op jit(solution)/shard_map/dot_general | solution.py:1575
  515.9 2.1 collective-permute-done.19
  518.1 1.5 convert_element_type.330
  521.0 3.8 pack_sums.1.refs_0_
  524.8 3.8 exchange.6
  528.6 2.0 fusion.33
  530.7 1.4 fusion.22
  533.6 59.7 %scatter_dot.1 = (f32[256,2048]{1,0:T(8,128)}, bf16[8,64,1536]{2,1,0:T(8,128)(2,1)}) custom-call(bf16[2048,640]{1,0:T(8,128)(2,1)} %copy-done.14, bf16[2048,640]{1,0:T(8,128)(2,1)} %all-gather.7.cloned.1.call-done.w_ref, bf16[8,64,1536]{2,1,0:T(8,128)(2,1)} %bitcast.169), custom_call_target="tpu_custom_call" | custom-call | bytes 165000000 | tf_op jit(solution)/shard_map/scatter_dot/pallas_call | solution.py:291
  593.3 12.2 %exchange.7.x_ref = bf16[8,64,640]{2,1,0:T(8,128)(2,1)} custom-call(bf16[8,64,640]{2,1,0:T(8,128)(2,1)} %bitcast.172), custom_call_target="tpu_custom_call" | custom-call | bytes 45000000 | tf_op jit(solution)/shard_map/exchange/pallas_call | solution.py:605
  605.5 2.5 join_blocks.2
  608.0 4.0 join_blocks.3
  612.4 1.9 fusion.20
  614.3 8.4 %reduce-scatter.7.cloned.1.call-done.x_ref = bf16[80,2432]{1,0:T(8,128)(2,1)} async-done(((bf16[320,2432]{1,0:T(8,128)(2,1)}), bf16[80,2432]{1,0:T(8,128)(2,1)}) %reduce-scatter.7.cloned.1.call-update) | async-done | bytes 389136 | tf_op jit(solution)/shard_map/reduce_scatter | solution.py:1589
  622.7 1.9 unpack_sums.1
  624.6 1.4 copy.91
  (200 shorter events, 43.6 us)
Async XLA Ops:
  7.2 97.9 %all-gather.5.cloned.1.call-start = ((), (), s32[]{:S(2)}) async-start(), calls=%async_computation.4 | async-start | bytes 1638400 | tf_op jit(solution)/shard_map/all_gather | solution.py:1424
  7.9 102.4 %all-gather.7.cloned.1.call-start = ((), (), s32[]{:S(2)}) async-start(), calls=%async_computation.5 | async-start | bytes 3276800 | tf_op jit(solution)/shard_map/all_gather | solution.py:1435
  10.9 22.4 %copy-start.28 = (bf16[80,4]{0,1:T(4,128)(2,1)S(1)}, bf16[80,4]{0,1:T(4,128)(2,1)}, u32[]{:S(2)}) copy-start(bf16[80,4]{0,1:T(4,128)(2,1)} %param.24) | copy-start | bytes 1924
  10.9 22.5 %copy-start.31 = (bf16[80]{0:T(256)(128)(2,1)S(1)}, bf16[80]{0:T(256)(128)(2,1)}, u32[]{:S(2)}) copy-start(bf16[80]{0:T(256)(128)(2,1)} %param.25) | copy-start | bytes 484
  11.7 21.8 %copy-start.32 = (bf16[80]{0:T(256)(128)(2,1)S(1)}, bf16[80]{0:T(256)(128)(2,1)}, u32[]{:S(2)}) copy-start(bf16[80]{0:T(256)(128)(2,1)} %param.27) | copy-start | bytes 484
  11.7 21.9 %copy-start.33 = (bf16[80]{0:T(256)(128)(2,1)S(1)}, bf16[80]{0:T(256)(128)(2,1)}, u32[]{:S(2)}) copy-start(bf16[80]{0:T(256)(128)(2,1)} %param.29) | copy-start | bytes 484
  11.7 22.1 %copy-start.34 = (bf16[80]{0:T(256)(128)(2,1)S(1)}, bf16[80]{0:T(256)(128)(2,1)}, u32[]{:S(2)}) copy-start(bf16[80]{0:T(256)(128)(2,1)} %param.30) | copy-start | bytes 484
  11.7 22.2 %copy-start.25 = (bf16[80,160]{1,0:T(8,128)(2,1)S(1)}, bf16[80,160]{1,0:T(8,128)(2,1)}, u32[]{:S(2)}) copy-start(bf16[80,160]{1,0:T(8,128)(2,1)} %param.26) | copy-start | bytes 76804
  11.7 22.2 %copy-start.26 = (bf16[80,160]{1,0:T(8,128)(2,1)S(1)}, bf16[80,160]{1,0:T(8,128)(2,1)}, u32[]{:S(2)}) copy-start(bf16[80,160]{1,0:T(8,128)(2,1)} %param.28) | copy-start | bytes 76804
  31.5 252.4 %all-gather.11.cloned.1.call-start = ((), (), s32[]{:S(2)}) async-start(), calls=%async_computation.7 | async-start | bytes 3932160 | tf_op jit(solution)/shard_map/all_gather | solution.py:1457
  32.2 251.7 %all-gather.9.cloned.1.call-start = ((), (), s32[]{:S(2)}) async-start(), calls=%async_computation.6 | async-start | bytes 7864320 | tf_op jit(solution)/shard_map/all_gather | solution.py:1456
  34.7 67.9 %copy-start.11 = (bf16[256,2048]{1,0:T(8,128)(2,1)S(1)}, bf16[256,2048]{1,0:T(8,128)(2,1)}, u32[]{:S(2)}) copy-start(bf16[256,2048]{1,0:T(8,128)(2,1)} %param.20) | copy-start | bytes 3145732
  100.2 338.6 %reduce-scatter.5.cloned.1.call-start = ((), (), s32[]{:S(2)}) async-start(), calls=%async_computation.8 | async-start | bytes 3932160 | tf_op jit(solution)/shard_map/reduce_scatter | solution.py:1528
  105.0 19.9 %copy-start.27 = (s32[8]{0:T(128)}, s32[8]{0:T(128)S(1)}, u32[]{:S(2)}) copy-start(s32[8]{0:T(128)S(1)} %fusion.62.order_ref) | copy-start | bytes 100
  121.9 36.1 %collective-permute-start.1 = (bf16[256,2048]{1,0:T(8,128)(2,1)S(1)}, bf16[256,2048]{1,0:T(8,128)(2,1)S(1)}, u32[]{:S(2)}, u32[]{:S(2)}) collective-permute-start(bf16[256,2048]{1,0:T(8,128)(2,1)S(1)} %copy-done.11), channel_id=1, source_target_pairs={{0,4},{4,0},{1,5},{5,1},{2,6},{6,2},{3,7},{7,3},{8,12},{12,8},{9,1... | collective-permute-start | bytes 3145736 | tf_op jit(solution)/shard_map/ppermute | solution.py:348
  122.6 35.4 %collective-permute-start.2 = (bf16[256,2048]{1,0:T(8,128)(2,1)S(1)}, bf16[256,2048]{1,0:T(8,128)(2,1)S(1)}, u32[]{:S(2)}, u32[]{:S(2)}) collective-permute-start(bf16[256,2048]{1,0:T(8,128)(2,1)S(1)} %copy-done.11), channel_id=1, source_target_pairs={{0,2},{2,0},{1,3},{3,1},{4,6},{6,4},{5,7},{7,5},{8,10},{10,8},{9,1... | collective-permute-start | bytes 3145736 | tf_op jit(solution)/shard_map/ppermute | solution.py:348
  134.2 6.1 collective-permute-start
  166.4 13.3 %copy-start.2 = (f32[2048,320]{1,0:T(8,128)S(1)}, f32[2048,320]{1,0:T(8,128)}, u32[]{:S(2)}) copy-start(f32[2048,320]{1,0:T(8,128)} %get-tuple-element.137.prod_ref.prod_before_ref) | copy-start | bytes 7864324
  168.4 21.2 %collective-permute-start.3 = (bf16[128,2048]{1,0:T(8,128)(2,1)}, bf16[128,2048]{1,0:T(8,128)(2,1)}, u32[]{:S(2)}, u32[]{:S(2)}) collective-permute-start(bf16[128,2048]{1,0:T(8,128)(2,1)} %slice.210), channel_id=1, source_target_pairs={{0,2},{2,0},{1,3},{3,1},{4,6},{6,4},{5,7},{7,5},{8,10},{10,8},{9,1... | collective-permute-start | bytes 1572872 | tf_op jit(solution)/shard_map/ppermute | solution.py:348
  171.0 18.7 %collective-permute-start.4 = (bf16[128,2048]{1,0:T(8,128)(2,1)}, bf16[128,2048]{1,0:T(8,128)(2,1)}, u32[]{:S(2)}, u32[]{:S(2)}) collective-permute-start(bf16[128,2048]{1,0:T(8,128)(2,1)} %slice.211), channel_id=1, source_target_pairs={{0,4},{4,0},{1,5},{5,1},{2,6},{6,2},{3,7},{7,3},{8,12},{12,8},{9,1... | collective-permute-start | bytes 1572872 | tf_op jit(solution)/shard_map/ppermute | solution.py:348
  173.3 6.3 copy-start.3
  179.6 3.4 copy-start.7
  183.0 6.7 %copy-start.19 = (bf16[2048,320]{1,0:T(8,128)(2,1)}, bf16[2048,320]{1,0:T(8,128)(2,1)S(1)}, u32[]{:S(2)}) copy-start(bf16[2048,320]{1,0:T(8,128)(2,1)S(1)} %fusion.11) | copy-start | bytes 3932164
  193.4 90.6 %collective-permute-start.5 = (bf16[1024,2048]{1,0:T(8,128)(2,1)}, bf16[1024,2048]{1,0:T(8,128)(2,1)}, u32[]{:S(2)}, u32[]{:S(2)}) collective-permute-start(bf16[1024,2048]{1,0:T(8,128)(2,1)} %constant_dynamic-update-slice_fusion.mine_ref), channel_id=1, source_target_pairs={{0,1},{1,0},{2,3},{3,2},{4,5},{5,4},{6,7},{7,6},{8,9},{9,8},{10,11... | collective-permute-start | bytes 12582920 | tf_op jit(solution)/shard_map/ppermute | solution.py:348
  193.4 46.3 %copy-start.1 = (bf16[256,2048]{1,0:T(8,128)(2,1)S(1)}, bf16[256,2048]{1,0:T(8,128)(2,1)}, u32[]{:S(2)}) copy-start(bf16[256,2048]{1,0:T(8,128)(2,1)} %refs_0_.1) | copy-start | bytes 3145732
  239.8 2.3 copy-start
  315.2 10.4 %copy-start.35 = (bf16[2048,1536]{1,0:T(8,128)(2,1)S(1)}, bf16[2048,1536]{1,0:T(8,128)(2,1)}, u32[]{:S(2)}) copy-start(bf16[2048,1536]{1,0:T(8,128)(2,1)} %all-gather.9.cloned.1.call-done.w_ref) | copy-start | bytes 18874372
  315.2 10.4 %copy-start.36 = (bf16[2048,1536]{1,0:T(8,128)(2,1)S(1)}, bf16[2048,1536]{1,0:T(8,128)(2,1)}, u32[]{:S(2)}) copy-start(bf16[2048,1536]{1,0:T(8,128)(2,1)} %get-tuple-element.168) | copy-start | bytes 18874372
  325.1 7.6 %collective-permute-start.6 = (bf16[1024,2048]{1,0:T(8,128)(2,1)S(1)}, bf16[1024,2048]{1,0:T(8,128)(2,1)S(1)}, u32[]{:S(2)}, u32[]{:S(2)}) collective-permute-start(bf16[1024,2048]{1,0:T(8,128)(2,1)S(1)} %convolution_convert_fusion.3), channel_id=1, source_target_pairs={{0,1},{1,0},{2,3},{3,2},{4,5},{5,4},{6,7},{7,6},{8,9},{9,8},{10,11... | collective-permute-start | bytes 12582920 | tf_op jit(solution)/shard_map/ppermute | solution.py:348
  332.7 11.4 %copy-start.10 = (bf16[1024,2048]{1,0:T(8,128)(2,1)}, bf16[1024,2048]{1,0:T(8,128)(2,1)S(1)}, u32[]{:S(2)}) copy-start(bf16[1024,2048]{1,0:T(8,128)(2,1)S(1)} %convolution_convert_fusion.2) | copy-start | bytes 12582916
  332.8 2.6 copy-start.9
  335.4 3.4 copy-start.12
  336.8 32.0 %collective-permute-start.7 = (bf16[2,128,2048]{2,1,0:T(8,128)(2,1)}, bf16[2,128,2048]{2,1,0:T(8,128)(2,1)}, u32[]{:S(2)}, u32[]{:S(2)}) collective-permute-start(bf16[2,128,2048]{2,1,0:T(8,128)(2,1)} %get-tuple-element.161), channel_id=1, source_target_pairs={{0,4},{4,0},{1,5},{5,1},{2,6},{6,2},{3,7},{7,3},{8,12},{12,8},{9,1... | collective-permute-start | bytes 3145736 | tf_op jit(solution)/shard_map/ppermute | solution.py:348
  337.9 30.9 %collective-permute-start.8 = (bf16[2,128,2048]{2,1,0:T(8,128)(2,1)}, bf16[2,128,2048]{2,1,0:T(8,128)(2,1)}, u32[]{:S(2)}, u32[]{:S(2)}) collective-permute-start(bf16[2,128,2048]{2,1,0:T(8,128)(2,1)} %get-tuple-element.162), channel_id=1, source_target_pairs={{0,2},{2,0},{1,3},{3,1},{4,6},{6,4},{5,7},{7,5},{8,10},{10,8},{9,1... | collective-permute-start | bytes 3145736 | tf_op jit(solution)/shard_map/ppermute | solution.py:348
  351.6 182.0 %reduce-scatter.9.cloned.1.call-start = ((), (), s32[]{:S(2)}) async-start(), calls=%async_computation.10 | async-start | bytes 7864320 | tf_op jit(solution)/shard_map/reduce_scatter | solution.py:1545
  368.8 25.0 %slice-start.2 = ((s8[8388608]{0:T(1024)(128)(4,1)}), s8[4194304]{0:T(1024)(128)(4,1)S(1)}, s32[]{:S(2)}) async-start(s8[8388608]{0:T(1024)(128)(4,1)} %bitcast.151), calls=%async_computation.14 | async-start | bytes 8388608
  385.4 2.4 copy-start.4
  385.4 8.4 %slice-start.3 = ((s8[8388608]{0:T(1024)(128)(4,1)}), s8[4194304]{0:T(1024)(128)(4,1)S(1)}, s32[]{:S(2)}) async-start(s8[8388608]{0:T(1024)(128)(4,1)} %bitcast.151), calls=%async_computation.15 | async-start | bytes 8388608
  391.7 18.7 %collective-permute-start.11 = (bf16[1024,2048]{1,0:T(8,128)(2,1)}, bf16[1024,2048]{1,0:T(8,128)(2,1)}, u32[]{:S(2)}, u32[]{:S(2)}) collective-permute-start(bf16[1024,2048]{1,0:T(8,128)(2,1)} %get-tuple-element.170), channel_id=1, source_target_pairs={{0,1},{1,0},{2,3},{3,2},{4,5},{5,4},{6,7},{7,6},{8,9},{9,8},{10,11... | collective-permute-start | bytes 12582920 | tf_op jit(solution)/shard_map/ppermute | solution.py:348
  391.7 28.4 %collective-permute-start.9 = (bf16[256,2048]{1,0:T(8,128)(2,1)}, bf16[256,2048]{1,0:T(8,128)(2,1)}, u32[]{:S(2)}, u32[]{:S(2)}) collective-permute-start(bf16[256,2048]{1,0:T(8,128)(2,1)} %get-tuple-element.167.x_ref), channel_id=1, source_target_pairs={{0,4},{4,0},{1,5},{5,1},{2,6},{6,2},{3,7},{7,3},{8,12},{12,8},{9,1... | collective-permute-start | bytes 3145736 | tf_op jit(solution)/shard_map/ppermute | solution.py:348
  392.6 27.5 %collective-permute-start.10 = (bf16[256,2048]{1,0:T(8,128)(2,1)}, bf16[256,2048]{1,0:T(8,128)(2,1)}, u32[]{:S(2)}, u32[]{:S(2)}) collective-permute-start(bf16[256,2048]{1,0:T(8,128)(2,1)} %get-tuple-element.167.x_ref), channel_id=1, source_target_pairs={{0,2},{2,0},{1,3},{3,1},{4,6},{6,4},{5,7},{7,5},{8,10},{10,8},{9,1... | collective-permute-start | bytes 3145736 | tf_op jit(solution)/shard_map/ppermute | solution.py:348
  410.5 6.0 copy-start.8
  420.1 173.2 %reduce-scatter.11.cloned.1.call-start = ((), (), s32[]{:S(2)}) async-start(), calls=%async_computation.11 | async-start | bytes 3276800 | tf_op jit(solution)/shard_map/reduce_scatter | solution.py:1582
  438.8 29.3 %collective-permute-start.15 = (bf16[2,128,2048]{2,1,0:T(8,128)(2,1)}, bf16[2,128,2048]{2,1,0:T(8,128)(2,1)S(1)}, u32[]{:S(2)}, u32[]{:S(2)}) collective-permute-start(bf16[2,128,2048]{2,1,0:T(8,128)(2,1)} %get-tuple-element.184), channel_id=1, source_target_pairs={{0,4},{4,0},{1,5},{5,1},{2,6},{6,2},{3,7},{7,3},{8,12},{12,8},{9,1... | collective-permute-start | bytes 3145736 | tf_op jit(solution)/shard_map/ppermute | solution.py:348
  439.7 28.3 %collective-permute-start.16 = (bf16[2,128,2048]{2,1,0:T(8,128)(2,1)}, bf16[2,128,2048]{2,1,0:T(8,128)(2,1)S(1)}, u32[]{:S(2)}, u32[]{:S(2)}) collective-permute-start(bf16[2,128,2048]{2,1,0:T(8,128)(2,1)} %get-tuple-element.185), channel_id=1, source_target_pairs={{0,2},{2,0},{1,3},{3,1},{4,6},{6,4},{5,7},{7,5},{8,10},{10,8},{9,1... | collective-permute-start | bytes 3145736 | tf_op jit(solution)/shard_map/ppermute | solution.py:348
  458.6 8.2 %collective-permute-start.12 = (f32[8,320]{1,0:T(8,128)}, f32[8,320]{1,0:T(8,128)S(1)}, u32[]{:S(2)}, u32[]{:S(2)}) collective-permute-start(f32[8,320]{1,0:T(8,128)} %get-tuple-element.183), channel_id=1, source_target_pairs={{24,0},{25,1},{26,2},{27,3},{28,4},{29,5},{30,6},{31,7}} | collective-permute-start | bytes 30728 | tf_op jit(solution)/shard_map/ppermute | solution.py:1554
  459.8 8.2 %collective-permute-start.13 = (f32[8,320]{1,0:T(8,128)}, f32[8,320]{1,0:T(8,128)S(1)}, u32[]{:S(2)}, u32[]{:S(2)}) collective-permute-start(f32[8,320]{1,0:T(8,128)} %get-tuple-element.183), channel_id=1, source_target_pairs={{16,0},{24,8},{17,1},{25,9},{18,2},{26,10},{19,3},{27,11},{20,4},{... | collective-permute-start | bytes 30728 | tf_op jit(solution)/shard_map/ppermute | solution.py:1554
  461.1 6.9 %collective-permute-start.14 = (f32[8,320]{1,0:T(8,128)}, f32[8,320]{1,0:T(8,128)S(1)}, u32[]{:S(2)}, u32[]{:S(2)}) collective-permute-start(f32[8,320]{1,0:T(8,128)} %get-tuple-element.183), channel_id=1, source_target_pairs={{8,0},{16,8},{24,16},{9,1},{17,9},{25,17},{10,2},{18,10},{26,18},{... | collective-permute-start | bytes 30728 | tf_op jit(solution)/shard_map/ppermute | solution.py:1554
  468.1 24.3 %copy-start.21 = (bf16[2,128,2048]{2,1,0:T(8,128)(2,1)}, bf16[2,128,2048]{2,1,0:T(8,128)(2,1)S(1)}, u32[]{:S(2)}) copy-start(bf16[2,128,2048]{2,1,0:T(8,128)(2,1)S(1)} %collective-permute-done.15) | copy-start | bytes 3145732
  468.1 34.8 %copy-start.22 = (bf16[2,128,2048]{2,1,0:T(8,128)(2,1)}, bf16[2,128,2048]{2,1,0:T(8,128)(2,1)S(1)}, u32[]{:S(2)}) copy-start(bf16[2,128,2048]{2,1,0:T(8,128)(2,1)S(1)} %collective-permute-done.16) | copy-start | bytes 3145732
  468.9 23.5 %copy-start.18 = (bf16[128,2048]{1,0:T(8,128)(2,1)S(1)}, bf16[128,2048]{1,0:T(8,128)(2,1)}, u32[]{:S(2)}) copy-start(bf16[128,2048]{1,0:T(8,128)(2,1)} %get-tuple-element.197) | copy-start | bytes 1572868
  468.9 25.9 %copy-start.20 = (bf16[2048,320]{1,0:T(8,128)(2,1)S(1)}, bf16[2048,320]{1,0:T(8,128)(2,1)}, u32[]{:S(2)}) copy-start(bf16[2048,320]{1,0:T(8,128)(2,1)} %copy-done.19) | copy-start | bytes 3932164
  491.1 14.1 %collective-permute-start.17 = (f32[8,320]{1,0:T(8,128)}, f32[8,320]{1,0:T(8,128)S(1)}, u32[]{:S(2)}, u32[]{:S(2)}) collective-permute-start(f32[8,320]{1,0:T(8,128)} %get-tuple-element.189), channel_id=1, source_target_pairs={{8,0},{16,8},{24,16},{9,1},{17,9},{25,17},{10,2},{18,10},{26,18},{... | collective-permute-start | bytes 30728 | tf_op jit(solution)/shard_map/ppermute | solution.py:1567
  492.4 14.5 %slice-start = ((s8[8388608]{0:T(1024)(128)(4,1)}), s8[4194304]{0:T(1024)(128)(4,1)S(1)}, s32[]{:S(2)}) async-start(s8[8388608]{0:T(1024)(128)(4,1)} %bitcast.147), calls=%async_computation.12 | async-start | bytes 8388608
  493.3 9.5 %copy-start.17 = (bf16[128,2048]{1,0:T(8,128)(2,1)S(1)}, bf16[128,2048]{1,0:T(8,128)(2,1)}, u32[]{:S(2)}) copy-start(bf16[128,2048]{1,0:T(8,128)(2,1)} %get-tuple-element.199) | copy-start | bytes 1572868
  493.3 12.0 %copy-start.13 = (bf16[2048,640]{1,0:T(8,128)(2,1)S(1)}, bf16[2048,640]{1,0:T(8,128)(2,1)}, u32[]{:S(2)}) copy-start(bf16[2048,640]{1,0:T(8,128)(2,1)} %get-tuple-element.192) | copy-start | bytes 7864324
  493.3 13.5 %slice-start.1 = ((s8[8388608]{0:T(1024)(128)(4,1)}), s8[4194304]{0:T(1024)(128)(4,1)S(1)}, s32[]{:S(2)}) async-start(s8[8388608]{0:T(1024)(128)(4,1)} %bitcast.147), calls=%async_computation.13 | async-start | bytes 8388608
  493.3 22.5 %collective-permute-start.18 = (bf16[128,2048]{1,0:T(8,128)(2,1)}, bf16[128,2048]{1,0:T(8,128)(2,1)}, u32[]{:S(2)}, u32[]{:S(2)}) collective-permute-start(bf16[128,2048]{1,0:T(8,128)(2,1)} %fusion.35), channel_id=1, source_target_pairs={{0,2},{2,0},{1,3},{3,1},{4,6},{6,4},{5,7},{7,5},{8,10},{10,8},{9,1... | collective-permute-start | bytes 1572872 | tf_op jit(solution)/shard_map/ppermute | solution.py:348
  503.8 14.3 %collective-permute-start.19 = (bf16[128,2048]{1,0:T(8,128)(2,1)}, bf16[128,2048]{1,0:T(8,128)(2,1)}, u32[]{:S(2)}, u32[]{:S(2)}) collective-permute-start(bf16[128,2048]{1,0:T(8,128)(2,1)} %fusion.34), channel_id=1, source_target_pairs={{0,4},{4,0},{1,5},{5,1},{2,6},{6,2},{3,7},{7,3},{8,12},{12,8},{9,1... | collective-permute-start | bytes 1572872 | tf_op jit(solution)/shard_map/ppermute | solution.py:348
  518.1 104.6 %reduce-scatter.7.cloned.1.call-start = ((), (), s32[]{:S(2)}) async-start(), calls=%async_computation.9 | async-start | bytes 1945600 | tf_op jit(solution)/shard_map/reduce_scatter | solution.py:1589
  518.1 1.6 copy-start.23
  530.6 2.2 copy-start.30
  593.3 18.7 %copy-start.5 = (f32[256,2048]{1,0:T(8,128)S(1)}, f32[256,2048]{1,0:T(8,128)}, u32[]{:S(2)}) copy-start(f32[256,2048]{1,0:T(8,128)} %get-tuple-element.221) | copy-start | bytes 6291460
  608.0 4.3 copy-start.6
  (5 other events, 5.8 us)
Sparse Core Ops, SparseCore 0:
  9.6 35.3 all-gather.4
  47.2 54.0 all-gather.6
  102.8 63.1 all-gather.10
  167.5 113.9 all-gather.8
  351.7 58.7 reduce-scatter.4
  420.3 110.2 reduce-scatter.8
  532.9 52.6 reduce-scatter.10
  587.8 34.8 reduce-scatter.6

commit v7 on v6

--- a/solution.py
+++ b/solution.py
@@ -395,13 +395,19 @@
     return scatter_keeps(mine, got), across(by_x, "x"), across(by_y, "y")
 
 
-def scatter_relay(keeps, by_x, by_y):
-    near_y, near_x, _ = keeps
-    return across(add_low(near_y, by_x[1]), "y"), across(add_low(near_x, by_y[1]), "x")
-
-
-def scatter_sum(keeps, by_x, by_y, y_last, x_last):
-    own = keeps[2].astype(f32)
+def scatter_relay(mine, got, by_x, by_y):
+    mine, got = scatter_halves(mine, got)
+
+    def joined(chip, side, arrived):
+        near = mine[chip, side].astype(f32) + got[chip, side].astype(f32)
+        return (near + arrived[1].astype(f32)).astype(arrived.dtype)
+
+    return across(joined(ACROSS_Y, 0, by_x), "y"), across(joined(ACROSS_X, 1, by_y), "x")
+
+
+def scatter_sum(mine, got, by_x, by_y, y_last, x_last):
+    mine, got = scatter_halves(mine, got)
+    own = mine[OWN].astype(f32) + got[OWN].astype(f32)
     upper = own[0] + by_x[0].astype(f32) + y_last.astype(f32)
     lower = own[1] + by_y[0].astype(f32) + x_last.astype(f32)
     return jnp.concatenate([upper, lower])
@@ -1537,11 +1543,8 @@
     mlp_part = lax.dot_general(
         normed_two, d_mlp, contract_first, preferred_element_type=f32
     ).astype(bf16)
-    out_keeps = scatter_keeps(out_mine, out_got)
     out_x, out_y = scatter_sends(out_mine, out_got)
-    d_x, d_y, mlp_part, out_x, out_y, *out_keeps = hold(
-        d_x, d_y, mlp_part, out_x, out_y, *out_keeps
-    )
+    d_x, d_y, mlp_part, out_x, out_y = hold(d_x, d_y, mlp_part, out_x, out_y)
     mlp_sum = lax.psum_scatter(mlp_part, "z", scatter_dimension=0, tiled=True)
     d_rec = gather_tail(d_own, d_x, d_y)
     d_rec, down_sum, out_x, out_y = hold(d_rec, down_sum, out_x, out_y)
@@ -1555,7 +1558,7 @@
         for hop in range(count - 1, 0, -1)
     ]
     *from_later, out_x, out_y = hold(*from_later, out_x, out_y)
-    out_last = scatter_relay(out_keeps, out_x, out_y)
+    out_last = scatter_relay(out_mine, out_got, out_x, out_y)
     adj_in = jnp.zeros((1, chans), f32)
     for one in from_later:
         adj_in = one[0:1] * adj_in + one[1:2]
@@ -1578,7 +1581,7 @@
     rec_part, d_rec_pre, grad_a, grad_x, sums, *out_last = hold(
         rec_part, d_rec_pre, grad_a, grad_x, sums, *out_last
     )
-    layer_out = (middle + scatter_sum(out_keeps, out_x, out_y, *out_last)).astype(bf16)
+    layer_out = (middle + scatter_sum(out_mine, out_got, out_x, out_y, *out_last)).astype(bf16)
     rec_sum = lax.psum_scatter(rec_part, "z", scatter_dimension=0, tiled=True)
     back_pack = pack_sums(grad_out, grad_a, grad_x, sums, spread, chan_rows, pack_width)
     (back_swap,) = exchange([back_pack], swap_axes, 5)

time: 641 us -> 639 us (level)
    convert_element_type x8 -> x4, other arithmetic: 18.3 us -> 11.3 us  [add_low(): return (a.astype(f32) + b.astype(f32)).astype(a.dtype)]
    unnamed x88 -> x78, local copies, waits for them, and re-layouts: 13.5 us -> 13.6 us
  transfers between devices with their start and end apart: 28 -> 28, of which waited for: 4 -> 5; matrix products, arithmetic and copies ran while one was open for 24% -> 24% of each run, Pallas kernels for 59% -> 59%
where the time goes in v7:
time: 639 us; the launch traced here: 631 us
  Pallas kernels  405 us (63%)
  matrix products  83.9 us (13%)
  other arithmetic  51.4 us (8%)
  local copies, waits for them, and re-layouts  34 us (5%)
  starting transfers between devices  22.6 us (4%)
  waiting for transfers between devices  17.4 us (3%)
  between operations  17 us (3%)
    pallas_call x1, Pallas kernels, gather_exchange(): pl.pallas_call(gather_kernel, out_shape=(jax.ShapeDtypeStruct((NF, rows,...  61.9 us
    pallas_call x1, Pallas kernels, scatter_dot(): pl.pallas_call(scatter_dot_kernel, out_shape=(jax.ShapeDtypeStruct((rows,...  59.5 us
    pallas_call x1, Pallas kernels, scatter_feature(): pl.pallas_call(scatter_kernel, out_shape=jax.ShapeDtypeStruct((rows, widt...  46.4 us
    pallas_call x1, Pallas kernels, gather_feature(): pl.pallas_call(gather_kernel, out_shape=jax.ShapeDtypeStruct((NF, rows, w...  40.6 us
    pallas_call x4, Pallas kernels, exchange(): pl.pallas_call(functools.partial(exchange_kernel, axes), out_shape=tuple(...  35 us
    pallas_call x1, Pallas kernels, gated_unit(): pl.pallas_call(gated_kernel, grid=(steps,), out_shape=(jax.ShapeDtypeStru...  31.2 us
    pallas_call x1, Pallas kernels, backward_scan(): pl.pallas_call(backward_kernel, out_shape=(jax.ShapeDtypeStruct((rows, 2...  22 us
    pallas_call x1, Pallas kernels, gather_tail(): pl.pallas_call(gather_tail_kernel, out_shape=jax.ShapeDtypeStruct((NF, ro...  18.7 us
  transfers between devices with their start and end apart: 28, of which 5 were waited for; matrix products, arithmetic and copies ran while one was open for 24% of the time, Pallas kernels for 59%

profile of v7, /device:TPU:0, one launch (start us, length us, event | category | flops | bytes accessed | tf_op | source)
XLA Modules:
  0.0 631.5 jit_solution(4937426447408121371)
XLA Ops:
  8.7 2.2 split_blocks.3
  11.8 2.1 pad_maximum_fusion.refs_0_
  13.8 15.6 %exchange.4 = bf16[8,80,640]{2,1,0:T(8,128)(2,1)} custom-call(bf16[8,80,640]{2,1,0:T(8,128)(2,1)} %pad_maximum_fusion.refs_0_), custom_call_target="tpu_custom_call" | custom-call | bytes 45000000 | tf_op jit(solution)/shard_map/exchange/pallas_call | solution.py:611
  29.5 2.0 slice.198
  34.7 3.0 split_blocks.2.refs_1_
  38.2 61.9 %gather_exchange.1 = (bf16[8,256,2048]{2,1,0:T(8,128)(2,1)}, bf16[8,64,1536]{2,1,0:T(8,128)(2,1)}, f32[4,8,512]{2,1,0:T(8,128)}, bf16[4,80,384]{2,1,0:T(8,128)(2,1)}) custom-call(bf16[256,2048]{1,0:T(8,128)(2,1)} %refs_0_.1, bf16[8,64,1536]{2,1,0:T(8,128)(2,1)} %split_blocks.2.refs_1_, f32[8,512]{1,0:T(8,128)} %fusion.56.refs_2_, bf16[80,384]{1,0:T(8,128)(2,1)} %pad.31.refs_3_), custom_call_target="tpu_custom_call" | custom-call | bytes 165000000 | tf_op jit(solution)/shard_map/gather_exchange/pallas_call | solution.py:631
  105.1 5.2 fusion
  110.3 11.6 %fusion.15.pre_ref = f32[2048,640]{1,0:T(8,128)} fusion(bf16[2048,640]{1,0:T(8,128)(2,1)} %all-gather.7.cloned.1.call-done.w_ref, bf16[2048,2048]{1,0:T(8,128)(2,1)} %bitcast.161, f32[2048]{0:T(1024)S(1)} %bitcast.193, f32[2048]{0:T(1024)S(1)} %add_rsqrt_fusion), kind=kOutput, calls=%fused_computation.27 | convolution fusion | flops 5385486336 | bytes 16269312 | tf_op jit(solution)/shard_map/dot_general | solution.py:1488
  122.6 1.5 collective-permute-start.2
  127.4 3.8 exchange.5
  134.2 2.9 collective-permute-start
  137.9 2.6 copy.78
  141.1 17.0 %forward_scan.1 = (bf16[2048,320]{1,0:T(8,128)(2,1)}, bf16[2048,320]{1,0:T(8,128)(2,1)}, f32[2048,320]{1,0:T(8,128)}, f32[2048,320]{1,0:T(8,128)}, f32[2048,320]{1,0:T(8,128)}, /*index=5*/f32[8,320]{1,0:T(8,128)}) custom-call(s32[8]{0:T(128)} %copy-done.24, f32[2048,640]{1,0:T(8,128)} %fusion.15.pre_ref, f32[8,320]{1,0:T(8,128)} %copy-done.21, ...), custom_call_target="tpu_custom_call" | custom-call | bytes 45000000 | tf_op jit(solution)/shard_map/forward_scan/pallas_call | solution.py:818
  159.4 7.0 %gather_groups.1 = f32[4,8,320]{2,1,0:T(8,128)} custom-call(f32[8,320]{1,0:T(8,128)} %get-tuple-element.137.refs_0_), custom_call_target="tpu_custom_call" | custom-call | bytes 15000000 | tf_op jit(solution)/shard_map/gather_groups/pallas_call | solution.py:688
  166.5 2.0 slice.216
  169.2 1.9 slice.217
  174.3 2.9 constant_dynamic-update-slice_fusion.3
  177.2 2.4 constant_dynamic-update-slice_fusion.2
  179.6 3.3 fusion.11
  183.0 6.6 %convolution_convert_fusion = bf16[2048,2048]{1,0:T(8,128)(2,1)} fusion(bf16[2048,320]{1,0:T(8,128)(2,1)S(1)} %fusion.11, bf16[320,2048]{1,0:T(8,128)(2,1)S(1)} %bitcast.169), kind=kOutput, calls=%fused_computation.5 | convolution fusion | flops 2688548864 | bytes 11010048 | tf_op jit(solution)/shard_map/dot_general | solution.py:1505
  189.7 1.9 constant_dynamic-update-slice_fusion.1
  191.5 1.9 constant_dynamic-update-slice_fusion.mine_ref
  193.4 46.4 %scatter_feature.1 = f32[256,2048]{1,0:T(8,128)} custom-call(bf16[8,256,2048]{2,1,0:T(8,128)(2,1)} %bitcast.159), custom_call_target="tpu_custom_call" | custom-call | bytes 135000000 | tf_op jit(solution)/shard_map/scatter_feature/pallas_call | solution.py:321
  239.9 2.1 multiply_reduce_fusion.1
  243.5 40.6 %gather_feature.1 = bf16[8,256,2048]{2,1,0:T(8,128)(2,1)} custom-call(bf16[256,2048]{1,0:T(8,128)(2,1)} %multiply_convert_fusion.refs_0_), custom_call_target="tpu_custom_call" | custom-call | bytes 120000000 | tf_op jit(solution)/shard_map/gather_feature/pallas_call | solution.py:124
  284.2 31.2 %gated_unit.1 = (bf16[2048,768]{1,0:T(8,128)(2,1)}, bf16[2048,1536]{1,0:T(8,128)(2,1)}) custom-call(bf16[2048,2048]{1,0:T(8,128)(2,1)} %bitcast.163, bf16[1024,2048]{1,0:T(8,128)(2,1)} %constant_dynamic-update-slice_fusion.mine_ref, bf16[1024,2048]{1,0:T(8,128)(2,1)} %collective-permute-done.5.theirs_ref, ...), custom_call_target="tpu_custom_call" | custom-call | flops 19327352832 | bytes 41943040 | tf_op jit(solution)/shard_map/gated_unit/pallas_call | solution.py:1143
  315.4 9.9 %convolution_convert_fusion.3 = bf16[1024,2048]{1,0:T(8,128)(2,1)S(1)} fusion(bf16[2048,1536]{1,0:T(8,128)(2,1)} %all-gather.9.cloned.1.call-done.w_ref, bf16[2048,1536]{1,0:T(8,128)(2,1)} %get-tuple-element.165), kind=kOutput, calls=%fused_computation.10 | convolution fusion | flops 6444548096 | bytes 13631488 | tf_op jit(solution)/shard_map/dot_general | solution.py:1517
  325.8 7.4 %convolution_convert_fusion.2 = bf16[1024,2048]{1,0:T(8,128)(2,1)S(1)} fusion(bf16[2048,1536]{1,0:T(8,128)(2,1)S(1)} %copy-done.32, bf16[2048,1536]{1,0:T(8,128)(2,1)S(1)} %copy-done.33), kind=kOutput, calls=%fused_computation.9 | convolution fusion | flops 6444548096 | bytes 13631488 | tf_op jit(solution)/shard_map/dot_general | solution.py:1517
  333.2 2.6 fusion.27
  339.2 5.4 fusion.23
  344.6 7.3 %add_convert_fusion = bf16[768,2048]{1,0:T(8,128)(2,1)} fusion(f32[768,2048]{1,0:T(8,128)S(1)} %fusion.23, bf16[1024,2048]{1,0:T(8,128)(2,1)} %constant_dynamic-update-slice_fusion.mine_ref, bf16[2048,768]{1,0:T(8,128)(2,1)S(1)} %copy-done.11), kind=kOutput, calls=%fused_computation.7 | convolution fusion | flops 3224371200 | bytes 15204352 | tf_op jit(solution)/shard_map/dot_general | solution.py:1521
  352.1 13.9 %down_rows.1 = (bf16[1024,2048]{1,0:T(8,128)(2,1)}, bf16[1024,2048]{1,0:T(8,128)(2,1)}) custom-call(bf16[2048,768]{1,0:T(8,128)(2,1)} %get-tuple-element.155.h_ref, bf16[768,2048]{1,0:T(8,128)(2,1)} %all-gather.11.cloned.1.call-done.down_ref.w_ref), custom_call_target="tpu_custom_call" | custom-call | bytes 300000 | tf_op jit(solution)/shard_map/down_rows/pallas_call | solution.py:1190
  366.0 2.9 add_convert_fusion.3
  368.9 16.8 %scatter_tail.1 = f32[256,2048]{1,0:T(8,128)} custom-call(bf16[128,2048]{1,0:T(8,128)(2,1)} %get-tuple-element.153.ny_ref, bf16[128,2048]{1,0:T(8,128)(2,1)} %get-tuple-element.302.nx_ref, bf16[2,128,2048]{2,1,0:T(8,128)(2,1)} %bitcast.176, bf16[2,128,2048]{2,1,0:T(8,128)(2,1)} %collective-permute-done.7.bx_ref, ...), custom_call_target="tpu_custom_call" | custom-call | bytes 48000000 | tf_op jit(solution)/shard_map/scatter_tail/pallas_call | solution.py:539
  385.7 2.3 fusion.17
  388.1 4.0 fusion.65
  392.7 1.4 collective-permute-start.10
  394.1 16.7 %convolution_convert_fusion.1 = bf16[2048,1536]{1,0:T(8,128)(2,1)} fusion(bf16[2048,2048]{1,0:T(8,128)(2,1)S(1)} %bitcast.166, bf16[2048,1536]{1,0:T(8,128)(2,1)} %get-tuple-element.165), kind=kOutput, calls=%fused_computation.6 | convolution fusion | flops 12888047616 | bytes 20971520 | tf_op jit(solution)/shard_map/dot_general | solution.py:1543
  410.8 4.4 fusion.29
  415.2 2.7 collective-permute-done.9.bx_ref
  418.4 18.7 %gather_tail.1 = bf16[8,256,2048]{2,1,0:T(8,128)(2,1)} custom-call(bf16[256,2048]{1,0:T(8,128)(2,1)} %get-tuple-element.164.x_ref, bf16[256,2048]{1,0:T(8,128)(2,1)} %collective-permute-done.9.bx_ref, bf16[256,2048]{1,0:T(8,128)(2,1)} %collective-permute-done.10.by_ref), custom_call_target="tpu_custom_call" | custom-call | bytes 48000000 | tf_op jit(solution)/shard_map/gather_tail/pallas_call | solution.py:452
  439.2 17.6 %adjoint_scan.1 = (f32[2048,320]{1,0:T(8,128)}, f32[2048,320]{1,0:T(8,128)}, f32[2048,320]{1,0:T(8,128)}, f32[8,320]{1,0:T(8,128)}) custom-call(s32[8]{0:T(128)} %copy-done.24, bf16[2048,2048]{1,0:T(8,128)(2,1)} %bitcast.157, bf16[320,2048]{1,0:T(8,128)(2,1)} %bitcast.168, f32[2048,640]{1,0:T(8,128)} %fusion.15.pre_ref, f32[2048,320]{1,0:T(8,128)} %get-tuple-element.174.keep_ref), custom_call_target="tpu_custom_call" | custom-call | bytes 36000000 | tf_op jit(solution)/shard_map/adjoint_scan/pallas_call | solution.py:897
  460.9 4.2 collective-permute-done.12
  467.1 22.0 %backward_scan.1 = (bf16[2048,640]{1,0:T(8,128)(2,1)}, f32[8,320]{1,0:T(8,128)}, f32[8,320]{1,0:T(8,128)}, f32[320,320]{1,0:T(8,128)}, f32[320,320]{1,0:T(8,128)}) custom-call(s32[8]{0:T(128)} %copy-done.24, f32[2048,320]{1,0:T(8,128)} %get-tuple-element.175.d_mixed_ref, f32[2048,640]{1,0:T(8,128)} %fusion.15.pre_ref, ...), custom_call_target="tpu_custom_call" | custom-call | bytes 63000000 | tf_op jit(solution)/shard_map/backward_scan/pallas_call | solution.py:1060
  489.2 1.5 collective-permute-start.17
  490.7 7.9 %fusion.70.out_ref = f32[320,2048]{1,0:T(8,128)} fusion(bf16[2048,320]{1,0:T(8,128)(2,1)S(1)} %copy-done.17, bf16[2048,2048]{1,0:T(8,128)(2,1)} %bitcast.158), kind=kOutput, calls=%fused_computation.165 | convolution fusion | flops 2684354560 | bytes 12320768 | tf_op jit(solution)/shard_map/dot_general | solution.py:1572
  498.6 3.2 fusion.36
  501.8 1.5 collective-permute-start.18
  503.3 1.5 collective-permute-start.19
  504.9 1.6 copy-done.13
  506.4 11.1 %convolution_convert_fusion.4 = bf16[2048,640]{1,0:T(8,128)(2,1)} fusion(bf16[2048,640]{1,0:T(8,128)(2,1)S(1)} %fusion.52.a_ref, bf16[2048,2048]{1,0:T(8,128)(2,1)} %bitcast.162, f32[2048]{0:T(1024)S(1)} %bitcast.194, f32[2048]{0:T(1024)S(1)} %add_rsqrt_fusion), kind=kOutput, calls=%fused_computation.15 | convolution fusion | flops 5386797056 | bytes 13647872 | tf_op jit(solution)/shard_map/dot_general | solution.py:1578
  517.8 2.0 convert_add_fusion.1
  521.1 3.6 pack_sums.1.refs_0_
  524.8 3.8 exchange.6
  528.6 2.0 fusion.35
  530.7 1.4 fusion.22
  533.6 59.5 %scatter_dot.1 = (f32[256,2048]{1,0:T(8,128)}, bf16[8,64,1536]{2,1,0:T(8,128)(2,1)}) custom-call(bf16[2048,640]{1,0:T(8,128)(2,1)} %copy-done.13, bf16[2048,640]{1,0:T(8,128)(2,1)} %all-gather.7.cloned.1.call-done.w_ref, bf16[8,64,1536]{2,1,0:T(8,128)(2,1)} %bitcast.181), custom_call_target="tpu_custom_call" | custom-call | bytes 165000000 | tf_op jit(solution)/shard_map/scatter_dot/pallas_call | solution.py:291
  593.2 11.7 %exchange.7.x_ref = bf16[8,64,640]{2,1,0:T(8,128)(2,1)} custom-call(bf16[8,64,640]{2,1,0:T(8,128)(2,1)} %bitcast.184), custom_call_target="tpu_custom_call" | custom-call | bytes 45000000 | tf_op jit(solution)/shard_map/exchange/pallas_call | solution.py:611
  604.9 2.5 join_blocks.2
  607.4 4.0 join_blocks.3
  611.8 1.9 fusion.20
  613.7 7.3 %reduce-scatter.7.cloned.1.call-done.x_ref = bf16[80,2432]{1,0:T(8,128)(2,1)} async-done(((bf16[320,2432]{1,0:T(8,128)(2,1)}), bf16[80,2432]{1,0:T(8,128)(2,1)}) %reduce-scatter.7.cloned.1.call-update) | async-done | bytes 389136 | tf_op jit(solution)/shard_map/reduce_scatter | solution.py:1592
  621.0 1.9 unpack_sums.1
  622.9 1.4 copy.91
  (186 shorter events, 40.9 us)
Async XLA Ops:
  7.2 97.9 %all-gather.5.cloned.1.call-start = ((), (), s32[]{:S(2)}) async-start(), calls=%async_computation.4 | async-start | bytes 1638400 | tf_op jit(solution)/shard_map/all_gather | solution.py:1430
  7.9 102.4 %all-gather.7.cloned.1.call-start = ((), (), s32[]{:S(2)}) async-start(), calls=%async_computation.5 | async-start | bytes 3276800 | tf_op jit(solution)/shard_map/all_gather | solution.py:1441
  10.9 22.4 %copy-start.25 = (bf16[80,4]{0,1:T(4,128)(2,1)S(1)}, bf16[80,4]{0,1:T(4,128)(2,1)}, u32[]{:S(2)}) copy-start(bf16[80,4]{0,1:T(4,128)(2,1)} %param.24) | copy-start | bytes 1924
  10.9 22.5 %copy-start.28 = (bf16[80]{0:T(256)(128)(2,1)S(1)}, bf16[80]{0:T(256)(128)(2,1)}, u32[]{:S(2)}) copy-start(bf16[80]{0:T(256)(128)(2,1)} %param.25) | copy-start | bytes 484
  11.7 21.8 %copy-start.29 = (bf16[80]{0:T(256)(128)(2,1)S(1)}, bf16[80]{0:T(256)(128)(2,1)}, u32[]{:S(2)}) copy-start(bf16[80]{0:T(256)(128)(2,1)} %param.27) | copy-start | bytes 484
  11.7 21.9 %copy-start.30 = (bf16[80]{0:T(256)(128)(2,1)S(1)}, bf16[80]{0:T(256)(128)(2,1)}, u32[]{:S(2)}) copy-start(bf16[80]{0:T(256)(128)(2,1)} %param.29) | copy-start | bytes 484
  11.7 22.1 %copy-start.31 = (bf16[80]{0:T(256)(128)(2,1)S(1)}, bf16[80]{0:T(256)(128)(2,1)}, u32[]{:S(2)}) copy-start(bf16[80]{0:T(256)(128)(2,1)} %param.30) | copy-start | bytes 484
  11.7 22.2 %copy-start.22 = (bf16[80,160]{1,0:T(8,128)(2,1)S(1)}, bf16[80,160]{1,0:T(8,128)(2,1)}, u32[]{:S(2)}) copy-start(bf16[80,160]{1,0:T(8,128)(2,1)} %param.26) | copy-start | bytes 76804
  11.7 22.2 %copy-start.23 = (bf16[80,160]{1,0:T(8,128)(2,1)S(1)}, bf16[80,160]{1,0:T(8,128)(2,1)}, u32[]{:S(2)}) copy-start(bf16[80,160]{1,0:T(8,128)(2,1)} %param.28) | copy-start | bytes 76804
  31.5 252.6 %all-gather.11.cloned.1.call-start = ((), (), s32[]{:S(2)}) async-start(), calls=%async_computation.7 | async-start | bytes 3932160 | tf_op jit(solution)/shard_map/all_gather | solution.py:1463
  32.2 251.9 %all-gather.9.cloned.1.call-start = ((), (), s32[]{:S(2)}) async-start(), calls=%async_computation.6 | async-start | bytes 7864320 | tf_op jit(solution)/shard_map/all_gather | solution.py:1462
  34.7 67.9 %copy-start.10 = (bf16[256,2048]{1,0:T(8,128)(2,1)S(1)}, bf16[256,2048]{1,0:T(8,128)(2,1)}, u32[]{:S(2)}) copy-start(bf16[256,2048]{1,0:T(8,128)(2,1)} %param.20) | copy-start | bytes 3145732
  100.2 337.0 %reduce-scatter.5.cloned.1.call-start = ((), (), s32[]{:S(2)}) async-start(), calls=%async_computation.8 | async-start | bytes 3932160 | tf_op jit(solution)/shard_map/reduce_scatter | solution.py:1534
  105.0 19.8 %copy-start.24 = (s32[8]{0:T(128)}, s32[8]{0:T(128)S(1)}, u32[]{:S(2)}) copy-start(s32[8]{0:T(128)S(1)} %fusion.62.order_ref) | copy-start | bytes 100
  121.9 36.2 %collective-permute-start.1 = (bf16[256,2048]{1,0:T(8,128)(2,1)S(1)}, bf16[256,2048]{1,0:T(8,128)(2,1)S(1)}, u32[]{:S(2)}, u32[]{:S(2)}) collective-permute-start(bf16[256,2048]{1,0:T(8,128)(2,1)S(1)} %copy-done.10), channel_id=1, source_target_pairs={{0,4},{4,0},{1,5},{5,1},{2,6},{6,2},{3,7},{7,3},{8,12},{12,8},{9,1... | collective-permute-start | bytes 3145736 | tf_op jit(solution)/shard_map/ppermute | solution.py:348
  122.6 35.5 %collective-permute-start.2 = (bf16[256,2048]{1,0:T(8,128)(2,1)S(1)}, bf16[256,2048]{1,0:T(8,128)(2,1)S(1)}, u32[]{:S(2)}, u32[]{:S(2)}) collective-permute-start(bf16[256,2048]{1,0:T(8,128)(2,1)S(1)} %copy-done.10), channel_id=1, source_target_pairs={{0,2},{2,0},{1,3},{3,1},{4,6},{6,4},{5,7},{7,5},{8,10},{10,8},{9,1... | collective-permute-start | bytes 3145736 | tf_op jit(solution)/shard_map/ppermute | solution.py:348
  134.2 6.3 collective-permute-start
  140.5 0.6 copy-start.21
  158.1 1.0 copy-start.14
  158.2 1.3 copy-start.15
  166.5 13.2 %copy-start.2 = (f32[2048,320]{1,0:T(8,128)S(1)}, f32[2048,320]{1,0:T(8,128)}, u32[]{:S(2)}) copy-start(f32[2048,320]{1,0:T(8,128)} %get-tuple-element.134.prod_ref.prod_before_ref) | copy-start | bytes 7864324
  168.5 21.2 %collective-permute-start.3 = (bf16[128,2048]{1,0:T(8,128)(2,1)}, bf16[128,2048]{1,0:T(8,128)(2,1)}, u32[]{:S(2)}, u32[]{:S(2)}) collective-permute-start(bf16[128,2048]{1,0:T(8,128)(2,1)} %slice.216), channel_id=1, source_target_pairs={{0,2},{2,0},{1,3},{3,1},{4,6},{6,4},{5,7},{7,5},{8,10},{10,8},{9,1... | collective-permute-start | bytes 1572872 | tf_op jit(solution)/shard_map/ppermute | solution.py:348
  171.1 18.6 %collective-permute-start.4 = (bf16[128,2048]{1,0:T(8,128)(2,1)}, bf16[128,2048]{1,0:T(8,128)(2,1)}, u32[]{:S(2)}, u32[]{:S(2)}) collective-permute-start(bf16[128,2048]{1,0:T(8,128)(2,1)} %slice.217), channel_id=1, source_target_pairs={{0,4},{4,0},{1,5},{5,1},{2,6},{6,2},{3,7},{7,3},{8,12},{12,8},{9,1... | collective-permute-start | bytes 1572872 | tf_op jit(solution)/shard_map/ppermute | solution.py:348
  173.3 6.3 %copy-start.3 = (f32[2048,320]{1,0:T(8,128)S(1)}, f32[2048,320]{1,0:T(8,128)}, u32[]{:S(2)}) copy-start(f32[2048,320]{1,0:T(8,128)} %get-tuple-element.133.state_ref.state_before_ref) | copy-start | bytes 7864324
  179.6 3.4 copy-start.7
  183.0 6.7 %copy-start.16 = (bf16[2048,320]{1,0:T(8,128)(2,1)}, bf16[2048,320]{1,0:T(8,128)(2,1)S(1)}, u32[]{:S(2)}) copy-start(bf16[2048,320]{1,0:T(8,128)(2,1)S(1)} %fusion.11) | copy-start | bytes 3932164
  193.4 90.7 %collective-permute-start.5 = (bf16[1024,2048]{1,0:T(8,128)(2,1)}, bf16[1024,2048]{1,0:T(8,128)(2,1)}, u32[]{:S(2)}, u32[]{:S(2)}) collective-permute-start(bf16[1024,2048]{1,0:T(8,128)(2,1)} %constant_dynamic-update-slice_fusion.mine_ref), channel_id=1, source_target_pairs={{0,1},{1,0},{2,3},{3,2},{4,5},{5,4},{6,7},{7,6},{8,9},{9,8},{10,11... | collective-permute-start | bytes 12582920 | tf_op jit(solution)/shard_map/ppermute | solution.py:348
  193.4 46.5 %copy-start.1 = (bf16[256,2048]{1,0:T(8,128)(2,1)S(1)}, bf16[256,2048]{1,0:T(8,128)(2,1)}, u32[]{:S(2)}) copy-start(bf16[256,2048]{1,0:T(8,128)(2,1)} %refs_0_.1) | copy-start | bytes 3145732
  239.9 2.3 copy-start
  315.4 10.4 %copy-start.32 = (bf16[2048,1536]{1,0:T(8,128)(2,1)S(1)}, bf16[2048,1536]{1,0:T(8,128)(2,1)}, u32[]{:S(2)}) copy-start(bf16[2048,1536]{1,0:T(8,128)(2,1)} %all-gather.9.cloned.1.call-done.w_ref) | copy-start | bytes 18874372
  315.4 10.4 %copy-start.33 = (bf16[2048,1536]{1,0:T(8,128)(2,1)S(1)}, bf16[2048,1536]{1,0:T(8,128)(2,1)}, u32[]{:S(2)}) copy-start(bf16[2048,1536]{1,0:T(8,128)(2,1)} %get-tuple-element.165) | copy-start | bytes 18874372
  325.3 7.9 %collective-permute-start.6 = (bf16[1024,2048]{1,0:T(8,128)(2,1)S(1)}, bf16[1024,2048]{1,0:T(8,128)(2,1)S(1)}, u32[]{:S(2)}, u32[]{:S(2)}) collective-permute-start(bf16[1024,2048]{1,0:T(8,128)(2,1)S(1)} %convolution_convert_fusion.3), channel_id=1, source_target_pairs={{0,1},{1,0},{2,3},{3,2},{4,5},{5,4},{6,7},{7,6},{8,9},{9,8},{10,11... | collective-permute-start | bytes 12582920 | tf_op jit(solution)/shard_map/ppermute | solution.py:348
  333.2 11.5 %copy-start.9 = (bf16[1024,2048]{1,0:T(8,128)(2,1)}, bf16[1024,2048]{1,0:T(8,128)(2,1)S(1)}, u32[]{:S(2)}) copy-start(bf16[1024,2048]{1,0:T(8,128)(2,1)S(1)} %convolution_convert_fusion.2) | copy-start | bytes 12582916
  333.2 2.7 copy-start.8
  335.8 3.5 copy-start.11
  337.2 31.7 %collective-permute-start.7 = (bf16[2,128,2048]{2,1,0:T(8,128)(2,1)}, bf16[2,128,2048]{2,1,0:T(8,128)(2,1)}, u32[]{:S(2)}, u32[]{:S(2)}) collective-permute-start(bf16[2,128,2048]{2,1,0:T(8,128)(2,1)} %get-tuple-element.158), channel_id=1, source_target_pairs={{0,4},{4,0},{1,5},{5,1},{2,6},{6,2},{3,7},{7,3},{8,12},{12,8},{9,1... | collective-permute-start | bytes 3145736 | tf_op jit(solution)/shard_map/ppermute | solution.py:348
  338.6 30.3 %collective-permute-start.8 = (bf16[2,128,2048]{2,1,0:T(8,128)(2,1)}, bf16[2,128,2048]{2,1,0:T(8,128)(2,1)}, u32[]{:S(2)}, u32[]{:S(2)}) collective-permute-start(bf16[2,128,2048]{2,1,0:T(8,128)(2,1)} %get-tuple-element.159), channel_id=1, source_target_pairs={{0,2},{2,0},{1,3},{3,1},{4,6},{6,4},{5,7},{7,5},{8,10},{10,8},{9,1... | collective-permute-start | bytes 3145736 | tf_op jit(solution)/shard_map/ppermute | solution.py:348
  352.0 181.6 %reduce-scatter.9.cloned.1.call-start = ((), (), s32[]{:S(2)}) async-start(), calls=%async_computation.10 | async-start | bytes 7864320 | tf_op jit(solution)/shard_map/reduce_scatter | solution.py:1548
  368.9 25.2 %slice-start = ((s8[8388608]{0:T(1024)(128)(4,1)}), s8[4194304]{0:T(1024)(128)(4,1)S(1)}, s32[]{:S(2)}) async-start(s8[8388608]{0:T(1024)(128)(4,1)} %bitcast.164), calls=%async_computation.12 | async-start | bytes 8388608
  385.7 2.4 copy-start.4
  385.7 8.4 %slice-start.1 = ((s8[8388608]{0:T(1024)(128)(4,1)}), s8[4194304]{0:T(1024)(128)(4,1)S(1)}, s32[]{:S(2)}) async-start(s8[8388608]{0:T(1024)(128)(4,1)} %bitcast.164), calls=%async_computation.13 | async-start | bytes 8388608
  392.0 18.8 %collective-permute-start.11 = (bf16[1024,2048]{1,0:T(8,128)(2,1)}, bf16[1024,2048]{1,0:T(8,128)(2,1)}, u32[]{:S(2)}, u32[]{:S(2)}) collective-permute-start(bf16[1024,2048]{1,0:T(8,128)(2,1)} %get-tuple-element.167), channel_id=1, source_target_pairs={{0,1},{1,0},{2,3},{3,2},{4,5},{5,4},{6,7},{7,6},{8,9},{9,8},{10,11... | collective-permute-start | bytes 12582920 | tf_op jit(solution)/shard_map/ppermute | solution.py:348
  392.0 25.9 %collective-permute-start.9 = (bf16[256,2048]{1,0:T(8,128)(2,1)}, bf16[256,2048]{1,0:T(8,128)(2,1)}, u32[]{:S(2)}, u32[]{:S(2)}) collective-permute-start(bf16[256,2048]{1,0:T(8,128)(2,1)} %get-tuple-element.164.x_ref), channel_id=1, source_target_pairs={{0,4},{4,0},{1,5},{5,1},{2,6},{6,2},{3,7},{7,3},{8,12},{12,8},{9,1... | collective-permute-start | bytes 3145736 | tf_op jit(solution)/shard_map/ppermute | solution.py:348
  392.7 25.6 %collective-permute-start.10 = (bf16[256,2048]{1,0:T(8,128)(2,1)}, bf16[256,2048]{1,0:T(8,128)(2,1)}, u32[]{:S(2)}, u32[]{:S(2)}) collective-permute-start(bf16[256,2048]{1,0:T(8,128)(2,1)} %get-tuple-element.164.x_ref), channel_id=1, source_target_pairs={{0,2},{2,0},{1,3},{3,1},{4,6},{6,4},{5,7},{7,5},{8,10},{10,8},{9,1... | collective-permute-start | bytes 3145736 | tf_op jit(solution)/shard_map/ppermute | solution.py:348
  418.3 174.9 %reduce-scatter.11.cloned.1.call-start = ((), (), s32[]{:S(2)}) async-start(), calls=%async_computation.11 | async-start | bytes 3276800 | tf_op jit(solution)/shard_map/reduce_scatter | solution.py:1585
  437.1 29.1 %collective-permute-start.15 = (bf16[2,128,2048]{2,1,0:T(8,128)(2,1)}, bf16[2,128,2048]{2,1,0:T(8,128)(2,1)S(1)}, u32[]{:S(2)}, u32[]{:S(2)}) collective-permute-start(bf16[2,128,2048]{2,1,0:T(8,128)(2,1)} %get-tuple-element.181), channel_id=1, source_target_pairs={{0,4},{4,0},{1,5},{5,1},{2,6},{6,2},{3,7},{7,3},{8,12},{12,8},{9,1... | collective-permute-start | bytes 3145736 | tf_op jit(solution)/shard_map/ppermute | solution.py:348
  437.9 28.4 %collective-permute-start.16 = (bf16[2,128,2048]{2,1,0:T(8,128)(2,1)}, bf16[2,128,2048]{2,1,0:T(8,128)(2,1)S(1)}, u32[]{:S(2)}, u32[]{:S(2)}) collective-permute-start(bf16[2,128,2048]{2,1,0:T(8,128)(2,1)} %get-tuple-element.182), channel_id=1, source_target_pairs={{0,2},{2,0},{1,3},{3,1},{4,6},{6,4},{5,7},{7,5},{8,10},{10,8},{9,1... | collective-permute-start | bytes 3145736 | tf_op jit(solution)/shard_map/ppermute | solution.py:348
  456.9 8.2 %collective-permute-start.12 = (f32[8,320]{1,0:T(8,128)}, f32[8,320]{1,0:T(8,128)S(1)}, u32[]{:S(2)}, u32[]{:S(2)}) collective-permute-start(f32[8,320]{1,0:T(8,128)} %get-tuple-element.180), channel_id=1, source_target_pairs={{24,0},{25,1},{26,2},{27,3},{28,4},{29,5},{30,6},{31,7}} | collective-permute-start | bytes 30728 | tf_op jit(solution)/shard_map/ppermute | solution.py:1557
  458.2 8.0 %collective-permute-start.13 = (f32[8,320]{1,0:T(8,128)}, f32[8,320]{1,0:T(8,128)S(1)}, u32[]{:S(2)}, u32[]{:S(2)}) collective-permute-start(f32[8,320]{1,0:T(8,128)} %get-tuple-element.180), channel_id=1, source_target_pairs={{16,0},{24,8},{17,1},{25,9},{18,2},{26,10},{19,3},{27,11},{20,4},{... | collective-permute-start | bytes 30728 | tf_op jit(solution)/shard_map/ppermute | solution.py:1557
  459.5 6.8 %collective-permute-start.14 = (f32[8,320]{1,0:T(8,128)}, f32[8,320]{1,0:T(8,128)S(1)}, u32[]{:S(2)}, u32[]{:S(2)}) collective-permute-start(f32[8,320]{1,0:T(8,128)} %get-tuple-element.180), channel_id=1, source_target_pairs={{8,0},{16,8},{24,16},{9,1},{17,9},{25,17},{10,2},{18,10},{26,18},{... | collective-permute-start | bytes 30728 | tf_op jit(solution)/shard_map/ppermute | solution.py:1557
  466.3 32.3 %copy-start.18 = (bf16[2,128,2048]{2,1,0:T(8,128)(2,1)}, bf16[2,128,2048]{2,1,0:T(8,128)(2,1)S(1)}, u32[]{:S(2)}) copy-start(bf16[2,128,2048]{2,1,0:T(8,128)(2,1)S(1)} %collective-permute-done.15) | copy-start | bytes 3145732
  466.3 32.3 %copy-start.19 = (bf16[2,128,2048]{2,1,0:T(8,128)(2,1)}, bf16[2,128,2048]{2,1,0:T(8,128)(2,1)S(1)}, u32[]{:S(2)}) copy-start(bf16[2,128,2048]{2,1,0:T(8,128)(2,1)S(1)} %collective-permute-done.16) | copy-start | bytes 3145732
  467.1 23.6 %copy-start.17 = (bf16[2048,320]{1,0:T(8,128)(2,1)S(1)}, bf16[2048,320]{1,0:T(8,128)(2,1)}, u32[]{:S(2)}) copy-start(bf16[2048,320]{1,0:T(8,128)(2,1)} %copy-done.16) | copy-start | bytes 3932164
  489.2 15.6 %collective-permute-start.17 = (f32[8,320]{1,0:T(8,128)}, f32[8,320]{1,0:T(8,128)S(1)}, u32[]{:S(2)}, u32[]{:S(2)}) collective-permute-start(f32[8,320]{1,0:T(8,128)} %get-tuple-element.186), channel_id=1, source_target_pairs={{8,0},{16,8},{24,16},{9,1},{17,9},{25,17},{10,2},{18,10},{26,18},{... | collective-permute-start | bytes 30728 | tf_op jit(solution)/shard_map/ppermute | solution.py:1570
  498.6 6.2 copy-start.12
  501.8 15.7 %collective-permute-start.18 = (bf16[128,2048]{1,0:T(8,128)(2,1)}, bf16[128,2048]{1,0:T(8,128)(2,1)}, u32[]{:S(2)}, u32[]{:S(2)}) collective-permute-start(bf16[128,2048]{1,0:T(8,128)(2,1)} %get-tuple-element.299), channel_id=1, source_target_pairs={{0,2},{2,0},{1,3},{3,1},{4,6},{6,4},{5,7},{7,5},{8,10},{10,8},{9,1... | collective-permute-start | bytes 1572872 | tf_op jit(solution)/shard_map/ppermute | solution.py:348
  503.3 14.2 %collective-permute-start.19 = (bf16[128,2048]{1,0:T(8,128)(2,1)}, bf16[128,2048]{1,0:T(8,128)(2,1)}, u32[]{:S(2)}, u32[]{:S(2)}) collective-permute-start(bf16[128,2048]{1,0:T(8,128)(2,1)} %get-tuple-element.298), channel_id=1, source_target_pairs={{0,4},{4,0},{1,5},{5,1},{2,6},{6,2},{3,7},{7,3},{8,12},{12,8},{9,1... | collective-permute-start | bytes 1572872 | tf_op jit(solution)/shard_map/ppermute | solution.py:348
  504.9 1.6 copy-start.13
  517.5 103.5 %reduce-scatter.7.cloned.1.call-start = ((), (), s32[]{:S(2)}) async-start(), calls=%async_computation.9 | async-start | bytes 1945600 | tf_op jit(solution)/shard_map/reduce_scatter | solution.py:1592
  517.8 2.0 copy-start.20
  530.6 1.5 copy-start.26
  530.7 2.2 copy-start.27
  593.1 18.3 %copy-start.5 = (f32[256,2048]{1,0:T(8,128)S(1)}, f32[256,2048]{1,0:T(8,128)}, u32[]{:S(2)}) copy-start(f32[256,2048]{1,0:T(8,128)} %get-tuple-element.215) | copy-start | bytes 6291460
  607.4 4.4 copy-start.6
Sparse Core Ops, SparseCore 0:
  9.6 35.3 all-gather.4
  47.2 54.0 all-gather.6
  102.8 63.0 all-gather.10
  167.3 114.0 all-gather.8
  352.1 58.7 reduce-scatter.4
  418.4 110.3 reduce-scatter.8
  531.1 52.6 reduce-scatter.10
  586.1 34.8 reduce-scatter.6

commit v8 on v7

--- a/solution.py
+++ b/solution.py
@@ -1165,7 +1165,7 @@
 
 def down_kernel(h_ref, w_ref, mine_ref, theirs_ref):
     width = w_ref.shape[1]
-    tile = 512
+    tile = 1024
     hidden = h_ref[...]
 
     def into(ref):

time: 639 us -> 638 us (level)
  no operation moved by 1% of the time
where the time goes in v8:
time: 638 us; the launch traced here: 630 us
  Pallas kernels  404 us (63%)
  matrix products  83.6 us (13%)
  other arithmetic  51.5 us (8%)
  local copies, waits for them, and re-layouts  34 us (5%)
  starting transfers between devices  22.1 us (3%)
  waiting for transfers between devices  18 us (3%)
  between operations  17 us (3%)
    pallas_call x1, Pallas kernels, gather_exchange(): pl.pallas_call(gather_kernel, out_shape=(jax.ShapeDtypeStruct((NF, rows,...  61.9 us
    pallas_call x1, Pallas kernels, scatter_dot(): pl.pallas_call(scatter_dot_kernel, out_shape=(jax.ShapeDtypeStruct((rows,...  59.5 us
    pallas_call x1, Pallas kernels, scatter_feature(): pl.pallas_call(scatter_kernel, out_shape=jax.ShapeDtypeStruct((rows, widt...  46.4 us
    pallas_call x1, Pallas kernels, gather_feature(): pl.pallas_call(gather_kernel, out_shape=jax.ShapeDtypeStruct((NF, rows, w...  40.6 us
    pallas_call x4, Pallas kernels, exchange(): pl.pallas_call(functools.partial(exchange_kernel, axes), out_shape=tuple(...  35 us
    pallas_call x1, Pallas kernels, gated_unit(): pl.pallas_call(gated_kernel, grid=(steps,), out_shape=(jax.ShapeDtypeStru...  31.2 us
    pallas_call x1, Pallas kernels, backward_scan(): pl.pallas_call(backward_kernel, out_shape=(jax.ShapeDtypeStruct((rows, 2...  22.2 us
    pallas_call x1, Pallas kernels, gather_tail(): pl.pallas_call(gather_tail_kernel, out_shape=jax.ShapeDtypeStruct((NF, ro...  18.5 us
  transfers between devices with their start and end apart: 28, of which 5 were waited for; matrix products, arithmetic and copies ran while one was open for 24% of the time, Pallas kernels for 59%

profile of v8, /device:TPU:0, one launch (start us, length us, event | category | flops | bytes accessed | tf_op | source)
XLA Modules:
  0.0 630.0 jit_solution(16448635996798011671)
XLA Ops:
  8.7 2.2 split_blocks.3
  11.8 2.1 pad_maximum_fusion.refs_0_
  13.8 15.6 %exchange.4 = bf16[8,80,640]{2,1,0:T(8,128)(2,1)} custom-call(bf16[8,80,640]{2,1,0:T(8,128)(2,1)} %pad_maximum_fusion.refs_0_), custom_call_target="tpu_custom_call" | custom-call | bytes 45000000 | tf_op jit(solution)/shard_map/exchange/pallas_call | solution.py:611
  29.5 2.0 slice.198
  34.7 3.0 split_blocks.2.refs_1_
  38.2 61.9 %gather_exchange.1 = (bf16[8,256,2048]{2,1,0:T(8,128)(2,1)}, bf16[8,64,1536]{2,1,0:T(8,128)(2,1)}, f32[4,8,512]{2,1,0:T(8,128)}, bf16[4,80,384]{2,1,0:T(8,128)(2,1)}) custom-call(bf16[256,2048]{1,0:T(8,128)(2,1)} %refs_0_.1, bf16[8,64,1536]{2,1,0:T(8,128)(2,1)} %split_blocks.2.refs_1_, f32[8,512]{1,0:T(8,128)} %fusion.56.refs_2_, bf16[80,384]{1,0:T(8,128)(2,1)} %pad.31.refs_3_), custom_call_target="tpu_custom_call" | custom-call | bytes 165000000 | tf_op jit(solution)/shard_map/gather_exchange/pallas_call | solution.py:631
  105.1 5.2 fusion
  110.3 11.6 %fusion.15.pre_ref = f32[2048,640]{1,0:T(8,128)} fusion(bf16[2048,640]{1,0:T(8,128)(2,1)} %all-gather.7.cloned.1.call-done.w_ref, bf16[2048,2048]{1,0:T(8,128)(2,1)} %bitcast.161, f32[2048]{0:T(1024)S(1)} %bitcast.193, f32[2048]{0:T(1024)S(1)} %add_rsqrt_fusion), kind=kOutput, calls=%fused_computation.27 | convolution fusion | flops 5385486336 | bytes 16269312 | tf_op jit(solution)/shard_map/dot_general | solution.py:1488
  122.6 1.5 collective-permute-start.2
  127.4 3.8 exchange.5
  134.2 2.8 collective-permute-start
  137.9 2.6 copy.78
  141.0 17.0 %forward_scan.1 = (bf16[2048,320]{1,0:T(8,128)(2,1)}, bf16[2048,320]{1,0:T(8,128)(2,1)}, f32[2048,320]{1,0:T(8,128)}, f32[2048,320]{1,0:T(8,128)}, f32[2048,320]{1,0:T(8,128)}, /*index=5*/f32[8,320]{1,0:T(8,128)}) custom-call(s32[8]{0:T(128)} %copy-done.24, f32[2048,640]{1,0:T(8,128)} %fusion.15.pre_ref, f32[8,320]{1,0:T(8,128)} %copy-done.21, ...), custom_call_target="tpu_custom_call" | custom-call | bytes 45000000 | tf_op jit(solution)/shard_map/forward_scan/pallas_call | solution.py:818
  159.4 7.0 %gather_groups.1 = f32[4,8,320]{2,1,0:T(8,128)} custom-call(f32[8,320]{1,0:T(8,128)} %get-tuple-element.137.refs_0_), custom_call_target="tpu_custom_call" | custom-call | bytes 15000000 | tf_op jit(solution)/shard_map/gather_groups/pallas_call | solution.py:688
  166.4 2.0 slice.216
  169.1 1.9 slice.217
  171.0 1.4 collective-permute-start.4
  174.3 2.9 constant_dynamic-update-slice_fusion.3
  177.2 2.4 constant_dynamic-update-slice_fusion.2
  179.6 3.3 fusion.11
  183.0 6.6 %convolution_convert_fusion = bf16[2048,2048]{1,0:T(8,128)(2,1)} fusion(bf16[2048,320]{1,0:T(8,128)(2,1)S(1)} %fusion.11, bf16[320,2048]{1,0:T(8,128)(2,1)S(1)} %bitcast.169), kind=kOutput, calls=%fused_computation.5 | convolution fusion | flops 2688548864 | bytes 11010048 | tf_op jit(solution)/shard_map/dot_general | solution.py:1505
  189.7 1.9 constant_dynamic-update-slice_fusion.1
  191.5 1.9 constant_dynamic-update-slice_fusion.mine_ref
  193.4 46.4 %scatter_feature.1 = f32[256,2048]{1,0:T(8,128)} custom-call(bf16[8,256,2048]{2,1,0:T(8,128)(2,1)} %bitcast.159), custom_call_target="tpu_custom_call" | custom-call | bytes 135000000 | tf_op jit(solution)/shard_map/scatter_feature/pallas_call | solution.py:321
  239.9 2.1 multiply_reduce_fusion.1
  243.4 40.6 %gather_feature.1 = bf16[8,256,2048]{2,1,0:T(8,128)(2,1)} custom-call(bf16[256,2048]{1,0:T(8,128)(2,1)} %multiply_convert_fusion.refs_0_), custom_call_target="tpu_custom_call" | custom-call | bytes 120000000 | tf_op jit(solution)/shard_map/gather_feature/pallas_call | solution.py:124
  284.1 31.2 %gated_unit.1 = (bf16[2048,768]{1,0:T(8,128)(2,1)}, bf16[2048,1536]{1,0:T(8,128)(2,1)}) custom-call(bf16[2048,2048]{1,0:T(8,128)(2,1)} %bitcast.163, bf16[1024,2048]{1,0:T(8,128)(2,1)} %constant_dynamic-update-slice_fusion.mine_ref, bf16[1024,2048]{1,0:T(8,128)(2,1)} %collective-permute-done.5.theirs_ref, ...), custom_call_target="tpu_custom_call" | custom-call | flops 19327352832 | bytes 41943040 | tf_op jit(solution)/shard_map/gated_unit/pallas_call | solution.py:1143
  315.3 9.9 %convolution_convert_fusion.3 = bf16[1024,2048]{1,0:T(8,128)(2,1)S(1)} fusion(bf16[2048,1536]{1,0:T(8,128)(2,1)} %all-gather.9.cloned.1.call-done.w_ref, bf16[2048,1536]{1,0:T(8,128)(2,1)} %get-tuple-element.165), kind=kOutput, calls=%fused_computation.10 | convolution fusion | flops 6444548096 | bytes 13631488 | tf_op jit(solution)/shard_map/dot_general | solution.py:1517
  325.7 7.2 %convolution_convert_fusion.2 = bf16[1024,2048]{1,0:T(8,128)(2,1)S(1)} fusion(bf16[2048,1536]{1,0:T(8,128)(2,1)S(1)} %copy-done.32, bf16[2048,1536]{1,0:T(8,128)(2,1)S(1)} %copy-done.33), kind=kOutput, calls=%fused_computation.9 | convolution fusion | flops 6444548096 | bytes 13631488 | tf_op jit(solution)/shard_map/dot_general | solution.py:1517
  332.9 2.6 fusion.27
  335.5 1.4 fusion.39
  338.9 5.4 fusion.23
  344.3 7.3 %add_convert_fusion = bf16[768,2048]{1,0:T(8,128)(2,1)} fusion(f32[768,2048]{1,0:T(8,128)S(1)} %fusion.23, bf16[1024,2048]{1,0:T(8,128)(2,1)} %constant_dynamic-update-slice_fusion.mine_ref, bf16[2048,768]{1,0:T(8,128)(2,1)S(1)} %copy-done.11), kind=kOutput, calls=%fused_computation.7 | convolution fusion | flops 3224371200 | bytes 15204352 | tf_op jit(solution)/shard_map/dot_general | solution.py:1521
  351.7 12.9 %down_rows.1 = (bf16[1024,2048]{1,0:T(8,128)(2,1)}, bf16[1024,2048]{1,0:T(8,128)(2,1)}) custom-call(bf16[2048,768]{1,0:T(8,128)(2,1)} %get-tuple-element.155.h_ref, bf16[768,2048]{1,0:T(8,128)(2,1)} %all-gather.11.cloned.1.call-done.down_ref.w_ref), custom_call_target="tpu_custom_call" | custom-call | bytes 300000 | tf_op jit(solution)/shard_map/down_rows/pallas_call | solution.py:1190
  364.6 2.9 add_convert_fusion.3
  367.5 16.6 %scatter_tail.1 = f32[256,2048]{1,0:T(8,128)} custom-call(bf16[128,2048]{1,0:T(8,128)(2,1)} %get-tuple-element.153.ny_ref, bf16[128,2048]{1,0:T(8,128)(2,1)} %get-tuple-element.302.nx_ref, bf16[2,128,2048]{2,1,0:T(8,128)(2,1)} %bitcast.176, bf16[2,128,2048]{2,1,0:T(8,128)(2,1)} %collective-permute-done.7.bx_ref, ...), custom_call_target="tpu_custom_call" | custom-call | bytes 48000000 | tf_op jit(solution)/shard_map/scatter_tail/pallas_call | solution.py:539
  384.2 2.3 fusion.17
  386.5 4.0 fusion.65
  392.5 16.7 %convolution_convert_fusion.1 = bf16[2048,1536]{1,0:T(8,128)(2,1)} fusion(bf16[2048,2048]{1,0:T(8,128)(2,1)S(1)} %bitcast.166, bf16[2048,1536]{1,0:T(8,128)(2,1)} %get-tuple-element.165), kind=kOutput, calls=%fused_computation.6 | convolution fusion | flops 12888047616 | bytes 20971520 | tf_op jit(solution)/shard_map/dot_general | solution.py:1543
  409.2 4.5 fusion.29
  413.7 2.7 collective-permute-done.9.bx_ref
  417.0 18.5 %gather_tail.1 = bf16[8,256,2048]{2,1,0:T(8,128)(2,1)} custom-call(bf16[256,2048]{1,0:T(8,128)(2,1)} %get-tuple-element.164.x_ref, bf16[256,2048]{1,0:T(8,128)(2,1)} %collective-permute-done.9.bx_ref, bf16[256,2048]{1,0:T(8,128)(2,1)} %collective-permute-done.10.by_ref), custom_call_target="tpu_custom_call" | custom-call | bytes 48000000 | tf_op jit(solution)/shard_map/gather_tail/pallas_call | solution.py:452
  437.7 17.6 %adjoint_scan.1 = (f32[2048,320]{1,0:T(8,128)}, f32[2048,320]{1,0:T(8,128)}, f32[2048,320]{1,0:T(8,128)}, f32[8,320]{1,0:T(8,128)}) custom-call(s32[8]{0:T(128)} %copy-done.24, bf16[2048,2048]{1,0:T(8,128)(2,1)} %bitcast.157, bf16[320,2048]{1,0:T(8,128)(2,1)} %bitcast.168, f32[2048,640]{1,0:T(8,128)} %fusion.15.pre_ref, f32[2048,320]{1,0:T(8,128)} %get-tuple-element.174.keep_ref), custom_call_target="tpu_custom_call" | custom-call | bytes 36000000 | tf_op jit(solution)/shard_map/adjoint_scan/pallas_call | solution.py:897
  459.3 4.2 collective-permute-done.12
  465.8 22.2 %backward_scan.1 = (bf16[2048,640]{1,0:T(8,128)(2,1)}, f32[8,320]{1,0:T(8,128)}, f32[8,320]{1,0:T(8,128)}, f32[320,320]{1,0:T(8,128)}, f32[320,320]{1,0:T(8,128)}) custom-call(s32[8]{0:T(128)} %copy-done.24, f32[2048,320]{1,0:T(8,128)} %get-tuple-element.175.d_mixed_ref, f32[2048,640]{1,0:T(8,128)} %fusion.15.pre_ref, ...), custom_call_target="tpu_custom_call" | custom-call | bytes 63000000 | tf_op jit(solution)/shard_map/backward_scan/pallas_call | solution.py:1060
  489.3 7.9 %fusion.70.out_ref = f32[320,2048]{1,0:T(8,128)} fusion(bf16[2048,320]{1,0:T(8,128)(2,1)S(1)} %copy-done.17, bf16[2048,2048]{1,0:T(8,128)(2,1)} %bitcast.158), kind=kOutput, calls=%fused_computation.165 | convolution fusion | flops 2684354560 | bytes 12320768 | tf_op jit(solution)/shard_map/dot_general | solution.py:1572
  497.2 3.2 fusion.36
  500.4 1.5 collective-permute-start.18
  501.9 1.5 collective-permute-start.19
  503.5 1.6 copy-done.13
  505.1 11.0 %convolution_convert_fusion.4 = bf16[2048,640]{1,0:T(8,128)(2,1)} fusion(bf16[2048,640]{1,0:T(8,128)(2,1)S(1)} %fusion.52.a_ref, bf16[2048,2048]{1,0:T(8,128)(2,1)} %bitcast.162, f32[2048]{0:T(1024)S(1)} %bitcast.194, f32[2048]{0:T(1024)S(1)} %add_rsqrt_fusion), kind=kOutput, calls=%fused_computation.15 | convolution fusion | flops 5386797056 | bytes 13647872 | tf_op jit(solution)/shard_map/dot_general | solution.py:1578
  516.2 2.0 convert_add_fusion.1
  519.5 3.6 pack_sums.1.refs_0_
  523.2 3.8 exchange.6
  527.0 2.0 fusion.35
  529.1 1.4 fusion.22
  532.0 59.5 %scatter_dot.1 = (f32[256,2048]{1,0:T(8,128)}, bf16[8,64,1536]{2,1,0:T(8,128)(2,1)}) custom-call(bf16[2048,640]{1,0:T(8,128)(2,1)} %copy-done.13, bf16[2048,640]{1,0:T(8,128)(2,1)} %all-gather.7.cloned.1.call-done.w_ref, bf16[8,64,1536]{2,1,0:T(8,128)(2,1)} %bitcast.181), custom_call_target="tpu_custom_call" | custom-call | bytes 165000000 | tf_op jit(solution)/shard_map/scatter_dot/pallas_call | solution.py:291
  591.6 11.7 %exchange.7.x_ref = bf16[8,64,640]{2,1,0:T(8,128)(2,1)} custom-call(bf16[8,64,640]{2,1,0:T(8,128)(2,1)} %bitcast.184), custom_call_target="tpu_custom_call" | custom-call | bytes 45000000 | tf_op jit(solution)/shard_map/exchange/pallas_call | solution.py:611
  603.3 2.5 join_blocks.2
  605.8 4.0 join_blocks.3
  610.2 1.9 fusion.20
  612.1 7.5 %reduce-scatter.7.cloned.1.call-done.x_ref = bf16[80,2432]{1,0:T(8,128)(2,1)} async-done(((bf16[320,2432]{1,0:T(8,128)(2,1)}), bf16[80,2432]{1,0:T(8,128)(2,1)}) %reduce-scatter.7.cloned.1.call-update) | async-done | bytes 389136 | tf_op jit(solution)/shard_map/reduce_scatter | solution.py:1592
  619.6 1.9 unpack_sums.1
  621.5 1.4 copy.91
  (186 shorter events, 40.9 us)
Async XLA Ops:
  7.2 97.9 %all-gather.5.cloned.1.call-start = ((), (), s32[]{:S(2)}) async-start(), calls=%async_computation.4 | async-start | bytes 1638400 | tf_op jit(solution)/shard_map/all_gather | solution.py:1430
  7.9 102.4 %all-gather.7.cloned.1.call-start = ((), (), s32[]{:S(2)}) async-start(), calls=%async_computation.5 | async-start | bytes 3276800 | tf_op jit(solution)/shard_map/all_gather | solution.py:1441
  10.9 22.4 %copy-start.25 = (bf16[80,4]{0,1:T(4,128)(2,1)S(1)}, bf16[80,4]{0,1:T(4,128)(2,1)}, u32[]{:S(2)}) copy-start(bf16[80,4]{0,1:T(4,128)(2,1)} %param.24) | copy-start | bytes 1924
  10.9 22.5 %copy-start.28 = (bf16[80]{0:T(256)(128)(2,1)S(1)}, bf16[80]{0:T(256)(128)(2,1)}, u32[]{:S(2)}) copy-start(bf16[80]{0:T(256)(128)(2,1)} %param.25) | copy-start | bytes 484
  11.7 21.8 %copy-start.29 = (bf16[80]{0:T(256)(128)(2,1)S(1)}, bf16[80]{0:T(256)(128)(2,1)}, u32[]{:S(2)}) copy-start(bf16[80]{0:T(256)(128)(2,1)} %param.27) | copy-start | bytes 484
  11.7 21.9 %copy-start.30 = (bf16[80]{0:T(256)(128)(2,1)S(1)}, bf16[80]{0:T(256)(128)(2,1)}, u32[]{:S(2)}) copy-start(bf16[80]{0:T(256)(128)(2,1)} %param.29) | copy-start | bytes 484
  11.7 22.1 %copy-start.31 = (bf16[80]{0:T(256)(128)(2,1)S(1)}, bf16[80]{0:T(256)(128)(2,1)}, u32[]{:S(2)}) copy-start(bf16[80]{0:T(256)(128)(2,1)} %param.30) | copy-start | bytes 484
  11.7 22.2 %copy-start.22 = (bf16[80,160]{1,0:T(8,128)(2,1)S(1)}, bf16[80,160]{1,0:T(8,128)(2,1)}, u32[]{:S(2)}) copy-start(bf16[80,160]{1,0:T(8,128)(2,1)} %param.26) | copy-start | bytes 76804
  11.7 22.2 %copy-start.23 = (bf16[80,160]{1,0:T(8,128)(2,1)S(1)}, bf16[80,160]{1,0:T(8,128)(2,1)}, u32[]{:S(2)}) copy-start(bf16[80,160]{1,0:T(8,128)(2,1)} %param.28) | copy-start | bytes 76804
  31.5 252.6 %all-gather.11.cloned.1.call-start = ((), (), s32[]{:S(2)}) async-start(), calls=%async_computation.7 | async-start | bytes 3932160 | tf_op jit(solution)/shard_map/all_gather | solution.py:1463
  32.2 251.9 %all-gather.9.cloned.1.call-start = ((), (), s32[]{:S(2)}) async-start(), calls=%async_computation.6 | async-start | bytes 7864320 | tf_op jit(solution)/shard_map/all_gather | solution.py:1462
  34.7 67.9 %copy-start.10 = (bf16[256,2048]{1,0:T(8,128)(2,1)S(1)}, bf16[256,2048]{1,0:T(8,128)(2,1)}, u32[]{:S(2)}) copy-start(bf16[256,2048]{1,0:T(8,128)(2,1)} %param.20) | copy-start | bytes 3145732
  100.2 335.4 %reduce-scatter.5.cloned.1.call-start = ((), (), s32[]{:S(2)}) async-start(), calls=%async_computation.8 | async-start | bytes 3932160 | tf_op jit(solution)/shard_map/reduce_scatter | solution.py:1534
  105.0 19.8 %copy-start.24 = (s32[8]{0:T(128)}, s32[8]{0:T(128)S(1)}, u32[]{:S(2)}) copy-start(s32[8]{0:T(128)S(1)} %fusion.62.order_ref) | copy-start | bytes 100
  121.9 36.1 %collective-permute-start.1 = (bf16[256,2048]{1,0:T(8,128)(2,1)S(1)}, bf16[256,2048]{1,0:T(8,128)(2,1)S(1)}, u32[]{:S(2)}, u32[]{:S(2)}) collective-permute-start(bf16[256,2048]{1,0:T(8,128)(2,1)S(1)} %copy-done.10), channel_id=1, source_target_pairs={{0,4},{4,0},{1,5},{5,1},{2,6},{6,2},{3,7},{7,3},{8,12},{12,8},{9,1... | collective-permute-start | bytes 3145736 | tf_op jit(solution)/shard_map/ppermute | solution.py:348
  122.6 35.5 %collective-permute-start.2 = (bf16[256,2048]{1,0:T(8,128)(2,1)S(1)}, bf16[256,2048]{1,0:T(8,128)(2,1)S(1)}, u32[]{:S(2)}, u32[]{:S(2)}) collective-permute-start(bf16[256,2048]{1,0:T(8,128)(2,1)S(1)} %copy-done.10), channel_id=1, source_target_pairs={{0,2},{2,0},{1,3},{3,1},{4,6},{6,4},{5,7},{7,5},{8,10},{10,8},{9,1... | collective-permute-start | bytes 3145736 | tf_op jit(solution)/shard_map/ppermute | solution.py:348
  134.2 6.2 collective-permute-start
  140.4 0.6 copy-start.21
  158.1 1.0 copy-start.14
  158.1 1.3 copy-start.15
  166.4 13.3 %copy-start.2 = (f32[2048,320]{1,0:T(8,128)S(1)}, f32[2048,320]{1,0:T(8,128)}, u32[]{:S(2)}) copy-start(f32[2048,320]{1,0:T(8,128)} %get-tuple-element.134.prod_ref.prod_before_ref) | copy-start | bytes 7864324
  168.4 21.2 %collective-permute-start.3 = (bf16[128,2048]{1,0:T(8,128)(2,1)}, bf16[128,2048]{1,0:T(8,128)(2,1)}, u32[]{:S(2)}, u32[]{:S(2)}) collective-permute-start(bf16[128,2048]{1,0:T(8,128)(2,1)} %slice.216), channel_id=1, source_target_pairs={{0,2},{2,0},{1,3},{3,1},{4,6},{6,4},{5,7},{7,5},{8,10},{10,8},{9,1... | collective-permute-start | bytes 1572872 | tf_op jit(solution)/shard_map/ppermute | solution.py:348
  171.0 18.6 %collective-permute-start.4 = (bf16[128,2048]{1,0:T(8,128)(2,1)}, bf16[128,2048]{1,0:T(8,128)(2,1)}, u32[]{:S(2)}, u32[]{:S(2)}) collective-permute-start(bf16[128,2048]{1,0:T(8,128)(2,1)} %slice.217), channel_id=1, source_target_pairs={{0,4},{4,0},{1,5},{5,1},{2,6},{6,2},{3,7},{7,3},{8,12},{12,8},{9,1... | collective-permute-start | bytes 1572872 | tf_op jit(solution)/shard_map/ppermute | solution.py:348
  173.3 6.3 %copy-start.3 = (f32[2048,320]{1,0:T(8,128)S(1)}, f32[2048,320]{1,0:T(8,128)}, u32[]{:S(2)}) copy-start(f32[2048,320]{1,0:T(8,128)} %get-tuple-element.133.state_ref.state_before_ref) | copy-start | bytes 7864324
  179.6 3.4 copy-start.7
  183.0 6.7 %copy-start.16 = (bf16[2048,320]{1,0:T(8,128)(2,1)}, bf16[2048,320]{1,0:T(8,128)(2,1)S(1)}, u32[]{:S(2)}) copy-start(bf16[2048,320]{1,0:T(8,128)(2,1)S(1)} %fusion.11) | copy-start | bytes 3932164
  193.4 90.7 %collective-permute-start.5 = (bf16[1024,2048]{1,0:T(8,128)(2,1)}, bf16[1024,2048]{1,0:T(8,128)(2,1)}, u32[]{:S(2)}, u32[]{:S(2)}) collective-permute-start(bf16[1024,2048]{1,0:T(8,128)(2,1)} %constant_dynamic-update-slice_fusion.mine_ref), channel_id=1, source_target_pairs={{0,1},{1,0},{2,3},{3,2},{4,5},{5,4},{6,7},{7,6},{8,9},{9,8},{10,11... | collective-permute-start | bytes 12582920 | tf_op jit(solution)/shard_map/ppermute | solution.py:348
  193.4 46.4 %copy-start.1 = (bf16[256,2048]{1,0:T(8,128)(2,1)S(1)}, bf16[256,2048]{1,0:T(8,128)(2,1)}, u32[]{:S(2)}) copy-start(bf16[256,2048]{1,0:T(8,128)(2,1)} %refs_0_.1) | copy-start | bytes 3145732
  239.8 2.3 copy-start
  315.3 10.4 %copy-start.32 = (bf16[2048,1536]{1,0:T(8,128)(2,1)S(1)}, bf16[2048,1536]{1,0:T(8,128)(2,1)}, u32[]{:S(2)}) copy-start(bf16[2048,1536]{1,0:T(8,128)(2,1)} %all-gather.9.cloned.1.call-done.w_ref) | copy-start | bytes 18874372
  315.3 10.4 %copy-start.33 = (bf16[2048,1536]{1,0:T(8,128)(2,1)S(1)}, bf16[2048,1536]{1,0:T(8,128)(2,1)}, u32[]{:S(2)}) copy-start(bf16[2048,1536]{1,0:T(8,128)(2,1)} %get-tuple-element.165) | copy-start | bytes 18874372
  325.2 7.6 %collective-permute-start.6 = (bf16[1024,2048]{1,0:T(8,128)(2,1)S(1)}, bf16[1024,2048]{1,0:T(8,128)(2,1)S(1)}, u32[]{:S(2)}, u32[]{:S(2)}) collective-permute-start(bf16[1024,2048]{1,0:T(8,128)(2,1)S(1)} %convolution_convert_fusion.3), channel_id=1, source_target_pairs={{0,1},{1,0},{2,3},{3,2},{4,5},{5,4},{6,7},{7,6},{8,9},{9,8},{10,11... | collective-permute-start | bytes 12582920 | tf_op jit(solution)/shard_map/ppermute | solution.py:348
  332.9 11.4 %copy-start.9 = (bf16[1024,2048]{1,0:T(8,128)(2,1)}, bf16[1024,2048]{1,0:T(8,128)(2,1)S(1)}, u32[]{:S(2)}) copy-start(bf16[1024,2048]{1,0:T(8,128)(2,1)S(1)} %convolution_convert_fusion.2) | copy-start | bytes 12582916
  332.9 2.7 copy-start.8
  335.5 3.5 copy-start.11
  336.9 30.6 %collective-permute-start.7 = (bf16[2,128,2048]{2,1,0:T(8,128)(2,1)}, bf16[2,128,2048]{2,1,0:T(8,128)(2,1)}, u32[]{:S(2)}, u32[]{:S(2)}) collective-permute-start(bf16[2,128,2048]{2,1,0:T(8,128)(2,1)} %get-tuple-element.158), channel_id=1, source_target_pairs={{0,4},{4,0},{1,5},{5,1},{2,6},{6,2},{3,7},{7,3},{8,12},{12,8},{9,1... | collective-permute-start | bytes 3145736 | tf_op jit(solution)/shard_map/ppermute | solution.py:348
  338.0 29.5 %collective-permute-start.8 = (bf16[2,128,2048]{2,1,0:T(8,128)(2,1)}, bf16[2,128,2048]{2,1,0:T(8,128)(2,1)}, u32[]{:S(2)}, u32[]{:S(2)}) collective-permute-start(bf16[2,128,2048]{2,1,0:T(8,128)(2,1)} %get-tuple-element.159), channel_id=1, source_target_pairs={{0,2},{2,0},{1,3},{3,1},{4,6},{6,4},{5,7},{7,5},{8,10},{10,8},{9,1... | collective-permute-start | bytes 3145736 | tf_op jit(solution)/shard_map/ppermute | solution.py:348
  351.7 180.3 %reduce-scatter.9.cloned.1.call-start = ((), (), s32[]{:S(2)}) async-start(), calls=%async_computation.10 | async-start | bytes 7864320 | tf_op jit(solution)/shard_map/reduce_scatter | solution.py:1548
  367.5 24.9 %slice-start = ((s8[8388608]{0:T(1024)(128)(4,1)}), s8[4194304]{0:T(1024)(128)(4,1)S(1)}, s32[]{:S(2)}) async-start(s8[8388608]{0:T(1024)(128)(4,1)} %bitcast.164), calls=%async_computation.12 | async-start | bytes 8388608
  384.2 2.3 copy-start.4
  384.2 8.3 %slice-start.1 = ((s8[8388608]{0:T(1024)(128)(4,1)}), s8[4194304]{0:T(1024)(128)(4,1)S(1)}, s32[]{:S(2)}) async-start(s8[8388608]{0:T(1024)(128)(4,1)} %bitcast.164), calls=%async_computation.13 | async-start | bytes 8388608
  390.5 18.7 %collective-permute-start.11 = (bf16[1024,2048]{1,0:T(8,128)(2,1)}, bf16[1024,2048]{1,0:T(8,128)(2,1)}, u32[]{:S(2)}, u32[]{:S(2)}) collective-permute-start(bf16[1024,2048]{1,0:T(8,128)(2,1)} %get-tuple-element.167), channel_id=1, source_target_pairs={{0,1},{1,0},{2,3},{3,2},{4,5},{5,4},{6,7},{7,6},{8,9},{9,8},{10,11... | collective-permute-start | bytes 12582920 | tf_op jit(solution)/shard_map/ppermute | solution.py:348
  390.5 25.9 %collective-permute-start.9 = (bf16[256,2048]{1,0:T(8,128)(2,1)}, bf16[256,2048]{1,0:T(8,128)(2,1)}, u32[]{:S(2)}, u32[]{:S(2)}) collective-permute-start(bf16[256,2048]{1,0:T(8,128)(2,1)} %get-tuple-element.164.x_ref), channel_id=1, source_target_pairs={{0,4},{4,0},{1,5},{5,1},{2,6},{6,2},{3,7},{7,3},{8,12},{12,8},{9,1... | collective-permute-start | bytes 3145736 | tf_op jit(solution)/shard_map/ppermute | solution.py:348
  391.3 25.6 %collective-permute-start.10 = (bf16[256,2048]{1,0:T(8,128)(2,1)}, bf16[256,2048]{1,0:T(8,128)(2,1)}, u32[]{:S(2)}, u32[]{:S(2)}) collective-permute-start(bf16[256,2048]{1,0:T(8,128)(2,1)} %get-tuple-element.164.x_ref), channel_id=1, source_target_pairs={{0,2},{2,0},{1,3},{3,1},{4,6},{6,4},{5,7},{7,5},{8,10},{10,8},{9,1... | collective-permute-start | bytes 3145736 | tf_op jit(solution)/shard_map/ppermute | solution.py:348
  417.0 174.6 %reduce-scatter.11.cloned.1.call-start = ((), (), s32[]{:S(2)}) async-start(), calls=%async_computation.11 | async-start | bytes 3276800 | tf_op jit(solution)/shard_map/reduce_scatter | solution.py:1585
  435.6 29.3 %collective-permute-start.15 = (bf16[2,128,2048]{2,1,0:T(8,128)(2,1)}, bf16[2,128,2048]{2,1,0:T(8,128)(2,1)S(1)}, u32[]{:S(2)}, u32[]{:S(2)}) collective-permute-start(bf16[2,128,2048]{2,1,0:T(8,128)(2,1)} %get-tuple-element.181), channel_id=1, source_target_pairs={{0,4},{4,0},{1,5},{5,1},{2,6},{6,2},{3,7},{7,3},{8,12},{12,8},{9,1... | collective-permute-start | bytes 3145736 | tf_op jit(solution)/shard_map/ppermute | solution.py:348
  436.5 28.4 %collective-permute-start.16 = (bf16[2,128,2048]{2,1,0:T(8,128)(2,1)}, bf16[2,128,2048]{2,1,0:T(8,128)(2,1)S(1)}, u32[]{:S(2)}, u32[]{:S(2)}) collective-permute-start(bf16[2,128,2048]{2,1,0:T(8,128)(2,1)} %get-tuple-element.182), channel_id=1, source_target_pairs={{0,2},{2,0},{1,3},{3,1},{4,6},{6,4},{5,7},{7,5},{8,10},{10,8},{9,1... | collective-permute-start | bytes 3145736 | tf_op jit(solution)/shard_map/ppermute | solution.py:348
  455.3 8.2 %collective-permute-start.12 = (f32[8,320]{1,0:T(8,128)}, f32[8,320]{1,0:T(8,128)S(1)}, u32[]{:S(2)}, u32[]{:S(2)}) collective-permute-start(f32[8,320]{1,0:T(8,128)} %get-tuple-element.180), channel_id=1, source_target_pairs={{24,0},{25,1},{26,2},{27,3},{28,4},{29,5},{30,6},{31,7}} | collective-permute-start | bytes 30728 | tf_op jit(solution)/shard_map/ppermute | solution.py:1557
  456.6 8.3 %collective-permute-start.13 = (f32[8,320]{1,0:T(8,128)}, f32[8,320]{1,0:T(8,128)S(1)}, u32[]{:S(2)}, u32[]{:S(2)}) collective-permute-start(f32[8,320]{1,0:T(8,128)} %get-tuple-element.180), channel_id=1, source_target_pairs={{16,0},{24,8},{17,1},{25,9},{18,2},{26,10},{19,3},{27,11},{20,4},{... | collective-permute-start | bytes 30728 | tf_op jit(solution)/shard_map/ppermute | solution.py:1557
  457.9 7.0 %collective-permute-start.14 = (f32[8,320]{1,0:T(8,128)}, f32[8,320]{1,0:T(8,128)S(1)}, u32[]{:S(2)}, u32[]{:S(2)}) collective-permute-start(f32[8,320]{1,0:T(8,128)} %get-tuple-element.180), channel_id=1, source_target_pairs={{8,0},{16,8},{24,16},{9,1},{17,9},{25,17},{10,2},{18,10},{26,18},{... | collective-permute-start | bytes 30728 | tf_op jit(solution)/shard_map/ppermute | solution.py:1557
  464.9 32.2 %copy-start.18 = (bf16[2,128,2048]{2,1,0:T(8,128)(2,1)}, bf16[2,128,2048]{2,1,0:T(8,128)(2,1)S(1)}, u32[]{:S(2)}) copy-start(bf16[2,128,2048]{2,1,0:T(8,128)(2,1)S(1)} %collective-permute-done.15) | copy-start | bytes 3145732
  464.9 32.2 %copy-start.19 = (bf16[2,128,2048]{2,1,0:T(8,128)(2,1)}, bf16[2,128,2048]{2,1,0:T(8,128)(2,1)S(1)}, u32[]{:S(2)}) copy-start(bf16[2,128,2048]{2,1,0:T(8,128)(2,1)S(1)} %collective-permute-done.16) | copy-start | bytes 3145732
  465.8 23.5 %copy-start.17 = (bf16[2048,320]{1,0:T(8,128)(2,1)S(1)}, bf16[2048,320]{1,0:T(8,128)(2,1)}, u32[]{:S(2)}) copy-start(bf16[2048,320]{1,0:T(8,128)(2,1)} %copy-done.16) | copy-start | bytes 3932164
  488.0 15.4 %collective-permute-start.17 = (f32[8,320]{1,0:T(8,128)}, f32[8,320]{1,0:T(8,128)S(1)}, u32[]{:S(2)}, u32[]{:S(2)}) collective-permute-start(f32[8,320]{1,0:T(8,128)} %get-tuple-element.186), channel_id=1, source_target_pairs={{8,0},{16,8},{24,16},{9,1},{17,9},{25,17},{10,2},{18,10},{26,18},{... | collective-permute-start | bytes 30728 | tf_op jit(solution)/shard_map/ppermute | solution.py:1570
  497.2 6.3 copy-start.12
  500.4 15.7 %collective-permute-start.18 = (bf16[128,2048]{1,0:T(8,128)(2,1)}, bf16[128,2048]{1,0:T(8,128)(2,1)}, u32[]{:S(2)}, u32[]{:S(2)}) collective-permute-start(bf16[128,2048]{1,0:T(8,128)(2,1)} %get-tuple-element.299), channel_id=1, source_target_pairs={{0,2},{2,0},{1,3},{3,1},{4,6},{6,4},{5,7},{7,5},{8,10},{10,8},{9,1... | collective-permute-start | bytes 1572872 | tf_op jit(solution)/shard_map/ppermute | solution.py:348
  501.9 14.2 %collective-permute-start.19 = (bf16[128,2048]{1,0:T(8,128)(2,1)}, bf16[128,2048]{1,0:T(8,128)(2,1)}, u32[]{:S(2)}, u32[]{:S(2)}) collective-permute-start(bf16[128,2048]{1,0:T(8,128)(2,1)} %get-tuple-element.298), channel_id=1, source_target_pairs={{0,4},{4,0},{1,5},{5,1},{2,6},{6,2},{3,7},{7,3},{8,12},{12,8},{9,1... | collective-permute-start | bytes 1572872 | tf_op jit(solution)/shard_map/ppermute | solution.py:348
  503.5 1.6 copy-start.13
  516.1 103.4 %reduce-scatter.7.cloned.1.call-start = ((), (), s32[]{:S(2)}) async-start(), calls=%async_computation.9 | async-start | bytes 1945600 | tf_op jit(solution)/shard_map/reduce_scatter | solution.py:1592
  516.2 2.0 copy-start.20
  529.1 1.5 copy-start.26
  529.1 2.2 copy-start.27
  591.6 18.2 %copy-start.5 = (f32[256,2048]{1,0:T(8,128)S(1)}, f32[256,2048]{1,0:T(8,128)}, u32[]{:S(2)}) copy-start(f32[256,2048]{1,0:T(8,128)} %get-tuple-element.215) | copy-start | bytes 6291460
  605.8 4.4 copy-start.6
Sparse Core Ops, SparseCore 0:
  9.6 35.3 all-gather.4
  47.2 54.0 all-gather.6
  102.8 63.1 all-gather.10
  167.4 113.9 all-gather.8
  351.8 58.7 reduce-scatter.4
  417.1 110.3 reduce-scatter.8
  529.8 52.5 reduce-scatter.10
  584.7 34.8 reduce-scatter.6
